TPU v7x, 128 devices: a whole 4x4x4 slice. The times are simulated.
128 devices in a mesh: seq: 16 (over y, z), head: 4 (over x), batch: 2 (over core).
Axes of the slice: x: 4, y: 4, z: 4, core: 2. Of those that a mesh axis runs over, the one named last changes fastest.
Arguments:
- tokens: bfloat16 [16384, 2560], P(('batch', 'seq'), 'head'), parts along dimension 0, may hold values from -6 to 6
- resets: int32 [16384], P(('batch', 'seq')), parts along dimension 0, may hold values 0 or 1
- w_x: bfloat16 [2560, 5120], P(None, 'head'), may hold values from -0.125 to 0.125
- w_z: bfloat16 [2560, 5120], P(None, 'head'), may hold values from -0.125 to 0.125
- w_bc: bfloat16 [2560, 256], replicated, may hold values from -0.125 to 0.125
- w_dt: bfloat16 [2560, 80], P(None, 'head'), may hold values from -0.125 to 0.125
- dt_bias: float32 [80], P('head'), may hold values from -2 to 1
- decay_rate: float32 [80], P('head'), may hold values from 6.1035156e-05 to 0.08
- d_skip: float32 [80], P('head'), may hold values from 0.5 to 1.5
- norm_gain: float32 [5120], P('head'), may hold values from 0.5 to 1.5
- w_out: bfloat16 [5120, 2560], P('head'), may hold values from -0.078125 to 0.078125
Outputs:
- mixed: bfloat16 [16384, 2560], P(('batch', 'seq'), 'head'), parts along dimension 0
There are 2 independent parts, one for each index of `batch`. A program takes and returns all parts, laid end to end along the dimension named above; an argument that names none is the same for every part. Nothing has to cross between parts.
All inputs are finite; a program needn't handle non-finite values. No bound on the sum of `resets` on one device may be relied on, other than what follows from the above.
Results may differ from a plain program's by a relative error of at most 0.013.
Values may be sent and summed in bfloat16 or wider, within the bound.
No kernel may reach another device: no remote copies, remote signals or barrier semaphores. Data moves between devices by JAX's collectives and lax.ppermute only.
A program may use at most 128 MiB of HBM per device.

v0:
```python
import jax
import jax.numpy as jnp
from jax import lax
from jax.sharding import Mesh
from jax.sharding import PartitionSpec as P

DI = 5120
HEADDIM = 64
NSTATE = 128
GROUP = 256
SEQ = ("seq_0", "seq_1")
BATCH_SEQ = ("batch", "seq_0", "seq_1")


def sent_to_all(array, axis):
    copies = jnp.broadcast_to(array, (lax.axis_size(axis), *array.shape))
    return lax.all_to_all(copies, axis, split_axis=0, concat_axis=0, tiled=True)


def laid_out(blocks, dim):
    blocks = jnp.moveaxis(blocks, 0, dim)
    dims = blocks.shape
    return blocks.reshape(*dims[:dim], dims[dim] * dims[dim + 1], *dims[dim + 2 :])


def gathered_copies(array, axis, dim):
    blocks = sent_to_all(array, axis)
    return laid_out(blocks, dim)


def neutral_like(array, identity):
    return jax.tree.map(
        lambda part, zero: jnp.zeros_like(part) + jnp.asarray(zero, part.dtype), array, identity
    )


def carried_in(array, axes, combine, identity):
    before = start = neutral_like(array, identity)
    so_far = array
    for axis in reversed(axes):
        count, mine = (lax.axis_size(axis), lax.axis_index(axis))
        pieces = jax.tree.map(lambda part: lax.all_gather(part, axis), so_far)
        inside, so_far = (start, start)
        for k in range(count):
            passed = k < mine
            so_far = combine(so_far, jax.tree.map(lambda part: part[k], pieces))
            inside = jax.tree.map(lambda new, old: jnp.where(passed, new, old), so_far, inside)
        before = combine(inside, before)
    return before


def over_copies(array, axis):
    everything = sent_to_all(array, axis)
    return jnp.sum(everything, axis=0)


def decay_block(inputs, step_size, log_decay, in_proj, out_proj, restart, state_in):
    cumulative = jnp.cumsum(log_decay, axis=0)
    segment = jnp.cumsum(restart)
    places = jnp.arange(restart.shape[0], dtype=jnp.int32)
    same_doc = (segment[:, None] == segment[None, :]) & (places[:, None] >= places[None, :])
    scores = jnp.dot(out_proj, in_proj.T, preferred_element_type=jnp.float32)
    spread = cumulative.T[:, :, None] - cumulative.T[:, None, :]
    factor = jnp.exp(jnp.where(same_doc[None], spread, -jnp.inf))
    mixing = (factor * scores[None] * step_size.T[:, None, :]).astype(jnp.bfloat16)
    output = jnp.einsum("hts,shp->thp", mixing, inputs, preferred_element_type=jnp.float32)
    entering = jnp.where((segment == 0)[:, None], jnp.exp(cumulative), 0.0)
    carried = jnp.einsum(
        "tn,hpn->thp", out_proj.astype(jnp.float32), state_in, precision=lax.Precision.HIGHEST
    )
    output = output + entering[:, :, None] * carried
    closing = segment[-1]
    keeping = (
        jnp.where((segment == closing)[:, None], jnp.exp(cumulative[-1][None, :] - cumulative), 0.0)
        * step_size
    )
    scaled = (keeping[:, :, None] * inputs.astype(jnp.float32)).astype(jnp.bfloat16)
    update = jnp.einsum("shp,sn->hpn", scaled, in_proj, preferred_element_type=jnp.float32)
    through = jnp.where(closing == 0, jnp.exp(cumulative[-1]), 0.0)
    return (output, update + through[:, None, None] * state_in)


def on_device(tokens, resets, w_x, w_z, w_bc, w_dt, dt_bias, decay_rate, d_skip, norm_gain, w_out):
    tok_rows = tokens.shape[0]
    heads_dev = w_dt.shape[1]
    width_dev = w_x.shape[1]
    column_piece = gathered_copies(tokens, "head", 1)
    acc_inner, acc_gate, acc_mapped, acc_step = tuple(
        (
            jnp.dot(column_piece, matrix, preferred_element_type=jnp.float32)
            for matrix in (w_x, w_z, w_bc, w_dt)
        )
    )
    inner = jax.nn.silu(acc_inner).astype(jnp.bfloat16)
    gating = acc_gate.astype(jnp.bfloat16)
    mapped = jax.nn.silu(acc_mapped).astype(jnp.bfloat16)
    step_size = jax.nn.softplus(acc_step + dt_bias)
    log_decay = -step_size * decay_rate
    blocks = tok_rows // GROUP
    out_proj = mapped[:, NSTATE:]
    sliced = (
        inner.reshape(blocks, GROUP, heads_dev, HEADDIM),
        step_size.reshape(blocks, GROUP, heads_dev),
        log_decay.reshape(blocks, GROUP, heads_dev),
        mapped[:, :NSTATE].reshape(blocks, GROUP, NSTATE),
        out_proj.reshape(blocks, GROUP, NSTATE),
        resets.reshape(blocks, GROUP),
    )

    def advance(state_in, pieces):
        output, state_out = decay_block(
            pieces[0], pieces[1], pieces[2], pieces[3], pieces[4], pieces[5], state_in
        )
        return (state_out, output)

    final_state, outputs = lax.scan(
        advance, jnp.zeros((heads_dev, HEADDIM, NSTATE), jnp.float32), sliced
    )
    cumulative = jnp.cumsum(log_decay, axis=0)
    segment = jnp.cumsum(resets)
    through = jnp.where(segment[-1] == 0, jnp.exp(cumulative[-1]), 0.0)

    def compose(earlier, latter):
        return (earlier[0] * latter[0], latter[0][:, None, None] * earlier[1] + latter[1])

    prefix = carried_in(
        (through, final_state), SEQ, compose, (jnp.ones_like(through), jnp.zeros_like(final_state))
    )
    incoming = prefix[1]
    entering = jnp.where((segment == 0)[:, None], jnp.exp(cumulative), 0.0)
    carried = jnp.einsum(
        "tn,hpn->thp", out_proj.astype(jnp.float32), incoming, precision=lax.Precision.HIGHEST
    )
    mixed_heads = (
        outputs.reshape(tok_rows, heads_dev, HEADDIM)
        + entering[:, :, None] * carried
        + d_skip[None, :, None] * inner.reshape(tok_rows, heads_dev, HEADDIM).astype(jnp.float32)
    )
    gated = mixed_heads.reshape(tok_rows, width_dev) * jax.nn.silu(gating.astype(jnp.float32))
    squares = over_copies(jnp.sum(gated * gated, axis=1), "head")
    normed = (gated * lax.rsqrt(squares[:, None] / DI + 1e-05) * norm_gain).astype(jnp.bfloat16)
    partial_terms = jnp.dot(normed, w_out, preferred_element_type=jnp.float32)
    result = lax.psum_scatter(partial_terms, "head", scatter_dimension=1, tiled=True)
    return result.astype(jnp.bfloat16)


def solution(mesh):
    split = Mesh(
        mesh.devices.reshape(4, 4, mesh.shape["head"], mesh.shape["batch"]),
        ("seq_0", "seq_1", "head", "batch"),
    )
    placed = (
        P(BATCH_SEQ, "head"),
        P(BATCH_SEQ),
        P(None, "head"),
        P(None, "head"),
        P(),
        P(None, "head"),
        P("head"),
        P("head"),
        P("head"),
        P("head"),
        P("head", None),
    )
    return jax.shard_map(
        on_device, mesh=split, in_specs=placed, out_specs=P(BATCH_SEQ, "head"), check_vma=False
    )
```

profile of v0, /device:TPU:0, one launch (start us, length us, event | category | flops | bytes accessed | tf_op | source)
XLA Modules:
  0.0 324.4 jit_solution(15444057808073170419)
XLA Ops:
  6.5 1.4 copy.74
  8.0 1.7 broadcast_in_dim.83
  9.7 4.7 %all-to-all-start = ((bf16[4,512,640]{1,2,0:T(8,128)(2,1)}), bf16[4,512,640]{1,2,0:T(8,128)(2,1)}, u32[]{:S(2)}, u32[]{:S(2)}) async-start(bf16[4,512,640]{1,2,0:T(8,128)(2,1)} %broadcast_in_dim.83), calls=%async_computation | async-start | bytes 5242880 | tf_op jit(solution)/shard_map/all_to_all | solution.py:17
  14.5 32.1 %all-to-all-done = bf16[4,512,640]{1,2,0:T(8,128)(2,1)} async-done(((bf16[4,512,640]{1,2,0:T(8,128)(2,1)}), bf16[4,512,640]{1,2,0:T(8,128)(2,1)}, u32[]{:S(2)}, u32[]{:S(2)}) %all-to-all-start) | async-done | bytes 2621472 | tf_op jit(solution)/shard_map/all_to_all | solution.py:17
  46.6 8.7 %multiply_convert_fusion.6 = bf16[512,1280]{1,0:T(8,128)(2,1)} fusion(bf16[512,2560]{0,1:T(8,128)(2,1)} %bitcast.1, bf16[2560,1280]{1,0:T(8,128)(2,1)} %param.15), kind=kOutput, calls=%fused_computation.65 | convolution fusion | flops 3358720000 | bytes 10485760 | tf_op jit(solution)/shard_map/dot_general | solution.py:90
  55.3 2.8 compare_select_fusion.1
  58.1 1.6 copy.75
  59.8 1.3 reshape.258
  61.0 1.6 copy.78
  62.6 2.6 multiply_convert_fusion.8
  65.3 0.7 copy-done.9
  65.9 0.7 fusion.108
  66.6 80.5 %while.13 = (s32[]{:T(128)}, f32[20,64,128]{2,1,0:T(8,128)S(1)}, f32[2,256,20,64]{1,0,3,2:T(2,128)}, s32[2,256]{1,0:T(2,128)S(1)}, f32[2,256,20]{1,0,2:T(2,128)S...) while((s32[]{:T(128)}, f32[20,64,128]{2,1,0:T(8,128)S(1)}, ...), condition=%wide.region_5.6_spmd.clone, body=%wide.region_0.5_spmd.clone.sunk | while | flops 781505152 | bytes 25446028 | solution.py:116
  66.7 0.7 copy.113
  67.4 1.1 fusion.136
  68.5 0.6 reduce-window.56
  69.1 0.2 slice_reduce_fusion.9
  69.5 0.6 copy.112
  70.1 0.3 reduce-window.54
  70.5 0.1 slice_reduce_fusion.8
  70.8 2.3 fusion.138
  73.1 0.2 slice_reduce_fusion.10
  73.3 0.6 slice.253
  73.9 0.6 broadcast_compare_fusion.6
  74.7 1.5 fusion.139
  76.8 1.5 convolution_add_fusion.3
  78.4 1.3 copy.114
  79.7 27.1 %dynamic_update_slice.6 = f32[2,256,20,64]{1,0,3,2:T(2,128)} dynamic-update-slice(f32[2,256,20,64]{1,0,3,2:T(2,128)} %get-tuple-element.263, f32[1,256,20,64]{1,0,3,2:T(1,128)S(1)} %copy.114, s32[]{:T(128)S(6)} %copy.119, s32[]{:T(128)} %constant.46.clone.1..sunk, s32[]{:T(128)} %constant.46.clone.1..sunk, s32[]{:T(128)} %constant.46.clone.1..sunk) | dynamic-update-slice | bytes 2621444 | tf_op jit(solution)/shard_map/while/body/jit(dynamic_update_index_in_dim)/dynamic_update_slice | solution.py:116
  107.0 0.7 copy.113
  107.7 1.0 fusion.136
  108.8 0.6 reduce-window.56
  109.4 0.2 slice_reduce_fusion.9
  109.7 0.6 copy.112
  110.3 0.3 reduce-window.54
  111.1 2.3 fusion.138
  113.4 0.2 slice_reduce_fusion.10
  113.6 0.6 slice.253
  114.2 0.6 broadcast_compare_fusion.6
  114.9 1.5 fusion.139
  117.1 1.5 convolution_add_fusion.3
  118.6 1.3 copy.114
  120.0 27.1 %dynamic_update_slice.6 = f32[2,256,20,64]{1,0,3,2:T(2,128)} dynamic-update-slice(f32[2,256,20,64]{1,0,3,2:T(2,128)} %get-tuple-element.263, f32[1,256,20,64]{1,0,3,2:T(1,128)S(1)} %copy.114, s32[]{:T(128)S(6)} %copy.119, s32[]{:T(128)} %constant.46.clone.1..sunk, s32[]{:T(128)} %constant.46.clone.1..sunk, s32[]{:T(128)} %constant.46.clone.1..sunk) | dynamic-update-slice | bytes 2621444 | tf_op jit(solution)/shard_map/while/body/jit(dynamic_update_index_in_dim)/dynamic_update_slice | solution.py:116
  147.2 0.8 copy-done.2
  148.0 0.2 all-gather.6.cloned.1.call-start
  148.3 0.3 reduce-window.34
  148.9 0.7 slice.99
  150.2 0.9 fusion.98
  151.1 1.2 reduce-window.38
  152.3 0.2 slice_reduce_fusion.3
  152.6 0.2 fusion.104
  152.8 11.1 %all-gather.1 = f32[4,1,20]{2,1,0:T(1,128)S(1)} all-gather(f32[1,1,20]{2,1,0:T(1,128)S(1)} %bitcast.225), channel_id=1, replica_groups=mesh['seq_0'=4,'seq_1'=4,'head'=4,'batch'=2] {'seq_1'}, dimensions={0}, use_global_device_ids=true | all-gather | bytes 400 | tf_op jit(solution)/shard_map/all_gather | solution.py:42
  164.0 20.3 %all-gather.8.cloned.1.call-done = f32[80,64,128]{2,1,0:T(8,128)} async-done(((f32[20,64,128]{2,1,0:T(8,128)}), f32[80,64,128]{2,1,0:T(8,128)}) %all-gather.8.cloned.1.call-update) | async-done | bytes 2621456 | tf_op jit(solution)/shard_map/all_gather | solution.py:42
  184.3 2.8 bitcast_add_fusion
  187.2 1.9 copy.82
  189.1 4.8 %reshape.261 = f32[512,20,64]{0,2,1:T(8,128)} reshape(f32[2,256,20,64]{1,0,3,2:T(2,128)} %get-tuple-element.53) | data formatting | bytes 5242880 | tf_op jit(solution)/shard_map/reshape | solution.py:135
  193.9 9.6 %all-gather.2 = f32[4,1,20]{2,1,0:T(1,128)S(1)} all-gather(f32[1,1,20]{2,1,0:T(1,128)S(1)} %get-tuple-element.175), channel_id=1, replica_groups=mesh['seq_0'=4,'seq_1'=4,'head'=4,'batch'=2] {'seq_0'}, dimensions={0}, use_global_device_ids=true | all-gather | bytes 400 | tf_op jit(solution)/shard_map/all_gather | solution.py:42
  203.5 18.9 %all-gather.6.cloned.1.call-done = f32[4,20,64,128]{3,2,1,0:T(8,128)} async-done(((f32[1,20,64,128]{3,2,1,0:T(8,128)}), f32[4,20,64,128]{3,2,1,0:T(8,128)}) %all-gather.6.cloned.1.call-update) | async-done | bytes 2621456 | tf_op jit(solution)/shard_map/all_gather | solution.py:42
  222.4 7.4 %multiply_add_fusion = f32[512,20,64]{0,2,1:T(8,128)} fusion(f32[512,20,64]{0,2,1:T(8,128)} %bitcast.213, f32[512,20,64]{0,2,1:T(8,128)} %reshape.261, f32[20]{0:T(128)S(1)} %copy-done.19, f32[512,20]{0,1:T(8,128)S(1)} %exponential_select_fusion.1, f32[4,20,64,128]{3,2,1,0:T(8,128)} %all-gather.6.cloned.1.call-done, ...), kind=kOutput, calls=%fused_computation.64 | convolution fusion | flops 1013186560 | bytes 13292552 | tf_op jit(solution)/shard_map/tn,hpn->thp/dot_general | solution.py:131
  229.8 3.2 copy.83
  233.0 9.9 %multiply_reduce_fusion = (f32[512]{0:T(512)S(1)}, f32[512,1280]{1,0:T(8,128)}) fusion(f32[512,1280]{1,0:T(8,128)} %copy.83, bf16[512,2560]{0,1:T(8,128)(2,1)} %bitcast.1, bf16[2560,1280]{1,0:T(8,128)(2,1)} %param.16), kind=kOutput, calls=%fused_computation.63 | convolution fusion | flops 3361340928 | bytes 14419968 | tf_op jit(solution)/shard_map/dot_general | solution.py:90
  242.9 9.4 %all_to_all.11 = f32[4,1,512]{2,1,0:T(1,128)S(1)} all-to-all(f32[4,1,512]{2,1,0:T(1,128)S(1)} %broadcast_in_dim.86), channel_id=1, replica_groups=mesh['seq_0'=4,'seq_1'=4,'head'=4,'batch'=2] {'head'}, dimensions={0} | all-to-all | bytes 16384 | tf_op jit(solution)/shard_map/all_to_all | solution.py:17
  252.3 9.6 %fusion.40 = f32[512,2560]{1,0:T(8,128)} fusion(bf16[1280,2560]{1,0:T(8,128)(2,1)} %param.23, f32[512,1280]{1,0:T(8,128)} %get-tuple-element.181, f32[1280]{0:T(1024)S(1)} %copy-done.20, f32[512]{0:T(512)S(1)} %add_rsqrt_fusion), kind=kOutput, calls=%fused_computation.66 | convolution fusion | flops 3357409280 | bytes 14425088 | tf_op jit(solution)/shard_map/dot_general | solution.py:142
  261.9 53.8 %reduce-scatter.2.cloned.1.call-done = f32[512,640]{1,0:T(8,128)} async-done(((f32[512,2560]{1,0:T(8,128)}), f32[512,640]{1,0:T(8,128)}) %reduce-scatter.2.cloned.1.call-update) | async-done | bytes 1310736 | tf_op jit(solution)/shard_map/reduce_scatter | solution.py:143
  315.7 2.2 convert_element_type.46
  (120 shorter events, 2.2 us)
Async XLA Ops:
  6.5 56.0 %copy-start = (bf16[2560,256]{1,0:T(8,128)(2,1)S(1)}, bf16[2560,256]{1,0:T(8,128)(2,1)}, u32[]{:S(2)}) copy-start(bf16[2560,256]{1,0:T(8,128)(2,1)} %param.17) | copy-start | bytes 3932164
  9.7 4.8 %copy-start.16 = (s32[512]{0:T(512)S(1)}, s32[512]{0:T(512)}, u32[]{:S(2)}) copy-start(s32[512]{0:T(512)} %param.14) | copy-start | bytes 6148
  9.7 36.9 %all-to-all-start = ((bf16[4,512,640]{1,2,0:T(8,128)(2,1)}), bf16[4,512,640]{1,2,0:T(8,128)(2,1)}, u32[]{:S(2)}, u32[]{:S(2)}) async-start(bf16[4,512,640]{1,2,0:T(8,128)(2,1)} %broadcast_in_dim.83), calls=%async_computation | async-start | bytes 5242880 | tf_op jit(solution)/shard_map/all_to_all | solution.py:17
  14.4 169.9 %all-gather.8.cloned.1.call-start = ((), (), s32[]{:S(2)}) async-start(), calls=%async_computation.5 | async-start | bytes 3276800 | tf_op jit(solution)/shard_map/all_gather | solution.py:42
  46.6 8.7 %copy-start.15 = (bf16[2560,20]{0,1:T(8,128)(2,1)S(1)}, bf16[2560,20]{0,1:T(8,128)(2,1)}, u32[]{:S(2)}) copy-start(bf16[2560,20]{0,1:T(8,128)(2,1)} %param.18) | copy-start | bytes 307204
  46.6 8.7 %copy-start.17 = (f32[20]{0:T(128)S(1)}, f32[20]{0:T(128)}, u32[]{:S(2)}) copy-start(f32[20]{0:T(128)} %param.20) | copy-start | bytes 244
  46.6 8.7 %copy-start.18 = (f32[20]{0:T(128)S(1)}, f32[20]{0:T(128)}, u32[]{:S(2)}) copy-start(f32[20]{0:T(128)} %param.19) | copy-start | bytes 244
  65.2 0.7 copy-start.9
  66.6 0.8 copy-start.11
  66.6 0.8 copy-start.13
  66.7 6.4 %copy-start.3 = (bf16[2,256,20,64]{1,3,2,0:T(8,128)(2,1)}, bf16[2,256,20,64]{1,3,2,0:T(8,128)(2,1)S(1)}, u32[]{:S(2)}) copy-start(bf16[2,256,20,64]{1,3,2,0:T(8,128)(2,1)S(1)} %get-tuple-element.279) | copy-start | bytes 3932164 | tf_op jit(solution)/shard_map/while
  66.7 1.8 copy-start.6
  70.8 2.3 copy-start.8
  70.8 3.8 %copy-start.7 = (f32[1,256,20]{1,0,2:T(1,128)S(1)}, f32[1,256,20]{1,0,2:T(1,128)}, u32[]{:S(2)}) copy-start(f32[1,256,20]{1,0,2:T(1,128)} %copy-done.6) | copy-start | bytes 61444 | tf_op jit(solution)/shard_map/while
  78.3 28.5 %copy-start.12 = (f32[2,256,20]{1,0,2:T(2,128)S(1)}, f32[2,256,20]{1,0,2:T(2,128)}, u32[]{:S(2)}) copy-start(f32[2,256,20]{1,0,2:T(2,128)} %copy-done.11) | copy-start | bytes 122884 | tf_op jit(solution)/shard_map/while
  78.4 28.5 %copy-start.14 = (f32[2,256,20]{1,0,2:T(2,128)S(1)}, f32[2,256,20]{1,0,2:T(2,128)}, u32[]{:S(2)}) copy-start(f32[2,256,20]{1,0,2:T(2,128)} %copy-done.13) | copy-start | bytes 122884 | tf_op jit(solution)/shard_map/while
  79.7 27.2 %copy-start.4 = (bf16[2,256,20,64]{1,3,2,0:T(8,128)(2,1)S(1)}, bf16[2,256,20,64]{1,3,2,0:T(8,128)(2,1)}, u32[]{:S(2)}) copy-start(bf16[2,256,20,64]{1,3,2,0:T(8,128)(2,1)} %copy-done.3) | copy-start | bytes 3932164 | tf_op jit(solution)/shard_map/while
  106.9 0.8 copy-start.11
  106.9 0.8 copy-start.13
  106.9 6.5 %copy-start.3 = (bf16[2,256,20,64]{1,3,2,0:T(8,128)(2,1)}, bf16[2,256,20,64]{1,3,2,0:T(8,128)(2,1)S(1)}, u32[]{:S(2)}) copy-start(bf16[2,256,20,64]{1,3,2,0:T(8,128)(2,1)S(1)} %get-tuple-element.279) | copy-start | bytes 3932164 | tf_op jit(solution)/shard_map/while
  107.0 1.8 copy-start.6
  111.1 2.3 copy-start.8
  111.1 3.8 %copy-start.7 = (f32[1,256,20]{1,0,2:T(1,128)S(1)}, f32[1,256,20]{1,0,2:T(1,128)}, u32[]{:S(2)}) copy-start(f32[1,256,20]{1,0,2:T(1,128)} %copy-done.6) | copy-start | bytes 61444 | tf_op jit(solution)/shard_map/while
  118.6 28.5 %copy-start.12 = (f32[2,256,20]{1,0,2:T(2,128)S(1)}, f32[2,256,20]{1,0,2:T(2,128)}, u32[]{:S(2)}) copy-start(f32[2,256,20]{1,0,2:T(2,128)} %copy-done.11) | copy-start | bytes 122884 | tf_op jit(solution)/shard_map/while
  118.6 28.5 %copy-start.14 = (f32[2,256,20]{1,0,2:T(2,128)S(1)}, f32[2,256,20]{1,0,2:T(2,128)}, u32[]{:S(2)}) copy-start(f32[2,256,20]{1,0,2:T(2,128)} %copy-done.13) | copy-start | bytes 122884 | tf_op jit(solution)/shard_map/while
  120.0 27.2 %copy-start.4 = (bf16[2,256,20,64]{1,3,2,0:T(8,128)(2,1)S(1)}, bf16[2,256,20,64]{1,3,2,0:T(8,128)(2,1)}, u32[]{:S(2)}) copy-start(bf16[2,256,20,64]{1,3,2,0:T(8,128)(2,1)} %copy-done.3) | copy-start | bytes 3932164 | tf_op jit(solution)/shard_map/while
  147.2 0.8 copy-start.2
  147.2 40.0 %copy-start.5 = (bf16[512,1280]{1,0:T(8,128)(2,1)S(1)}, bf16[512,1280]{1,0:T(8,128)(2,1)}, u32[]{:S(2)}) copy-start(bf16[512,1280]{1,0:T(8,128)(2,1)} %multiply_convert_fusion.6) | copy-start | bytes 3932164
  148.0 74.4 %all-gather.6.cloned.1.call-start = ((), (), s32[]{:S(2)}) async-start(), calls=%async_computation.3 | async-start | bytes 3276800 | tf_op jit(solution)/shard_map/all_gather | solution.py:42
  187.1 128.6 %reduce-scatter.2.cloned.1.call-start = ((), (), s32[]{:S(2)}) async-start(), calls=%async_computation.4 | async-start | bytes 6553600 | tf_op jit(solution)/shard_map/reduce_scatter | solution.py:143
  189.1 33.4 %copy-start.10 = (bf16[512,256]{1,0:T(8,128)(2,1)S(1)}, bf16[512,256]{1,0:T(8,128)(2,1)}, u32[]{:S(2)}) copy-start(bf16[512,256]{1,0:T(8,128)(2,1)} %copy-done.9) | copy-start | bytes 786436
  189.1 33.4 %copy-start.19 = (f32[20]{0:T(128)S(1)}, f32[20]{0:T(128)}, u32[]{:S(2)}) copy-start(f32[20]{0:T(128)} %param.21) | copy-start | bytes 244
  233.0 19.3 %copy-start.20 = (f32[1280]{0:T(1024)S(1)}, f32[1280]{0:T(1024)}, u32[]{:S(2)}) copy-start(f32[1280]{0:T(1024)} %param.22) | copy-start | bytes 15364
  261.9 56.0 %copy-start.1 = (bf16[2560,256]{1,0:T(8,128)(2,1)S(1)}, bf16[2560,256]{1,0:T(8,128)(2,1)}, u32[]{:S(2)}) copy-start(bf16[2560,256]{1,0:T(8,128)(2,1)} %param.17) | copy-start | bytes 3932164
Sparse Core Ops, SparseCore 0:
  148.1 36.1 all-gather.7
  187.2 35.1 all-gather.5
  262.1 53.5 reduce-scatter.1
where the time goes:
time: 330 us; the launch traced here: 324 us
  waiting for transfers between devices  125 us (38%)
  local copies, waits for them, and re-layouts  83.1 us (25%)
  matrix products  53.7 us (16%)
  blocking collectives  30.1 us (9%)
  between operations  14 us (4%)
  other arithmetic  11.7 us (4%)
  starting transfers between devices  4.98 us (2%)
    dynamic_update_slice x4, local copies, waits for them, and re-layouts, on_device(): lax.scan(advance, jnp.zeros((heads_dev, HEADDIM, NSTATE), jnp.float32), s...  57 us
    reduce_scatter x1, waiting for transfers between devices, on_device(): lax.psum_scatter(partial_terms, 'head', scatter_dimension=1, tiled=True)  53.8 us
    all_gather x2, waiting for transfers between devices, carried_in(): pieces = jax.tree.map(lambda part: lax.all_gather(part, axis), so_far)  39.2 us
    all_to_all x1, waiting for transfers between devices, sent_to_all(): return lax.all_to_all(copies, axis, split_axis=0, concat_axis=0, tiled=True)  32.1 us
    dot_general x4, matrix products, on_device(): jnp.dot(column_piece, matrix, preferred_element_type=jnp.float32)  24 us
    all_gather x2, blocking collectives, carried_in(): pieces = jax.tree.map(lambda part: lax.all_gather(part, axis), so_far)  20.8 us
    dot_general x1, matrix products, on_device(): partial_terms = jnp.dot(normed, w_out, preferred_element_type=jnp.float32)  9.58 us
    all_to_all x1, blocking collectives, sent_to_all(): return lax.all_to_all(copies, axis, split_axis=0, concat_axis=0, tiled=True)  9.36 us
  transfers between devices with their start and end apart: 4, of which 4 were waited for; matrix products, arithmetic and copies ran while one was open for 3% of the time, Pallas kernels for 0%

commit v1 on v0

v1 whole, which is shorter than its diff:
```python
import functools

import jax
import jax.numpy as jnp
from jax import lax
from jax.experimental import pallas as pl
from jax.experimental.pallas import tpu as pltpu
from jax.sharding import Mesh
from jax.sharding import PartitionSpec as P

DI = 5120
HEADDIM = 64
NSTATE = 128
GROUP = 256
ROWS = 512
FEAT = 640
WIDTH = 1280
TILE = 256
STEPS = WIDTH // TILE
PER = TILE // HEADDIM
LANES = 128
BD = 384
QUARTER = NSTATE // 4
MSG = QUARTER + 16
OUTROWS = ROWS + 16
LOG2E = 1.4426950408889634
BATCH_SEQ = ("batch", "seq_0", "seq_1")
F32 = jnp.float32
BF16 = jnp.bfloat16
MIB = 1 << 20


def dot(a, b):
    return lax.dot_general(a, b, (((1,), (0,)), ((), ())), preferred_element_type=F32)


def dot_nt(a, b):
    return lax.dot_general(a, b, (((1,), (1,)), ((), ())), preferred_element_type=F32)


def dot_tn(a, b):
    return lax.dot_general(a, b, (((0,), (0,)), ((), ())), preferred_element_type=F32)


def silu(v):
    return v / (1.0 + jnp.exp(-v))


def three(v):
    hi = v.astype(BF16)
    rest = v - hi.astype(F32)
    mid = rest.astype(BF16)
    return hi, mid, (rest - mid.astype(F32)).astype(BF16)


def shifted(array, axis, shift):
    return lax.ppermute(array, axis, [(i, (i + shift) % 4) for i in range(4)])


def whole(shape):
    return pl.BlockSpec(shape, lambda *_: (0,) * len(shape))


def tile(rows):
    return pl.BlockSpec((rows, TILE), lambda j, s: (0, j))


def params(mib):
    return pltpu.CompilerParams(vmem_limit_bytes=mib * MIB)


def cost(flops, nbytes, trans=0):
    return pl.CostEstimate(flops=int(flops), bytes_accessed=int(nbytes), transcendentals=int(trans))


def sds(shape, dtype):
    return jax.ShapeDtypeStruct(shape, dtype)


def project_body(add, idx, tok, w_x, w_z, w_bd, *refs):
    tokens = tok[...]
    out_x, out_z, out_bd = refs[-3:]
    part_x, part_z = dot(tokens, w_x[...]), dot(tokens, w_z[...])
    if add:
        part_x, part_z = refs[0][...] + part_x, refs[1][...] + part_z
    out_x[...] = part_x
    out_z[...] = part_z

    @pl.when(pl.program_id(0) == 0)
    def _():
        part = dot(tokens, w_bd[...])
        out_bd[...] = refs[2][...] + part if add else part


def project(owner, tok, w_x, w_z, w_bd, sums=()):
    weight = pl.BlockSpec((FEAT, TILE), lambda j, s: (s[0], j))
    narrow = pl.BlockSpec((FEAT, BD), lambda j, s: (s[0], 0))
    add = bool(sums)
    outs = [tile(ROWS), tile(ROWS), whole((ROWS, BD))]
    return pl.pallas_call(
        functools.partial(project_body, add),
        grid_spec=pltpu.PrefetchScalarGridSpec(
            num_scalar_prefetch=1,
            grid=(STEPS,),
            in_specs=[whole((ROWS, FEAT)), weight, weight, narrow, *(outs if add else [])],
            out_specs=outs,
        ),
        out_shape=[sds((ROWS, WIDTH), F32), sds((ROWS, WIDTH), F32), sds((ROWS, BD), F32)],
        input_output_aliases={5: 0, 6: 1, 7: 2} if add else {},
        compiler_params=params(20),
        cost_estimate=cost(2 * ROWS * FEAT * (2 * WIDTH + BD), 10e6),
        name="project_add" if add else "project",
    )(owner, tok, w_x, w_z, w_bd, *sums)


def head_rows(j):
    head = lax.broadcasted_iota(jnp.int32, (LANES, TILE), 0)
    channel = lax.broadcasted_iota(jnp.int32, (LANES, TILE), 1)
    return (head == PER * j + channel // HEADDIM).astype(BF16)


def state_body(
    idx, tok, w_x, w_bd, acc_x, acc_bd, resets, bias, rate,
    inner_o, b_o, c_o, cum_o, step_o, first_o, thr_o, m0, m1, m2, m3,
    b_t, keep_hi, keep_lo, thr_s, state_s,
):
    j = pl.program_id(0)
    tokens = tok[...]

    @pl.when(j == 0)
    def _():
        bd = acc_bd[...] + dot(tokens, w_bd[...])
        mapped = silu(bd[:, : 2 * NSTATE])
        b_t[...] = mapped[:, :NSTATE].T.astype(BF16)
        b_o[...] = mapped[:, :NSTATE].astype(BF16)
        c_o[...] = mapped[:, NSTATE:].astype(BF16)
        logits = bd[:, 2 * NSTATE :] + bias[...]
        step = jnp.maximum(logits, 0.0) + jnp.log1p(jnp.exp(-jnp.abs(logits)))
        step_o[...] = step
        lane = lax.broadcasted_iota(jnp.int32, (ROWS, LANES), 1)
        decay = jnp.where(lane == LANES - 1, resets[...], -step * rate[...])
        row = lax.broadcasted_iota(jnp.int32, (GROUP, GROUP), 0)
        col = lax.broadcasted_iota(jnp.int32, (GROUP, GROUP), 1)
        lower = (row >= col).astype(BF16)
        thr_s[...] = jnp.zeros_like(thr_s)
        for g in range(2):
            span = slice(g * GROUP, (g + 1) * GROUP)
            hi, mid, lo = three(decay[span])
            cum = dot(lower, hi) + (dot(lower, mid) + dot(lower, lo))
            cum_o[span, :] = cum
            last = cum[GROUP - 1 :, :]
            seg, closing = cum[:, LANES - 1 :], last[:, LANES - 1 :]
            keep = jnp.where(seg == closing, jnp.exp(last - cum), 0.0) * step[span]
            hi = keep.astype(BF16)
            keep_hi[span, :] = hi
            keep_lo[span, :] = (keep - hi.astype(F32)).astype(BF16)
            through = jnp.where(closing == 0.0, jnp.exp(last), 0.0)
            for k, part in enumerate(three(through)):
                thr_s[pl.ds(8 * g + k, 1), :] = part.astype(F32)

    acc = acc_x[...] + dot(tokens, w_x[...])
    inner = silu(acc).astype(BF16)
    inner_o[...] = inner
    heads = head_rows(j)
    keep = dot(keep_hi[...], heads) + dot(keep_lo[...], heads)
    scaled = (keep * inner.astype(F32)).astype(BF16)
    state0 = dot(b_t[:, :GROUP], scaled[:GROUP])
    state1 = dot(b_t[:, GROUP:], scaled[GROUP:])
    thr = dot(thr_s[...].astype(BF16), heads)
    thr0 = thr[0:1] + thr[1:2] + thr[2:3]
    thr1 = thr[8:9] + thr[9:10] + thr[10:11]
    first_o[...] = state0
    thr_o[...] = jnp.broadcast_to(thr0, (8, TILE))
    state_s[...] = thr1 * state0 + state1
    hi, mid, lo = three(thr0 * thr1)
    row = lax.broadcasted_iota(jnp.int32, (16, TILE), 0)
    tail = jnp.where(
        row == 0, hi.astype(F32), jnp.where(row == 1, mid.astype(F32), lo.astype(F32))
    ).astype(BF16)
    for d, message in enumerate((m0, m1, m2, m3)):
        quarter = lax.rem(idx[1] + d, 4)
        start = pl.multiple_of(quarter * QUARTER, QUARTER)
        message[:QUARTER, :] = state_s[pl.ds(start, QUARTER), :].astype(BF16)
        message[QUARTER:, :] = tail


def device_state(idx, tok, w_x, w_bd, acc_x, acc_bd, resets, bias, rate):
    weight = pl.BlockSpec((FEAT, TILE), lambda j, s: (s[0], j))
    narrow = pl.BlockSpec((FEAT, BD), lambda j, s: (s[0], 0))
    small = whole((ROWS, LANES))
    return pl.pallas_call(
        state_body,
        grid_spec=pltpu.PrefetchScalarGridSpec(
            num_scalar_prefetch=1,
            grid=(STEPS,),
            in_specs=[
                whole((ROWS, FEAT)), weight, narrow, tile(ROWS), whole((ROWS, BD)),
                small, whole((1, LANES)), whole((1, LANES)),
            ],
            out_specs=[
                tile(ROWS), small, small, small, small, tile(NSTATE), tile(8),
                tile(MSG), tile(MSG), tile(MSG), tile(MSG),
            ],
            scratch_shapes=[
                pltpu.VMEM((NSTATE, ROWS), BF16),
                pltpu.VMEM((ROWS, LANES), BF16),
                pltpu.VMEM((ROWS, LANES), BF16),
                pltpu.VMEM((16, LANES), F32),
                pltpu.VMEM((NSTATE, TILE), F32),
            ],
        ),
        out_shape=[
            sds((ROWS, WIDTH), BF16), sds((ROWS, LANES), BF16), sds((ROWS, LANES), BF16),
            sds((ROWS, LANES), F32), sds((ROWS, LANES), F32), sds((NSTATE, WIDTH), F32),
            sds((8, WIDTH), F32), *[sds((MSG, WIDTH), BF16)] * 4,
        ],
        compiler_params=params(24),
        cost_estimate=cost(2 * ROWS * FEAT * (WIDTH + BD), 9e6),
        name="device_state",
    )(idx, tok, w_x, w_bd, acc_x, acc_bd, resets, bias, rate)


def decay_of(message):
    tail = message[QUARTER : QUARTER + 3, :].astype(F32)
    return tail[0:1] + tail[1:2] + tail[2:3]


def total_body(idx, m0, m1, m2, m3, out, held):
    for d, message in enumerate((m0, m1, m2, m3)):
        held[lax.rem(idx[1] + 4 - d, 4)] = message[...]
    state = held[0][:QUARTER].astype(F32)
    through = decay_of(held[0])
    for k in range(1, 4):
        decay = decay_of(held[k])
        state = decay * state + held[k][:QUARTER].astype(F32)
        through = through * decay
    hi, mid, lo = three(through)
    row = lax.broadcasted_iota(jnp.int32, (16, WIDTH), 0)
    out[:QUARTER, :] = state.astype(BF16)
    out[QUARTER:, :] = jnp.where(
        row == 0, hi.astype(F32), jnp.where(row == 1, mid.astype(F32), lo.astype(F32))
    ).astype(BF16)


def prefix_body(idx, m0, m1, m2, m3, t0, t1, t2, t3, h0, h1, h2, h3, held, rows, found):
    for d, message in enumerate((m0, m1, m2, m3)):
        held[lax.rem(idx[1] + 4 - d, 4)] = message[...]
    for d, message in enumerate((t0, t1, t2, t3)):
        rows[lax.rem(idx[0] + 4 - d, 4)] = message[...]
    state = jnp.zeros((QUARTER, WIDTH), F32)
    for k in range(3):
        after = decay_of(rows[k]) * state + rows[k][:QUARTER].astype(F32)
        state = jnp.where(k < idx[0], after, state)
    for k in range(4):
        found[k] = state.astype(BF16)
        if k < 3:
            state = decay_of(held[k]) * state + held[k][:QUARTER].astype(F32)
    for d, out in enumerate((h0, h1, h2, h3)):
        out[...] = found[lax.rem(idx[1] + d, 4)]


def row_total(idx, messages):
    return pl.pallas_call(
        total_body,
        grid_spec=pltpu.PrefetchScalarGridSpec(
            num_scalar_prefetch=1,
            grid=(1,),
            in_specs=[whole((MSG, WIDTH))] * 4,
            out_specs=whole((MSG, WIDTH)),
            scratch_shapes=[pltpu.VMEM((4, MSG, WIDTH), BF16)],
        ),
        out_shape=sds((MSG, WIDTH), BF16),
        compiler_params=params(12),
        cost_estimate=cost(1e6, 1e6),
        name="row_total",
    )(idx, *messages)


def prefixes(idx, messages, totals):
    return pl.pallas_call(
        prefix_body,
        grid_spec=pltpu.PrefetchScalarGridSpec(
            num_scalar_prefetch=1,
            grid=(1,),
            in_specs=[whole((MSG, WIDTH))] * 8,
            out_specs=[whole((QUARTER, WIDTH))] * 4,
            scratch_shapes=[
                pltpu.VMEM((4, MSG, WIDTH), BF16),
                pltpu.VMEM((4, MSG, WIDTH), BF16),
                pltpu.VMEM((4, QUARTER, WIDTH), BF16),
            ],
        ),
        out_shape=[sds((QUARTER, WIDTH), BF16)] * 4,
        compiler_params=params(16),
        cost_estimate=cost(1e6, 1.5e6),
        name="prefixes",
    )(idx, *messages, *totals)


def gate_body(idx, tok, w_z, acc_z, out):
    gating = (acc_z[...] + dot(tok[...], w_z[...])).astype(BF16).astype(F32)
    out[...] = silu(gating)


def gate(idx, tok, w_z, acc_z):
    weight = pl.BlockSpec((FEAT, TILE), lambda j, s: (s[0], j))
    return pl.pallas_call(
        gate_body,
        grid_spec=pltpu.PrefetchScalarGridSpec(
            num_scalar_prefetch=1,
            grid=(STEPS,),
            in_specs=[whole((ROWS, FEAT)), weight, tile(ROWS)],
            out_specs=tile(ROWS),
        ),
        out_shape=sds((ROWS, WIDTH), F32),
        input_output_aliases={3: 0},
        compiler_params=params(16),
        cost_estimate=cost(2 * ROWS * FEAT * WIDTH, 8e6),
        name="gate",
    )(idx, tok, w_z, acc_z)


def mix_body(inner_r, b_r, c_r, cum_r, step_r, skip, out, ent_o, scores, cum_t, step_t, cum_2, ent):
    j = pl.program_id(1)
    half = GROUP // 2

    @pl.when(j == 0)
    def _():
        cum = cum_r[...]
        across = cum.T
        cum_2[...] = cum * LOG2E
        cum_t[...] = across * LOG2E
        step_t[...] = step_r[...].T
        row = lax.broadcasted_iota(jnp.int32, (GROUP, GROUP), 0)
        col = lax.broadcasted_iota(jnp.int32, (GROUP, GROUP), 1)
        seg = cum[:, LANES - 1 :]
        same = (seg == across[LANES - 1 :, :]) & (row >= col)
        scores[...] = jnp.where(same, dot_nt(c_r[...], b_r[...]), 0.0)
        ent[...] = jnp.where(seg == 0.0, jnp.exp(cum), 0.0)

    heads = head_rows(j)
    enter = ent[...]
    hi = enter.astype(BF16)
    lo = (enter - hi.astype(F32)).astype(BF16)
    ent_o[...] = dot(hi, heads) + dot(lo, heads)

    turned = pltpu.roll(cum_2[...], lax.rem(LANES - PER * j, LANES), 1)
    for pair in range(PER // 2):
        lanes = slice(pair * LANES, (pair + 1) * LANES)
        both = inner_r[:, lanes]
        ys = []
        for k in (2 * pair, 2 * pair + 1):
            head = PER * j + k
            before = cum_t[pl.ds(head, 1), :]
            step = step_t[pl.ds(head, 1), :]
            top = jnp.exp2(jnp.minimum(turned[:half, k : k + 1] - before[:, :half], 0.0))
            top = (top * scores[:half, :half] * step[:, :half]).astype(BF16)
            low = jnp.exp2(jnp.minimum(turned[half:, k : k + 1] - before, 0.0))
            low = (low * scores[half:, :] * step).astype(BF16)
            ys.append(jnp.concatenate([dot(top, both[:half]), dot(low, both)], 0))
        lane = lax.broadcasted_iota(jnp.int32, (GROUP, LANES), 1)
        y = jnp.where(lane < HEADDIM, ys[0], ys[1])
        out[:, lanes] = y + skip[:, lanes] * both.astype(F32)


def mix(inner, b, c, cum, step, skip):
    block = pl.BlockSpec((GROUP, TILE), lambda g, j: (g, j))
    small = pl.BlockSpec((GROUP, LANES), lambda g, j: (g, 0))
    return pl.pallas_call(
        mix_body,
        grid=(ROWS // GROUP, STEPS),
        in_specs=[block, small, small, small, small, pl.BlockSpec((1, TILE), lambda g, j: (0, j))],
        out_specs=[block, block],
        out_shape=[sds((ROWS, WIDTH), F32), sds((ROWS, WIDTH), F32)],
        scratch_shapes=[
            pltpu.VMEM((GROUP, GROUP), F32),
            pltpu.VMEM((LANES, GROUP), F32),
            pltpu.VMEM((LANES, GROUP), F32),
            pltpu.VMEM((GROUP, LANES), F32),
            pltpu.VMEM((GROUP, LANES), F32),
        ],
        compiler_params=params(16),
        cost_estimate=cost(3e9, 8e6, 3e6),
        name="mix",
    )(inner, b, c, cum, step, skip)


def squares_rows(total, out):
    hi, mid, lo = three(total)
    row = lax.broadcasted_iota(jnp.int32, (16, ROWS), 0)
    rows = jnp.where(
        row == 0,
        hi.astype(F32),
        jnp.where(row == 1, mid.astype(F32), jnp.where(row == 2, lo.astype(F32), 0.0)),
    ).astype(BF16)
    out[ROWS:, :] = jnp.concatenate([rows, jnp.zeros((16, FEAT - ROWS), BF16)], 1)


def gated_body(
    idx, h0, h1, h2, h3, first, thr, c_r, u_r, ent_r, zs_r, gain, w_out,
    rows_o, sums_o, out, state, acc, squares,
):
    j = pl.program_id(0)
    for d, part in enumerate((h0, h1, h2, h3)):
        start = pl.multiple_of(lax.rem(idx[1] + 4 - d, 4) * QUARTER, QUARTER)
        state[pl.ds(start, QUARTER), :] = part[...]
    enter = state[...]
    second = (first[...] + thr[0:1, :] * enter.astype(F32)).astype(BF16)
    carried = jnp.concatenate([dot(c_r[:GROUP], enter), dot(c_r[GROUP:], second)], 0)
    gated = (u_r[...] + ent_r[...] * carried) * zs_r[...]
    rows = (gated * gain[...]).astype(BF16)
    rows_o[...] = rows
    square = gated * gated
    hi = square.astype(BF16)
    lo = (square - hi.astype(F32)).astype(BF16)
    ones = jnp.ones((8, TILE), BF16)
    part_squares = dot_nt(ones, hi) + dot_nt(ones, lo)
    part = dot(rows, w_out[...])

    @pl.when(j == 0)
    def _():
        squares[...] = part_squares
        acc[...] = part

    @pl.when(j > 0)
    def _():
        squares[...] += part_squares
        acc[...] += part

    @pl.when(j == STEPS - 1)
    def _():
        sums_o[...] = squares[...]
        out[:ROWS, :] = acc[...].astype(BF16)
        squares_rows(squares[0:1, :], out)


def gated_rows(idx, parts, first, thr, c, u, ent, zs, gain, w_out):
    weight = pl.BlockSpec((TILE, FEAT), lambda j, s: (j, s[2]))
    return pl.pallas_call(
        gated_body,
        grid_spec=pltpu.PrefetchScalarGridSpec(
            num_scalar_prefetch=1,
            grid=(STEPS,),
            in_specs=[
                *[tile(QUARTER)] * 4, tile(NSTATE), tile(8), whole((ROWS, LANES)),
                tile(ROWS), tile(ROWS), tile(ROWS), tile(1), weight,
            ],
            out_specs=[tile(ROWS), whole((8, ROWS)), whole((OUTROWS, FEAT))],
            scratch_shapes=[
                pltpu.VMEM((NSTATE, TILE), BF16),
                pltpu.VMEM((ROWS, FEAT), F32),
                pltpu.VMEM((8, ROWS), F32),
            ],
        ),
        out_shape=[sds((ROWS, WIDTH), BF16), sds((8, ROWS), F32), sds((OUTROWS, FEAT), BF16)],
        compiler_params=params(24),
        cost_estimate=cost(2 * ROWS * WIDTH * FEAT * 1.3, 12e6),
        name="gated_rows",
    )(idx, *parts, first, thr, c, u, ent, zs, gain, w_out)


def block_body(send, idx, rows, sums, w_out, out):
    part = dot(rows[...], w_out[...])
    if send:
        out[:ROWS, :] = part.astype(BF16)
        squares_rows(sums[0:1, :], out)
    else:
        out[...] = part


def out_block(send, target, rows, sums, w_out):
    shape = sds((OUTROWS, FEAT), BF16) if send else sds((ROWS, FEAT), F32)
    return pl.pallas_call(
        functools.partial(block_body, send),
        grid_spec=pltpu.PrefetchScalarGridSpec(
            num_scalar_prefetch=1,
            grid=(1,),
            in_specs=[
                whole((ROWS, WIDTH)),
                whole((8, ROWS)),
                pl.BlockSpec((WIDTH, FEAT), lambda j, s: (0, s[0])),
            ],
            out_specs=whole(shape.shape),
        ),
        out_shape=shape,
        compiler_params=params(16),
        cost_estimate=cost(2 * ROWS * WIDTH * FEAT, 4e6),
        name="out_block",
    )(target, rows, sums, w_out)


def norm_body(own, sums, r1, r2, r3, out):
    parts = [*three(sums[0:1, :])]
    for arrived in (r1, r2, r3):
        tail = arrived[ROWS : ROWS + 3, :ROWS]
        parts += [tail[0:1], tail[1:2], tail[2:3]]
    row = lax.broadcasted_iota(jnp.int32, (16, ROWS), 0)
    stack = jnp.zeros((16, ROWS), F32)
    for k, part in enumerate(parts):
        stack = jnp.where(row == k, part.astype(F32), stack)
    squares = dot_tn(stack.astype(BF16), jnp.ones((16, LANES), BF16))
    factor = lax.rsqrt(squares / DI + 1e-05)
    for k in range(FEAT // LANES):
        lanes = slice(k * LANES, (k + 1) * LANES)
        total = own[:, lanes] + r1[:ROWS, lanes].astype(F32)
        total = total + (r2[:ROWS, lanes].astype(F32) + r3[:ROWS, lanes].astype(F32))
        out[:, lanes] = (total * factor).astype(BF16)


def norm(own, sums, arrived):
    return pl.pallas_call(
        norm_body,
        grid=(1,),
        in_specs=[whole((ROWS, FEAT)), whole((8, ROWS)), *[whole((OUTROWS, FEAT))] * 3],
        out_specs=whole((ROWS, FEAT)),
        out_shape=sds((ROWS, FEAT), BF16),
        compiler_params=params(24),
        cost_estimate=cost(2e6, 5e6),
        name="norm",
    )(own, sums, *arrived)


def on_device(tokens, resets, w_x, w_z, w_bc, w_dt, dt_bias, decay_rate, d_skip, norm_gain, w_out):
    me = lax.axis_index("head")
    y, z = lax.axis_index("seq_0"), lax.axis_index("seq_1")
    heads = w_dt.shape[1]
    arrived = {d: shifted(tokens, "head", d) for d in (1, 3, 2)}

    def owner(d):
        return ((me - d) % 4).reshape(1).astype(jnp.int32)

    w_bd = jnp.concatenate([w_bc, jnp.pad(w_dt, ((0, 0), (0, LANES - heads)))], 1)
    bias = jnp.pad(dt_bias, (0, LANES - heads)).reshape(1, LANES)
    rate = jnp.pad(decay_rate, (0, LANES - heads)).reshape(1, LANES)
    starts = jnp.broadcast_to(resets.astype(F32)[:, None], (ROWS, LANES))
    skip = jnp.repeat(d_skip, HEADDIM).reshape(1, WIDTH)
    gain = norm_gain.reshape(1, WIDTH)

    sums = project(owner(0), tokens, w_x, w_z, w_bd)
    sums = project(owner(1), arrived[1], w_x, w_z, w_bd, sums)
    acc_x, acc_z, acc_bd = project(owner(3), arrived[3], w_x, w_z, w_bd, sums)
    last = jnp.stack([(me - 2) % 4, z]).astype(jnp.int32)
    inner, b, c, cum, step, first, thr, *messages = device_state(
        last, arrived[2], w_x, w_bd, acc_x, acc_bd, starts, bias, rate
    )
    place = jnp.stack([y, z, (me + 2) % 4]).astype(jnp.int32)
    quarters = [messages[0], *(shifted(messages[d], "seq_1", d) for d in (1, 2, 3))]
    zs = gate(last, arrived[2], w_z, acc_z)
    u, ent = mix(inner, b, c, cum, step, skip)
    total = row_total(place, quarters)
    totals = [total, *(shifted(total, "seq_0", d) for d in (1, 2, 3))]
    parts = prefixes(place, quarters, totals)
    parts = [parts[0], *(shifted(parts[d], "seq_1", d) for d in (1, 2, 3))]
    rows, squares, far = gated_rows(place, parts, first, thr, c, u, ent, zs, gain, w_out)
    results = [shifted(far, "head", 2)]
    for d in (1, 3):
        target = ((me + d) % 4).reshape(1).astype(jnp.int32)
        results.append(shifted(out_block(True, target, rows, squares, w_out), "head", d))
    own = out_block(False, me.reshape(1).astype(jnp.int32), rows, squares, w_out)
    return norm(own, squares, results)


def solution(mesh):
    split = Mesh(
        mesh.devices.reshape(4, 4, mesh.shape["head"], mesh.shape["batch"]),
        ("seq_0", "seq_1", "head", "batch"),
    )
    placed = (
        P(BATCH_SEQ, "head"),
        P(BATCH_SEQ),
        P(None, "head"),
        P(None, "head"),
        P(),
        P(None, "head"),
        P("head"),
        P("head"),
        P("head"),
        P("head"),
        P("head", None),
    )
    return jax.shard_map(
        on_device, mesh=split, in_specs=placed, out_specs=P(BATCH_SEQ, "head"), check_vma=False
    )
```

time: 330 us -> 124 us (0.38); the launches traced: 324 us -> 123 us
  waiting for transfers between devices: 125 us -> 29.1 us
  local copies, waits for them, and re-layouts: 83.1 us -> 17.9 us
  matrix products: 53.7 us -> 0 us
  Pallas kernels: 0 us -> 43.8 us
  blocking collectives: 30.1 us -> 0 us
  starting transfers between devices: 4.98 us -> 29.1 us
  between operations: 14 us -> 0.34 us
  other arithmetic: 11.7 us -> 3.22 us
    dynamic_update_slice x4 -> x0, local copies, waits for them, and re-layouts: 57 us -> none  [on_device(): lax.scan(advance, jnp.zeros((heads_dev, HEADDIM, NSTATE), jnp.float32), s...]
    reduce_scatter x1 -> x0, waiting for transfers between devices: 53.8 us -> none  [on_device(): lax.psum_scatter(partial_terms, 'head', scatter_dimension=1, tiled=True)]
    dot_general x14 -> x0, matrix products: 53.7 us -> none  [the longest x4 24 us: on_device(): jnp.dot(column_piece, matrix, preferred_element_type=jnp.float32)]
    pallas_call x0 -> x13, Pallas kernels: none -> 43.8 us  [the longest x3 15.2 us: project(): pl.pallas_call(functools.partial(project_body, add), grid_spec=pltpu.Pref...]
    all_gather x2 -> x0, waiting for transfers between devices: 39.2 us -> none  [carried_in(): pieces = jax.tree.map(lambda part: lax.all_gather(part, axis), so_far)]
    all_to_all x1 -> x0, waiting for transfers between devices: 32.1 us -> none  [sent_to_all(): return lax.all_to_all(copies, axis, split_axis=0, concat_axis=0, tiled=True)]
    ppermute x0 -> x15, starting transfers between devices: none -> 29.1 us  [shifted(): return lax.ppermute(array, axis, [(i, (i + shift) % 4) for i in range(4)])]
    ppermute x0 -> x15, waiting for transfers between devices: none -> 29.1 us  [shifted(): return lax.ppermute(array, axis, [(i, (i + shift) % 4) for i in range(4)])]
  transfers between devices with their start and end apart: 4 -> 15, of which waited for: 4 -> 8; matrix products, arithmetic and copies ran while one was open for 3% -> 4% of each run, Pallas kernels for 0% -> 21%
where the time goes in v1:
time: 124 us; the launch traced here: 123 us
  Pallas kernels  43.8 us (35%)
  starting transfers between devices  29.1 us (23%)
  waiting for transfers between devices  29.1 us (23%)
  local copies, waits for them, and re-layouts  17.9 us (14%)
  other arithmetic  3.22 us (3%)
    ppermute x15, starting transfers between devices, shifted(): return lax.ppermute(array, axis, [(i, (i + shift) % 4) for i in range(4)])  29.1 us
    ppermute x15, waiting for transfers between devices, shifted(): return lax.ppermute(array, axis, [(i, (i + shift) % 4) for i in range(4)])  29.1 us
    unnamed x55, local copies, waits for them, and re-layouts  17.6 us
    pallas_call x3, Pallas kernels, project(): pl.pallas_call(functools.partial(project_body, add), grid_spec=pltpu.Pref...  15.2 us
    pallas_call x1, Pallas kernels, device_state(): pl.pallas_call(state_body, grid_spec=pltpu.PrefetchScalarGridSpec(num_sca...  7.34 us
    pallas_call x1, Pallas kernels, gated_rows(): pl.pallas_call(gated_body, grid_spec=pltpu.PrefetchScalarGridSpec(num_sca...  5.75 us
    pallas_call x1, Pallas kernels, mix(): pl.pallas_call(mix_body, grid=(ROWS // GROUP, STEPS), in_specs=[block, sm...  5.64 us
    pallas_call x3, Pallas kernels, out_block(): pl.pallas_call(functools.partial(block_body, send), grid_spec=pltpu.Prefe...  3.72 us
  transfers between devices with their start and end apart: 15, of which 8 were waited for; matrix products, arithmetic and copies ran while one was open for 4% of the time, Pallas kernels for 21%

profile of v1, /device:TPU:0, one launch (start us, length us, event | category | flops | bytes accessed | tf_op | source)
XLA Modules:
  0.0 123.4 jit_solution(17980132571583855506)
XLA Ops:
  0.0 1.6 %collective-permute-start.2 = (bf16[512,640]{1,0:T(8,128)(2,1)}, bf16[512,640]{1,0:T(8,128)(2,1)}, u32[]{:S(2)}, u32[]{:S(2)}) collective-permute-start(bf16[512,640]{1,0:T(8,128)(2,1)} %tok.1), channel_id=1, source_target_pairs={{0,2},{2,4},{4,6},{6,0},{1,3},{3,5},{5,7},{7,1},{8,10},{10,12},{12... | collective-permute-start | bytes 1966088 | tf_op jit(solution)/shard_map/ppermute | solution.py:57
  1.7 1.6 %collective-permute-start.1 = (bf16[512,640]{1,0:T(8,128)(2,1)}, bf16[512,640]{1,0:T(8,128)(2,1)}, u32[]{:S(2)}, u32[]{:S(2)}) collective-permute-start(bf16[512,640]{1,0:T(8,128)(2,1)} %tok.1), channel_id=1, source_target_pairs={{0,6},{2,0},{4,2},{6,4},{1,7},{3,1},{5,3},{7,5},{8,14},{10,8},{12,... | collective-permute-start | bytes 1966088 | tf_op jit(solution)/shard_map/ppermute | solution.py:57
  3.2 2.0 %collective-permute-start = (bf16[512,640]{1,0:T(8,128)(2,1)}, bf16[512,640]{1,0:T(8,128)(2,1)S(1)}, u32[]{:S(2)}, u32[]{:S(2)}) collective-permute-start(bf16[512,640]{1,0:T(8,128)(2,1)} %tok.1), channel_id=1, source_target_pairs={{0,4},{2,6},{4,0},{6,2},{1,5},{3,7},{5,1},{7,3},{8,12},{10,14},{12... | collective-permute-start | bytes 1966088 | tf_op jit(solution)/shard_map/ppermute | solution.py:57
  5.2 2.2 %copy.19 = bf16[2560,20]{1,0:T(8,128)(2,1)} copy(bf16[2560,20]{0,1:T(8,128)(2,1)} %param.16) | data formatting | bytes 204800 | tf_op args[5]
  7.4 3.1 %fusion.1.w_bd = bf16[2560,384]{1,0:T(8,128)(2,1)} fusion(bf16[2560,20]{1,0:T(8,128)(2,1)} %copy.19, bf16[2560,256]{1,0:T(8,128)(2,1)} %param.15), kind=kLoop, calls=%fused_computation.2 | loop fusion | flops 5898240 | bytes 3379200 | tf_op jit(solution)/shard_map/concatenate | solution.py:532
  10.5 0.1 pad_add_fusion.1.idx
  10.5 0.0 copy-start
  10.6 2.9 %copy-done = bf16[2560,1280]{1,0:T(8,128)(2,1)S(1)} copy-done((bf16[2560,1280]{1,0:T(8,128)(2,1)S(1)}, bf16[2560,1280]{1,0:T(8,128)(2,1)}, u32[]{:S(2)}) %copy-start) | copy-done | bytes 6553624
  13.4 2.9 %copy-done.1 = bf16[2560,1280]{1,0:T(8,128)(2,1)S(1)} copy-done((bf16[2560,1280]{1,0:T(8,128)(2,1)S(1)}, bf16[2560,1280]{1,0:T(8,128)(2,1)}, u32[]{:S(2)}) %copy-start.1) | copy-done | bytes 6553624
  16.3 1.5 %copy-done.3 = bf16[2560,384]{1,0:T(8,128)(2,1)S(1)} copy-done((bf16[2560,384]{1,0:T(8,128)(2,1)S(1)}, bf16[2560,384]{1,0:T(8,128)(2,1)}, u32[]{:S(2)}) %copy-start.3) | copy-done | bytes 1966104
  17.8 1.1 copy-done.7
  18.9 4.1 %project.1 = (f32[512,1280]{1,0:T(8,128)S(1)}, f32[512,1280]{1,0:T(8,128)S(1)}, f32[512,384]{1,0:T(8,128)S(1)}) custom-call(s32[1]{0:T(128)} %bitcast.7.idx, bf16[512,640]{1,0:T(8,128)(2,1)S(1)} %copy-done.7, bf16[2560,1280]{1,0:T(8,128)(2,1)S(1)} %copy-done, bf16[2560,1280]{1,0:T(8,128)(2,1)S(1)} %copy-done.1, bf16[2560,384]{1,0:T(8,128)(2,1)S(1)} %copy-done.3), custom_call_target="tpu_custom_call" | custom-call | flops 1929379840 | bytes 10000000 | tf_op jit(solution)/shard_map/project/pallas_call | solution.py:100
  23.0 0.0 collective-permute-done.2.tok
  23.1 0.5 copy-done.4
  23.6 5.5 %project_add.2 = (f32[512,1280]{1,0:T(8,128)S(1)}, f32[512,1280]{1,0:T(8,128)S(1)}, f32[512,384]{1,0:T(8,128)S(1)}) custom-call(s32[1]{0:T(128)} %bitcast.6.idx, bf16[512,640]{1,0:T(8,128)(2,1)} %collective-permute-done.2.tok, bf16[2560,1280]{1,0:T(8,128)(2,1)S(1)} %bitcast.15, ...), custom_call_target="tpu_custom_call", output_to_operand_aliasing={{0}: (5, {}), {1}: (6, {}), {2}: (7, {})} | custom-call | flops 1929379840 | bytes 10000000 | tf_op jit(solution)/shard_map/project_add/pallas_call | solution.py:100
  29.2 5.6 %project_add.3 = (f32[512,1280]{1,0:T(8,128)S(1)}, f32[512,1280]{1,0:T(8,128)S(1)}, f32[512,384]{1,0:T(8,128)S(1)}) custom-call(s32[1]{0:T(128)} %bitcast.5.idx, bf16[512,640]{1,0:T(8,128)(2,1)} %collective-permute-done.1.tok, bf16[2560,1280]{1,0:T(8,128)(2,1)S(1)} %bitcast.15, ...), custom_call_target="tpu_custom_call", output_to_operand_aliasing={{0}: (5, {}), {1}: (6, {}), {2}: (7, {})} | custom-call | flops 1929379840 | bytes 10000000 | tf_op jit(solution)/shard_map/project_add/pallas_call | solution.py:100
  34.7 0.0 collective-permute-done.tok
  34.8 0.1 broadcast_in_dim.4.resets
  34.9 0.0 copy-start.18
  34.9 0.0 copy-start.16
  34.9 7.3 %device_state.1 = (bf16[512,1280]{1,0:T(8,128)(2,1)S(1)}, bf16[512,128]{1,0:T(8,128)(2,1)S(1)}, bf16[512,128]{1,0:T(8,128)(2,1)S(1)}, f32[512,128]{1,0:T(8,128)S...) custom-call(s32[2]{0:T(128)S(1)} %pad_add_fusion.1.idx, ...), custom_call_target="tpu_custom_call" | custom-call | flops 1090519040 | bytes 9000000 | tf_op jit(solution)/shard_map/device_state/pallas_call | solution.py:191
  42.3 0.8 copy-done.8
  43.1 1.1 copy-done.10
  44.2 0.7 copy-done.12
  44.9 0.7 copy-done.14
  45.6 4.2 %collective-permute-start.3 = (bf16[48,1280]{1,0:T(8,128)(2,1)}, bf16[48,1280]{1,0:T(8,128)(2,1)S(1)}, u32[]{:S(2)}, u32[]{:S(2)}) collective-permute-start(bf16[48,1280]{1,0:T(8,128)(2,1)} %get-tuple-element.43), channel_id=1, source_target_pairs={{0,8},{8,16},{16,24},{24,0},{1,9},{9,17},{17,25},{25,1},{2,10},{10... | collective-permute-start | bytes 368648 | tf_op jit(solution)/shard_map/ppermute | solution.py:57
  49.8 3.6 %collective-permute-start.4 = (bf16[48,1280]{1,0:T(8,128)(2,1)}, bf16[48,1280]{1,0:T(8,128)(2,1)S(1)}, u32[]{:S(2)}, u32[]{:S(2)}) collective-permute-start(bf16[48,1280]{1,0:T(8,128)(2,1)} %get-tuple-element.44), channel_id=1, source_target_pairs={{0,16},{8,24},{16,0},{24,8},{1,17},{9,25},{17,1},{25,9},{2,18},{10... | collective-permute-start | bytes 368648 | tf_op jit(solution)/shard_map/ppermute | solution.py:57
  53.4 1.0 collective-permute-start.5
  54.4 0.1 pad_add_fusion.idx
  54.5 0.5 collective-permute-done.3.m1
  55.0 2.8 %collective-permute-done.4.m2 = bf16[48,1280]{1,0:T(8,128)(2,1)S(1)} collective-permute-done((bf16[48,1280]{1,0:T(8,128)(2,1)}, bf16[48,1280]{1,0:T(8,128)(2,1)S(1)}, u32[]{:S(2)}, u32[]{:S(2)}) %collective-permute-start.4) | collective-permute-done | bytes 122912 | tf_op jit(solution)/shard_map/ppermute | solution.py:57
  57.8 0.7 collective-permute-done.5.m3
  58.5 0.7 row_total.1.t0
  59.2 1.6 %collective-permute-start.6 = (bf16[48,1280]{1,0:T(8,128)(2,1)S(1)}, bf16[48,1280]{1,0:T(8,128)(2,1)S(1)}, u32[]{:S(2)}, u32[]{:S(2)}) collective-permute-start(bf16[48,1280]{1,0:T(8,128)(2,1)S(1)} %row_total.1.t0), channel_id=1, source_target_pairs={{0,32},{32,64},{64,96},{96,0},{1,33},{33,65},{65,97},{97,1},{2,34}... | collective-permute-start | bytes 368648 | tf_op jit(solution)/shard_map/ppermute | solution.py:57
  60.8 2.9 %collective-permute-start.7 = (bf16[48,1280]{1,0:T(8,128)(2,1)S(1)}, bf16[48,1280]{1,0:T(8,128)(2,1)S(1)}, u32[]{:S(2)}, u32[]{:S(2)}) collective-permute-start(bf16[48,1280]{1,0:T(8,128)(2,1)S(1)} %row_total.1.t0), channel_id=1, source_target_pairs={{0,64},{32,96},{64,0},{96,32},{1,65},{33,97},{65,1},{97,33},{2,66}... | collective-permute-start | bytes 368648 | tf_op jit(solution)/shard_map/ppermute | solution.py:57
  63.8 1.3 %collective-permute-start.8 = (bf16[48,1280]{1,0:T(8,128)(2,1)S(1)}, bf16[48,1280]{1,0:T(8,128)(2,1)S(1)}, u32[]{:S(2)}, u32[]{:S(2)}) collective-permute-start(bf16[48,1280]{1,0:T(8,128)(2,1)S(1)} %row_total.1.t0), channel_id=1, source_target_pairs={{0,96},{32,0},{64,32},{96,64},{1,97},{33,1},{65,33},{97,65},{2,98}... | collective-permute-start | bytes 368648 | tf_op jit(solution)/shard_map/ppermute | solution.py:57
  65.1 0.1 broadcast_in_dim.10
  65.2 0.1 reshape_reshape.3.skip
  65.3 0.1 collective-permute-done.6.t1
  65.4 2.6 %collective-permute-done.7.t2 = bf16[48,1280]{1,0:T(8,128)(2,1)S(1)} collective-permute-done((bf16[48,1280]{1,0:T(8,128)(2,1)S(1)}, bf16[48,1280]{1,0:T(8,128)(2,1)S(1)}, u32[]{:S(2)}, u32[]{:S(2)}) %collective-permute-start.7) | collective-permute-done | bytes 122912 | tf_op jit(solution)/shard_map/ppermute | solution.py:57
  67.9 0.7 collective-permute-done.8.t3
  68.6 0.8 prefixes.1
  69.5 1.9 %collective-permute-start.10 = (bf16[32,1280]{1,0:T(8,128)(2,1)S(1)}, bf16[32,1280]{1,0:T(8,128)(2,1)S(1)}, u32[]{:S(2)}, u32[]{:S(2)}) collective-permute-start(bf16[32,1280]{1,0:T(8,128)(2,1)S(1)} %get-tuple-element.48), channel_id=1, source_target_pairs={{0,16},{8,24},{16,0},{24,8},{1,17},{9,25},{17,1},{25,9},{2,18},{10... | collective-permute-start | bytes 245768 | tf_op jit(solution)/shard_map/ppermute | solution.py:57
  71.3 1.6 %collective-permute-start.11 = (bf16[32,1280]{1,0:T(8,128)(2,1)S(1)}, bf16[32,1280]{1,0:T(8,128)(2,1)S(1)}, u32[]{:S(2)}, u32[]{:S(2)}) collective-permute-start(bf16[32,1280]{1,0:T(8,128)(2,1)S(1)} %get-tuple-element.49), channel_id=1, source_target_pairs={{0,24},{8,0},{16,8},{24,16},{1,25},{9,1},{17,9},{25,17},{2,26},{10... | collective-permute-start | bytes 245768 | tf_op jit(solution)/shard_map/ppermute | solution.py:57
  72.9 0.4 collective-permute-start.9
  73.4 1.3 %copy-done.11 = bf16[512,1280]{1,0:T(8,128)(2,1)S(1)} copy-done((bf16[512,1280]{1,0:T(8,128)(2,1)S(1)}, bf16[512,1280]{1,0:T(8,128)(2,1)}, u32[]{:S(2)}) %copy-start.11) | copy-done | bytes 1310744
  74.7 0.9 copy-done.13
  75.6 0.9 copy-done.15
  76.6 5.6 %mix.1 = (f32[512,1280]{1,0:T(8,128)S(1)}, f32[512,1280]{1,0:T(8,128)S(1)}) custom-call(bf16[512,1280]{1,0:T(8,128)(2,1)S(1)} %copy-done.11, bf16[512,128]{1,0:T(8,128)(2,1)S(1)} %get-tuple-element.54.b_r, bf16[512,128]{1,0:T(8,128)(2,1)S(1)} %get-tuple-element.52.c_r, f32[512,128]{1,0:T(8,128)S(1)} %copy-done.13, f32[512,128]{1,0:T(8,128)S(1)} %copy-done.15, ...), custom_call_target="tpu_custom_call" | custom-call | flops 3000000000 | bytes 8000000 | tf_op jit(solution)/shard_map/mix/pallas_call | solution.py:369
  82.2 0.0 slice-start.4
  82.3 0.0 copy-start.9
  82.3 3.2 %gate.1.zs_r = f32[512,1280]{1,0:T(8,128)S(1)} custom-call(s32[2]{0:T(128)S(1)} %pad_add_fusion.1.idx, bf16[512,640]{1,0:T(8,128)(2,1)S(1)} %collective-permute-done.tok, bf16[2560,1280]{1,0:T(8,128)(2,1)S(1)} %bitcast.17, f32[512,1280]{1,0:T(8,128)S(1)} %copy-done.6), custom_call_target="tpu_custom_call", output_to_operand_aliasing={{}: (3, {})} | custom-call | flops 838860800 | bytes 8000000 | tf_op jit(solution)/shard_map/gate/pallas_call | solution.py:307
  85.5 0.0 collective-permute-done.11.h3
  85.5 0.0 collective-permute-done.9.h1
  85.6 5.8 %gated_rows.1 = (bf16[512,1280]{1,0:T(8,128)(2,1)S(1)}, f32[8,512]{1,0:T(8,128)S(1)}, bf16[528,640]{1,0:T(8,128)(2,1)S(1)}) custom-call(s32[3]{0:T(128)S(1)} %pad_add_fusion.idx, bf16[32,1280]{1,0:T(8,128)(2,1)S(1)} %get-tuple-element.46.h0, bf16[32,1280]{1,0:T(8,128)(2,1)S(1)} %collective-permute-done.9.h1, ...), custom_call_target="tpu_custom_call" | custom-call | flops 1090519040 | bytes 12000000 | tf_op jit(solution)/shard_map/gated_rows/pallas_call | solution.py:439
  91.3 1.2 %out_block.5 = bf16[528,640]{1,0:T(8,128)(2,1)S(1)} custom-call(s32[1]{0:T(128)} %bitcast.11.idx, bf16[512,1280]{1,0:T(8,128)(2,1)S(1)} %get-tuple-element.60.rows, f32[8,512]{1,0:T(8,128)S(1)} %get-tuple-element.61.sums, bf16[1280,2560]{1,0:T(8,128)(2,1)S(1)} %bitcast.19), custom_call_target="tpu_custom_call" | custom-call | flops 838860800 | bytes 4000000 | tf_op jit(solution)/shard_map/out_block/pallas_call | solution.py:473
  92.6 3.7 %collective-permute-start.14 = (bf16[528,640]{1,0:T(8,128)(2,1)S(1)}, bf16[528,640]{1,0:T(8,128)(2,1)S(1)}, u32[]{:S(2)}, u32[]{:S(2)}) collective-permute-start(bf16[528,640]{1,0:T(8,128)(2,1)S(1)} %out_block.5), channel_id=1, source_target_pairs={{0,6},{2,0},{4,2},{6,4},{1,7},{3,1},{5,3},{7,5},{8,14},{10,8},{12,... | collective-permute-start | bytes 2027528 | tf_op jit(solution)/shard_map/ppermute | solution.py:57
  96.3 1.2 %out_block.4 = bf16[528,640]{1,0:T(8,128)(2,1)S(1)} custom-call(s32[1]{0:T(128)} %bitcast.10.idx, bf16[512,1280]{1,0:T(8,128)(2,1)S(1)} %get-tuple-element.60.rows, f32[8,512]{1,0:T(8,128)S(1)} %get-tuple-element.61.sums, bf16[1280,2560]{1,0:T(8,128)(2,1)S(1)} %bitcast.19), custom_call_target="tpu_custom_call" | custom-call | flops 838860800 | bytes 4000000 | tf_op jit(solution)/shard_map/out_block/pallas_call | solution.py:473
  97.6 0.1 collective-permute-start.13
  97.6 1.5 %collective-permute-start.12 = (bf16[528,640]{1,0:T(8,128)(2,1)S(1)}, bf16[528,640]{1,0:T(8,128)(2,1)S(1)}, u32[]{:S(2)}, u32[]{:S(2)}) collective-permute-start(bf16[528,640]{1,0:T(8,128)(2,1)S(1)} %get-tuple-element.62), channel_id=1, source_target_pairs={{0,4},{2,6},{4,0},{6,2},{1,5},{3,7},{5,1},{7,3},{8,12},{10,14},{12... | collective-permute-start | bytes 2027528 | tf_op jit(solution)/shard_map/ppermute | solution.py:57
  99.1 1.2 out_block.3.own
  100.3 17.0 %collective-permute-done.14.r3 = bf16[528,640]{1,0:T(8,128)(2,1)S(1)} collective-permute-done((bf16[528,640]{1,0:T(8,128)(2,1)S(1)}, bf16[528,640]{1,0:T(8,128)(2,1)S(1)}, u32[]{:S(2)}, u32[]{:S(2)}) %collective-permute-start.14) | collective-permute-done | bytes 675872 | tf_op jit(solution)/shard_map/ppermute | solution.py:57
  117.4 4.7 %collective-permute-done.13.r2 = bf16[528,640]{1,0:T(8,128)(2,1)S(1)} collective-permute-done((bf16[528,640]{1,0:T(8,128)(2,1)S(1)}, bf16[528,640]{1,0:T(8,128)(2,1)S(1)}, u32[]{:S(2)}, u32[]{:S(2)}) %collective-permute-start.13) | collective-permute-done | bytes 675872 | tf_op jit(solution)/shard_map/ppermute | solution.py:57
  122.0 1.4 %norm.1 = bf16[512,640]{1,0:T(8,128)(2,1)} custom-call(f32[512,640]{1,0:T(8,128)S(1)} %out_block.3.own, f32[8,512]{1,0:T(8,128)S(1)} %get-tuple-element.61.sums, bf16[528,640]{1,0:T(8,128)(2,1)S(1)} %collective-permute-done.12.r1, bf16[528,640]{1,0:T(8,128)(2,1)S(1)} %collective-permute-done.13.r2, bf16[528,640]{1,0:T(8,128)(2,1)S(1)} %collective-permute-done.14.r3), custom_call_target="tpu_custom_call" | custom-call | flops 2000000 | bytes 5000000 | tf_op jit(solution)/shard_map/norm/pallas_call | solution.py:511
  (46 shorter events, 0.1 us)
Async XLA Ops:
  0.0 10.5 %copy-start.17 = (s32[512]{0:T(512)S(1)}, s32[512]{0:T(512)}, u32[]{:S(2)}) copy-start(s32[512]{0:T(512)} %param.12) | copy-start | bytes 6148
  0.0 10.5 %copy-start.20 = (f32[20]{0:T(128)S(1)}, f32[20]{0:T(128)}, u32[]{:S(2)}) copy-start(f32[20]{0:T(128)} %param.17) | copy-start | bytes 244
  0.0 10.5 %copy-start.19 = (f32[20]{0:T(128)S(1)}, f32[20]{0:T(128)}, u32[]{:S(2)}) copy-start(f32[20]{0:T(128)} %param.18) | copy-start | bytes 244
  0.0 23.0 %collective-permute-start.2 = (bf16[512,640]{1,0:T(8,128)(2,1)}, bf16[512,640]{1,0:T(8,128)(2,1)}, u32[]{:S(2)}, u32[]{:S(2)}) collective-permute-start(bf16[512,640]{1,0:T(8,128)(2,1)} %tok.1), channel_id=1, source_target_pairs={{0,2},{2,4},{4,6},{6,0},{1,3},{3,5},{5,7},{7,1},{8,10},{10,12},{12... | collective-permute-start | bytes 1966088 | tf_op jit(solution)/shard_map/ppermute | solution.py:57
  1.7 27.5 %collective-permute-start.1 = (bf16[512,640]{1,0:T(8,128)(2,1)}, bf16[512,640]{1,0:T(8,128)(2,1)}, u32[]{:S(2)}, u32[]{:S(2)}) collective-permute-start(bf16[512,640]{1,0:T(8,128)(2,1)} %tok.1), channel_id=1, source_target_pairs={{0,6},{2,0},{4,2},{6,4},{1,7},{3,1},{5,3},{7,5},{8,14},{10,8},{12,... | collective-permute-start | bytes 1966088 | tf_op jit(solution)/shard_map/ppermute | solution.py:57
  3.2 31.5 %collective-permute-start = (bf16[512,640]{1,0:T(8,128)(2,1)}, bf16[512,640]{1,0:T(8,128)(2,1)S(1)}, u32[]{:S(2)}, u32[]{:S(2)}) collective-permute-start(bf16[512,640]{1,0:T(8,128)(2,1)} %tok.1), channel_id=1, source_target_pairs={{0,4},{2,6},{4,0},{6,2},{1,5},{3,7},{5,1},{7,3},{8,12},{10,14},{12... | collective-permute-start | bytes 1966088 | tf_op jit(solution)/shard_map/ppermute | solution.py:57
  5.2 17.8 %slice-start = ((s8[6553600]{0:T(1024)(128)(4,1)}), s8[2359296]{0:T(1024)(128)(4,1)S(1)}, s32[]{:S(2)}) async-start(s8[6553600]{0:T(1024)(128)(4,1)} %bitcast.14), calls=%async_computation | async-start | bytes 4718592
  10.5 2.9 %copy-start = (bf16[2560,1280]{1,0:T(8,128)(2,1)S(1)}, bf16[2560,1280]{1,0:T(8,128)(2,1)}, u32[]{:S(2)}) copy-start(bf16[2560,1280]{1,0:T(8,128)(2,1)} %w_x.7) | copy-start | bytes 19660804
  13.4 2.9 %copy-start.1 = (bf16[2560,1280]{1,0:T(8,128)(2,1)S(1)}, bf16[2560,1280]{1,0:T(8,128)(2,1)}, u32[]{:S(2)}) copy-start(bf16[2560,1280]{1,0:T(8,128)(2,1)} %w_z.7) | copy-start | bytes 19660804
  16.3 1.5 %copy-start.3 = (bf16[2560,384]{1,0:T(8,128)(2,1)S(1)}, bf16[2560,384]{1,0:T(8,128)(2,1)}, u32[]{:S(2)}) copy-start(bf16[2560,384]{1,0:T(8,128)(2,1)} %fusion.1.w_bd) | copy-start | bytes 5898244
  17.8 1.1 copy-start.7
  18.9 4.2 %slice-start.1 = ((s8[6553600]{0:T(1024)(128)(4,1)}), s8[4194304]{0:T(1024)(128)(4,1)S(1)}, s32[]{:S(2)}) async-start(s8[6553600]{0:T(1024)(128)(4,1)} %bitcast.14), calls=%async_computation.1 | async-start | bytes 8388608
  18.9 4.2 %copy-start.2 = (bf16[2560,1280]{1,0:T(8,128)(2,1)S(1)}, bf16[2560,1280]{1,0:T(8,128)(2,1)}, u32[]{:S(2)}) copy-start(bf16[2560,1280]{1,0:T(8,128)(2,1)} %w_z.7) | copy-start | bytes 19660804
  18.9 4.7 %copy-start.4 = (bf16[2560,384]{1,0:T(8,128)(2,1)S(1)}, bf16[2560,384]{1,0:T(8,128)(2,1)}, u32[]{:S(2)}) copy-start(bf16[2560,384]{1,0:T(8,128)(2,1)} %fusion.1.w_bd) | copy-start | bytes 5898244
  34.7 7.5 %copy-start.5 = (f32[512,1280]{1,0:T(8,128)}, f32[512,1280]{1,0:T(8,128)S(1)}, u32[]{:S(2)}) copy-start(f32[512,1280]{1,0:T(8,128)S(1)} %get-tuple-element.59.acc_z) | copy-start | bytes 7864324
  34.9 30.2 %copy-start.18 = (f32[20]{0:T(128)S(1)}, f32[20]{0:T(128)}, u32[]{:S(2)}) copy-start(f32[20]{0:T(128)} %param.19) | copy-start | bytes 244
  34.9 30.4 %copy-start.16 = (f32[1280]{0:T(1024)S(1)}, f32[1280]{0:T(1024)}, u32[]{:S(2)}) copy-start(f32[1280]{0:T(1024)} %param.20) | copy-start | bytes 15364
  42.3 0.8 copy-start.8
  43.1 1.1 copy-start.10
  44.2 0.7 copy-start.12
  44.9 0.7 copy-start.14
  45.6 9.4 %collective-permute-start.3 = (bf16[48,1280]{1,0:T(8,128)(2,1)}, bf16[48,1280]{1,0:T(8,128)(2,1)S(1)}, u32[]{:S(2)}, u32[]{:S(2)}) collective-permute-start(bf16[48,1280]{1,0:T(8,128)(2,1)} %get-tuple-element.43), channel_id=1, source_target_pairs={{0,8},{8,16},{16,24},{24,0},{1,9},{9,17},{17,25},{25,1},{2,10},{10... | collective-permute-start | bytes 368648 | tf_op jit(solution)/shard_map/ppermute | solution.py:57
  49.8 8.0 %collective-permute-start.4 = (bf16[48,1280]{1,0:T(8,128)(2,1)}, bf16[48,1280]{1,0:T(8,128)(2,1)S(1)}, u32[]{:S(2)}, u32[]{:S(2)}) collective-permute-start(bf16[48,1280]{1,0:T(8,128)(2,1)} %get-tuple-element.44), channel_id=1, source_target_pairs={{0,16},{8,24},{16,0},{24,8},{1,17},{9,25},{17,1},{25,9},{2,18},{10... | collective-permute-start | bytes 368648 | tf_op jit(solution)/shard_map/ppermute | solution.py:57
  53.4 5.1 %collective-permute-start.5 = (bf16[48,1280]{1,0:T(8,128)(2,1)}, bf16[48,1280]{1,0:T(8,128)(2,1)S(1)}, u32[]{:S(2)}, u32[]{:S(2)}) collective-permute-start(bf16[48,1280]{1,0:T(8,128)(2,1)} %get-tuple-element.45), channel_id=1, source_target_pairs={{0,24},{8,0},{16,8},{24,16},{1,25},{9,1},{17,9},{25,17},{2,26},{10... | collective-permute-start | bytes 368648 | tf_op jit(solution)/shard_map/ppermute | solution.py:57
  59.2 6.2 %collective-permute-start.6 = (bf16[48,1280]{1,0:T(8,128)(2,1)S(1)}, bf16[48,1280]{1,0:T(8,128)(2,1)S(1)}, u32[]{:S(2)}, u32[]{:S(2)}) collective-permute-start(bf16[48,1280]{1,0:T(8,128)(2,1)S(1)} %row_total.1.t0), channel_id=1, source_target_pairs={{0,32},{32,64},{64,96},{96,0},{1,33},{33,65},{65,97},{97,1},{2,34}... | collective-permute-start | bytes 368648 | tf_op jit(solution)/shard_map/ppermute | solution.py:57
  60.8 7.1 %collective-permute-start.7 = (bf16[48,1280]{1,0:T(8,128)(2,1)S(1)}, bf16[48,1280]{1,0:T(8,128)(2,1)S(1)}, u32[]{:S(2)}, u32[]{:S(2)}) collective-permute-start(bf16[48,1280]{1,0:T(8,128)(2,1)S(1)} %row_total.1.t0), channel_id=1, source_target_pairs={{0,64},{32,96},{64,0},{96,32},{1,65},{33,97},{65,1},{97,33},{2,66}... | collective-permute-start | bytes 368648 | tf_op jit(solution)/shard_map/ppermute | solution.py:57
  63.8 4.9 %collective-permute-start.8 = (bf16[48,1280]{1,0:T(8,128)(2,1)S(1)}, bf16[48,1280]{1,0:T(8,128)(2,1)S(1)}, u32[]{:S(2)}, u32[]{:S(2)}) collective-permute-start(bf16[48,1280]{1,0:T(8,128)(2,1)S(1)} %row_total.1.t0), channel_id=1, source_target_pairs={{0,96},{32,0},{64,32},{96,64},{1,97},{33,1},{65,33},{97,65},{2,98}... | collective-permute-start | bytes 368648 | tf_op jit(solution)/shard_map/ppermute | solution.py:57
  68.6 13.6 %slice-start.2 = ((s8[6553600]{0:T(1024)(128)(4,1)}), s8[4194304]{0:T(1024)(128)(4,1)S(1)}, s32[]{:S(2)}) async-start(s8[6553600]{0:T(1024)(128)(4,1)} %bitcast.16), calls=%async_computation.2 | async-start | bytes 8388608
  69.5 16.0 %collective-permute-start.10 = (bf16[32,1280]{1,0:T(8,128)(2,1)S(1)}, bf16[32,1280]{1,0:T(8,128)(2,1)S(1)}, u32[]{:S(2)}, u32[]{:S(2)}) collective-permute-start(bf16[32,1280]{1,0:T(8,128)(2,1)S(1)} %get-tuple-element.48), channel_id=1, source_target_pairs={{0,16},{8,24},{16,0},{24,8},{1,17},{9,25},{17,1},{25,9},{2,18},{10... | collective-permute-start | bytes 245768 | tf_op jit(solution)/shard_map/ppermute | solution.py:57
  71.3 14.2 %collective-permute-start.11 = (bf16[32,1280]{1,0:T(8,128)(2,1)S(1)}, bf16[32,1280]{1,0:T(8,128)(2,1)S(1)}, u32[]{:S(2)}, u32[]{:S(2)}) collective-permute-start(bf16[32,1280]{1,0:T(8,128)(2,1)S(1)} %get-tuple-element.49), channel_id=1, source_target_pairs={{0,24},{8,0},{16,8},{24,16},{1,25},{9,1},{17,9},{25,17},{2,26},{10... | collective-permute-start | bytes 245768 | tf_op jit(solution)/shard_map/ppermute | solution.py:57
  72.9 12.6 %collective-permute-start.9 = (bf16[32,1280]{1,0:T(8,128)(2,1)S(1)}, bf16[32,1280]{1,0:T(8,128)(2,1)S(1)}, u32[]{:S(2)}, u32[]{:S(2)}) collective-permute-start(bf16[32,1280]{1,0:T(8,128)(2,1)S(1)} %get-tuple-element.47), channel_id=1, source_target_pairs={{0,8},{8,16},{16,24},{24,0},{1,9},{9,17},{17,25},{25,1},{2,10},{10... | collective-permute-start | bytes 245768 | tf_op jit(solution)/shard_map/ppermute | solution.py:57
  73.4 1.3 %copy-start.11 = (bf16[512,1280]{1,0:T(8,128)(2,1)S(1)}, bf16[512,1280]{1,0:T(8,128)(2,1)}, u32[]{:S(2)}) copy-start(bf16[512,1280]{1,0:T(8,128)(2,1)} %copy-done.10) | copy-start | bytes 3932164
  74.7 0.9 copy-start.13
  75.6 0.9 copy-start.15
  76.6 5.7 %slice-start.3 = ((s8[6553600]{0:T(1024)(128)(4,1)}), s8[2359296]{0:T(1024)(128)(4,1)S(1)}, s32[]{:S(2)}) async-start(s8[6553600]{0:T(1024)(128)(4,1)} %bitcast.16), calls=%async_computation.3 | async-start | bytes 4718592
  76.6 5.7 %copy-start.6 = (f32[512,1280]{1,0:T(8,128)S(1)}, f32[512,1280]{1,0:T(8,128)}, u32[]{:S(2)}) copy-start(f32[512,1280]{1,0:T(8,128)} %copy-done.5) | copy-start | bytes 7864324
  82.2 3.3 %slice-start.4 = ((s8[6553600]{0:T(1024)(128)(4,1)}), s8[4194304]{0:T(1024)(128)(4,1)S(1)}, s32[]{:S(2)}) async-start(s8[6553600]{0:T(1024)(128)(4,1)} %bitcast.18), calls=%async_computation.4 | async-start | bytes 8388608
  82.3 3.2 %slice-start.5 = ((s8[6553600]{0:T(1024)(128)(4,1)}), s8[2359296]{0:T(1024)(128)(4,1)S(1)}, s32[]{:S(2)}) async-start(s8[6553600]{0:T(1024)(128)(4,1)} %bitcast.18), calls=%async_computation.5 | async-start | bytes 4718592
  82.3 3.2 %copy-start.9 = (f32[128,1280]{1,0:T(8,128)S(1)}, f32[128,1280]{1,0:T(8,128)}, u32[]{:S(2)}) copy-start(f32[128,1280]{1,0:T(8,128)} %copy-done.8) | copy-start | bytes 1966084
  92.6 24.8 %collective-permute-start.14 = (bf16[528,640]{1,0:T(8,128)(2,1)S(1)}, bf16[528,640]{1,0:T(8,128)(2,1)S(1)}, u32[]{:S(2)}, u32[]{:S(2)}) collective-permute-start(bf16[528,640]{1,0:T(8,128)(2,1)S(1)} %out_block.5), channel_id=1, source_target_pairs={{0,6},{2,0},{4,2},{6,4},{1,7},{3,1},{5,3},{7,5},{8,14},{10,8},{12,... | collective-permute-start | bytes 2027528 | tf_op jit(solution)/shard_map/ppermute | solution.py:57
  97.6 24.5 %collective-permute-start.13 = (bf16[528,640]{1,0:T(8,128)(2,1)S(1)}, bf16[528,640]{1,0:T(8,128)(2,1)S(1)}, u32[]{:S(2)}, u32[]{:S(2)}) collective-permute-start(bf16[528,640]{1,0:T(8,128)(2,1)S(1)} %out_block.4), channel_id=1, source_target_pairs={{0,2},{2,4},{4,6},{6,0},{1,3},{3,5},{5,7},{7,1},{8,10},{10,12},{12... | collective-permute-start | bytes 2027528 | tf_op jit(solution)/shard_map/ppermute | solution.py:57
  97.6 24.4 %collective-permute-start.12 = (bf16[528,640]{1,0:T(8,128)(2,1)S(1)}, bf16[528,640]{1,0:T(8,128)(2,1)S(1)}, u32[]{:S(2)}, u32[]{:S(2)}) collective-permute-start(bf16[528,640]{1,0:T(8,128)(2,1)S(1)} %get-tuple-element.62), channel_id=1, source_target_pairs={{0,4},{2,6},{4,0},{6,2},{1,5},{3,7},{5,1},{7,3},{8,12},{10,14},{12... | collective-permute-start | bytes 2027528 | tf_op jit(solution)/shard_map/ppermute | solution.py:57

commit v2 on v0

v2 whole, which is shorter than its diff:
```python
import functools

import jax
import jax.numpy as jnp
from jax import lax
from jax.experimental import pallas as pl
from jax.experimental.pallas import tpu as pltpu
from jax.sharding import Mesh
from jax.sharding import PartitionSpec as P

DI = 5120
HEADDIM = 64
NSTATE = 128
GROUP = 256
ROWS = 512
FEAT = 640
WIDTH = 1280
TILE = 256
STEPS = WIDTH // TILE
PER = TILE // HEADDIM
LANES = 128
BD = 384
QUARTER = NSTATE // 4
MSG = QUARTER + 16
OUTROWS = ROWS + 16
HALFROWS = GROUP + 16
LOG2E = 1.4426950408889634
BATCH_SEQ = ("batch", "seq_0", "seq_1")
F32 = jnp.float32
BF16 = jnp.bfloat16
MIB = 1 << 20


def dot(a, b):
    return lax.dot_general(a, b, (((1,), (0,)), ((), ())), preferred_element_type=F32)


def dot_nt(a, b):
    return lax.dot_general(a, b, (((1,), (1,)), ((), ())), preferred_element_type=F32)


def dot_tn(a, b):
    return lax.dot_general(a, b, (((0,), (0,)), ((), ())), preferred_element_type=F32)


def silu(v):
    return v / (1.0 + jnp.exp(-v))


def three(v):
    hi = v.astype(BF16)
    rest = v - hi.astype(F32)
    mid = rest.astype(BF16)
    return hi, mid, (rest - mid.astype(F32)).astype(BF16)


def shifted(array, axis, shift):
    return lax.ppermute(array, axis, [(i, (i + shift) % 4) for i in range(4)])


VMEM = pl.BlockSpec(memory_space=pltpu.VMEM)
HBM = pl.BlockSpec(memory_space=pltpu.HBM)
SMEM = pl.BlockSpec(memory_space=pltpu.SMEM)


def cost(flops, nbytes, trans=0):
    return pl.CostEstimate(flops=int(flops), bytes_accessed=int(nbytes), transcendentals=int(trans))


def call(body, name, idx, args, outs, scratch=(), mib=16, flops=1e8, aliases=None, kept=True):
    args = [pltpu.with_memory_space_constraint(a, pltpu.VMEM) for a in args]
    made = [pltpu.VMEM(*o) if kept else jax.ShapeDtypeStruct(*o) for o in outs]
    return pl.pallas_call(
        body,
        in_specs=[SMEM, *[VMEM] * len(args)],
        out_specs=[VMEM] * len(outs),
        out_shape=made,
        scratch_shapes=[pltpu.VMEM(*s) for s in scratch],
        input_output_aliases=aliases or {},
        compiler_params=pltpu.CompilerParams(vmem_limit_bytes=mib * MIB),
        cost_estimate=cost(flops, 1e6),
        name=name,
    )(idx, *args)


def span(j, size=TILE):
    return slice(j * size, (j + 1) * size)


def block_of(idx, shift):
    owner = lax.rem(idx[0] + 4 - shift, 4)
    return pl.ds(pl.multiple_of(owner * FEAT, FEAT), FEAT)


def add_parts(shift, idx, tokens, w_x, w_bc, w_dt, sums, outs):
    feats = block_of(idx, shift)
    parts = [dot(tokens, w_x[feats, span(j)]) for j in range(STEPS)]
    for j, part in enumerate(parts):
        outs[0][:, span(j)] = sums[0][:, span(j)] + part if sums else part
    part = dot(tokens, w_bc[feats, :])
    outs[1][:, : 2 * NSTATE] = sums[1][:, : 2 * NSTATE] + part if sums else part
    part = dot_nt(tokens, w_dt[:, feats])
    outs[1][:, 2 * NSTATE :] = sums[1][:, 2 * NSTATE :] + part if sums else part


def load_body(idx, tok, w_dt, w_x, w_z, w_bc, acc_x, acc_bd, v_x, v_z, v_bc, sems):
    copies = []
    for shift in range(4):
        feats = block_of(idx, shift)
        for source, target in ((w_x, v_x), (w_bc, v_bc)):
            sem = sems.at[len(copies)]
            copies.append(pltpu.make_async_copy(source.at[feats, :], target.at[feats, :], sem))
    copies.append(pltpu.make_async_copy(w_z, v_z, sems.at[len(copies)]))
    for copy in copies:
        copy.start()
    copies[0].wait()
    copies[1].wait()
    add_parts(0, idx, tok[...], v_x, v_bc, w_dt, (), (acc_x, acc_bd))
    for copy in copies[2:]:
        copy.wait()


def load_weights(idx, tok, w_dt, w_x, w_z, w_bc):
    tok, w_dt = (pltpu.with_memory_space_constraint(a, pltpu.VMEM) for a in (tok, w_dt))
    return pl.pallas_call(
        load_body,
        in_specs=[SMEM, VMEM, VMEM, HBM, HBM, HBM],
        out_specs=[VMEM] * 5,
        out_shape=[
            pltpu.VMEM((ROWS, WIDTH), F32),
            pltpu.VMEM((ROWS, BD), F32),
            pltpu.VMEM(w_x.shape, BF16),
            pltpu.VMEM(w_z.shape, BF16),
            pltpu.VMEM(w_bc.shape, BF16),
        ],
        scratch_shapes=[pltpu.SemaphoreType.DMA((9,))],
        compiler_params=pltpu.CompilerParams(vmem_limit_bytes=36 * MIB),
        cost_estimate=cost(2 * ROWS * FEAT * (WIDTH + BD), 15e6),
        name="load_weights",
    )(idx, tok, w_dt, w_x, w_z, w_bc)


def project_body(shift, idx, tok, w_x, w_bc, w_dt, acc_x, acc_bd, out_x, out_bd):
    add_parts(shift, idx, tok[...], w_x, w_bc, w_dt, (acc_x, acc_bd), (out_x, out_bd))


def project(shift, idx, tok, w_x, w_bc, w_dt, sums):
    return call(
        functools.partial(project_body, shift),
        "project",
        idx,
        [tok, w_x, w_bc, w_dt, *sums],
        [((ROWS, WIDTH), F32), ((ROWS, BD), F32)],
        flops=2 * ROWS * FEAT * (WIDTH + BD),
        aliases={5: 0, 6: 1},
    )


def head_rows(j):
    head = lax.broadcasted_iota(jnp.int32, (LANES, TILE), 0)
    channel = lax.broadcasted_iota(jnp.int32, (LANES, TILE), 1)
    return (head == PER * j + channel // HEADDIM).astype(BF16)


def terms(v, rows, width):
    hi, mid, lo = (part.astype(F32) for part in three(v))
    row = lax.broadcasted_iota(jnp.int32, (rows, width), 0)
    return jnp.where(row == 0, hi, jnp.where(row == 1, mid, jnp.where(row == 2, lo, 0.0)))


def state_body(
    idx, tok_0, tok_1, w_x, w_bc, w_dt, acc_x, acc_bd, resets, bias, rate,
    inner_o, b_o, c_o, cum_o, step_o, first_o, thr_o, m0, m1, m2, m3, state_s,
):
    tokens = jnp.concatenate([tok_0[...], tok_1[...]], 0)
    feats = block_of(idx, 2)
    mapped = silu(acc_bd[:, : 2 * NSTATE] + dot(tokens, w_bc[feats, :]))
    b_t = mapped[:, :NSTATE].T.astype(BF16)
    b_o[...] = mapped[:, :NSTATE].astype(BF16)
    c_o[...] = mapped[:, NSTATE:].astype(BF16)
    logits = acc_bd[:, 2 * NSTATE :] + dot_nt(tokens, w_dt[:, feats]) + bias[...]
    step = jnp.maximum(logits, 0.0) + jnp.log1p(jnp.exp(-jnp.abs(logits)))
    step_o[...] = step
    lane = lax.broadcasted_iota(jnp.int32, (ROWS, LANES), 1)
    decay = jnp.where(lane == LANES - 1, resets[...], -step * rate[...])
    row = lax.broadcasted_iota(jnp.int32, (GROUP, GROUP), 0)
    col = lax.broadcasted_iota(jnp.int32, (GROUP, GROUP), 1)
    lower = (row >= col).astype(BF16)
    keeps, throughs = [], []
    for g in range(2):
        hi, mid, lo = three(decay[span(g, GROUP)])
        cum = dot(lower, hi) + (dot(lower, mid) + dot(lower, lo))
        cum_o[span(g, GROUP), :] = cum
        last = cum[GROUP - 1 :, :]
        seg, closing = cum[:, LANES - 1 :], last[:, LANES - 1 :]
        keeps.append(jnp.where(seg == closing, jnp.exp(last - cum), 0.0) * step[span(g, GROUP)])
        throughs.append(jnp.where(closing == 0.0, jnp.exp(last), 0.0))
    keep = jnp.concatenate(keeps, 0)
    keep_hi = keep.astype(BF16)
    keep_lo = (keep - keep_hi.astype(F32)).astype(BF16)
    through = jnp.concatenate([terms(t, 8, LANES) for t in throughs], 0).astype(BF16)
    for j in range(STEPS):
        inner = silu(acc_x[:, span(j)] + dot(tokens, w_x[feats, span(j)])).astype(BF16)
        inner_o[:, span(j)] = inner
        heads = head_rows(j)
        wide = dot(keep_hi, heads) + dot(keep_lo, heads)
        scaled = (wide * inner.astype(F32)).astype(BF16)
        state0 = dot(b_t[:, :GROUP], scaled[:GROUP])
        state1 = dot(b_t[:, GROUP:], scaled[GROUP:])
        thr = dot(through, heads)
        thr0 = thr[0:1] + thr[1:2] + thr[2:3]
        thr1 = thr[8:9] + thr[9:10] + thr[10:11]
        first_o[:, span(j)] = state0
        thr_o[:, span(j)] = jnp.broadcast_to(thr0, (8, TILE))
        state_s[:, span(j)] = thr1 * state0 + state1
        last_rows = terms(thr0 * thr1, 16, TILE).astype(BF16)
        for message in (m0, m1, m2, m3):
            message[QUARTER:, span(j)] = last_rows
    for d, message in enumerate((m0, m1, m2, m3)):
        start = pl.multiple_of(lax.rem(idx[2] + d, 4) * QUARTER, QUARTER)
        message[:QUARTER, :] = state_s[pl.ds(start, QUARTER), :].astype(BF16)


def device_state(idx, far, w_x, w_bc, w_dt, sums, resets, bias, rate):
    small = (ROWS, LANES)
    return call(
        state_body,
        "device_state",
        idx,
        [*far, w_x, w_bc, w_dt, *sums, resets, bias, rate],
        [
            ((ROWS, WIDTH), BF16), (small, BF16), (small, BF16), (small, F32), (small, F32),
            ((NSTATE, WIDTH), F32), ((8, WIDTH), F32), *[((MSG, WIDTH), BF16)] * 4,
        ],
        [((NSTATE, WIDTH), F32)],
        flops=2 * ROWS * FEAT * (WIDTH + BD),
    )


def decay_of(message):
    tail = message[QUARTER : QUARTER + 3, :].astype(F32)
    return tail[0:1] + tail[1:2] + tail[2:3]


def total_body(idx, m0, m1, m2, m3, out, held):
    for d, message in enumerate((m0, m1, m2, m3)):
        held[lax.rem(idx[2] + 4 - d, 4)] = message[...]
    state = held[0][:QUARTER].astype(F32)
    through = decay_of(held[0])
    for k in range(1, 4):
        decay = decay_of(held[k])
        state = decay * state + held[k][:QUARTER].astype(F32)
        through = through * decay
    out[:QUARTER, :] = state.astype(BF16)
    out[QUARTER:, :] = terms(through, 16, WIDTH).astype(BF16)


def prefix_body(idx, m0, m1, m2, m3, t0, t1, t2, t3, h0, h1, h2, h3, held, rows, found):
    for d, message in enumerate((m0, m1, m2, m3)):
        held[lax.rem(idx[2] + 4 - d, 4)] = message[...]
    for d, message in enumerate((t0, t1, t2, t3)):
        rows[lax.rem(idx[1] + 4 - d, 4)] = message[...]
    state = jnp.zeros((QUARTER, WIDTH), F32)
    for k in range(3):
        after = decay_of(rows[k]) * state + rows[k][:QUARTER].astype(F32)
        state = jnp.where(k < idx[1], after, state)
    for k in range(4):
        found[k] = state.astype(BF16)
        if k < 3:
            state = decay_of(held[k]) * state + held[k][:QUARTER].astype(F32)
    for d, out in enumerate((h0, h1, h2, h3)):
        out[...] = found[lax.rem(idx[2] + d, 4)]


def row_total(idx, messages):
    return call(
        total_body,
        "row_total",
        idx,
        messages,
        [((MSG, WIDTH), BF16)],
        [((4, MSG, WIDTH), BF16)],
        mib=8,
    )[0]


def prefixes(idx, messages, totals):
    return call(
        prefix_body,
        "prefixes",
        idx,
        [*messages, *totals],
        [((QUARTER, WIDTH), BF16)] * 4,
        [((4, MSG, WIDTH), BF16), ((4, MSG, WIDTH), BF16), ((4, QUARTER, WIDTH), BF16)],
        mib=8,
    )


def gate_part_body(idx, t0, t1, t3, w_z, out):
    for j in range(STEPS):
        part = dot(t0[...], w_z[block_of(idx, 0), span(j)])
        for shift, tokens in ((1, t1), (3, t3)):
            part = part + dot(tokens[...], w_z[block_of(idx, shift), span(j)])
        out[:, span(j)] = part


def gate_part(idx, tokens, w_z):
    return call(
        gate_part_body,
        "gate_part",
        idx,
        [*tokens, w_z],
        [((ROWS, WIDTH), F32)],
        flops=6 * ROWS * FEAT * WIDTH,
    )[0]


def gate_body(idx, t_0, t_1, w_z, acc_z, out):
    tokens = jnp.concatenate([t_0[...], t_1[...]], 0)
    feats = block_of(idx, 2)
    for j in range(STEPS):
        gating = acc_z[:, span(j)] + dot(tokens, w_z[feats, span(j)])
        out[:, span(j)] = silu(gating.astype(BF16).astype(F32))


def gate(idx, far, w_z, acc_z):
    return call(
        gate_body,
        "gate",
        idx,
        [*far, w_z, acc_z],
        [((ROWS, WIDTH), F32)],
        flops=2 * ROWS * FEAT * WIDTH,
        aliases={4: 0},
    )[0]


def mix_body(g, idx, inner_r, b_r, c_r, cum_r, step_r, skip, out, ent_o, scores, cum_t, step_t):
    half = GROUP // 2
    rows = span(g, GROUP)
    cum = cum_r[rows, :]
    across = cum.T
    cum_2 = cum * LOG2E
    cum_t[...] = across * LOG2E
    step_t[...] = step_r[rows, :].T
    row = lax.broadcasted_iota(jnp.int32, (GROUP, GROUP), 0)
    col = lax.broadcasted_iota(jnp.int32, (GROUP, GROUP), 1)
    seg = cum[:, LANES - 1 :]
    same = (seg == across[LANES - 1 :, :]) & (row >= col)
    scores[...] = jnp.where(same, dot_nt(c_r[rows, :], b_r[rows, :]), 0.0)
    enter = jnp.where(seg == 0.0, jnp.exp(cum), 0.0)
    hi = enter.astype(BF16)
    lo = (enter - hi.astype(F32)).astype(BF16)
    lane = lax.broadcasted_iota(jnp.int32, (GROUP, LANES), 1)
    for j in range(STEPS):
        heads = head_rows(j)
        ent_o[:, span(j)] = dot(hi, heads) + dot(lo, heads)
    for pair in range(WIDTH // LANES):
        both = inner_r[rows, span(pair, LANES)]
        ys = []
        for head in (2 * pair, 2 * pair + 1):
            before = cum_t[head : head + 1, :]
            step = step_t[head : head + 1, :]
            top = jnp.exp2(jnp.minimum(cum_2[:half, head : head + 1] - before[:, :half], 0.0))
            top = (top * scores[:half, :half] * step[:, :half]).astype(BF16)
            low = jnp.exp2(jnp.minimum(cum_2[half:, head : head + 1] - before, 0.0))
            low = (low * scores[half:, :] * step).astype(BF16)
            ys.append(jnp.concatenate([dot(top, both[:half]), dot(low, both)], 0))
        y = jnp.where(lane < HEADDIM, ys[0], ys[1])
        out[:, span(pair, LANES)] = y + skip[:, span(pair, LANES)] * both.astype(F32)


def mix(g, idx, inner, b, c, cum, step, skip):
    return call(
        functools.partial(mix_body, g),
        "mix",
        idx,
        [inner, b, c, cum, step, skip],
        [((GROUP, WIDTH), F32), ((GROUP, WIDTH), F32)],
        [((GROUP, GROUP), F32), ((LANES, GROUP), F32), ((LANES, GROUP), F32)],
        flops=2e9,
    )


def block_cols(idx, shift):
    target = lax.rem(idx[0] + shift, 4)
    return pl.ds(pl.multiple_of(target * FEAT, FEAT), FEAT)


def squares_rows(total):
    width = total.shape[1]
    rows = terms(total, 16, width).astype(BF16)
    return jnp.concatenate([rows, jnp.zeros((16, FEAT - width), BF16)], 1)


def row_of(message, start, width):
    tail = message[start : start + 3, :width].astype(F32)
    return tail[0:1] + (tail[1:2] + tail[2:3])


def gated_body(
    g, idx, h0, h1, h2, h3, first, thr, c_r, u, ent, zs_r, gain, w_out, rows_o, sums_o, out, state
):
    for d, part in enumerate((h0, h1, h2, h3)):
        start = pl.multiple_of(lax.rem(idx[2] + 4 - d, 4) * QUARTER, QUARTER)
        state[pl.ds(start, QUARTER), :] = part[...]
    ones = jnp.ones((8, LANES), BF16)
    rows = span(g, GROUP)
    squares = jnp.zeros((GROUP, LANES), F32)
    for j in range(STEPS):
        enter = state[:, span(j)]
        if g:
            enter = first[:, span(j)] + thr[0:1, span(j)] * enter.astype(F32)
            enter = enter.astype(BF16)
        carried = dot(c_r[rows, :], enter)
        gated = (u[:, span(j)] + ent[:, span(j)] * carried) * zs_r[rows, span(j)]
        rows_o[:, span(j)] = (gated * gain[:, span(j)]).astype(BF16)
        square = gated * gated
        squares = squares + (square[:, :LANES] + square[:, LANES:])
    hi, mid, lo = three(squares)
    sums = dot_nt(ones, hi) + (dot_nt(ones, mid) + dot_nt(ones, lo))
    sums_o[...] = sums
    out[:GROUP, :] = dot(rows_o[...], w_out[:, block_cols(idx, 2)]).astype(BF16)
    out[GROUP:, :] = squares_rows(sums[0:1, :])


def gated_rows(g, idx, parts, first, thr, c, u, ent, zs, gain, w_out):
    return call(
        functools.partial(gated_body, g),
        "gated_rows",
        idx,
        [*parts, first, thr, c, u, ent, zs, gain, w_out],
        [((GROUP, WIDTH), BF16), ((8, GROUP), F32), ((HALFROWS, FEAT), BF16)],
        [((NSTATE, WIDTH), BF16)],
        flops=1.3 * ROWS * WIDTH * FEAT,
    )


def part_body(shift, idx, rows, w_out, out):
    out[...] = dot(rows[...], w_out[:, block_cols(idx, shift)])


def out_part(shift, idx, rows, w_out):
    return call(
        functools.partial(part_body, shift),
        "out_part",
        idx,
        [rows, w_out],
        [((GROUP, FEAT), F32)],
        flops=ROWS * WIDTH * FEAT,
    )[0]


def send_body(shift, idx, rows, sums, w_out, out):
    out[:GROUP, :] = dot(rows[...], w_out[:, block_cols(idx, shift)]).astype(BF16)
    out[GROUP:, :] = squares_rows(sums[0:1, :])


def out_send(shift, idx, rows, sums, w_out):
    return call(
        functools.partial(send_body, shift),
        "out_send",
        idx,
        [rows, sums, w_out],
        [((HALFROWS, FEAT), BF16)],
        flops=ROWS * WIDTH * FEAT,
    )[0]


def join_body(idx, part, sums, half, out):
    out[:GROUP, :] = (part[...] + half[:GROUP, :].astype(F32)).astype(BF16)
    out[GROUP:, :] = squares_rows(sums[0:1, :] + row_of(half, GROUP, GROUP))


def join(idx, part, sums, half):
    return call(
        join_body,
        "join",
        idx,
        [part, sums, half],
        [((HALFROWS, FEAT), BF16)],
        mib=8,
    )[0]


def norm_body(idx, own_0, own_1, sums_0, sums_1, left_0, left_1, right_0, right_1, out):
    halves = ((own_0, sums_0, left_0, right_0), (own_1, sums_1, left_1, right_1))
    for g, (own, sums, left, right) in enumerate(halves):
        total = sums[0:1, :] + (row_of(left, GROUP, GROUP) + row_of(right, GROUP, GROUP))
        stack = terms(total, 16, GROUP).astype(BF16)
        squares = dot_tn(stack, jnp.ones((16, LANES), BF16))
        factor = lax.rsqrt(squares / DI + 1e-05)
        for k in range(FEAT // LANES):
            lanes = span(k, LANES)
            value = left[:GROUP, lanes].astype(F32) + right[:GROUP, lanes].astype(F32)
            out[span(g, GROUP), lanes] = ((own[:, lanes] + value) * factor).astype(BF16)


def norm(idx, owns, sums, left, right):
    return call(
        norm_body,
        "norm",
        idx,
        [*owns, *sums, *left, *right],
        [((ROWS, FEAT), BF16)],
        kept=False,
    )[0]


def on_device(tokens, resets, w_x, w_z, w_bc, w_dt, dt_bias, decay_rate, d_skip, norm_gain, w_out):
    places = ("head", "seq_0", "seq_1")
    idx = jnp.stack([lax.axis_index(axis) for axis in places]).astype(jnp.int32)
    heads = w_dt.shape[1]
    left, right = shifted(tokens, "head", 1), shifted(tokens, "head", 3)
    w_dt = jnp.pad(w_dt.T, ((0, LANES - heads), (0, 0)))
    bias = jnp.pad(dt_bias, (0, LANES - heads)).reshape(1, LANES)
    rate = jnp.pad(decay_rate, (0, LANES - heads)).reshape(1, LANES)
    starts = jnp.broadcast_to(resets.astype(F32)[:, None], (ROWS, LANES))
    skip = jnp.repeat(d_skip, HEADDIM).reshape(1, WIDTH)
    gain = norm_gain.reshape(1, WIDTH)

    acc_x, acc_bd, w_x, w_z, w_bc = load_weights(idx, tokens, w_dt, w_x, w_z, w_bc)
    left, right, acc_x = lax.optimization_barrier((left, right, acc_x))
    far = [shifted(left[:GROUP], "head", 1), shifted(right[GROUP:], "head", 3)]
    sums = project(1, idx, left, w_x, w_bc, w_dt, (acc_x, acc_bd))
    sums = project(3, idx, right, w_x, w_bc, w_dt, sums)
    acc_z = gate_part(idx, (tokens, left, right), w_z)
    far, acc_z, sums = lax.optimization_barrier((far, acc_z, sums))
    inner, b, c, cum, step, first, thr, *messages = device_state(
        idx, far, w_x, w_bc, w_dt, sums, starts, bias, rate
    )
    quarters = [messages[0], *(shifted(messages[d], "seq_1", d) for d in (1, 2, 3))]
    u0, e0 = mix(0, idx, inner, b, c, cum, step, skip)
    quarters, u0, e0, cum = lax.optimization_barrier((quarters, u0, e0, cum))
    total = row_total(idx, quarters)
    totals = [total, *(shifted(total, "seq_0", d) for d in (1, 2, 3))]
    u1, e1 = mix(1, idx, inner, b, c, cum, step, skip)
    totals, u1, e1, w_z = lax.optimization_barrier((totals, u1, e1, w_z))
    parts = prefixes(idx, quarters, totals)
    parts = [parts[0], *(shifted(parts[d], "seq_1", d) for d in (1, 2, 3))]
    zs = gate(idx, far, w_z, acc_z)
    block_0, sums_0, half_0 = gated_rows(0, idx, parts, first, thr, c, u0, e0, zs, gain, w_out)
    half_0 = shifted(half_0, "head", 1)
    block_1, sums_1, half_1 = gated_rows(1, idx, parts, first, thr, c, u1, e1, zs, gain, w_out)
    half_1 = shifted(half_1, "head", 3)
    right_0 = shifted(out_send(3, idx, block_0, sums_0, w_out), "head", 3)
    left_1 = shifted(out_send(1, idx, block_1, sums_1, w_out), "head", 1)
    near_0, near_1 = out_part(1, idx, block_0, w_out), out_part(3, idx, block_1, w_out)
    left_0 = shifted(join(idx, near_0, sums_0, half_0), "head", 1)
    right_1 = shifted(join(idx, near_1, sums_1, half_1), "head", 3)
    owns = [out_part(0, idx, block, w_out) for block in (block_0, block_1)]
    return norm(idx, owns, (sums_0, sums_1), (left_0, left_1), (right_0, right_1))


def solution(mesh):
    split = Mesh(
        mesh.devices.reshape(4, 4, mesh.shape["head"], mesh.shape["batch"]),
        ("seq_0", "seq_1", "head", "batch"),
    )
    placed = (
        P(BATCH_SEQ, "head"),
        P(BATCH_SEQ),
        P(None, "head"),
        P(None, "head"),
        P(),
        P(None, "head"),
        P("head"),
        P("head"),
        P("head"),
        P("head"),
        P("head", None),
    )
    return jax.shard_map(
        on_device, mesh=split, in_specs=placed, out_specs=P(BATCH_SEQ, "head"), check_vma=False
    )
```

time: 330 us -> 93.9 us (0.28); the launches traced: 324 us -> 93.7 us
  waiting for transfers between devices: 125 us -> 14.7 us
  local copies, waits for them, and re-layouts: 83.1 us -> 3.05 us
  matrix products: 53.7 us -> 0 us
  Pallas kernels: 0 us -> 41.9 us
  blocking collectives: 30.1 us -> 0 us
  starting transfers between devices: 4.98 us -> 32.4 us
  between operations: 14 us -> 0.27 us
  other arithmetic: 11.7 us -> 1.29 us
    dynamic_update_slice x4 -> x0, local copies, waits for them, and re-layouts: 57 us -> none  [on_device(): lax.scan(advance, jnp.zeros((heads_dev, HEADDIM, NSTATE), jnp.float32), s...]
    reduce_scatter x1 -> x0, waiting for transfers between devices: 53.8 us -> none  [on_device(): lax.psum_scatter(partial_terms, 'head', scatter_dimension=1, tiled=True)]
    dot_general x14 -> x0, matrix products: 53.7 us -> none  [the longest x4 24 us: on_device(): jnp.dot(column_piece, matrix, preferred_element_type=jnp.float32)]
    pallas_call x0 -> x21, Pallas kernels: none -> 41.9 us  [the longest x20 35.8 us: call(): pl.pallas_call(body, in_specs=[SMEM, *[VMEM] * len(args)], out_specs=[VME...]
    all_gather x2 -> x0, waiting for transfers between devices: 39.2 us -> none  [carried_in(): pieces = jax.tree.map(lambda part: lax.all_gather(part, axis), so_far)]
    ppermute x0 -> x19, starting transfers between devices: none -> 32.4 us  [shifted(): return lax.ppermute(array, axis, [(i, (i + shift) % 4) for i in range(4)])]
    all_to_all x1 -> x0, waiting for transfers between devices: 32.1 us -> none  [sent_to_all(): return lax.all_to_all(copies, axis, split_axis=0, concat_axis=0, tiled=True)]
    all_gather x2 -> x0, blocking collectives: 20.8 us -> none  [carried_in(): pieces = jax.tree.map(lambda part: lax.all_gather(part, axis), so_far)]
  transfers between devices with their start and end apart: 4 -> 19, of which waited for: 4 -> 9; matrix products, arithmetic and copies ran while one was open for 3% -> 3% of each run, Pallas kernels for 0% -> 34%
where the time goes in v2:
time: 93.9 us; the launch traced here: 93.7 us
  Pallas kernels  41.9 us (45%)
  starting transfers between devices  32.4 us (35%)
  waiting for transfers between devices  14.7 us (16%)
  local copies, waits for them, and re-layouts  3.05 us (3%)
  other arithmetic  1.29 us (1%)
    pallas_call x20, Pallas kernels, call(): pl.pallas_call(body, in_specs=[SMEM, *[VMEM] * len(args)], out_specs=[VME...  35.8 us
    ppermute x19, starting transfers between devices, shifted(): return lax.ppermute(array, axis, [(i, (i + shift) % 4) for i in range(4)])  32.4 us
    ppermute x19, waiting for transfers between devices, shifted(): return lax.ppermute(array, axis, [(i, (i + shift) % 4) for i in range(4)])  14.7 us
    pallas_call x1, Pallas kernels, load_weights(): pl.pallas_call(load_body, in_specs=[SMEM, VMEM, VMEM, HBM, HBM, HBM], out...  6.08 us
  transfers between devices with their start and end apart: 19, of which 9 were waited for; matrix products, arithmetic and copies ran while one was open for 3% of the time, Pallas kernels for 34%

profile of v2, /device:TPU:0, one launch (start us, length us, event | category | flops | bytes accessed | tf_op | source)
XLA Modules:
  0.0 93.7 jit_solution(10310179482129568750)
XLA Ops:
  0.0 1.6 %collective-permute-start = (bf16[512,640]{1,0:T(8,128)(2,1)}, bf16[512,640]{1,0:T(8,128)(2,1)S(1)}, u32[]{:S(2)}, u32[]{:S(2)}) collective-permute-start(bf16[512,640]{1,0:T(8,128)(2,1)} %t0.1), channel_id=1, source_target_pairs={{0,2},{2,4},{4,6},{6,0},{1,3},{3,5},{5,7},{7,1},{8,10},{10,12},{12... | collective-permute-start | bytes 1966088 | tf_op jit(solution)/shard_map/ppermute | solution.py:58
  1.6 1.7 %collective-permute-start.1 = (bf16[512,640]{1,0:T(8,128)(2,1)}, bf16[512,640]{1,0:T(8,128)(2,1)S(1)}, u32[]{:S(2)}, u32[]{:S(2)}) collective-permute-start(bf16[512,640]{1,0:T(8,128)(2,1)} %t0.1), channel_id=1, source_target_pairs={{0,6},{2,0},{4,2},{6,4},{1,7},{3,1},{5,3},{7,5},{8,14},{10,8},{12,... | collective-permute-start | bytes 1966088 | tf_op jit(solution)/shard_map/ppermute | solution.py:58
  3.2 0.7 convert_element_type.8
  3.9 0.7 broadcast_in_dim.10
  4.6 0.1 reshape_reshape.3.skip
  4.7 0.9 %pad.11.w_dt = bf16[128,2560]{1,0:T(8,128)(2,1)S(1)} pad(bf16[20,2560]{1,0:T(8,128)(2,1)} %bitcast.10, bf16[]{:T(256)} %constant.16.clone.1), padding=0_108x0_0 | pad | bytes 757762 | tf_op jit(solution)/shard_map/jit(_pad)/pad | solution.py:515
  5.7 0.6 pad_add_fusion.idx
  6.3 1.1 %copy-done = bf16[512,640]{1,0:T(8,128)(2,1)S(1)} copy-done((bf16[512,640]{1,0:T(8,128)(2,1)S(1)}, bf16[512,640]{1,0:T(8,128)(2,1)}, u32[]{:S(2)}) %copy-start) | copy-done | bytes 655384
  7.4 6.1 %load_weights.1 = (f32[512,1280]{1,0:T(8,128)S(1)}, f32[512,384]{1,0:T(8,128)S(1)}, bf16[2560,1280]{1,0:T(8,128)(2,1)S(1)}, bf16[2560,1280]{1,0:T(8,128)(2,1)S(1)}, bf16[2560,256]{1,0:T(8,128)(2,1)S(1)}) custom-call(s32[3]{0:T(128)} %pad_add_fusion.idx, bf16[512,640]{1,0:T(8,128)(2,1)S(1)} %copy-done, bf16[128,2560]{1,0:T(8,128)(2,1)S(1)} %pad.11.w_dt, ...), custom_call_target="tpu_custom_call" | custom-call | flops 1090519040 | bytes 15000000 | tf_op jit(solution)/shard_map/load_weights/pallas_call | solution.py:125
  13.5 4.3 %collective-permute-done.t1.tok = bf16[512,640]{1,0:T(8,128)(2,1)S(1)} collective-permute-done((bf16[512,640]{1,0:T(8,128)(2,1)}, bf16[512,640]{1,0:T(8,128)(2,1)S(1)}, u32[]{:S(2)}, u32[]{:S(2)}) %collective-permute-start) | collective-permute-done | bytes 655392 | tf_op jit(solution)/shard_map/ppermute | solution.py:58
  17.8 0.2 collective-permute-done.1.t3.tok
  18.0 1.6 %collective-permute-start.2 = (bf16[256,640]{1,0:T(8,128)(2,1)S(1)}, bf16[256,640]{1,0:T(8,128)(2,1)S(1)}, u32[]{:S(2)}, u32[]{:S(2)}) collective-permute-start(bf16[256,640]{1,0:T(8,128)(2,1)S(1)} %slice.6), channel_id=1, source_target_pairs={{0,2},{2,4},{4,6},{6,0},{1,3},{3,5},{5,7},{7,1},{8,10},{10,12},{12... | collective-permute-start | bytes 983048 | tf_op jit(solution)/shard_map/ppermute | solution.py:58
  19.6 1.8 %collective-permute-start.3 = (bf16[256,640]{1,0:T(8,128)(2,1)S(1)}, bf16[256,640]{1,0:T(8,128)(2,1)S(1)}, u32[]{:S(2)}, u32[]{:S(2)}) collective-permute-start(bf16[256,640]{1,0:T(8,128)(2,1)S(1)} %slice.7), channel_id=1, source_target_pairs={{0,6},{2,0},{4,2},{6,4},{1,7},{3,1},{5,3},{7,5},{8,14},{10,8},{12,... | collective-permute-start | bytes 983048 | tf_op jit(solution)/shard_map/ppermute | solution.py:58
  21.4 2.2 %project.2 = (f32[512,1280]{1,0:T(8,128)S(1)}, f32[512,384]{1,0:T(8,128)S(1)}) custom-call(s32[3]{0:T(128)S(1)} %copy-done.1, bf16[512,640]{1,0:T(8,128)(2,1)S(1)} %collective-permute-done.t1.tok, bf16[2560,1280]{1,0:T(8,128)(2,1)S(1)} %get-tuple-element.65.w_x, ...), custom_call_target="tpu_custom_call", output_to_operand_aliasing={{0}: (5, {}), {1}: (6, {})} | custom-call | flops 1090519040 | bytes 1000000 | tf_op jit(solution)/shard_map/project/pallas_call | solution.py:73
  23.7 2.2 %project.3 = (f32[512,1280]{1,0:T(8,128)S(1)}, f32[512,384]{1,0:T(8,128)S(1)}) custom-call(s32[3]{0:T(128)S(1)} %copy-done.1, bf16[512,640]{1,0:T(8,128)(2,1)S(1)} %collective-permute-done.1.t3.tok, bf16[2560,1280]{1,0:T(8,128)(2,1)S(1)} %get-tuple-element.65.w_x, ...), custom_call_target="tpu_custom_call", output_to_operand_aliasing={{0}: (5, {}), {1}: (6, {})} | custom-call | flops 1090519040 | bytes 1000000 | tf_op jit(solution)/shard_map/project/pallas_call | solution.py:73
  25.9 3.7 %gate_part.1.acc_z = f32[512,1280]{1,0:T(8,128)S(1)} custom-call(s32[3]{0:T(128)S(1)} %copy-done.1, bf16[512,640]{1,0:T(8,128)(2,1)S(1)} %copy-done, bf16[512,640]{1,0:T(8,128)(2,1)S(1)} %collective-permute-done.t1.tok, bf16[512,640]{1,0:T(8,128)(2,1)S(1)} %collective-permute-done.1.t3.tok, bf16[2560,1280]{1,0:T(8,128)(2,1)S(1)} %get-tuple-element.107.w_z), custom_call_target="tpu_custom_call" | custom-call | flops 2516582400 | bytes 1000000 | tf_op jit(solution)/shard_map/gate_part/pallas_call | solution.py:73
  29.7 0.0 collective-permute-done.2.tok_0.t_0
  29.7 0.0 collective-permute-done.3.tok_1.t_1
  29.7 0.1 broadcast_in_dim.4.resets
  29.8 4.7 %device_state.1 = (bf16[512,1280]{1,0:T(8,128)(2,1)S(1)}, bf16[512,128]{1,0:T(8,128)(2,1)S(1)}, bf16[512,128]{1,0:T(8,128)(2,1)S(1)}, f32[512,128]{1,0:T(8,128)S...) custom-call(s32[3]{0:T(128)S(1)} %copy-done.1, ...), custom_call_target="tpu_custom_call" | custom-call | flops 1090519040 | bytes 1000000 | tf_op jit(solution)/shard_map/device_state/pallas_call | solution.py:73
  34.6 2.0 %collective-permute-start.4 = (bf16[48,1280]{1,0:T(8,128)(2,1)S(1)}, bf16[48,1280]{1,0:T(8,128)(2,1)S(1)}, u32[]{:S(2)}, u32[]{:S(2)}) collective-permute-start(bf16[48,1280]{1,0:T(8,128)(2,1)S(1)} %get-tuple-element.78), channel_id=1, source_target_pairs={{0,8},{8,16},{16,24},{24,0},{1,9},{9,17},{17,25},{25,1},{2,10},{10... | collective-permute-start | bytes 368648 | tf_op jit(solution)/shard_map/ppermute | solution.py:58
  36.6 3.6 %collective-permute-start.5 = (bf16[48,1280]{1,0:T(8,128)(2,1)S(1)}, bf16[48,1280]{1,0:T(8,128)(2,1)S(1)}, u32[]{:S(2)}, u32[]{:S(2)}) collective-permute-start(bf16[48,1280]{1,0:T(8,128)(2,1)S(1)} %get-tuple-element.79), channel_id=1, source_target_pairs={{0,16},{8,24},{16,0},{24,8},{1,17},{9,25},{17,1},{25,9},{2,18},{10... | collective-permute-start | bytes 368648 | tf_op jit(solution)/shard_map/ppermute | solution.py:58
  40.1 1.0 %collective-permute-start.6 = (bf16[48,1280]{1,0:T(8,128)(2,1)S(1)}, bf16[48,1280]{1,0:T(8,128)(2,1)S(1)}, u32[]{:S(2)}, u32[]{:S(2)}) collective-permute-start(bf16[48,1280]{1,0:T(8,128)(2,1)S(1)} %get-tuple-element.80), channel_id=1, source_target_pairs={{0,24},{8,0},{16,8},{24,16},{1,25},{9,1},{17,9},{25,17},{2,26},{10... | collective-permute-start | bytes 368648 | tf_op jit(solution)/shard_map/ppermute | solution.py:58
  41.1 2.2 %mix.2 = (f32[256,1280]{1,0:T(8,128)S(1)}, f32[256,1280]{1,0:T(8,128)S(1)}) custom-call(s32[3]{0:T(128)S(1)} %copy-done.1, bf16[512,1280]{1,0:T(8,128)(2,1)S(1)} %get-tuple-element.81.inner_r, bf16[512,128]{1,0:T(8,128)(2,1)S(1)} %get-tuple-element.82.b_r, bf16[512,128]{1,0:T(8,128)(2,1)S(1)} %get-tuple-element.83.c_r, ...), custom_call_target="tpu_custom_call" | custom-call | flops 2000000000 | bytes 1000000 | tf_op jit(solution)/shard_map/mix/pallas_call | solution.py:73
  43.4 0.0 collective-permute-done.4.m1
  43.4 1.0 %collective-permute-done.5.m2 = bf16[48,1280]{1,0:T(8,128)(2,1)S(1)} collective-permute-done((bf16[48,1280]{1,0:T(8,128)(2,1)S(1)}, bf16[48,1280]{1,0:T(8,128)(2,1)S(1)}, u32[]{:S(2)}, u32[]{:S(2)}) %collective-permute-start.5) | collective-permute-done | bytes 122912 | tf_op jit(solution)/shard_map/ppermute | solution.py:58
  44.4 0.6 collective-permute-done.6.m3
  45.0 0.7 row_total.1.t0
  45.7 0.0 copy-start.2
  45.7 1.6 %collective-permute-start.7 = (bf16[48,1280]{1,0:T(8,128)(2,1)S(1)}, bf16[48,1280]{1,0:T(8,128)(2,1)S(1)}, u32[]{:S(2)}, u32[]{:S(2)}) collective-permute-start(bf16[48,1280]{1,0:T(8,128)(2,1)S(1)} %row_total.1.t0), channel_id=1, source_target_pairs={{0,32},{32,64},{64,96},{96,0},{1,33},{33,65},{65,97},{97,1},{2,34}... | collective-permute-start | bytes 368648 | tf_op jit(solution)/shard_map/ppermute | solution.py:58
  47.4 2.9 %collective-permute-start.8 = (bf16[48,1280]{1,0:T(8,128)(2,1)S(1)}, bf16[48,1280]{1,0:T(8,128)(2,1)S(1)}, u32[]{:S(2)}, u32[]{:S(2)}) collective-permute-start(bf16[48,1280]{1,0:T(8,128)(2,1)S(1)} %row_total.1.t0), channel_id=1, source_target_pairs={{0,64},{32,96},{64,0},{96,32},{1,65},{33,97},{65,1},{97,33},{2,66}... | collective-permute-start | bytes 368648 | tf_op jit(solution)/shard_map/ppermute | solution.py:58
  50.3 1.3 %collective-permute-start.9 = (bf16[48,1280]{1,0:T(8,128)(2,1)S(1)}, bf16[48,1280]{1,0:T(8,128)(2,1)S(1)}, u32[]{:S(2)}, u32[]{:S(2)}) collective-permute-start(bf16[48,1280]{1,0:T(8,128)(2,1)S(1)} %row_total.1.t0), channel_id=1, source_target_pairs={{0,96},{32,0},{64,32},{96,64},{1,97},{33,1},{65,33},{97,65},{2,98}... | collective-permute-start | bytes 368648 | tf_op jit(solution)/shard_map/ppermute | solution.py:58
  51.6 2.2 %mix.3 = (f32[256,1280]{1,0:T(8,128)S(1)}, f32[256,1280]{1,0:T(8,128)S(1)}) custom-call(s32[3]{0:T(128)S(1)} %copy-done.1, bf16[512,1280]{1,0:T(8,128)(2,1)S(1)} %get-tuple-element.81.inner_r, bf16[512,128]{1,0:T(8,128)(2,1)S(1)} %get-tuple-element.82.b_r, bf16[512,128]{1,0:T(8,128)(2,1)S(1)} %get-tuple-element.83.c_r, ...), custom_call_target="tpu_custom_call" | custom-call | flops 2000000000 | bytes 1000000 | tf_op jit(solution)/shard_map/mix/pallas_call | solution.py:73
  53.9 0.0 collective-permute-done.7.t1
  53.9 0.6 collective-permute-done.8.t2
  54.5 0.7 collective-permute-done.9.t3
  55.2 0.8 prefixes.1
  56.0 0.9 collective-permute-start.10
  56.9 2.9 %collective-permute-start.11 = (bf16[32,1280]{1,0:T(8,128)(2,1)S(1)}, bf16[32,1280]{1,0:T(8,128)(2,1)S(1)}, u32[]{:S(2)}, u32[]{:S(2)}) collective-permute-start(bf16[32,1280]{1,0:T(8,128)(2,1)S(1)} %get-tuple-element.101), channel_id=1, source_target_pairs={{0,16},{8,24},{16,0},{24,8},{1,17},{9,25},{17,1},{25,9},{2,18},{10... | collective-permute-start | bytes 245768 | tf_op jit(solution)/shard_map/ppermute | solution.py:58
  59.7 0.8 collective-permute-start.12
  60.5 0.0 slice-start.1
  60.5 2.6 %gate.1.zs_r = f32[512,1280]{1,0:T(8,128)S(1)} custom-call(s32[3]{0:T(128)S(1)} %copy-done.1, bf16[256,640]{1,0:T(8,128)(2,1)S(1)} %collective-permute-done.2.tok_0.t_0, bf16[256,640]{1,0:T(8,128)(2,1)S(1)} %collective-permute-done.3.tok_1.t_1, bf16[2560,1280]{1,0:T(8,128)(2,1)S(1)} %get-tuple-element.107.w_z, ...), custom_call_target="tpu_custom_call", output_to_operand_aliasing={{}: (4, {})} | custom-call | flops 838860800 | bytes 1000000 | tf_op jit(solution)/shard_map/gate/pallas_call | solution.py:73
  63.2 0.0 collective-permute-done.11.h2
  63.2 1.0 %collective-permute-done.12.h3 = bf16[32,1280]{1,0:T(8,128)(2,1)S(1)} collective-permute-done((bf16[32,1280]{1,0:T(8,128)(2,1)S(1)}, bf16[32,1280]{1,0:T(8,128)(2,1)S(1)}, u32[]{:S(2)}, u32[]{:S(2)}) %collective-permute-start.12) | collective-permute-done | bytes 81952 | tf_op jit(solution)/shard_map/ppermute | solution.py:58
  64.2 1.9 %gated_rows.3 = (bf16[256,1280]{1,0:T(8,128)(2,1)S(1)}, f32[8,256]{1,0:T(8,128)S(1)}, bf16[272,640]{1,0:T(8,128)(2,1)S(1)}) custom-call(s32[3]{0:T(128)S(1)} %copy-done.1, bf16[32,1280]{1,0:T(8,128)(2,1)S(1)} %get-tuple-element.99.h0, bf16[32,1280]{1,0:T(8,128)(2,1)S(1)} %collective-permute-done.10.h1, bf16[32,1280]{1,0:T(8,128)(2,1)S(1)} %collective-permute-done.11.h2, ...), custom_call_target="tpu_custom_call" | custom-call | flops 545259520 | bytes 1000000 | tf_op jit(solution)/shard_map/gated_rows/pallas_call | solution.py:73
  66.1 1.8 %collective-permute-start.17 = (bf16[272,640]{1,0:T(8,128)(2,1)S(1)}, bf16[272,640]{1,0:T(8,128)(2,1)S(1)}, u32[]{:S(2)}, u32[]{:S(2)}) collective-permute-start(bf16[272,640]{1,0:T(8,128)(2,1)S(1)} %get-tuple-element.116), channel_id=1, source_target_pairs={{0,6},{2,0},{4,2},{6,4},{1,7},{3,1},{5,3},{7,5},{8,14},{10,8},{12,... | collective-permute-start | bytes 1044488 | tf_op jit(solution)/shard_map/ppermute | solution.py:58
  67.9 1.9 %gated_rows.2 = (bf16[256,1280]{1,0:T(8,128)(2,1)S(1)}, f32[8,256]{1,0:T(8,128)S(1)}, bf16[272,640]{1,0:T(8,128)(2,1)S(1)}) custom-call(s32[3]{0:T(128)S(1)} %copy-done.1, bf16[32,1280]{1,0:T(8,128)(2,1)S(1)} %get-tuple-element.99.h0, bf16[32,1280]{1,0:T(8,128)(2,1)S(1)} %collective-permute-done.10.h1, bf16[32,1280]{1,0:T(8,128)(2,1)S(1)} %collective-permute-done.11.h2, ...), custom_call_target="tpu_custom_call" | custom-call | flops 545259520 | bytes 1000000 | tf_op jit(solution)/shard_map/gated_rows/pallas_call | solution.py:73
  69.8 0.3 collective-permute-start.13
  70.1 1.2 %out_send.3 = bf16[272,640]{1,0:T(8,128)(2,1)S(1)} custom-call(s32[3]{0:T(128)S(1)} %copy-done.1, bf16[256,1280]{1,0:T(8,128)(2,1)S(1)} %get-tuple-element.109.rows, f32[8,256]{1,0:T(8,128)S(1)} %get-tuple-element.113.sums.sums_0, bf16[1280,2560]{1,0:T(8,128)(2,1)S(1)} %bitcast.9), custom_call_target="tpu_custom_call" | custom-call | flops 419430400 | bytes 1000000 | tf_op jit(solution)/shard_map/out_send/pallas_call | solution.py:73
  71.4 3.0 %collective-permute-start.16 = (bf16[272,640]{1,0:T(8,128)(2,1)S(1)}, bf16[272,640]{1,0:T(8,128)(2,1)S(1)}, u32[]{:S(2)}, u32[]{:S(2)}) collective-permute-start(bf16[272,640]{1,0:T(8,128)(2,1)S(1)} %out_send.3), channel_id=1, source_target_pairs={{0,6},{2,0},{4,2},{6,4},{1,7},{3,1},{5,3},{7,5},{8,14},{10,8},{12,... | collective-permute-start | bytes 1044488 | tf_op jit(solution)/shard_map/ppermute | solution.py:58
  74.4 1.2 %out_send.2 = bf16[272,640]{1,0:T(8,128)(2,1)S(1)} custom-call(s32[3]{0:T(128)S(1)} %copy-done.1, bf16[256,1280]{1,0:T(8,128)(2,1)S(1)} %get-tuple-element.112.rows, f32[8,256]{1,0:T(8,128)S(1)} %get-tuple-element.114.sums.sums_1, bf16[1280,2560]{1,0:T(8,128)(2,1)S(1)} %bitcast.9), custom_call_target="tpu_custom_call" | custom-call | flops 419430400 | bytes 1000000 | tf_op jit(solution)/shard_map/out_send/pallas_call | solution.py:73
  75.6 0.3 collective-permute-start.15
  75.9 1.2 %out_part.7.part = f32[256,640]{1,0:T(8,128)S(1)} custom-call(s32[3]{0:T(128)S(1)} %copy-done.1, bf16[256,1280]{1,0:T(8,128)(2,1)S(1)} %get-tuple-element.112.rows, bf16[1280,2560]{1,0:T(8,128)(2,1)S(1)} %bitcast.9), custom_call_target="tpu_custom_call" | custom-call | flops 419430400 | bytes 1000000 | tf_op jit(solution)/shard_map/out_part/pallas_call | solution.py:73
  77.2 1.2 %out_part.6.part = f32[256,640]{1,0:T(8,128)S(1)} custom-call(s32[3]{0:T(128)S(1)} %copy-done.1, bf16[256,1280]{1,0:T(8,128)(2,1)S(1)} %get-tuple-element.109.rows, bf16[1280,2560]{1,0:T(8,128)(2,1)S(1)} %bitcast.9), custom_call_target="tpu_custom_call" | custom-call | flops 419430400 | bytes 1000000 | tf_op jit(solution)/shard_map/out_part/pallas_call | solution.py:73
  78.4 0.6 join.3
  79.1 3.3 %collective-permute-start.18 = (bf16[272,640]{1,0:T(8,128)(2,1)S(1)}, bf16[272,640]{1,0:T(8,128)(2,1)S(1)}, u32[]{:S(2)}, u32[]{:S(2)}) collective-permute-start(bf16[272,640]{1,0:T(8,128)(2,1)S(1)} %join.3), channel_id=1, source_target_pairs={{0,6},{2,0},{4,2},{6,4},{1,7},{3,1},{5,3},{7,5},{8,14},{10,8},{12,... | collective-permute-start | bytes 1044488 | tf_op jit(solution)/shard_map/ppermute | solution.py:58
  82.3 0.0 collective-permute-done.13.half
  82.3 0.6 join.2
  83.0 0.1 collective-permute-start.14
  83.1 1.2 %out_part.5.own_1 = f32[256,640]{1,0:T(8,128)S(1)} custom-call(s32[3]{0:T(128)S(1)} %copy-done.1, bf16[256,1280]{1,0:T(8,128)(2,1)S(1)} %get-tuple-element.112.rows, bf16[1280,2560]{1,0:T(8,128)(2,1)S(1)} %bitcast.9), custom_call_target="tpu_custom_call" | custom-call | flops 419430400 | bytes 1000000 | tf_op jit(solution)/shard_map/out_part/pallas_call | solution.py:73
  84.3 1.2 %out_part.4.own_0 = f32[256,640]{1,0:T(8,128)S(1)} custom-call(s32[3]{0:T(128)S(1)} %copy-done.1, bf16[256,1280]{1,0:T(8,128)(2,1)S(1)} %get-tuple-element.109.rows, bf16[1280,2560]{1,0:T(8,128)(2,1)S(1)} %bitcast.9), custom_call_target="tpu_custom_call" | custom-call | flops 419430400 | bytes 1000000 | tf_op jit(solution)/shard_map/out_part/pallas_call | solution.py:73
  85.5 2.6 %collective-permute-done.15.left_1 = bf16[272,640]{1,0:T(8,128)(2,1)S(1)} collective-permute-done((bf16[272,640]{1,0:T(8,128)(2,1)S(1)}, bf16[272,640]{1,0:T(8,128)(2,1)S(1)}, u32[]{:S(2)}, u32[]{:S(2)}) %collective-permute-start.15) | collective-permute-done | bytes 348192 | tf_op jit(solution)/shard_map/ppermute | solution.py:58
  88.1 3.7 %collective-permute-done.14.left_0 = bf16[272,640]{1,0:T(8,128)(2,1)S(1)} collective-permute-done((bf16[272,640]{1,0:T(8,128)(2,1)S(1)}, bf16[272,640]{1,0:T(8,128)(2,1)S(1)}, u32[]{:S(2)}, u32[]{:S(2)}) %collective-permute-start.14) | collective-permute-done | bytes 348192 | tf_op jit(solution)/shard_map/ppermute | solution.py:58
  91.8 1.8 %norm.1 = bf16[512,640]{1,0:T(8,128)(2,1)} custom-call(s32[3]{0:T(128)S(1)} %copy-done.1, f32[256,640]{1,0:T(8,128)S(1)} %out_part.4.own_0, f32[256,640]{1,0:T(8,128)S(1)} %out_part.5.own_1, f32[8,256]{1,0:T(8,128)S(1)} %get-tuple-element.113.sums.sums_0, f32[8,256]{1,0:T(8,128)S(1)} %get-tuple-element.114.sums.sums_1, ...), custom_call_target="tpu_custom_call" | custom-call | flops 100000000 | bytes 1000000 | tf_op jit(solution)/shard_map/norm/pallas_call | solution.py:73
  (20 shorter events, 0.1 us)
Async XLA Ops:
  0.0 17.8 %collective-permute-start = (bf16[512,640]{1,0:T(8,128)(2,1)}, bf16[512,640]{1,0:T(8,128)(2,1)S(1)}, u32[]{:S(2)}, u32[]{:S(2)}) collective-permute-start(bf16[512,640]{1,0:T(8,128)(2,1)} %t0.1), channel_id=1, source_target_pairs={{0,2},{2,4},{4,6},{6,0},{1,3},{3,5},{5,7},{7,1},{8,10},{10,12},{12... | collective-permute-start | bytes 1966088 | tf_op jit(solution)/shard_map/ppermute | solution.py:58
  1.6 16.4 %collective-permute-start.1 = (bf16[512,640]{1,0:T(8,128)(2,1)}, bf16[512,640]{1,0:T(8,128)(2,1)S(1)}, u32[]{:S(2)}, u32[]{:S(2)}) collective-permute-start(bf16[512,640]{1,0:T(8,128)(2,1)} %t0.1), channel_id=1, source_target_pairs={{0,6},{2,0},{4,2},{6,4},{1,7},{3,1},{5,3},{7,5},{8,14},{10,8},{12,... | collective-permute-start | bytes 1966088 | tf_op jit(solution)/shard_map/ppermute | solution.py:58
  6.3 1.1 %copy-start = (bf16[512,640]{1,0:T(8,128)(2,1)S(1)}, bf16[512,640]{1,0:T(8,128)(2,1)}, u32[]{:S(2)}) copy-start(bf16[512,640]{1,0:T(8,128)(2,1)} %t0.1) | copy-start | bytes 1966084
  7.4 6.1 %copy-start.3 = (f32[20]{0:T(128)S(1)}, f32[20]{0:T(128)}, u32[]{:S(2)}) copy-start(f32[20]{0:T(128)} %param.18) | copy-start | bytes 244
  7.4 6.1 %copy-start.4 = (f32[20]{0:T(128)S(1)}, f32[20]{0:T(128)}, u32[]{:S(2)}) copy-start(f32[20]{0:T(128)} %param.17) | copy-start | bytes 244
  7.4 14.0 %copy-start.1 = (s32[3]{0:T(128)S(1)}, s32[3]{0:T(128)}, u32[]{:S(2)}) copy-start(s32[3]{0:T(128)} %pad_add_fusion.idx) | copy-start | bytes 40
  18.0 11.7 %collective-permute-start.2 = (bf16[256,640]{1,0:T(8,128)(2,1)S(1)}, bf16[256,640]{1,0:T(8,128)(2,1)S(1)}, u32[]{:S(2)}, u32[]{:S(2)}) collective-permute-start(bf16[256,640]{1,0:T(8,128)(2,1)S(1)} %slice.6), channel_id=1, source_target_pairs={{0,2},{2,4},{4,6},{6,0},{1,3},{3,5},{5,7},{7,1},{8,10},{10,12},{12... | collective-permute-start | bytes 983048 | tf_op jit(solution)/shard_map/ppermute | solution.py:58
  19.6 10.1 %collective-permute-start.3 = (bf16[256,640]{1,0:T(8,128)(2,1)S(1)}, bf16[256,640]{1,0:T(8,128)(2,1)S(1)}, u32[]{:S(2)}, u32[]{:S(2)}) collective-permute-start(bf16[256,640]{1,0:T(8,128)(2,1)S(1)} %slice.7), channel_id=1, source_target_pairs={{0,6},{2,0},{4,2},{6,4},{1,7},{3,1},{5,3},{7,5},{8,14},{10,8},{12,... | collective-permute-start | bytes 983048 | tf_op jit(solution)/shard_map/ppermute | solution.py:58
  34.6 8.8 %collective-permute-start.4 = (bf16[48,1280]{1,0:T(8,128)(2,1)S(1)}, bf16[48,1280]{1,0:T(8,128)(2,1)S(1)}, u32[]{:S(2)}, u32[]{:S(2)}) collective-permute-start(bf16[48,1280]{1,0:T(8,128)(2,1)S(1)} %get-tuple-element.78), channel_id=1, source_target_pairs={{0,8},{8,16},{16,24},{24,0},{1,9},{9,17},{17,25},{25,1},{2,10},{10... | collective-permute-start | bytes 368648 | tf_op jit(solution)/shard_map/ppermute | solution.py:58
  36.6 7.9 %collective-permute-start.5 = (bf16[48,1280]{1,0:T(8,128)(2,1)S(1)}, bf16[48,1280]{1,0:T(8,128)(2,1)S(1)}, u32[]{:S(2)}, u32[]{:S(2)}) collective-permute-start(bf16[48,1280]{1,0:T(8,128)(2,1)S(1)} %get-tuple-element.79), channel_id=1, source_target_pairs={{0,16},{8,24},{16,0},{24,8},{1,17},{9,25},{17,1},{25,9},{2,18},{10... | collective-permute-start | bytes 368648 | tf_op jit(solution)/shard_map/ppermute | solution.py:58
  40.1 4.9 %collective-permute-start.6 = (bf16[48,1280]{1,0:T(8,128)(2,1)S(1)}, bf16[48,1280]{1,0:T(8,128)(2,1)S(1)}, u32[]{:S(2)}, u32[]{:S(2)}) collective-permute-start(bf16[48,1280]{1,0:T(8,128)(2,1)S(1)} %get-tuple-element.80), channel_id=1, source_target_pairs={{0,24},{8,0},{16,8},{24,16},{1,25},{9,1},{17,9},{25,17},{2,26},{10... | collective-permute-start | bytes 368648 | tf_op jit(solution)/shard_map/ppermute | solution.py:58
  45.7 14.8 %copy-start.2 = (f32[1280]{0:T(1024)S(1)}, f32[1280]{0:T(1024)}, u32[]{:S(2)}) copy-start(f32[1280]{0:T(1024)} %param.20) | copy-start | bytes 15364
  45.7 8.1 %collective-permute-start.7 = (bf16[48,1280]{1,0:T(8,128)(2,1)S(1)}, bf16[48,1280]{1,0:T(8,128)(2,1)S(1)}, u32[]{:S(2)}, u32[]{:S(2)}) collective-permute-start(bf16[48,1280]{1,0:T(8,128)(2,1)S(1)} %row_total.1.t0), channel_id=1, source_target_pairs={{0,32},{32,64},{64,96},{96,0},{1,33},{33,65},{65,97},{97,1},{2,34}... | collective-permute-start | bytes 368648 | tf_op jit(solution)/shard_map/ppermute | solution.py:58
  47.4 7.1 %collective-permute-start.8 = (bf16[48,1280]{1,0:T(8,128)(2,1)S(1)}, bf16[48,1280]{1,0:T(8,128)(2,1)S(1)}, u32[]{:S(2)}, u32[]{:S(2)}) collective-permute-start(bf16[48,1280]{1,0:T(8,128)(2,1)S(1)} %row_total.1.t0), channel_id=1, source_target_pairs={{0,64},{32,96},{64,0},{96,32},{1,65},{33,97},{65,1},{97,33},{2,66}... | collective-permute-start | bytes 368648 | tf_op jit(solution)/shard_map/ppermute | solution.py:58
  50.3 4.9 %collective-permute-start.9 = (bf16[48,1280]{1,0:T(8,128)(2,1)S(1)}, bf16[48,1280]{1,0:T(8,128)(2,1)S(1)}, u32[]{:S(2)}, u32[]{:S(2)}) collective-permute-start(bf16[48,1280]{1,0:T(8,128)(2,1)S(1)} %row_total.1.t0), channel_id=1, source_target_pairs={{0,96},{32,0},{64,32},{96,64},{1,97},{33,1},{65,33},{97,65},{2,98}... | collective-permute-start | bytes 368648 | tf_op jit(solution)/shard_map/ppermute | solution.py:58
  56.0 7.2 %collective-permute-start.10 = (bf16[32,1280]{1,0:T(8,128)(2,1)S(1)}, bf16[32,1280]{1,0:T(8,128)(2,1)S(1)}, u32[]{:S(2)}, u32[]{:S(2)}) collective-permute-start(bf16[32,1280]{1,0:T(8,128)(2,1)S(1)} %get-tuple-element.100), channel_id=1, source_target_pairs={{0,8},{8,16},{16,24},{24,0},{1,9},{9,17},{17,25},{25,1},{2,10},{10... | collective-permute-start | bytes 245768 | tf_op jit(solution)/shard_map/ppermute | solution.py:58
  56.9 6.3 %collective-permute-start.11 = (bf16[32,1280]{1,0:T(8,128)(2,1)S(1)}, bf16[32,1280]{1,0:T(8,128)(2,1)S(1)}, u32[]{:S(2)}, u32[]{:S(2)}) collective-permute-start(bf16[32,1280]{1,0:T(8,128)(2,1)S(1)} %get-tuple-element.101), channel_id=1, source_target_pairs={{0,16},{8,24},{16,0},{24,8},{1,17},{9,25},{17,1},{25,9},{2,18},{10... | collective-permute-start | bytes 245768 | tf_op jit(solution)/shard_map/ppermute | solution.py:58
  59.7 4.4 %collective-permute-start.12 = (bf16[32,1280]{1,0:T(8,128)(2,1)S(1)}, bf16[32,1280]{1,0:T(8,128)(2,1)S(1)}, u32[]{:S(2)}, u32[]{:S(2)}) collective-permute-start(bf16[32,1280]{1,0:T(8,128)(2,1)S(1)} %get-tuple-element.102), channel_id=1, source_target_pairs={{0,24},{8,0},{16,8},{24,16},{1,25},{9,1},{17,9},{25,17},{2,26},{10... | collective-permute-start | bytes 245768 | tf_op jit(solution)/shard_map/ppermute | solution.py:58
  60.5 3.7 %slice-start = ((s8[6553600]{0:T(1024)(128)(4,1)}), s8[4194304]{0:T(1024)(128)(4,1)S(1)}, s32[]{:S(2)}) async-start(s8[6553600]{0:T(1024)(128)(4,1)} %bitcast.8), calls=%async_computation | async-start | bytes 8388608
  60.5 3.7 %slice-start.1 = ((s8[6553600]{0:T(1024)(128)(4,1)}), s8[2359296]{0:T(1024)(128)(4,1)S(1)}, s32[]{:S(2)}) async-start(s8[6553600]{0:T(1024)(128)(4,1)} %bitcast.8), calls=%async_computation.1 | async-start | bytes 4718592
  66.1 12.3 %collective-permute-start.17 = (bf16[272,640]{1,0:T(8,128)(2,1)S(1)}, bf16[272,640]{1,0:T(8,128)(2,1)S(1)}, u32[]{:S(2)}, u32[]{:S(2)}) collective-permute-start(bf16[272,640]{1,0:T(8,128)(2,1)S(1)} %get-tuple-element.116), channel_id=1, source_target_pairs={{0,6},{2,0},{4,2},{6,4},{1,7},{3,1},{5,3},{7,5},{8,14},{10,8},{12,... | collective-permute-start | bytes 1044488 | tf_op jit(solution)/shard_map/ppermute | solution.py:58
  69.8 12.6 %collective-permute-start.13 = (bf16[272,640]{1,0:T(8,128)(2,1)S(1)}, bf16[272,640]{1,0:T(8,128)(2,1)S(1)}, u32[]{:S(2)}, u32[]{:S(2)}) collective-permute-start(bf16[272,640]{1,0:T(8,128)(2,1)S(1)} %get-tuple-element.115), channel_id=1, source_target_pairs={{0,2},{2,4},{4,6},{6,0},{1,3},{3,5},{5,7},{7,1},{8,10},{10,12},{12... | collective-permute-start | bytes 1044488 | tf_op jit(solution)/shard_map/ppermute | solution.py:58
  71.4 14.2 %collective-permute-start.16 = (bf16[272,640]{1,0:T(8,128)(2,1)S(1)}, bf16[272,640]{1,0:T(8,128)(2,1)S(1)}, u32[]{:S(2)}, u32[]{:S(2)}) collective-permute-start(bf16[272,640]{1,0:T(8,128)(2,1)S(1)} %out_send.3), channel_id=1, source_target_pairs={{0,6},{2,0},{4,2},{6,4},{1,7},{3,1},{5,3},{7,5},{8,14},{10,8},{12,... | collective-permute-start | bytes 1044488 | tf_op jit(solution)/shard_map/ppermute | solution.py:58
  75.6 12.5 %collective-permute-start.15 = (bf16[272,640]{1,0:T(8,128)(2,1)S(1)}, bf16[272,640]{1,0:T(8,128)(2,1)S(1)}, u32[]{:S(2)}, u32[]{:S(2)}) collective-permute-start(bf16[272,640]{1,0:T(8,128)(2,1)S(1)} %out_send.2), channel_id=1, source_target_pairs={{0,2},{2,4},{4,6},{6,0},{1,3},{3,5},{5,7},{7,1},{8,10},{10,12},{12... | collective-permute-start | bytes 1044488 | tf_op jit(solution)/shard_map/ppermute | solution.py:58
  79.1 9.0 %collective-permute-start.18 = (bf16[272,640]{1,0:T(8,128)(2,1)S(1)}, bf16[272,640]{1,0:T(8,128)(2,1)S(1)}, u32[]{:S(2)}, u32[]{:S(2)}) collective-permute-start(bf16[272,640]{1,0:T(8,128)(2,1)S(1)} %join.3), channel_id=1, source_target_pairs={{0,6},{2,0},{4,2},{6,4},{1,7},{3,1},{5,3},{7,5},{8,14},{10,8},{12,... | collective-permute-start | bytes 1044488 | tf_op jit(solution)/shard_map/ppermute | solution.py:58
  83.0 8.8 %collective-permute-start.14 = (bf16[272,640]{1,0:T(8,128)(2,1)S(1)}, bf16[272,640]{1,0:T(8,128)(2,1)S(1)}, u32[]{:S(2)}, u32[]{:S(2)}) collective-permute-start(bf16[272,640]{1,0:T(8,128)(2,1)S(1)} %join.2), channel_id=1, source_target_pairs={{0,2},{2,4},{4,6},{6,0},{1,3},{3,5},{5,7},{7,1},{8,10},{10,12},{12... | collective-permute-start | bytes 1044488 | tf_op jit(solution)/shard_map/ppermute | solution.py:58

commit v3 on v2

--- a/solution.py
+++ b/solution.py
@@ -21,8 +21,7 @@
 LANES = 128
 BD = 384
 QUARTER = NSTATE // 4
-MSG = QUARTER + 16
-OUTROWS = ROWS + 16
+MSG = WIDTH + LANES
 HALFROWS = GROUP + 16
 LOG2E = 1.4426950408889634
 BATCH_SEQ = ("batch", "seq_0", "seq_1")
@@ -54,8 +53,8 @@
     return hi, mid, (rest - mid.astype(F32)).astype(BF16)
 
 
-def shifted(array, axis, shift):
-    return lax.ppermute(array, axis, [(i, (i + shift) % 4) for i in range(4)])
+def swapped(array, axis, bits):
+    return lax.ppermute(array, axis, [(i, i ^ bits) for i in range(4)])
 
 
 VMEM = pl.BlockSpec(memory_space=pltpu.VMEM)
@@ -87,26 +86,23 @@
     return slice(j * size, (j + 1) * size)
 
 
-def block_of(idx, shift):
-    owner = lax.rem(idx[0] + 4 - shift, 4)
+def block_of(idx, bits):
+    owner = idx[0] ^ bits
     return pl.ds(pl.multiple_of(owner * FEAT, FEAT), FEAT)
 
 
-def add_parts(shift, idx, tokens, w_x, w_bc, w_dt, sums, outs):
-    feats = block_of(idx, shift)
-    parts = [dot(tokens, w_x[feats, span(j)]) for j in range(STEPS)]
-    for j, part in enumerate(parts):
-        outs[0][:, span(j)] = sums[0][:, span(j)] + part if sums else part
-    part = dot(tokens, w_bc[feats, :])
-    outs[1][:, : 2 * NSTATE] = sums[1][:, : 2 * NSTATE] + part if sums else part
-    part = dot_nt(tokens, w_dt[:, feats])
-    outs[1][:, 2 * NSTATE :] = sums[1][:, 2 * NSTATE :] + part if sums else part
+def own_parts(idx, tokens, w_x, w_bc, w_dt, out_x, out_bd):
+    feats = block_of(idx, 0)
+    for j in range(STEPS):
+        out_x[:, span(j)] = dot(tokens, w_x[feats, span(j)])
+    out_bd[:, : 2 * NSTATE] = dot(tokens, w_bc[feats, :])
+    out_bd[:, 2 * NSTATE :] = dot_nt(tokens, w_dt[:, feats])
 
 
 def load_body(idx, tok, w_dt, w_x, w_z, w_bc, acc_x, acc_bd, v_x, v_z, v_bc, sems):
     copies = []
-    for shift in range(4):
-        feats = block_of(idx, shift)
+    for bits in range(4):
+        feats = block_of(idx, bits)
         for source, target in ((w_x, v_x), (w_bc, v_bc)):
             sem = sems.at[len(copies)]
             copies.append(pltpu.make_async_copy(source.at[feats, :], target.at[feats, :], sem))
@@ -115,7 +111,7 @@
         copy.start()
     copies[0].wait()
     copies[1].wait()
-    add_parts(0, idx, tok[...], v_x, v_bc, w_dt, (), (acc_x, acc_bd))
+    own_parts(idx, tok[...], v_x, v_bc, w_dt, acc_x, acc_bd)
     for copy in copies[2:]:
         copy.wait()
 
@@ -140,19 +136,27 @@
     )(idx, tok, w_dt, w_x, w_z, w_bc)
 
 
-def project_body(shift, idx, tok, w_x, w_bc, w_dt, acc_x, acc_bd, out_x, out_bd):
-    add_parts(shift, idx, tok[...], w_x, w_bc, w_dt, (acc_x, acc_bd), (out_x, out_bd))
-
-
-def project(shift, idx, tok, w_x, w_bc, w_dt, sums):
-    return call(
-        functools.partial(project_body, shift),
+def project_body(idx, left, right, w_x, w_bc, w_dt, acc_x, acc_bd, out_x, out_bd):
+    tokens = jnp.concatenate([left[...], right[...]], 1)
+    one, other = block_of(idx, 1), block_of(idx, 3)
+    for j in range(STEPS):
+        weight = jnp.concatenate([w_x[one, span(j)], w_x[other, span(j)]], 0)
+        out_x[:, span(j)] = acc_x[:, span(j)] + dot(tokens, weight)
+    weight = jnp.concatenate([w_bc[one, :], w_bc[other, :]], 0)
+    out_bd[:, : 2 * NSTATE] = acc_bd[:, : 2 * NSTATE] + dot(tokens, weight)
+    weight = jnp.concatenate([w_dt[:, one], w_dt[:, other]], 1)
+    out_bd[:, 2 * NSTATE :] = acc_bd[:, 2 * NSTATE :] + dot_nt(tokens, weight)
+
+
+def project(idx, left, right, w_x, w_bc, w_dt, sums):
+    return call(
+        project_body,
         "project",
         idx,
-        [tok, w_x, w_bc, w_dt, *sums],
+        [left, right, w_x, w_bc, w_dt, *sums],
         [((ROWS, WIDTH), F32), ((ROWS, BD), F32)],
-        flops=2 * ROWS * FEAT * (WIDTH + BD),
-        aliases={5: 0, 6: 1},
+        flops=4 * ROWS * FEAT * (WIDTH + BD),
+        aliases={6: 0, 7: 1},
     )
 
 
@@ -199,6 +203,7 @@
     keep_hi = keep.astype(BF16)
     keep_lo = (keep - keep_hi.astype(F32)).astype(BF16)
     through = jnp.concatenate([terms(t, 8, LANES) for t in throughs], 0).astype(BF16)
+    tail = terms(throughs[0] * throughs[1], QUARTER, LANES).astype(BF16)
     for j in range(STEPS):
         inner = silu(acc_x[:, span(j)] + dot(tokens, w_x[feats, span(j)])).astype(BF16)
         inner_o[:, span(j)] = inner
@@ -213,12 +218,10 @@
         first_o[:, span(j)] = state0
         thr_o[:, span(j)] = jnp.broadcast_to(thr0, (8, TILE))
         state_s[:, span(j)] = thr1 * state0 + state1
-        last_rows = terms(thr0 * thr1, 16, TILE).astype(BF16)
-        for message in (m0, m1, m2, m3):
-            message[QUARTER:, span(j)] = last_rows
     for d, message in enumerate((m0, m1, m2, m3)):
-        start = pl.multiple_of(lax.rem(idx[2] + d, 4) * QUARTER, QUARTER)
-        message[:QUARTER, :] = state_s[pl.ds(start, QUARTER), :].astype(BF16)
+        start = pl.multiple_of((idx[2] ^ d) * QUARTER, QUARTER)
+        message[:, :WIDTH] = state_s[pl.ds(start, QUARTER), :].astype(BF16)
+        message[:, WIDTH:] = tail
 
 
 def device_state(idx, far, w_x, w_bc, w_dt, sums, resets, bias, rate):
@@ -230,46 +233,60 @@
         [*far, w_x, w_bc, w_dt, *sums, resets, bias, rate],
         [
             ((ROWS, WIDTH), BF16), (small, BF16), (small, BF16), (small, F32), (small, F32),
-            ((NSTATE, WIDTH), F32), ((8, WIDTH), F32), *[((MSG, WIDTH), BF16)] * 4,
+            ((NSTATE, WIDTH), F32), ((8, WIDTH), F32), *[((QUARTER, MSG), BF16)] * 4,
         ],
         [((NSTATE, WIDTH), F32)],
         flops=2 * ROWS * FEAT * (WIDTH + BD),
     )
 
 
-def decay_of(message):
-    tail = message[QUARTER : QUARTER + 3, :].astype(F32)
+def tail_of(message):
+    tail = message[:, WIDTH:].astype(F32)
     return tail[0:1] + tail[1:2] + tail[2:3]
+
+
+def decays_of(messages, j):
+    tails = jnp.concatenate([m[:16, WIDTH:] for m in messages], 0)
+    wide = dot(tails, head_rows(j))
+    rows = range(0, 16 * len(messages), 16)
+    return [wide[k : k + 1] + wide[k + 1 : k + 2] + wide[k + 2 : k + 3] for k in rows]
 
 
 def total_body(idx, m0, m1, m2, m3, out, held):
     for d, message in enumerate((m0, m1, m2, m3)):
-        held[lax.rem(idx[2] + 4 - d, 4)] = message[...]
-    state = held[0][:QUARTER].astype(F32)
-    through = decay_of(held[0])
-    for k in range(1, 4):
-        decay = decay_of(held[k])
-        state = decay * state + held[k][:QUARTER].astype(F32)
-        through = through * decay
-    out[:QUARTER, :] = state.astype(BF16)
-    out[QUARTER:, :] = terms(through, 16, WIDTH).astype(BF16)
+        held[idx[2] ^ d] = message[...]
+    messages = [held.at[k] for k in range(4)]
+    through = tail_of(messages[0])
+    for message in messages[1:]:
+        through = through * tail_of(message)
+    out[:, WIDTH:] = terms(through, QUARTER, LANES).astype(BF16)
+    for j in range(STEPS):
+        decays = decays_of(messages, j)
+        state = messages[0][:, span(j)].astype(F32)
+        for k in range(1, 4):
+            state = decays[k] * state + messages[k][:, span(j)].astype(F32)
+        out[:, span(j)] = state.astype(BF16)
 
 
 def prefix_body(idx, m0, m1, m2, m3, t0, t1, t2, t3, h0, h1, h2, h3, held, rows, found):
     for d, message in enumerate((m0, m1, m2, m3)):
-        held[lax.rem(idx[2] + 4 - d, 4)] = message[...]
+        held[idx[2] ^ d] = message[...]
     for d, message in enumerate((t0, t1, t2, t3)):
-        rows[lax.rem(idx[1] + 4 - d, 4)] = message[...]
-    state = jnp.zeros((QUARTER, WIDTH), F32)
-    for k in range(3):
-        after = decay_of(rows[k]) * state + rows[k][:QUARTER].astype(F32)
-        state = jnp.where(k < idx[1], after, state)
-    for k in range(4):
-        found[k] = state.astype(BF16)
-        if k < 3:
-            state = decay_of(held[k]) * state + held[k][:QUARTER].astype(F32)
+        rows[idx[1] ^ d] = message[...]
+    messages = [held.at[k] for k in range(4)]
+    totals = [rows.at[k] for k in range(4)]
+    for j in range(STEPS):
+        decays = decays_of([*messages, *totals], j)
+        state = jnp.zeros((QUARTER, TILE), F32)
+        for k in range(3):
+            after = decays[4 + k] * state + totals[k][:, span(j)].astype(F32)
+            state = jnp.where(k < idx[1], after, state)
+        for k in range(4):
+            found[k, :, span(j)] = state.astype(BF16)
+            if k < 3:
+                state = decays[k] * state + messages[k][:, span(j)].astype(F32)
     for d, out in enumerate((h0, h1, h2, h3)):
-        out[...] = found[lax.rem(idx[2] + d, 4)]
+        out[...] = found[idx[2] ^ d]
 
 
 def row_total(idx, messages):
@@ -278,8 +295,8 @@
         "row_total",
         idx,
         messages,
-        [((MSG, WIDTH), BF16)],
-        [((4, MSG, WIDTH), BF16)],
+        [((QUARTER, MSG), BF16)],
+        [((4, QUARTER, MSG), BF16)],
         mib=8,
     )[0]
 
@@ -291,7 +308,7 @@
         idx,
         [*messages, *totals],
         [((QUARTER, WIDTH), BF16)] * 4,
-        [((4, MSG, WIDTH), BF16), ((4, MSG, WIDTH), BF16), ((4, QUARTER, WIDTH), BF16)],
+        [((4, QUARTER, MSG), BF16), ((4, QUARTER, MSG), BF16), ((4, QUARTER, WIDTH), BF16)],
         mib=8,
     )
 
@@ -299,8 +316,8 @@
 def gate_part_body(idx, t0, t1, t3, w_z, out):
     for j in range(STEPS):
         part = dot(t0[...], w_z[block_of(idx, 0), span(j)])
-        for shift, tokens in ((1, t1), (3, t3)):
-            part = part + dot(tokens[...], w_z[block_of(idx, shift), span(j)])
+        for bits, tokens in ((1, t1), (3, t3)):
+            part = part + dot(tokens[...], w_z[block_of(idx, bits), span(j)])
         out[:, span(j)] = part
 
 
@@ -382,8 +399,8 @@
     )
 
 
-def block_cols(idx, shift):
-    target = lax.rem(idx[0] + shift, 4)
+def block_cols(idx, bits):
+    target = idx[0] ^ bits
     return pl.ds(pl.multiple_of(target * FEAT, FEAT), FEAT)
 
 
@@ -399,82 +416,87 @@
 
 
 def gated_body(
-    g, idx, h0, h1, h2, h3, first, thr, c_r, u, ent, zs_r, gain, w_out, rows_o, sums_o, out, state
+    idx, h0, h1, h2, h3, first, thr, c_r, u0, u1, e0, e1, zs_r, gain, w_out,
+    rows_o, sums_o, top, low, state,
 ):
     for d, part in enumerate((h0, h1, h2, h3)):
-        start = pl.multiple_of(lax.rem(idx[2] + 4 - d, 4) * QUARTER, QUARTER)
+        start = pl.multiple_of((idx[2] ^ d) * QUARTER, QUARTER)
         state[pl.ds(start, QUARTER), :] = part[...]
     ones = jnp.ones((8, LANES), BF16)
-    rows = span(g, GROUP)
-    squares = jnp.zeros((GROUP, LANES), F32)
-    for j in range(STEPS):
-        enter = state[:, span(j)]
-        if g:
-            enter = first[:, span(j)] + thr[0:1, span(j)] * enter.astype(F32)
-            enter = enter.astype(BF16)
-        carried = dot(c_r[rows, :], enter)
-        gated = (u[:, span(j)] + ent[:, span(j)] * carried) * zs_r[rows, span(j)]
-        rows_o[:, span(j)] = (gated * gain[:, span(j)]).astype(BF16)
-        square = gated * gated
-        squares = squares + (square[:, :LANES] + square[:, LANES:])
-    hi, mid, lo = three(squares)
-    sums = dot_nt(ones, hi) + (dot_nt(ones, mid) + dot_nt(ones, lo))
-    sums_o[...] = sums
-    out[:GROUP, :] = dot(rows_o[...], w_out[:, block_cols(idx, 2)]).astype(BF16)
-    out[GROUP:, :] = squares_rows(sums[0:1, :])
-
-
-def gated_rows(g, idx, parts, first, thr, c, u, ent, zs, gain, w_out):
-    return call(
-        functools.partial(gated_body, g),
+    for g, (u, ent) in enumerate(((u0, e0), (u1, e1))):
+        rows = span(g, GROUP)
+        squares = jnp.zeros((GROUP, LANES), F32)
+        for j in range(STEPS):
+            enter = state[:, span(j)]
+            if g:
+                enter = first[:, span(j)] + thr[0:1, span(j)] * enter.astype(F32)
+                enter = enter.astype(BF16)
+            carried = dot(c_r[rows, :], enter)
+            gated = (u[:, span(j)] + ent[:, span(j)] * carried) * zs_r[rows, span(j)]
+            rows_o[rows, span(j)] = (gated * gain[:, span(j)]).astype(BF16)
+            square = gated * gated
+            squares = squares + (square[:, :LANES] + square[:, LANES:])
+        hi, mid, lo = three(squares)
+        sums_o[:, rows] = dot_nt(ones, hi) + (dot_nt(ones, mid) + dot_nt(ones, lo))
+    part = dot(rows_o[...], w_out[:, block_cols(idx, 2)]).astype(BF16)
+    for g, out in enumerate((top, low)):
+        out[:GROUP, :] = part[span(g, GROUP)]
+        out[GROUP:, :] = squares_rows(sums_o[0:1, span(g, GROUP)])
+
+
+def gated_rows(idx, parts, first, thr, c, us, ents, zs, gain, w_out):
+    return call(
+        gated_body,
         "gated_rows",
         idx,
-        [*parts, first, thr, c, u, ent, zs, gain, w_out],
-        [((GROUP, WIDTH), BF16), ((8, GROUP), F32), ((HALFROWS, FEAT), BF16)],
+        [*parts, first, thr, c, *us, *ents, zs, gain, w_out],
+        [((ROWS, WIDTH), BF16), ((8, ROWS), F32), *[((HALFROWS, FEAT), BF16)] * 2],
         [((NSTATE, WIDTH), BF16)],
-        flops=1.3 * ROWS * WIDTH * FEAT,
-    )
-
-
-def part_body(shift, idx, rows, w_out, out):
-    out[...] = dot(rows[...], w_out[:, block_cols(idx, shift)])
-
-
-def out_part(shift, idx, rows, w_out):
-    return call(
-        functools.partial(part_body, shift),
-        "out_part",
+        flops=2.6 * ROWS * WIDTH * FEAT,
+    )
+
+
+def near_body(bits, g, idx, rows, sums, w_out, message, part):
+    value = dot(rows[...], w_out[:, block_cols(idx, bits)])
+    part[...] = value[span(g, GROUP)]
+    message[:GROUP, :] = value[span(1 - g, GROUP)].astype(BF16)
+    message[GROUP:, :] = squares_rows(sums[0:1, span(1 - g, GROUP)])
+
+
+def near_block(bits, g, idx, rows, sums, w_out):
+    return call(
+        functools.partial(near_body, bits, g),
+        "near_block",
+        idx,
+        [rows, sums, w_out],
+        [((HALFROWS, FEAT), BF16), ((GROUP, FEAT), F32)],
+        flops=2 * ROWS * WIDTH * FEAT,
+    )
+
+
+def own_body(idx, rows, w_out, out):
+    out[...] = dot(rows[...], w_out[:, block_cols(idx, 0)])
+
+
+def own_block(idx, rows, w_out):
+    return call(
+        own_body,
+        "own_block",
         idx,
         [rows, w_out],
-        [((GROUP, FEAT), F32)],
-        flops=ROWS * WIDTH * FEAT,
+        [((ROWS, FEAT), F32)],
+        flops=2 * ROWS * WIDTH * FEAT,
     )[0]
 
 
-def send_body(shift, idx, rows, sums, w_out, out):
-    out[:GROUP, :] = dot(rows[...], w_out[:, block_cols(idx, shift)]).astype(BF16)
-    out[GROUP:, :] = squares_rows(sums[0:1, :])
-
-
-def out_send(shift, idx, rows, sums, w_out):
-    return call(
-        functools.partial(send_body, shift),
-        "out_send",
-        idx,
-        [rows, sums, w_out],
-        [((HALFROWS, FEAT), BF16)],
-        flops=ROWS * WIDTH * FEAT,
-    )[0]
-
-
-def join_body(idx, part, sums, half, out):
+def join_body(g, idx, part, sums, half, out):
     out[:GROUP, :] = (part[...] + half[:GROUP, :].astype(F32)).astype(BF16)
-    out[GROUP:, :] = squares_rows(sums[0:1, :] + row_of(half, GROUP, GROUP))
-
-
-def join(idx, part, sums, half):
-    return call(
-        join_body,
+    out[GROUP:, :] = squares_rows(sums[0:1, span(g, GROUP)] + row_of(half, GROUP, GROUP))
+
+
+def join(g, idx, part, sums, half):
+    return call(
+        functools.partial(join_body, g),
         "join",
         idx,
         [part, sums, half],
@@ -483,25 +505,25 @@
     )[0]
 
 
-def norm_body(idx, own_0, own_1, sums_0, sums_1, left_0, left_1, right_0, right_1, out):
-    halves = ((own_0, sums_0, left_0, right_0), (own_1, sums_1, left_1, right_1))
-    for g, (own, sums, left, right) in enumerate(halves):
-        total = sums[0:1, :] + (row_of(left, GROUP, GROUP) + row_of(right, GROUP, GROUP))
+def norm_body(idx, own, sums, left_0, left_1, right_0, right_1, out):
+    for g, (left, right) in enumerate(((left_0, right_0), (left_1, right_1))):
+        rows = span(g, GROUP)
+        total = sums[0:1, rows] + (row_of(left, GROUP, GROUP) + row_of(right, GROUP, GROUP))
         stack = terms(total, 16, GROUP).astype(BF16)
         squares = dot_tn(stack, jnp.ones((16, LANES), BF16))
         factor = lax.rsqrt(squares / DI + 1e-05)
         for k in range(FEAT // LANES):
             lanes = span(k, LANES)
             value = left[:GROUP, lanes].astype(F32) + right[:GROUP, lanes].astype(F32)
-            out[span(g, GROUP), lanes] = ((own[:, lanes] + value) * factor).astype(BF16)
-
-
-def norm(idx, owns, sums, left, right):
+            out[rows, lanes] = ((own[rows, lanes] + value) * factor).astype(BF16)
+
+
+def norm(idx, own, sums, left, right):
     return call(
         norm_body,
         "norm",
         idx,
-        [*owns, *sums, *left, *right],
+        [own, sums, *left, *right],
         [((ROWS, FEAT), BF16)],
         kept=False,
     )[0]
@@ -511,7 +533,7 @@
     places = ("head", "seq_0", "seq_1")
     idx = jnp.stack([lax.axis_index(axis) for axis in places]).astype(jnp.int32)
     heads = w_dt.shape[1]
-    left, right = shifted(tokens, "head", 1), shifted(tokens, "head", 3)
+    left, right = swapped(tokens, "head", 1), swapped(tokens, "head", 3)
     w_dt = jnp.pad(w_dt.T, ((0, LANES - heads), (0, 0)))
     bias = jnp.pad(dt_bias, (0, LANES - heads)).reshape(1, LANES)
     rate = jnp.pad(decay_rate, (0, LANES - heads)).reshape(1, LANES)
@@ -521,35 +543,35 @@
 
     acc_x, acc_bd, w_x, w_z, w_bc = load_weights(idx, tokens, w_dt, w_x, w_z, w_bc)
     left, right, acc_x = lax.optimization_barrier((left, right, acc_x))
-    far = [shifted(left[:GROUP], "head", 1), shifted(right[GROUP:], "head", 3)]
-    sums = project(1, idx, left, w_x, w_bc, w_dt, (acc_x, acc_bd))
-    sums = project(3, idx, right, w_x, w_bc, w_dt, sums)
+    far = [swapped(left[:GROUP], "head", 3), swapped(right[GROUP:], "head", 1)]
+    sums = project(idx, left, right, w_x, w_bc, w_dt, (acc_x, acc_bd))
     acc_z = gate_part(idx, (tokens, left, right), w_z)
     far, acc_z, sums = lax.optimization_barrier((far, acc_z, sums))
     inner, b, c, cum, step, first, thr, *messages = device_state(
         idx, far, w_x, w_bc, w_dt, sums, starts, bias, rate
     )
-    quarters = [messages[0], *(shifted(messages[d], "seq_1", d) for d in (1, 2, 3))]
+    quarters = [messages[0], *(swapped(messages[d], "seq_1", d) for d in (1, 2, 3))]
     u0, e0 = mix(0, idx, inner, b, c, cum, step, skip)
     quarters, u0, e0, cum = lax.optimization_barrier((quarters, u0, e0, cum))
     total = row_total(idx, quarters)
-    totals = [total, *(shifted(total, "seq_0", d) for d in (1, 2, 3))]
+    totals = [total, *(swapped(total, "seq_0", d) for d in (1, 2, 3))]
     u1, e1 = mix(1, idx, inner, b, c, cum, step, skip)
     totals, u1, e1, w_z = lax.optimization_barrier((totals, u1, e1, w_z))
     parts = prefixes(idx, quarters, totals)
-    parts = [parts[0], *(shifted(parts[d], "seq_1", d) for d in (1, 2, 3))]
+    parts = [parts[0], *(swapped(parts[d], "seq_1", d) for d in (1, 2, 3))]
     zs = gate(idx, far, w_z, acc_z)
-    block_0, sums_0, half_0 = gated_rows(0, idx, parts, first, thr, c, u0, e0, zs, gain, w_out)
-    half_0 = shifted(half_0, "head", 1)
-    block_1, sums_1, half_1 = gated_rows(1, idx, parts, first, thr, c, u1, e1, zs, gain, w_out)
-    half_1 = shifted(half_1, "head", 3)
-    right_0 = shifted(out_send(3, idx, block_0, sums_0, w_out), "head", 3)
-    left_1 = shifted(out_send(1, idx, block_1, sums_1, w_out), "head", 1)
-    near_0, near_1 = out_part(1, idx, block_0, w_out), out_part(3, idx, block_1, w_out)
-    left_0 = shifted(join(idx, near_0, sums_0, half_0), "head", 1)
-    right_1 = shifted(join(idx, near_1, sums_1, half_1), "head", 3)
-    owns = [out_part(0, idx, block, w_out) for block in (block_0, block_1)]
-    return norm(idx, owns, (sums_0, sums_1), (left_0, left_1), (right_0, right_1))
+    rows, sums, top, low = gated_rows(
+        idx, parts, first, thr, c, (u0, u1), (e0, e1), zs, gain, w_out
+    )
+    top, low = swapped(top, "head", 1), swapped(low, "head", 3)
+    left_0, part_1 = near_block(1, 1, idx, rows, sums, w_out)
+    left_0 = swapped(left_0, "head", 1)
+    right_1, part_0 = near_block(3, 0, idx, rows, sums, w_out)
+    right_1 = swapped(right_1, "head", 3)
+    own = own_block(idx, rows, w_out)
+    right_0 = swapped(join(0, idx, part_0, sums, top), "head", 3)
+    left_1 = swapped(join(1, idx, part_1, sums, low), "head", 1)
+    return norm(idx, own, sums, (left_0, left_1), (right_0, right_1))
 
 
 def solution(mesh):

time: 93.9 us -> 92.6 us (0.986)
  waiting for transfers between devices: 14.7 us -> 22.6 us
  starting transfers between devices: 32.4 us -> 27.2 us
  Pallas kernels: 41.9 us -> 37.8 us
    ppermute x19, waiting for transfers between devices: 14.7 us -> 22.6 us  [swapped(): return lax.ppermute(array, axis, [(i, i ^ bits) for i in range(4)])]
    ppermute x19, starting transfers between devices: 32.4 us -> 27.2 us  [swapped(): return lax.ppermute(array, axis, [(i, i ^ bits) for i in range(4)])]
    pallas_call x20 -> x15, Pallas kernels: 35.8 us -> 31.7 us  [call(): pl.pallas_call(body, in_specs=[SMEM, *[VMEM] * len(args)], out_specs=[VME...]
  transfers between devices with their start and end apart: 19 -> 19, of which waited for: 9 -> 14; matrix products, arithmetic and copies ran while one was open for 3% -> 3% of each run, Pallas kernels for 34% -> 29%
where the time goes in v3:
time: 92.6 us; the launch traced here: 92.4 us
  Pallas kernels  37.8 us (41%)
  starting transfers between devices  27.2 us (29%)
  waiting for transfers between devices  22.6 us (24%)
  local copies, waits for them, and re-layouts  3.31 us (4%)
  other arithmetic  1.29 us (1%)
    pallas_call x15, Pallas kernels, call(): pl.pallas_call(body, in_specs=[SMEM, *[VMEM] * len(args)], out_specs=[VME...  31.7 us
    ppermute x19, starting transfers between devices, swapped(): return lax.ppermute(array, axis, [(i, i ^ bits) for i in range(4)])  27.2 us
    ppermute x19, waiting for transfers between devices, swapped(): return lax.ppermute(array, axis, [(i, i ^ bits) for i in range(4)])  22.6 us
    pallas_call x1, Pallas kernels, load_weights(): pl.pallas_call(load_body, in_specs=[SMEM, VMEM, VMEM, HBM, HBM, HBM], out...  6.07 us
  transfers between devices with their start and end apart: 19, of which 14 were waited for; matrix products, arithmetic and copies ran while one was open for 3% of the time, Pallas kernels for 29%

profile of v3, /device:TPU:0, one launch (start us, length us, event | category | flops | bytes accessed | tf_op | source)
XLA Modules:
  0.0 92.4 jit_solution(16716171009061880348)
XLA Ops:
  0.0 1.6 %collective-permute-start = (bf16[512,640]{1,0:T(8,128)(2,1)}, bf16[512,640]{1,0:T(8,128)(2,1)S(1)}, u32[]{:S(2)}, u32[]{:S(2)}) collective-permute-start(bf16[512,640]{1,0:T(8,128)(2,1)} %t0.1), channel_id=1, source_target_pairs={{0,2},{2,0},{4,6},{6,4},{1,3},{3,1},{5,7},{7,5},{8,10},{10,8},{12,... | collective-permute-start | bytes 1966088 | tf_op jit(solution)/shard_map/ppermute | solution.py:57
  1.6 2.1 %collective-permute-start.1 = (bf16[512,640]{1,0:T(8,128)(2,1)}, bf16[512,640]{1,0:T(8,128)(2,1)S(1)}, u32[]{:S(2)}, u32[]{:S(2)}) collective-permute-start(bf16[512,640]{1,0:T(8,128)(2,1)} %t0.1), channel_id=1, source_target_pairs={{0,6},{2,4},{4,2},{6,0},{1,7},{3,5},{5,3},{7,1},{8,14},{10,12},{12... | collective-permute-start | bytes 1966088 | tf_op jit(solution)/shard_map/ppermute | solution.py:57
  3.7 0.7 convert_element_type.8
  4.4 0.7 broadcast_in_dim.10
  5.1 0.1 reshape_reshape.3.skip
  5.2 0.9 %pad.11.w_dt = bf16[128,2560]{1,0:T(8,128)(2,1)S(1)} pad(bf16[20,2560]{1,0:T(8,128)(2,1)} %bitcast.10, bf16[]{:T(256)} %constant.16.clone.1), padding=0_108x0_0 | pad | bytes 757762 | tf_op jit(solution)/shard_map/jit(_pad)/pad | solution.py:537
  6.1 0.6 pad_add_fusion.idx
  6.7 1.1 %copy-done = bf16[512,640]{1,0:T(8,128)(2,1)S(1)} copy-done((bf16[512,640]{1,0:T(8,128)(2,1)S(1)}, bf16[512,640]{1,0:T(8,128)(2,1)}, u32[]{:S(2)}) %copy-start) | copy-done | bytes 655384
  7.8 6.1 %load_weights.1 = (f32[512,1280]{1,0:T(8,128)S(1)}, f32[512,384]{1,0:T(8,128)S(1)}, bf16[2560,1280]{1,0:T(8,128)(2,1)S(1)}, bf16[2560,1280]{1,0:T(8,128)(2,1)S(1)}, bf16[2560,256]{1,0:T(8,128)(2,1)S(1)}) custom-call(s32[3]{0:T(128)} %pad_add_fusion.idx, bf16[512,640]{1,0:T(8,128)(2,1)S(1)} %copy-done, bf16[128,2560]{1,0:T(8,128)(2,1)S(1)} %pad.11.w_dt, ...), custom_call_target="tpu_custom_call" | custom-call | flops 1090519040 | bytes 15000000 | tf_op jit(solution)/shard_map/load_weights/pallas_call | solution.py:121
  13.9 2.6 %collective-permute-done.t1.left = bf16[512,640]{1,0:T(8,128)(2,1)S(1)} collective-permute-done((bf16[512,640]{1,0:T(8,128)(2,1)}, bf16[512,640]{1,0:T(8,128)(2,1)S(1)}, u32[]{:S(2)}, u32[]{:S(2)}) %collective-permute-start) | collective-permute-done | bytes 655392 | tf_op jit(solution)/shard_map/ppermute | solution.py:57
  16.5 2.7 %collective-permute-done.1.t3.right = bf16[512,640]{1,0:T(8,128)(2,1)S(1)} collective-permute-done((bf16[512,640]{1,0:T(8,128)(2,1)}, bf16[512,640]{1,0:T(8,128)(2,1)S(1)}, u32[]{:S(2)}, u32[]{:S(2)}) %collective-permute-start.1) | collective-permute-done | bytes 655392 | tf_op jit(solution)/shard_map/ppermute | solution.py:57
  19.2 2.2 %collective-permute-start.2 = (bf16[256,640]{1,0:T(8,128)(2,1)S(1)}, bf16[256,640]{1,0:T(8,128)(2,1)S(1)}, u32[]{:S(2)}, u32[]{:S(2)}) collective-permute-start(bf16[256,640]{1,0:T(8,128)(2,1)S(1)} %slice.6), channel_id=1, source_target_pairs={{0,6},{2,4},{4,2},{6,0},{1,7},{3,5},{5,3},{7,1},{8,14},{10,12},{12... | collective-permute-start | bytes 983048 | tf_op jit(solution)/shard_map/ppermute | solution.py:57
  21.4 0.1 collective-permute-start.3
  21.5 3.3 %project.1 = (f32[512,1280]{1,0:T(8,128)S(1)}, f32[512,384]{1,0:T(8,128)S(1)}) custom-call(s32[3]{0:T(128)S(1)} %copy-done.1, bf16[512,640]{1,0:T(8,128)(2,1)S(1)} %collective-permute-done.t1.left, bf16[512,640]{1,0:T(8,128)(2,1)S(1)} %collective-permute-done.1.t3.right, ...), custom_call_target="tpu_custom_call", output_to_operand_aliasing={{0}: (6, {}), {1}: (7, {})} | custom-call | flops 2181038080 | bytes 1000000 | tf_op jit(solution)/shard_map/project/pallas_call | solution.py:72
  24.8 3.7 %gate_part.1.acc_z = f32[512,1280]{1,0:T(8,128)S(1)} custom-call(s32[3]{0:T(128)S(1)} %copy-done.1, bf16[512,640]{1,0:T(8,128)(2,1)S(1)} %copy-done, bf16[512,640]{1,0:T(8,128)(2,1)S(1)} %collective-permute-done.t1.left, bf16[512,640]{1,0:T(8,128)(2,1)S(1)} %collective-permute-done.1.t3.right, bf16[2560,1280]{1,0:T(8,128)(2,1)S(1)} %get-tuple-element.107.w_z), custom_call_target="tpu_custom_call" | custom-call | flops 2516582400 | bytes 1000000 | tf_op jit(solution)/shard_map/gate_part/pallas_call | solution.py:72
  28.5 0.2 collective-permute-done.2.tok_0.t_0
  28.8 0.7 collective-permute-done.3.tok_1.t_1
  29.5 0.1 broadcast_in_dim.4.resets
  29.6 4.7 %device_state.1 = (bf16[512,1280]{1,0:T(8,128)(2,1)S(1)}, bf16[512,128]{1,0:T(8,128)(2,1)S(1)}, bf16[512,128]{1,0:T(8,128)(2,1)S(1)}, f32[512,128]{1,0:T(8,128)S...) custom-call(s32[3]{0:T(128)S(1)} %copy-done.1, ...), custom_call_target="tpu_custom_call" | custom-call | flops 1090519040 | bytes 1000000 | tf_op jit(solution)/shard_map/device_state/pallas_call | solution.py:72
  34.4 2.0 %collective-permute-start.4 = (bf16[32,1408]{1,0:T(8,128)(2,1)S(1)}, bf16[32,1408]{1,0:T(8,128)(2,1)S(1)}, u32[]{:S(2)}, u32[]{:S(2)}) collective-permute-start(bf16[32,1408]{1,0:T(8,128)(2,1)S(1)} %get-tuple-element.76), channel_id=1, source_target_pairs={{0,8},{8,0},{16,24},{24,16},{1,9},{9,1},{17,25},{25,17},{2,10},{10... | collective-permute-start | bytes 270344 | tf_op jit(solution)/shard_map/ppermute | solution.py:57
  36.4 3.6 %collective-permute-start.5 = (bf16[32,1408]{1,0:T(8,128)(2,1)S(1)}, bf16[32,1408]{1,0:T(8,128)(2,1)S(1)}, u32[]{:S(2)}, u32[]{:S(2)}) collective-permute-start(bf16[32,1408]{1,0:T(8,128)(2,1)S(1)} %get-tuple-element.77), channel_id=1, source_target_pairs={{0,16},{8,24},{16,0},{24,8},{1,17},{9,25},{17,1},{25,9},{2,18},{10... | collective-permute-start | bytes 270344 | tf_op jit(solution)/shard_map/ppermute | solution.py:57
  40.0 0.0 collective-permute-start.6
  40.0 2.3 %mix.2 = (f32[256,1280]{1,0:T(8,128)S(1)}, f32[256,1280]{1,0:T(8,128)S(1)}) custom-call(s32[3]{0:T(128)S(1)} %copy-done.1, bf16[512,1280]{1,0:T(8,128)(2,1)S(1)} %get-tuple-element.79.inner_r, bf16[512,128]{1,0:T(8,128)(2,1)S(1)} %get-tuple-element.80.b_r, bf16[512,128]{1,0:T(8,128)(2,1)S(1)} %get-tuple-element.81.c_r, ...), custom_call_target="tpu_custom_call" | custom-call | flops 2000000000 | bytes 1000000 | tf_op jit(solution)/shard_map/mix/pallas_call | solution.py:72
  42.2 0.0 collective-permute-done.4.m1
  42.2 1.2 %collective-permute-done.5.m2 = bf16[32,1408]{1,0:T(8,128)(2,1)S(1)} collective-permute-done((bf16[32,1408]{1,0:T(8,128)(2,1)S(1)}, bf16[32,1408]{1,0:T(8,128)(2,1)S(1)}, u32[]{:S(2)}, u32[]{:S(2)}) %collective-permute-start.5) | collective-permute-done | bytes 90144 | tf_op jit(solution)/shard_map/ppermute | solution.py:57
  43.4 2.3 %collective-permute-done.6.m3 = bf16[32,1408]{1,0:T(8,128)(2,1)S(1)} collective-permute-done((bf16[32,1408]{1,0:T(8,128)(2,1)S(1)}, bf16[32,1408]{1,0:T(8,128)(2,1)S(1)}, u32[]{:S(2)}, u32[]{:S(2)}) %collective-permute-start.6) | collective-permute-done | bytes 90144 | tf_op jit(solution)/shard_map/ppermute | solution.py:57
  45.7 0.8 row_total.1.t0
  46.5 0.0 copy-start.2
  46.5 1.6 %collective-permute-start.7 = (bf16[32,1408]{1,0:T(8,128)(2,1)S(1)}, bf16[32,1408]{1,0:T(8,128)(2,1)S(1)}, u32[]{:S(2)}, u32[]{:S(2)}) collective-permute-start(bf16[32,1408]{1,0:T(8,128)(2,1)S(1)} %row_total.1.t0), channel_id=1, source_target_pairs={{0,32},{32,0},{64,96},{96,64},{1,33},{33,1},{65,97},{97,65},{2,34}... | collective-permute-start | bytes 270344 | tf_op jit(solution)/shard_map/ppermute | solution.py:57
  48.2 2.9 %collective-permute-start.8 = (bf16[32,1408]{1,0:T(8,128)(2,1)S(1)}, bf16[32,1408]{1,0:T(8,128)(2,1)S(1)}, u32[]{:S(2)}, u32[]{:S(2)}) collective-permute-start(bf16[32,1408]{1,0:T(8,128)(2,1)S(1)} %row_total.1.t0), channel_id=1, source_target_pairs={{0,64},{32,96},{64,0},{96,32},{1,65},{33,97},{65,1},{97,33},{2,66}... | collective-permute-start | bytes 270344 | tf_op jit(solution)/shard_map/ppermute | solution.py:57
  51.1 0.2 collective-permute-start.9
  51.3 2.3 %mix.3 = (f32[256,1280]{1,0:T(8,128)S(1)}, f32[256,1280]{1,0:T(8,128)S(1)}) custom-call(s32[3]{0:T(128)S(1)} %copy-done.1, bf16[512,1280]{1,0:T(8,128)(2,1)S(1)} %get-tuple-element.79.inner_r, bf16[512,128]{1,0:T(8,128)(2,1)S(1)} %get-tuple-element.80.b_r, bf16[512,128]{1,0:T(8,128)(2,1)S(1)} %get-tuple-element.81.c_r, ...), custom_call_target="tpu_custom_call" | custom-call | flops 2000000000 | bytes 1000000 | tf_op jit(solution)/shard_map/mix/pallas_call | solution.py:72
  53.5 0.0 collective-permute-done.7.t1
  53.6 1.0 %collective-permute-done.8.t2 = bf16[32,1408]{1,0:T(8,128)(2,1)S(1)} collective-permute-done((bf16[32,1408]{1,0:T(8,128)(2,1)S(1)}, bf16[32,1408]{1,0:T(8,128)(2,1)S(1)}, u32[]{:S(2)}, u32[]{:S(2)}) %collective-permute-start.8) | collective-permute-done | bytes 90144 | tf_op jit(solution)/shard_map/ppermute | solution.py:57
  54.5 2.3 %collective-permute-done.9.t3 = bf16[32,1408]{1,0:T(8,128)(2,1)S(1)} collective-permute-done((bf16[32,1408]{1,0:T(8,128)(2,1)S(1)}, bf16[32,1408]{1,0:T(8,128)(2,1)S(1)}, u32[]{:S(2)}, u32[]{:S(2)}) %collective-permute-start.9) | collective-permute-done | bytes 90144 | tf_op jit(solution)/shard_map/ppermute | solution.py:57
  56.8 0.9 prefixes.1
  57.7 0.1 collective-permute-start.10
  57.8 1.6 %collective-permute-start.11 = (bf16[32,1280]{1,0:T(8,128)(2,1)S(1)}, bf16[32,1280]{1,0:T(8,128)(2,1)S(1)}, u32[]{:S(2)}, u32[]{:S(2)}) collective-permute-start(bf16[32,1280]{1,0:T(8,128)(2,1)S(1)} %get-tuple-element.99), channel_id=1, source_target_pairs={{0,16},{8,24},{16,0},{24,8},{1,17},{9,25},{17,1},{25,9},{2,18},{10... | collective-permute-start | bytes 245768 | tf_op jit(solution)/shard_map/ppermute | solution.py:57
  59.5 3.0 %collective-permute-start.12 = (bf16[32,1280]{1,0:T(8,128)(2,1)S(1)}, bf16[32,1280]{1,0:T(8,128)(2,1)S(1)}, u32[]{:S(2)}, u32[]{:S(2)}) collective-permute-start(bf16[32,1280]{1,0:T(8,128)(2,1)S(1)} %get-tuple-element.100), channel_id=1, source_target_pairs={{0,24},{8,16},{16,8},{24,0},{1,25},{9,17},{17,9},{25,1},{2,26},{10... | collective-permute-start | bytes 245768 | tf_op jit(solution)/shard_map/ppermute | solution.py:57
  62.5 0.0 slice-start.1
  62.5 2.6 %gate.1.zs_r = f32[512,1280]{1,0:T(8,128)S(1)} custom-call(s32[3]{0:T(128)S(1)} %copy-done.1, bf16[256,640]{1,0:T(8,128)(2,1)S(1)} %collective-permute-done.2.tok_0.t_0, bf16[256,640]{1,0:T(8,128)(2,1)S(1)} %collective-permute-done.3.tok_1.t_1, bf16[2560,1280]{1,0:T(8,128)(2,1)S(1)} %get-tuple-element.107.w_z, ...), custom_call_target="tpu_custom_call", output_to_operand_aliasing={{}: (4, {})} | custom-call | flops 838860800 | bytes 1000000 | tf_op jit(solution)/shard_map/gate/pallas_call | solution.py:72
  65.1 0.0 collective-permute-done.10.h1
  65.2 0.0 collective-permute-done.11.h2
  65.2 0.0 collective-permute-done.12.h3
  65.2 0.3 slice-done.1
  65.4 2.9 %gated_rows.1 = (bf16[512,1280]{1,0:T(8,128)(2,1)S(1)}, f32[8,512]{1,0:T(8,128)S(1)}, bf16[272,640]{1,0:T(8,128)(2,1)S(1)}, bf16[272,640]{1,0:T(8,128)(2,1)S(1)}) custom-call(s32[3]{0:T(128)S(1)} %copy-done.1, bf16[32,1280]{1,0:T(8,128)(2,1)S(1)} %get-tuple-element.97.h0, bf16[32,1280]{1,0:T(8,128)(2,1)S(1)} %collective-permute-done.10.h1, ...), custom_call_target="tpu_custom_call" | custom-call | flops 1090519040 | bytes 1000000 | tf_op jit(solution)/shard_map/gated_rows/pallas_call | solution.py:72
  68.3 1.2 %collective-permute-start.16 = (bf16[272,640]{1,0:T(8,128)(2,1)S(1)}, bf16[272,640]{1,0:T(8,128)(2,1)S(1)}, u32[]{:S(2)}, u32[]{:S(2)}) collective-permute-start(bf16[272,640]{1,0:T(8,128)(2,1)S(1)} %get-tuple-element.115), channel_id=1, source_target_pairs={{0,2},{2,0},{4,6},{6,4},{1,3},{3,1},{5,7},{7,5},{8,10},{10,8},{12,... | collective-permute-start | bytes 1044488 | tf_op jit(solution)/shard_map/ppermute | solution.py:57
  69.5 1.1 %collective-permute-start.14 = (bf16[272,640]{1,0:T(8,128)(2,1)S(1)}, bf16[272,640]{1,0:T(8,128)(2,1)S(1)}, u32[]{:S(2)}, u32[]{:S(2)}) collective-permute-start(bf16[272,640]{1,0:T(8,128)(2,1)S(1)} %get-tuple-element.113), channel_id=1, source_target_pairs={{0,6},{2,4},{4,2},{6,0},{1,7},{3,5},{5,3},{7,1},{8,14},{10,12},{12... | collective-permute-start | bytes 1044488 | tf_op jit(solution)/shard_map/ppermute | solution.py:57
  70.6 1.7 %near_block.3 = (bf16[272,640]{1,0:T(8,128)(2,1)S(1)}, f32[256,640]{1,0:T(8,128)S(1)}) custom-call(s32[3]{0:T(128)S(1)} %copy-done.1, bf16[512,1280]{1,0:T(8,128)(2,1)S(1)} %get-tuple-element.109.rows, f32[8,512]{1,0:T(8,128)S(1)} %get-tuple-element.110.sums, bf16[1280,2560]{1,0:T(8,128)(2,1)S(1)} %bitcast.9), custom_call_target="tpu_custom_call" | custom-call | flops 838860800 | bytes 1000000 | tf_op jit(solution)/shard_map/near_block/pallas_call | solution.py:72
  72.4 2.2 %collective-permute-start.18 = (bf16[272,640]{1,0:T(8,128)(2,1)S(1)}, bf16[272,640]{1,0:T(8,128)(2,1)S(1)}, u32[]{:S(2)}, u32[]{:S(2)}) collective-permute-start(bf16[272,640]{1,0:T(8,128)(2,1)S(1)} %get-tuple-element.116), channel_id=1, source_target_pairs={{0,6},{2,4},{4,2},{6,0},{1,7},{3,5},{5,3},{7,1},{8,14},{10,12},{12... | collective-permute-start | bytes 1044488 | tf_op jit(solution)/shard_map/ppermute | solution.py:57
  74.5 1.7 %near_block.2 = (bf16[272,640]{1,0:T(8,128)(2,1)S(1)}, f32[256,640]{1,0:T(8,128)S(1)}) custom-call(s32[3]{0:T(128)S(1)} %copy-done.1, bf16[512,1280]{1,0:T(8,128)(2,1)S(1)} %get-tuple-element.109.rows, f32[8,512]{1,0:T(8,128)S(1)} %get-tuple-element.110.sums, bf16[1280,2560]{1,0:T(8,128)(2,1)S(1)} %bitcast.9), custom_call_target="tpu_custom_call" | custom-call | flops 838860800 | bytes 1000000 | tf_op jit(solution)/shard_map/near_block/pallas_call | solution.py:72
  76.3 0.1 collective-permute-start.13
  76.4 3.1 %collective-permute-done.16.half = bf16[272,640]{1,0:T(8,128)(2,1)S(1)} collective-permute-done((bf16[272,640]{1,0:T(8,128)(2,1)S(1)}, bf16[272,640]{1,0:T(8,128)(2,1)S(1)}, u32[]{:S(2)}, u32[]{:S(2)}) %collective-permute-start.16) | collective-permute-done | bytes 348192 | tf_op jit(solution)/shard_map/ppermute | solution.py:57
  79.4 0.6 join.3
  80.1 1.5 %collective-permute-start.17 = (bf16[272,640]{1,0:T(8,128)(2,1)S(1)}, bf16[272,640]{1,0:T(8,128)(2,1)S(1)}, u32[]{:S(2)}, u32[]{:S(2)}) collective-permute-start(bf16[272,640]{1,0:T(8,128)(2,1)S(1)} %join.3), channel_id=1, source_target_pairs={{0,6},{2,4},{4,2},{6,0},{1,7},{3,5},{5,3},{7,1},{8,14},{10,12},{12... | collective-permute-start | bytes 1044488 | tf_op jit(solution)/shard_map/ppermute | solution.py:57
  81.5 0.2 collective-permute-done.14.half
  81.8 0.6 join.2
  82.4 0.1 collective-permute-start.15
  82.5 1.7 %own_block.1.own = f32[512,640]{1,0:T(8,128)S(1)} custom-call(s32[3]{0:T(128)S(1)} %copy-done.1, bf16[512,1280]{1,0:T(8,128)(2,1)S(1)} %get-tuple-element.109.rows, bf16[1280,2560]{1,0:T(8,128)(2,1)S(1)} %bitcast.9), custom_call_target="tpu_custom_call" | custom-call | flops 838860800 | bytes 1000000 | tf_op jit(solution)/shard_map/own_block/pallas_call | solution.py:72
  84.2 1.3 %collective-permute-done.18.right_1 = bf16[272,640]{1,0:T(8,128)(2,1)S(1)} collective-permute-done((bf16[272,640]{1,0:T(8,128)(2,1)S(1)}, bf16[272,640]{1,0:T(8,128)(2,1)S(1)}, u32[]{:S(2)}, u32[]{:S(2)}) %collective-permute-start.18) | collective-permute-done | bytes 348192 | tf_op jit(solution)/shard_map/ppermute | solution.py:57
  85.5 1.4 %collective-permute-done.13.left_0 = bf16[272,640]{1,0:T(8,128)(2,1)S(1)} collective-permute-done((bf16[272,640]{1,0:T(8,128)(2,1)S(1)}, bf16[272,640]{1,0:T(8,128)(2,1)S(1)}, u32[]{:S(2)}, u32[]{:S(2)}) %collective-permute-start.13) | collective-permute-done | bytes 348192 | tf_op jit(solution)/shard_map/ppermute | solution.py:57
  86.9 2.4 %collective-permute-done.17.right_0 = bf16[272,640]{1,0:T(8,128)(2,1)S(1)} collective-permute-done((bf16[272,640]{1,0:T(8,128)(2,1)S(1)}, bf16[272,640]{1,0:T(8,128)(2,1)S(1)}, u32[]{:S(2)}, u32[]{:S(2)}) %collective-permute-start.17) | collective-permute-done | bytes 348192 | tf_op jit(solution)/shard_map/ppermute | solution.py:57
  89.2 1.4 %collective-permute-done.15.left_1 = bf16[272,640]{1,0:T(8,128)(2,1)S(1)} collective-permute-done((bf16[272,640]{1,0:T(8,128)(2,1)S(1)}, bf16[272,640]{1,0:T(8,128)(2,1)S(1)}, u32[]{:S(2)}, u32[]{:S(2)}) %collective-permute-start.15) | collective-permute-done | bytes 348192 | tf_op jit(solution)/shard_map/ppermute | solution.py:57
  90.6 1.8 %norm.1 = bf16[512,640]{1,0:T(8,128)(2,1)} custom-call(s32[3]{0:T(128)S(1)} %copy-done.1, f32[512,640]{1,0:T(8,128)S(1)} %own_block.1.own, f32[8,512]{1,0:T(8,128)S(1)} %get-tuple-element.110.sums, bf16[272,640]{1,0:T(8,128)(2,1)S(1)} %collective-permute-done.13.left_0, bf16[272,640]{1,0:T(8,128)(2,1)S(1)} %collective-permute-done.15.left_1, ...), custom_call_target="tpu_custom_call" | custom-call | flops 100000000 | bytes 1000000 | tf_op jit(solution)/shard_map/norm/pallas_call | solution.py:72
  (15 shorter events, 0.1 us)
Async XLA Ops:
  0.0 16.5 %collective-permute-start = (bf16[512,640]{1,0:T(8,128)(2,1)}, bf16[512,640]{1,0:T(8,128)(2,1)S(1)}, u32[]{:S(2)}, u32[]{:S(2)}) collective-permute-start(bf16[512,640]{1,0:T(8,128)(2,1)} %t0.1), channel_id=1, source_target_pairs={{0,2},{2,0},{4,6},{6,4},{1,3},{3,1},{5,7},{7,5},{8,10},{10,8},{12,... | collective-permute-start | bytes 1966088 | tf_op jit(solution)/shard_map/ppermute | solution.py:57
  1.6 17.6 %collective-permute-start.1 = (bf16[512,640]{1,0:T(8,128)(2,1)}, bf16[512,640]{1,0:T(8,128)(2,1)S(1)}, u32[]{:S(2)}, u32[]{:S(2)}) collective-permute-start(bf16[512,640]{1,0:T(8,128)(2,1)} %t0.1), channel_id=1, source_target_pairs={{0,6},{2,4},{4,2},{6,0},{1,7},{3,5},{5,3},{7,1},{8,14},{10,12},{12... | collective-permute-start | bytes 1966088 | tf_op jit(solution)/shard_map/ppermute | solution.py:57
  6.7 1.1 %copy-start = (bf16[512,640]{1,0:T(8,128)(2,1)S(1)}, bf16[512,640]{1,0:T(8,128)(2,1)}, u32[]{:S(2)}) copy-start(bf16[512,640]{1,0:T(8,128)(2,1)} %t0.1) | copy-start | bytes 1966084
  7.8 6.1 %copy-start.3 = (f32[20]{0:T(128)S(1)}, f32[20]{0:T(128)}, u32[]{:S(2)}) copy-start(f32[20]{0:T(128)} %param.18) | copy-start | bytes 244
  7.8 6.1 %copy-start.4 = (f32[20]{0:T(128)S(1)}, f32[20]{0:T(128)}, u32[]{:S(2)}) copy-start(f32[20]{0:T(128)} %param.17) | copy-start | bytes 244
  7.8 13.7 %copy-start.1 = (s32[3]{0:T(128)S(1)}, s32[3]{0:T(128)}, u32[]{:S(2)}) copy-start(s32[3]{0:T(128)} %pad_add_fusion.idx) | copy-start | bytes 40
  19.2 9.6 %collective-permute-start.2 = (bf16[256,640]{1,0:T(8,128)(2,1)S(1)}, bf16[256,640]{1,0:T(8,128)(2,1)S(1)}, u32[]{:S(2)}, u32[]{:S(2)}) collective-permute-start(bf16[256,640]{1,0:T(8,128)(2,1)S(1)} %slice.6), channel_id=1, source_target_pairs={{0,6},{2,4},{4,2},{6,0},{1,7},{3,5},{5,3},{7,1},{8,14},{10,12},{12... | collective-permute-start | bytes 983048 | tf_op jit(solution)/shard_map/ppermute | solution.py:57
  21.4 8.1 %collective-permute-start.3 = (bf16[256,640]{1,0:T(8,128)(2,1)S(1)}, bf16[256,640]{1,0:T(8,128)(2,1)S(1)}, u32[]{:S(2)}, u32[]{:S(2)}) collective-permute-start(bf16[256,640]{1,0:T(8,128)(2,1)S(1)} %slice.7), channel_id=1, source_target_pairs={{0,2},{2,0},{4,6},{6,4},{1,3},{3,1},{5,7},{7,5},{8,10},{10,8},{12,... | collective-permute-start | bytes 983048 | tf_op jit(solution)/shard_map/ppermute | solution.py:57
  34.4 7.9 %collective-permute-start.4 = (bf16[32,1408]{1,0:T(8,128)(2,1)S(1)}, bf16[32,1408]{1,0:T(8,128)(2,1)S(1)}, u32[]{:S(2)}, u32[]{:S(2)}) collective-permute-start(bf16[32,1408]{1,0:T(8,128)(2,1)S(1)} %get-tuple-element.76), channel_id=1, source_target_pairs={{0,8},{8,0},{16,24},{24,16},{1,9},{9,1},{17,25},{25,17},{2,10},{10... | collective-permute-start | bytes 270344 | tf_op jit(solution)/shard_map/ppermute | solution.py:57
  36.4 7.1 %collective-permute-start.5 = (bf16[32,1408]{1,0:T(8,128)(2,1)S(1)}, bf16[32,1408]{1,0:T(8,128)(2,1)S(1)}, u32[]{:S(2)}, u32[]{:S(2)}) collective-permute-start(bf16[32,1408]{1,0:T(8,128)(2,1)S(1)} %get-tuple-element.77), channel_id=1, source_target_pairs={{0,16},{8,24},{16,0},{24,8},{1,17},{9,25},{17,1},{25,9},{2,18},{10... | collective-permute-start | bytes 270344 | tf_op jit(solution)/shard_map/ppermute | solution.py:57
  40.0 5.7 %collective-permute-start.6 = (bf16[32,1408]{1,0:T(8,128)(2,1)S(1)}, bf16[32,1408]{1,0:T(8,128)(2,1)S(1)}, u32[]{:S(2)}, u32[]{:S(2)}) collective-permute-start(bf16[32,1408]{1,0:T(8,128)(2,1)S(1)} %get-tuple-element.78), channel_id=1, source_target_pairs={{0,24},{8,16},{16,8},{24,0},{1,25},{9,17},{17,9},{25,1},{2,26},{10... | collective-permute-start | bytes 270344 | tf_op jit(solution)/shard_map/ppermute | solution.py:57
  46.5 16.0 %copy-start.2 = (f32[1280]{0:T(1024)S(1)}, f32[1280]{0:T(1024)}, u32[]{:S(2)}) copy-start(f32[1280]{0:T(1024)} %param.20) | copy-start | bytes 15364
  46.5 7.0 %collective-permute-start.7 = (bf16[32,1408]{1,0:T(8,128)(2,1)S(1)}, bf16[32,1408]{1,0:T(8,128)(2,1)S(1)}, u32[]{:S(2)}, u32[]{:S(2)}) collective-permute-start(bf16[32,1408]{1,0:T(8,128)(2,1)S(1)} %row_total.1.t0), channel_id=1, source_target_pairs={{0,32},{32,0},{64,96},{96,64},{1,33},{33,1},{65,97},{97,65},{2,34}... | collective-permute-start | bytes 270344 | tf_op jit(solution)/shard_map/ppermute | solution.py:57
  48.2 6.4 %collective-permute-start.8 = (bf16[32,1408]{1,0:T(8,128)(2,1)S(1)}, bf16[32,1408]{1,0:T(8,128)(2,1)S(1)}, u32[]{:S(2)}, u32[]{:S(2)}) collective-permute-start(bf16[32,1408]{1,0:T(8,128)(2,1)S(1)} %row_total.1.t0), channel_id=1, source_target_pairs={{0,64},{32,96},{64,0},{96,32},{1,65},{33,97},{65,1},{97,33},{2,66}... | collective-permute-start | bytes 270344 | tf_op jit(solution)/shard_map/ppermute | solution.py:57
  51.1 5.7 %collective-permute-start.9 = (bf16[32,1408]{1,0:T(8,128)(2,1)S(1)}, bf16[32,1408]{1,0:T(8,128)(2,1)S(1)}, u32[]{:S(2)}, u32[]{:S(2)}) collective-permute-start(bf16[32,1408]{1,0:T(8,128)(2,1)S(1)} %row_total.1.t0), channel_id=1, source_target_pairs={{0,96},{32,64},{64,32},{96,0},{1,97},{33,65},{65,33},{97,1},{2,98}... | collective-permute-start | bytes 270344 | tf_op jit(solution)/shard_map/ppermute | solution.py:57
  57.7 7.4 %collective-permute-start.10 = (bf16[32,1280]{1,0:T(8,128)(2,1)S(1)}, bf16[32,1280]{1,0:T(8,128)(2,1)S(1)}, u32[]{:S(2)}, u32[]{:S(2)}) collective-permute-start(bf16[32,1280]{1,0:T(8,128)(2,1)S(1)} %get-tuple-element.98), channel_id=1, source_target_pairs={{0,8},{8,0},{16,24},{24,16},{1,9},{9,1},{17,25},{25,17},{2,10},{10... | collective-permute-start | bytes 245768 | tf_op jit(solution)/shard_map/ppermute | solution.py:57
  57.8 7.3 %collective-permute-start.11 = (bf16[32,1280]{1,0:T(8,128)(2,1)S(1)}, bf16[32,1280]{1,0:T(8,128)(2,1)S(1)}, u32[]{:S(2)}, u32[]{:S(2)}) collective-permute-start(bf16[32,1280]{1,0:T(8,128)(2,1)S(1)} %get-tuple-element.99), channel_id=1, source_target_pairs={{0,16},{8,24},{16,0},{24,8},{1,17},{9,25},{17,1},{25,9},{2,18},{10... | collective-permute-start | bytes 245768 | tf_op jit(solution)/shard_map/ppermute | solution.py:57
  59.5 5.7 %collective-permute-start.12 = (bf16[32,1280]{1,0:T(8,128)(2,1)S(1)}, bf16[32,1280]{1,0:T(8,128)(2,1)S(1)}, u32[]{:S(2)}, u32[]{:S(2)}) collective-permute-start(bf16[32,1280]{1,0:T(8,128)(2,1)S(1)} %get-tuple-element.100), channel_id=1, source_target_pairs={{0,24},{8,16},{16,8},{24,0},{1,25},{9,17},{17,9},{25,1},{2,26},{10... | collective-permute-start | bytes 245768 | tf_op jit(solution)/shard_map/ppermute | solution.py:57
  62.5 2.7 %slice-start = ((s8[6553600]{0:T(1024)(128)(4,1)}), s8[4194304]{0:T(1024)(128)(4,1)S(1)}, s32[]{:S(2)}) async-start(s8[6553600]{0:T(1024)(128)(4,1)} %bitcast.8), calls=%async_computation | async-start | bytes 8388608
  62.5 2.9 %slice-start.1 = ((s8[6553600]{0:T(1024)(128)(4,1)}), s8[2359296]{0:T(1024)(128)(4,1)S(1)}, s32[]{:S(2)}) async-start(s8[6553600]{0:T(1024)(128)(4,1)} %bitcast.8), calls=%async_computation.1 | async-start | bytes 4718592
  68.3 11.1 %collective-permute-start.16 = (bf16[272,640]{1,0:T(8,128)(2,1)S(1)}, bf16[272,640]{1,0:T(8,128)(2,1)S(1)}, u32[]{:S(2)}, u32[]{:S(2)}) collective-permute-start(bf16[272,640]{1,0:T(8,128)(2,1)S(1)} %get-tuple-element.115), channel_id=1, source_target_pairs={{0,2},{2,0},{4,6},{6,4},{1,3},{3,1},{5,7},{7,5},{8,10},{10,8},{12,... | collective-permute-start | bytes 1044488 | tf_op jit(solution)/shard_map/ppermute | solution.py:57
  69.5 12.3 %collective-permute-start.14 = (bf16[272,640]{1,0:T(8,128)(2,1)S(1)}, bf16[272,640]{1,0:T(8,128)(2,1)S(1)}, u32[]{:S(2)}, u32[]{:S(2)}) collective-permute-start(bf16[272,640]{1,0:T(8,128)(2,1)S(1)} %get-tuple-element.113), channel_id=1, source_target_pairs={{0,6},{2,4},{4,2},{6,0},{1,7},{3,5},{5,3},{7,1},{8,14},{10,12},{12... | collective-permute-start | bytes 1044488 | tf_op jit(solution)/shard_map/ppermute | solution.py:57
  72.4 13.1 %collective-permute-start.18 = (bf16[272,640]{1,0:T(8,128)(2,1)S(1)}, bf16[272,640]{1,0:T(8,128)(2,1)S(1)}, u32[]{:S(2)}, u32[]{:S(2)}) collective-permute-start(bf16[272,640]{1,0:T(8,128)(2,1)S(1)} %get-tuple-element.116), channel_id=1, source_target_pairs={{0,6},{2,4},{4,2},{6,0},{1,7},{3,5},{5,3},{7,1},{8,14},{10,12},{12... | collective-permute-start | bytes 1044488 | tf_op jit(solution)/shard_map/ppermute | solution.py:57
  76.3 10.6 %collective-permute-start.13 = (bf16[272,640]{1,0:T(8,128)(2,1)S(1)}, bf16[272,640]{1,0:T(8,128)(2,1)S(1)}, u32[]{:S(2)}, u32[]{:S(2)}) collective-permute-start(bf16[272,640]{1,0:T(8,128)(2,1)S(1)} %get-tuple-element.111), channel_id=1, source_target_pairs={{0,2},{2,0},{4,6},{6,4},{1,3},{3,1},{5,7},{7,5},{8,10},{10,8},{12,... | collective-permute-start | bytes 1044488 | tf_op jit(solution)/shard_map/ppermute | solution.py:57
  80.1 9.2 %collective-permute-start.17 = (bf16[272,640]{1,0:T(8,128)(2,1)S(1)}, bf16[272,640]{1,0:T(8,128)(2,1)S(1)}, u32[]{:S(2)}, u32[]{:S(2)}) collective-permute-start(bf16[272,640]{1,0:T(8,128)(2,1)S(1)} %join.3), channel_id=1, source_target_pairs={{0,6},{2,4},{4,2},{6,0},{1,7},{3,5},{5,3},{7,1},{8,14},{10,12},{12... | collective-permute-start | bytes 1044488 | tf_op jit(solution)/shard_map/ppermute | solution.py:57
  82.4 8.2 %collective-permute-start.15 = (bf16[272,640]{1,0:T(8,128)(2,1)S(1)}, bf16[272,640]{1,0:T(8,128)(2,1)S(1)}, u32[]{:S(2)}, u32[]{:S(2)}) collective-permute-start(bf16[272,640]{1,0:T(8,128)(2,1)S(1)} %join.2), channel_id=1, source_target_pairs={{0,2},{2,0},{4,6},{6,4},{1,3},{3,1},{5,7},{7,5},{8,10},{10,8},{12,... | collective-permute-start | bytes 1044488 | tf_op jit(solution)/shard_map/ppermute | solution.py:57

commit v4 on v3

--- a/solution.py
+++ b/solution.py
@@ -20,9 +20,9 @@
 PER = TILE // HEADDIM
 LANES = 128
 BD = 384
+TAILED = GROUP + 8
 QUARTER = NSTATE // 4
 MSG = WIDTH + LANES
-HALFROWS = GROUP + 16
 LOG2E = 1.4426950408889634
 BATCH_SEQ = ("batch", "seq_0", "seq_1")
 F32 = jnp.float32
@@ -99,8 +99,8 @@
     out_bd[:, 2 * NSTATE :] = dot_nt(tokens, w_dt[:, feats])
 
 
-def load_body(idx, tok, w_dt, w_x, w_z, w_bc, acc_x, acc_bd, v_x, v_z, v_bc, sems):
-    copies = []
+def load_body(idx, w_dt, tok, w_x, w_z, w_bc, acc_x, acc_bd, v_tok, v_dt, v_x, v_z, v_bc, sems):
+    copies = [pltpu.make_async_copy(tok, v_tok, sems.at[0])]
     for bits in range(4):
         feats = block_of(idx, bits)
         for source, target in ((w_x, v_x), (w_bc, v_bc)):
@@ -109,35 +109,44 @@
     copies.append(pltpu.make_async_copy(w_z, v_z, sems.at[len(copies)]))
     for copy in copies:
         copy.start()
-    copies[0].wait()
-    copies[1].wait()
-    own_parts(idx, tok[...], v_x, v_bc, w_dt, acc_x, acc_bd)
-    for copy in copies[2:]:
+    v_dt[...] = jnp.zeros_like(v_dt)
+    v_dt[: w_dt.shape[0], :] = w_dt[...]
+    for copy in copies[:3]:
         copy.wait()
+    own_parts(idx, v_tok[...], v_x, v_bc, v_dt, acc_x, acc_bd)
+    for copy in copies[3:]:
+        copy.wait()
 
 
 def load_weights(idx, tok, w_dt, w_x, w_z, w_bc):
-    tok, w_dt = (pltpu.with_memory_space_constraint(a, pltpu.VMEM) for a in (tok, w_dt))
+    w_dt = pltpu.with_memory_space_constraint(w_dt, pltpu.VMEM)
     return pl.pallas_call(
         load_body,
-        in_specs=[SMEM, VMEM, VMEM, HBM, HBM, HBM],
-        out_specs=[VMEM] * 5,
+        in_specs=[SMEM, VMEM, HBM, HBM, HBM, HBM],
+        out_specs=[VMEM] * 7,
         out_shape=[
             pltpu.VMEM((ROWS, WIDTH), F32),
             pltpu.VMEM((ROWS, BD), F32),
+            pltpu.VMEM(tok.shape, BF16),
+            pltpu.VMEM((LANES, w_dt.shape[1]), BF16),
             pltpu.VMEM(w_x.shape, BF16),
             pltpu.VMEM(w_z.shape, BF16),
             pltpu.VMEM(w_bc.shape, BF16),
         ],
-        scratch_shapes=[pltpu.SemaphoreType.DMA((9,))],
+        scratch_shapes=[pltpu.SemaphoreType.DMA((10,))],
         compiler_params=pltpu.CompilerParams(vmem_limit_bytes=36 * MIB),
         cost_estimate=cost(2 * ROWS * FEAT * (WIDTH + BD), 15e6),
         name="load_weights",
-    )(idx, tok, w_dt, w_x, w_z, w_bc)
-
-
-def project_body(idx, left, right, w_x, w_bc, w_dt, acc_x, acc_bd, out_x, out_bd):
-    tokens = jnp.concatenate([left[...], right[...]], 1)
+    )(idx, w_dt, tok, w_x, w_z, w_bc)
+
+
+def near_tokens(l_0, l_1, r_0, r_1):
+    left = jnp.concatenate([l_0[...], l_1[...]], 0)
+    return jnp.concatenate([left, jnp.concatenate([r_0[...], r_1[...]], 0)], 1)
+
+
+def project_body(idx, l_0, l_1, r_0, r_1, w_x, w_bc, w_dt, acc_x, acc_bd, out_x, out_bd):
+    tokens = near_tokens(l_0, l_1, r_0, r_1)
     one, other = block_of(idx, 1), block_of(idx, 3)
     for j in range(STEPS):
         weight = jnp.concatenate([w_x[one, span(j)], w_x[other, span(j)]], 0)
@@ -148,15 +157,15 @@
     out_bd[:, 2 * NSTATE :] = acc_bd[:, 2 * NSTATE :] + dot_nt(tokens, weight)
 
 
-def project(idx, left, right, w_x, w_bc, w_dt, sums):
+def project(idx, near, w_x, w_bc, w_dt, sums):
     return call(
         project_body,
         "project",
         idx,
-        [left, right, w_x, w_bc, w_dt, *sums],
+        [*near, w_x, w_bc, w_dt, *sums],
         [((ROWS, WIDTH), F32), ((ROWS, BD), F32)],
         flops=4 * ROWS * FEAT * (WIDTH + BD),
-        aliases={6: 0, 7: 1},
+        aliases={8: 0, 9: 1},
     )
 
 
@@ -186,7 +195,10 @@
     step = jnp.maximum(logits, 0.0) + jnp.log1p(jnp.exp(-jnp.abs(logits)))
     step_o[...] = step
     lane = lax.broadcasted_iota(jnp.int32, (ROWS, LANES), 1)
-    decay = jnp.where(lane == LANES - 1, resets[...], -step * rate[...])
+    first_row = lax.broadcasted_iota(jnp.int32, (16, ROWS), 0) == 0
+    marks = jnp.where(first_row, resets[...].astype(F32), 0.0).astype(BF16)
+    marks = dot_tn(marks, jnp.ones((16, LANES), BF16))
+    decay = jnp.where(lane == LANES - 1, marks, -step * rate[...])
     row = lax.broadcasted_iota(jnp.int32, (GROUP, GROUP), 0)
     col = lax.broadcasted_iota(jnp.int32, (GROUP, GROUP), 1)
     lower = (row >= col).astype(BF16)
@@ -313,22 +325,41 @@
     )
 
 
-def gate_part_body(idx, t0, t1, t3, w_z, out):
-    for j in range(STEPS):
-        part = dot(t0[...], w_z[block_of(idx, 0), span(j)])
-        for bits, tokens in ((1, t1), (3, t3)):
-            part = part + dot(tokens[...], w_z[block_of(idx, bits), span(j)])
-        out[:, span(j)] = part
-
-
-def gate_part(idx, tokens, w_z):
-    return call(
-        gate_part_body,
-        "gate_part",
-        idx,
-        [*tokens, w_z],
+def gate_first_body(idx, tok, l_0, r_1, w_z, out):
+    own, one, other = (block_of(idx, bits) for bits in (0, 1, 3))
+    for j in range(STEPS):
+        part = dot(tok[...], w_z[own, span(j)])
+        out[:GROUP, span(j)] = part[:GROUP] + dot(l_0[...], w_z[one, span(j)])
+        out[GROUP:, span(j)] = part[GROUP:] + dot(r_1[...], w_z[other, span(j)])
+
+
+def gate_first(idx, tok, l_0, r_1, w_z):
+    return call(
+        gate_first_body,
+        "gate_first",
+        idx,
+        [tok, l_0, r_1, w_z],
         [((ROWS, WIDTH), F32)],
-        flops=6 * ROWS * FEAT * WIDTH,
+        flops=4 * ROWS * FEAT * WIDTH,
+    )[0]
+
+
+def gate_second_body(idx, l_1, r_0, w_z, acc_z, out):
+    one, other = block_of(idx, 1), block_of(idx, 3)
+    for j in range(STEPS):
+        out[:GROUP, span(j)] = acc_z[:GROUP, span(j)] + dot(r_0[...], w_z[other, span(j)])
+        out[GROUP:, span(j)] = acc_z[GROUP:, span(j)] + dot(l_1[...], w_z[one, span(j)])
+
+
+def gate_second(idx, l_1, r_0, w_z, acc_z):
+    return call(
+        gate_second_body,
+        "gate_second",
+        idx,
+        [l_1, r_0, w_z, acc_z],
+        [((ROWS, WIDTH), F32)],
+        flops=2 * ROWS * FEAT * WIDTH,
+        aliases={4: 0},
     )[0]
 
 
@@ -404,14 +435,13 @@
     return pl.ds(pl.multiple_of(target * FEAT, FEAT), FEAT)
 
 
-def squares_rows(total):
-    width = total.shape[1]
-    rows = terms(total, 16, width).astype(BF16)
-    return jnp.concatenate([rows, jnp.zeros((16, FEAT - width), BF16)], 1)
-
-
-def row_of(message, start, width):
-    tail = message[start : start + 3, :width].astype(F32)
+def tail_rows(squares):
+    zeros = jnp.zeros((8, FEAT - ROWS), F32)
+    return jnp.concatenate([terms(squares, 8, ROWS), zeros], 1).astype(BF16)
+
+
+def squares_of(message):
+    tail = message[GROUP:, :ROWS].astype(F32)
     return tail[0:1] + (tail[1:2] + tail[2:3])
 
 
@@ -439,9 +469,10 @@
         hi, mid, lo = three(squares)
         sums_o[:, rows] = dot_nt(ones, hi) + (dot_nt(ones, mid) + dot_nt(ones, lo))
     part = dot(rows_o[...], w_out[:, block_cols(idx, 2)]).astype(BF16)
+    tail = tail_rows(sums_o[0:1, :])
     for g, out in enumerate((top, low)):
         out[:GROUP, :] = part[span(g, GROUP)]
-        out[GROUP:, :] = squares_rows(sums_o[0:1, span(g, GROUP)])
+        out[GROUP:, :] = tail
 
 
 def gated_rows(idx, parts, first, thr, c, us, ents, zs, gain, w_out):
@@ -450,27 +481,26 @@
         "gated_rows",
         idx,
         [*parts, first, thr, c, *us, *ents, zs, gain, w_out],
-        [((ROWS, WIDTH), BF16), ((8, ROWS), F32), *[((HALFROWS, FEAT), BF16)] * 2],
+        [((ROWS, WIDTH), BF16), ((8, ROWS), F32), *[((TAILED, FEAT), BF16)] * 2],
         [((NSTATE, WIDTH), BF16)],
         flops=2.6 * ROWS * WIDTH * FEAT,
     )
 
 
-def near_body(bits, g, idx, rows, sums, w_out, message, part):
+def near_body(bits, g, idx, rows, w_out, message, part):
     value = dot(rows[...], w_out[:, block_cols(idx, bits)])
     part[...] = value[span(g, GROUP)]
-    message[:GROUP, :] = value[span(1 - g, GROUP)].astype(BF16)
-    message[GROUP:, :] = squares_rows(sums[0:1, span(1 - g, GROUP)])
-
-
-def near_block(bits, g, idx, rows, sums, w_out):
+    message[...] = value[span(1 - g, GROUP)].astype(BF16)
+
+
+def near_block(bits, g, idx, rows, w_out):
     return call(
         functools.partial(near_body, bits, g),
         "near_block",
         idx,
-        [rows, sums, w_out],
-        [((HALFROWS, FEAT), BF16), ((GROUP, FEAT), F32)],
-        flops=2 * ROWS * WIDTH * FEAT,
+        [rows, w_out],
+        [((GROUP, FEAT), BF16), ((GROUP, FEAT), F32)],
+        flops=1e6,
     )
 
 
@@ -485,67 +515,90 @@
         idx,
         [rows, w_out],
         [((ROWS, FEAT), F32)],
-        flops=2 * ROWS * WIDTH * FEAT,
+        flops=1e6,
     )[0]
 
 
-def join_body(g, idx, part, sums, half, out):
+def join_body(idx, part, half, out):
     out[:GROUP, :] = (part[...] + half[:GROUP, :].astype(F32)).astype(BF16)
-    out[GROUP:, :] = squares_rows(sums[0:1, span(g, GROUP)] + row_of(half, GROUP, GROUP))
-
-
-def join(g, idx, part, sums, half):
-    return call(
-        functools.partial(join_body, g),
-        "join",
-        idx,
-        [part, sums, half],
-        [((HALFROWS, FEAT), BF16)],
+    out[GROUP:, :] = half[GROUP:, :]
+
+
+def join(idx, part, half):
+    return call(join_body, "join", idx, [part, half], [((TAILED, FEAT), BF16)], mib=8)[0]
+
+
+def add_body(idx, own, left_0, right_1, out):
+    out[:GROUP, :] = own[:GROUP, :] + left_0[...].astype(F32)
+    out[GROUP:, :] = own[GROUP:, :] + right_1[...].astype(F32)
+
+
+def add_near(idx, own, left_0, right_1):
+    return call(
+        add_body,
+        "add_near",
+        idx,
+        [own, left_0, right_1],
+        [((ROWS, FEAT), F32)],
         mib=8,
+        flops=5e9,
+        aliases={1: 0},
     )[0]
 
 
-def norm_body(idx, own, sums, left_0, left_1, right_0, right_1, out):
-    for g, (left, right) in enumerate(((left_0, right_0), (left_1, right_1))):
+def norm_body(idx, own, sums, near, other, right_0, left_1, out, made, sems):
+    squares = sums[0:1, :] + squares_of(right_0)
+    squares = squares + (squares_of(near) + squares_of(other))
+    stack = terms(squares, 16, ROWS).astype(BF16)
+    factor = lax.rsqrt(dot_tn(stack, jnp.ones((16, LANES), BF16)) / DI + 1e-05)
+    copies = []
+    for g, last in enumerate((right_0, left_1)):
         rows = span(g, GROUP)
-        total = sums[0:1, rows] + (row_of(left, GROUP, GROUP) + row_of(right, GROUP, GROUP))
-        stack = terms(total, 16, GROUP).astype(BF16)
-        squares = dot_tn(stack, jnp.ones((16, LANES), BF16))
-        factor = lax.rsqrt(squares / DI + 1e-05)
         for k in range(FEAT // LANES):
             lanes = span(k, LANES)
-            value = left[:GROUP, lanes].astype(F32) + right[:GROUP, lanes].astype(F32)
-            out[rows, lanes] = ((own[rows, lanes] + value) * factor).astype(BF16)
-
-
-def norm(idx, own, sums, left, right):
-    return call(
+            value = own[rows, lanes] + last[:GROUP, lanes].astype(F32)
+            made[rows, lanes] = (value * factor[rows]).astype(BF16)
+        copies.append(pltpu.make_async_copy(made.at[rows, :], out.at[rows, :], sems.at[g]))
+        copies[-1].start()
+    for copy in copies:
+        copy.wait()
+
+
+def norm(idx, *args):
+    args = [pltpu.with_memory_space_constraint(a, pltpu.VMEM) for a in args]
+    return pl.pallas_call(
         norm_body,
-        "norm",
-        idx,
-        [own, sums, *left, *right],
-        [((ROWS, FEAT), BF16)],
-        kept=False,
-    )[0]
+        in_specs=[SMEM, *[VMEM] * len(args)],
+        out_specs=HBM,
+        out_shape=jax.ShapeDtypeStruct((ROWS, FEAT), BF16),
+        scratch_shapes=[pltpu.VMEM((ROWS, FEAT), BF16), pltpu.SemaphoreType.DMA((2,))],
+        compiler_params=pltpu.CompilerParams(vmem_limit_bytes=8 * MIB),
+        cost_estimate=cost(1e6, 1e6),
+        name="norm",
+    )(idx, *args)
 
 
 def on_device(tokens, resets, w_x, w_z, w_bc, w_dt, dt_bias, decay_rate, d_skip, norm_gain, w_out):
     places = ("head", "seq_0", "seq_1")
     idx = jnp.stack([lax.axis_index(axis) for axis in places]).astype(jnp.int32)
     heads = w_dt.shape[1]
-    left, right = swapped(tokens, "head", 1), swapped(tokens, "head", 3)
-    w_dt = jnp.pad(w_dt.T, ((0, LANES - heads), (0, 0)))
+    top, low = tokens[:GROUP], tokens[GROUP:]
+    l_0, r_1 = swapped(top, "head", 1), swapped(low, "head", 3)
+    l_1, r_0 = swapped(low, "head", 1), swapped(top, "head", 3)
     bias = jnp.pad(dt_bias, (0, LANES - heads)).reshape(1, LANES)
     rate = jnp.pad(decay_rate, (0, LANES - heads)).reshape(1, LANES)
-    starts = jnp.broadcast_to(resets.astype(F32)[:, None], (ROWS, LANES))
+    starts = resets.reshape(1, ROWS)
     skip = jnp.repeat(d_skip, HEADDIM).reshape(1, WIDTH)
     gain = norm_gain.reshape(1, WIDTH)
 
-    acc_x, acc_bd, w_x, w_z, w_bc = load_weights(idx, tokens, w_dt, w_x, w_z, w_bc)
-    left, right, acc_x = lax.optimization_barrier((left, right, acc_x))
-    far = [swapped(left[:GROUP], "head", 3), swapped(right[GROUP:], "head", 1)]
-    sums = project(idx, left, right, w_x, w_bc, w_dt, (acc_x, acc_bd))
-    acc_z = gate_part(idx, (tokens, left, right), w_z)
+    acc_x, acc_bd, tokens, w_dt, w_x, w_z, w_bc = load_weights(
+        idx, tokens, w_dt.T, w_x, w_z, w_bc
+    )
+    far = [swapped(l_0, "head", 3), swapped(r_1, "head", 1)]
+    acc_z = gate_first(idx, tokens, l_0, r_1, w_z)
+    near = (l_0, l_1, r_0, r_1)
+    sums = project(idx, near, w_x, w_bc, w_dt, (acc_x, acc_bd))
+    acc_z = gate_second(idx, l_1, r_0, w_z, acc_z)
     far, acc_z, sums = lax.optimization_barrier((far, acc_z, sums))
     inner, b, c, cum, step, first, thr, *messages = device_state(
         idx, far, w_x, w_bc, w_dt, sums, starts, bias, rate
@@ -564,14 +617,15 @@
         idx, parts, first, thr, c, (u0, u1), (e0, e1), zs, gain, w_out
     )
     top, low = swapped(top, "head", 1), swapped(low, "head", 3)
-    left_0, part_1 = near_block(1, 1, idx, rows, sums, w_out)
+    left_0, part_1 = near_block(1, 1, idx, rows, w_out)
     left_0 = swapped(left_0, "head", 1)
-    right_1, part_0 = near_block(3, 0, idx, rows, sums, w_out)
+    right_1, part_0 = near_block(3, 0, idx, rows, w_out)
     right_1 = swapped(right_1, "head", 3)
     own = own_block(idx, rows, w_out)
-    right_0 = swapped(join(0, idx, part_0, sums, top), "head", 3)
-    left_1 = swapped(join(1, idx, part_1, sums, low), "head", 1)
-    return norm(idx, own, sums, (left_0, left_1), (right_0, right_1))
+    right_0 = swapped(join(idx, part_0, top), "head", 3)
+    left_1 = swapped(join(idx, part_1, low), "head", 1)
+    own = add_near(idx, own, left_0, right_1)
+    return norm(idx, own, sums, top, low, right_0, left_1)
 
 
 def solution(mesh):

time: 92.6 us -> 89.7 us (0.969)
  waiting for transfers between devices: 22.6 us -> 16.3 us
  starting transfers between devices: 27.2 us -> 29.3 us
  Pallas kernels: 37.8 us -> 39.7 us
    ppermute x19 -> x21, waiting for transfers between devices: 22.6 us -> 16.3 us  [swapped(): return lax.ppermute(array, axis, [(i, i ^ bits) for i in range(4)])]
    ppermute x19 -> x21, starting transfers between devices: 27.2 us -> 29.3 us  [swapped(): return lax.ppermute(array, axis, [(i, i ^ bits) for i in range(4)])]
    pallas_call x1 -> x2, Pallas kernels: 6.07 us -> 7.99 us  [the longest x1 6.28 us: load_weights(): pl.pallas_call(load_body, in_specs=[SMEM, VMEM, HBM, HBM, HBM, HBM], out_...]
    slice x2 -> x1, local copies, waits for them, and re-layouts: 0.06 us -> 1.13 us  [on_device(): top, low = (tokens[:GROUP], tokens[GROUP:])]
    pad x1 -> x0, local copies, waits for them, and re-layouts: 0.95 us -> none  [on_device(): w_dt = jnp.pad(w_dt.T, ((0, LANES - heads), (0, 0)))]
    pallas_call x15 -> x16, Pallas kernels: 31.7 us -> 31.7 us  [call(): pl.pallas_call(body, in_specs=[SMEM, *[VMEM] * len(args)], out_specs=[VME...]
  transfers between devices with their start and end apart: 19 -> 21, of which waited for: 14 -> 10; matrix products, arithmetic and copies ran while one was open for 3% -> 2% of each run, Pallas kernels for 29% -> 32%
where the time goes in v4:
time: 89.7 us; the launch traced here: 89.5 us
  Pallas kernels  39.7 us (44%)
  starting transfers between devices  29.3 us (33%)
  waiting for transfers between devices  16.3 us (18%)
  local copies, waits for them, and re-layouts  3.13 us (3%)
    pallas_call x16, Pallas kernels, call(): pl.pallas_call(body, in_specs=[SMEM, *[VMEM] * len(args)], out_specs=[VME...  31.7 us
    ppermute x21, starting transfers between devices, swapped(): return lax.ppermute(array, axis, [(i, i ^ bits) for i in range(4)])  29.3 us
    ppermute x21, waiting for transfers between devices, swapped(): return lax.ppermute(array, axis, [(i, i ^ bits) for i in range(4)])  16.3 us
    pallas_call x1, Pallas kernels, load_weights(): pl.pallas_call(load_body, in_specs=[SMEM, VMEM, HBM, HBM, HBM, HBM], out_...  6.28 us
  transfers between devices with their start and end apart: 21, of which 10 were waited for; matrix products, arithmetic and copies ran while one was open for 2% of the time, Pallas kernels for 32%

profile of v4, /device:TPU:0, one launch (start us, length us, event | category | flops | bytes accessed | tf_op | source)
XLA Modules:
  0.0 89.5 jit_solution(7886294532648344673)
XLA Ops:
  0.0 1.1 %fusion = (bf16[256,640]{1,0:T(8,128)(2,1)S(1)}, bf16[256,640]{1,0:T(8,128)(2,1)S(1)}) fusion(bf16[512,640]{1,0:T(8,128)(2,1)} %tok.1), kind=kLoop, calls=%fused_computation.3 | loop fusion | bytes 1310720 | tf_op jit(solution)/shard_map/slice | solution.py:585
  1.1 1.7 %collective-permute-start = (bf16[256,640]{1,0:T(8,128)(2,1)S(1)}, bf16[256,640]{1,0:T(8,128)(2,1)S(1)}, u32[]{:S(2)}, u32[]{:S(2)}) collective-permute-start(bf16[256,640]{1,0:T(8,128)(2,1)S(1)} %get-tuple-element.116), channel_id=1, source_target_pairs={{0,2},{2,0},{4,6},{6,4},{1,3},{3,1},{5,7},{7,5},{8,10},{10,8},{12,... | collective-permute-start | bytes 983048 | tf_op jit(solution)/shard_map/ppermute | solution.py:57
  2.8 2.1 %collective-permute-start.2 = (bf16[256,640]{1,0:T(8,128)(2,1)S(1)}, bf16[256,640]{1,0:T(8,128)(2,1)S(1)}, u32[]{:S(2)}, u32[]{:S(2)}) collective-permute-start(bf16[256,640]{1,0:T(8,128)(2,1)S(1)} %get-tuple-element.115), channel_id=1, source_target_pairs={{0,6},{2,4},{4,2},{6,0},{1,7},{3,5},{5,3},{7,1},{8,14},{10,12},{12... | collective-permute-start | bytes 983048 | tf_op jit(solution)/shard_map/ppermute | solution.py:57
  4.9 0.6 collective-permute-start.4
  5.5 0.6 collective-permute-start.5
  6.1 0.7 broadcast_in_dim.3
  6.8 0.1 reshape_reshape.3.skip
  6.9 0.6 pad_add_fusion.idx
  7.5 0.9 %copy-done.1 = bf16[2560,20]{0,1:T(8,128)(2,1)S(1)} copy-done((bf16[2560,20]{0,1:T(8,128)(2,1)S(1)}, bf16[2560,20]{0,1:T(8,128)(2,1)}, u32[]{:S(2)}) %copy-start.1) | copy-done | bytes 102424
  8.4 6.3 %load_weights.1 = (f32[512,1280]{1,0:T(8,128)S(1)}, f32[512,384]{1,0:T(8,128)S(1)}, bf16[512,640]{1,0:T(8,128)(2,1)S(1)}, bf16[128,2560]{1,0:T(8,128)(2,1)S(1)},...) custom-call(s32[3]{0:T(128)} %pad_add_fusion.idx, ...), custom_call_target="tpu_custom_call" | custom-call | flops 1090519040 | bytes 15000000 | tf_op jit(solution)/shard_map/load_weights/pallas_call | solution.py:123
  14.7 0.0 collective-permute-done.l_0
  14.7 2.7 %collective-permute-start.1 = (bf16[256,640]{1,0:T(8,128)(2,1)S(1)}, bf16[256,640]{1,0:T(8,128)(2,1)S(1)}, u32[]{:S(2)}, u32[]{:S(2)}) collective-permute-start(bf16[256,640]{1,0:T(8,128)(2,1)S(1)} %collective-permute-done.l_0), channel_id=1, source_target_pairs={{0,6},{2,4},{4,2},{6,0},{1,7},{3,5},{5,3},{7,1},{8,14},{10,12},{12... | collective-permute-start | bytes 983048 | tf_op jit(solution)/shard_map/ppermute | solution.py:57
  17.5 0.2 collective-permute-start.3
  17.7 2.8 %gate_first.1.acc_z = f32[512,1280]{1,0:T(8,128)S(1)} custom-call(s32[3]{0:T(128)S(1)} %copy-done, bf16[512,640]{1,0:T(8,128)(2,1)S(1)} %get-tuple-element.61.tok, bf16[256,640]{1,0:T(8,128)(2,1)S(1)} %collective-permute-done.l_0, bf16[256,640]{1,0:T(8,128)(2,1)S(1)} %collective-permute-done.2.r_1, bf16[2560,1280]{1,0:T(8,128)(2,1)S(1)} %get-tuple-element.105.w_z), custom_call_target="tpu_custom_call" | custom-call | flops 1677721600 | bytes 1000000 | tf_op jit(solution)/shard_map/gate_first/pallas_call | solution.py:72
  20.5 0.0 collective-permute-done.4.l_1
  20.5 1.2 %collective-permute-done.5.r_0 = bf16[256,640]{1,0:T(8,128)(2,1)S(1)} collective-permute-done((bf16[256,640]{1,0:T(8,128)(2,1)S(1)}, bf16[256,640]{1,0:T(8,128)(2,1)S(1)}, u32[]{:S(2)}, u32[]{:S(2)}) %collective-permute-start.5) | collective-permute-done | bytes 327712 | tf_op jit(solution)/shard_map/ppermute | solution.py:57
  21.7 1.9 %gate_second.1.acc_z = f32[512,1280]{1,0:T(8,128)S(1)} custom-call(s32[3]{0:T(128)S(1)} %copy-done, bf16[256,640]{1,0:T(8,128)(2,1)S(1)} %collective-permute-done.4.l_1, bf16[256,640]{1,0:T(8,128)(2,1)S(1)} %collective-permute-done.5.r_0, bf16[2560,1280]{1,0:T(8,128)(2,1)S(1)} %get-tuple-element.105.w_z, ...), custom_call_target="tpu_custom_call", output_to_operand_aliasing={{}: (4, {})} | custom-call | flops 838860800 | bytes 1000000 | tf_op jit(solution)/shard_map/gate_second/pallas_call | solution.py:72
  23.6 0.0 copy-start.2
  23.6 3.3 %project.1 = (f32[512,1280]{1,0:T(8,128)S(1)}, f32[512,384]{1,0:T(8,128)S(1)}) custom-call(s32[3]{0:T(128)S(1)} %copy-done, bf16[256,640]{1,0:T(8,128)(2,1)S(1)} %collective-permute-done.l_0, bf16[256,640]{1,0:T(8,128)(2,1)S(1)} %collective-permute-done.4.l_1, ...), custom_call_target="tpu_custom_call", output_to_operand_aliasing={{0}: (8, {}), {1}: (9, {})} | custom-call | flops 2181038080 | bytes 1000000 | tf_op jit(solution)/shard_map/project/pallas_call | solution.py:72
  26.8 0.4 collective-permute-done.1.tok_0.t_0
  27.2 0.0 collective-permute-done.3.tok_1.t_1
  27.2 5.0 %device_state.1 = (bf16[512,1280]{1,0:T(8,128)(2,1)S(1)}, bf16[512,128]{1,0:T(8,128)(2,1)S(1)}, bf16[512,128]{1,0:T(8,128)(2,1)S(1)}, f32[512,128]{1,0:T(8,128)S...) custom-call(s32[3]{0:T(128)S(1)} %copy-done, ...), custom_call_target="tpu_custom_call" | custom-call | flops 1090519040 | bytes 1000000 | tf_op jit(solution)/shard_map/device_state/pallas_call | solution.py:72
  32.2 2.0 %collective-permute-start.6 = (bf16[32,1408]{1,0:T(8,128)(2,1)S(1)}, bf16[32,1408]{1,0:T(8,128)(2,1)S(1)}, u32[]{:S(2)}, u32[]{:S(2)}) collective-permute-start(bf16[32,1408]{1,0:T(8,128)(2,1)S(1)} %get-tuple-element.74), channel_id=1, source_target_pairs={{0,8},{8,0},{16,24},{24,16},{1,9},{9,1},{17,25},{25,17},{2,10},{10... | collective-permute-start | bytes 270344 | tf_op jit(solution)/shard_map/ppermute | solution.py:57
  34.2 3.6 %collective-permute-start.7 = (bf16[32,1408]{1,0:T(8,128)(2,1)S(1)}, bf16[32,1408]{1,0:T(8,128)(2,1)S(1)}, u32[]{:S(2)}, u32[]{:S(2)}) collective-permute-start(bf16[32,1408]{1,0:T(8,128)(2,1)S(1)} %get-tuple-element.75), channel_id=1, source_target_pairs={{0,16},{8,24},{16,0},{24,8},{1,17},{9,25},{17,1},{25,9},{2,18},{10... | collective-permute-start | bytes 270344 | tf_op jit(solution)/shard_map/ppermute | solution.py:57
  37.8 0.0 collective-permute-start.8
  37.8 2.2 %mix.2 = (f32[256,1280]{1,0:T(8,128)S(1)}, f32[256,1280]{1,0:T(8,128)S(1)}) custom-call(s32[3]{0:T(128)S(1)} %copy-done, bf16[512,1280]{1,0:T(8,128)(2,1)S(1)} %get-tuple-element.77.inner_r, bf16[512,128]{1,0:T(8,128)(2,1)S(1)} %get-tuple-element.78.b_r, bf16[512,128]{1,0:T(8,128)(2,1)S(1)} %get-tuple-element.79.c_r, ...), custom_call_target="tpu_custom_call" | custom-call | flops 2000000000 | bytes 1000000 | tf_op jit(solution)/shard_map/mix/pallas_call | solution.py:72
  40.0 0.0 collective-permute-done.6.m1
  40.0 1.4 %collective-permute-done.7.m2 = bf16[32,1408]{1,0:T(8,128)(2,1)S(1)} collective-permute-done((bf16[32,1408]{1,0:T(8,128)(2,1)S(1)}, bf16[32,1408]{1,0:T(8,128)(2,1)S(1)}, u32[]{:S(2)}, u32[]{:S(2)}) %collective-permute-start.7) | collective-permute-done | bytes 90144 | tf_op jit(solution)/shard_map/ppermute | solution.py:57
  41.4 2.2 %collective-permute-done.8.m3 = bf16[32,1408]{1,0:T(8,128)(2,1)S(1)} collective-permute-done((bf16[32,1408]{1,0:T(8,128)(2,1)S(1)}, bf16[32,1408]{1,0:T(8,128)(2,1)S(1)}, u32[]{:S(2)}, u32[]{:S(2)}) %collective-permute-start.8) | collective-permute-done | bytes 90144 | tf_op jit(solution)/shard_map/ppermute | solution.py:57
  43.6 0.8 row_total.1.t0
  44.3 0.0 copy-start.3
  44.4 3.3 %collective-permute-start.10 = (bf16[32,1408]{1,0:T(8,128)(2,1)S(1)}, bf16[32,1408]{1,0:T(8,128)(2,1)S(1)}, u32[]{:S(2)}, u32[]{:S(2)}) collective-permute-start(bf16[32,1408]{1,0:T(8,128)(2,1)S(1)} %row_total.1.t0), channel_id=1, source_target_pairs={{0,64},{32,96},{64,0},{96,32},{1,65},{33,97},{65,1},{97,33},{2,66}... | collective-permute-start | bytes 270344 | tf_op jit(solution)/shard_map/ppermute | solution.py:57
  47.6 1.1 %collective-permute-start.11 = (bf16[32,1408]{1,0:T(8,128)(2,1)S(1)}, bf16[32,1408]{1,0:T(8,128)(2,1)S(1)}, u32[]{:S(2)}, u32[]{:S(2)}) collective-permute-start(bf16[32,1408]{1,0:T(8,128)(2,1)S(1)} %row_total.1.t0), channel_id=1, source_target_pairs={{0,96},{32,64},{64,32},{96,0},{1,97},{33,65},{65,33},{97,1},{2,98}... | collective-permute-start | bytes 270344 | tf_op jit(solution)/shard_map/ppermute | solution.py:57
  48.7 0.0 collective-permute-start.9
  48.7 2.2 %mix.3 = (f32[256,1280]{1,0:T(8,128)S(1)}, f32[256,1280]{1,0:T(8,128)S(1)}) custom-call(s32[3]{0:T(128)S(1)} %copy-done, bf16[512,1280]{1,0:T(8,128)(2,1)S(1)} %get-tuple-element.77.inner_r, bf16[512,128]{1,0:T(8,128)(2,1)S(1)} %get-tuple-element.78.b_r, bf16[512,128]{1,0:T(8,128)(2,1)S(1)} %get-tuple-element.79.c_r, ...), custom_call_target="tpu_custom_call" | custom-call | flops 2000000000 | bytes 1000000 | tf_op jit(solution)/shard_map/mix/pallas_call | solution.py:72
  50.9 0.0 collective-permute-done.10.t2
  50.9 2.5 %collective-permute-done.11.t3 = bf16[32,1408]{1,0:T(8,128)(2,1)S(1)} collective-permute-done((bf16[32,1408]{1,0:T(8,128)(2,1)S(1)}, bf16[32,1408]{1,0:T(8,128)(2,1)S(1)}, u32[]{:S(2)}, u32[]{:S(2)}) %collective-permute-start.11) | collective-permute-done | bytes 90144 | tf_op jit(solution)/shard_map/ppermute | solution.py:57
  53.4 0.9 %prefixes.1 = (bf16[32,1280]{1,0:T(8,128)(2,1)S(1)}, bf16[32,1280]{1,0:T(8,128)(2,1)S(1)}, bf16[32,1280]{1,0:T(8,128)(2,1)S(1)}, bf16[32,1280]{1,0:T(8,128)(2,1)S(1)}) custom-call(s32[3]{0:T(128)S(1)} %copy-done, bf16[32,1408]{1,0:T(8,128)(2,1)S(1)} %get-tuple-element.84.m0, bf16[32,1408]{1,0:T(8,128)(2,1)S(1)} %collective-permute-done.6.m1, ...), custom_call_target="tpu_custom_call" | custom-call | flops 100000000 | bytes 1000000 | tf_op jit(solution)/shard_map/prefixes/pallas_call | solution.py:72
  54.3 0.1 collective-permute-start.12
  54.4 1.7 %collective-permute-start.13 = (bf16[32,1280]{1,0:T(8,128)(2,1)S(1)}, bf16[32,1280]{1,0:T(8,128)(2,1)S(1)}, u32[]{:S(2)}, u32[]{:S(2)}) collective-permute-start(bf16[32,1280]{1,0:T(8,128)(2,1)S(1)} %get-tuple-element.97), channel_id=1, source_target_pairs={{0,16},{8,24},{16,0},{24,8},{1,17},{9,25},{17,1},{25,9},{2,18},{10... | collective-permute-start | bytes 245768 | tf_op jit(solution)/shard_map/ppermute | solution.py:57
  56.0 3.0 %collective-permute-start.14 = (bf16[32,1280]{1,0:T(8,128)(2,1)S(1)}, bf16[32,1280]{1,0:T(8,128)(2,1)S(1)}, u32[]{:S(2)}, u32[]{:S(2)}) collective-permute-start(bf16[32,1280]{1,0:T(8,128)(2,1)S(1)} %get-tuple-element.98), channel_id=1, source_target_pairs={{0,24},{8,16},{16,8},{24,0},{1,25},{9,17},{17,9},{25,1},{2,26},{10... | collective-permute-start | bytes 245768 | tf_op jit(solution)/shard_map/ppermute | solution.py:57
  59.1 0.0 slice-start.1
  59.1 2.6 %gate.1.zs_r = f32[512,1280]{1,0:T(8,128)S(1)} custom-call(s32[3]{0:T(128)S(1)} %copy-done, bf16[256,640]{1,0:T(8,128)(2,1)S(1)} %collective-permute-done.1.tok_0.t_0, bf16[256,640]{1,0:T(8,128)(2,1)S(1)} %collective-permute-done.3.tok_1.t_1, bf16[2560,1280]{1,0:T(8,128)(2,1)S(1)} %get-tuple-element.105.w_z, ...), custom_call_target="tpu_custom_call", output_to_operand_aliasing={{}: (4, {})} | custom-call | flops 838860800 | bytes 1000000 | tf_op jit(solution)/shard_map/gate/pallas_call | solution.py:72
  61.7 0.0 collective-permute-done.12.h1
  61.7 0.0 collective-permute-done.13.h2
  61.8 0.3 slice-done.1
  62.0 2.9 %gated_rows.1 = (bf16[512,1280]{1,0:T(8,128)(2,1)S(1)}, f32[8,512]{1,0:T(8,128)S(1)}, bf16[264,640]{1,0:T(8,128)(2,1)S(1)}, bf16[264,640]{1,0:T(8,128)(2,1)S(1)}) custom-call(s32[3]{0:T(128)S(1)} %copy-done, bf16[32,1280]{1,0:T(8,128)(2,1)S(1)} %get-tuple-element.95.h0, bf16[32,1280]{1,0:T(8,128)(2,1)S(1)} %collective-permute-done.12.h1, ...), custom_call_target="tpu_custom_call" | custom-call | flops 1090519040 | bytes 1000000 | tf_op jit(solution)/shard_map/gated_rows/pallas_call | solution.py:72
  64.9 2.2 %collective-permute-start.18 = (bf16[264,640]{1,0:T(8,128)(2,1)S(1)}, bf16[264,640]{1,0:T(8,128)(2,1)S(1)}, u32[]{:S(2)}, u32[]{:S(2)}) collective-permute-start(bf16[264,640]{1,0:T(8,128)(2,1)S(1)} %get-tuple-element.112), channel_id=1, source_target_pairs={{0,6},{2,4},{4,2},{6,0},{1,7},{3,5},{5,3},{7,1},{8,14},{10,12},{12... | collective-permute-start | bytes 1013768 | tf_op jit(solution)/shard_map/ppermute | solution.py:57
  67.1 1.7 %near_block.2 = (bf16[256,640]{1,0:T(8,128)(2,1)S(1)}, f32[256,640]{1,0:T(8,128)S(1)}) custom-call(s32[3]{0:T(128)S(1)} %copy-done, bf16[512,1280]{1,0:T(8,128)(2,1)S(1)} %get-tuple-element.107.rows, bf16[1280,2560]{1,0:T(8,128)(2,1)S(1)} %bitcast.10), custom_call_target="tpu_custom_call" | custom-call | flops 1000000 | bytes 1000000 | tf_op jit(solution)/shard_map/near_block/pallas_call | solution.py:72
  68.8 2.1 %collective-permute-start.15 = (bf16[256,640]{1,0:T(8,128)(2,1)S(1)}, bf16[256,640]{1,0:T(8,128)(2,1)S(1)}, u32[]{:S(2)}, u32[]{:S(2)}) collective-permute-start(bf16[256,640]{1,0:T(8,128)(2,1)S(1)} %get-tuple-element.108), channel_id=1, source_target_pairs={{0,2},{2,0},{4,6},{6,4},{1,3},{3,1},{5,7},{7,5},{8,10},{10,8},{12,... | collective-permute-start | bytes 983048 | tf_op jit(solution)/shard_map/ppermute | solution.py:57
  70.9 1.7 %near_block.3 = (bf16[256,640]{1,0:T(8,128)(2,1)S(1)}, f32[256,640]{1,0:T(8,128)S(1)}) custom-call(s32[3]{0:T(128)S(1)} %copy-done, bf16[512,1280]{1,0:T(8,128)(2,1)S(1)} %get-tuple-element.107.rows, bf16[1280,2560]{1,0:T(8,128)(2,1)S(1)} %bitcast.10), custom_call_target="tpu_custom_call" | custom-call | flops 1000000 | bytes 1000000 | tf_op jit(solution)/shard_map/near_block/pallas_call | solution.py:72
  72.7 1.2 %collective-permute-start.16 = (bf16[256,640]{1,0:T(8,128)(2,1)S(1)}, bf16[256,640]{1,0:T(8,128)(2,1)S(1)}, u32[]{:S(2)}, u32[]{:S(2)}) collective-permute-start(bf16[256,640]{1,0:T(8,128)(2,1)S(1)} %get-tuple-element.109), channel_id=1, source_target_pairs={{0,6},{2,4},{4,2},{6,0},{1,7},{3,5},{5,3},{7,1},{8,14},{10,12},{12... | collective-permute-start | bytes 983048 | tf_op jit(solution)/shard_map/ppermute | solution.py:57
  73.9 1.7 %own_block.1.own = f32[512,640]{1,0:T(8,128)S(1)} custom-call(s32[3]{0:T(128)S(1)} %copy-done, bf16[512,1280]{1,0:T(8,128)(2,1)S(1)} %get-tuple-element.107.rows, bf16[1280,2560]{1,0:T(8,128)(2,1)S(1)} %bitcast.10), custom_call_target="tpu_custom_call" | custom-call | flops 1000000 | bytes 1000000 | tf_op jit(solution)/shard_map/own_block/pallas_call | solution.py:72
  75.6 0.6 join.3
  76.2 0.1 collective-permute-start.20
  76.3 1.6 %collective-permute-done.17.half.near = bf16[264,640]{1,0:T(8,128)(2,1)S(1)} collective-permute-done((bf16[264,640]{1,0:T(8,128)(2,1)S(1)}, bf16[264,640]{1,0:T(8,128)(2,1)S(1)}, u32[]{:S(2)}, u32[]{:S(2)}) %collective-permute-start.17) | collective-permute-done | bytes 337952 | tf_op jit(solution)/shard_map/ppermute | solution.py:57
  78.0 0.6 join.2
  78.6 1.2 %collective-permute-start.19 = (bf16[264,640]{1,0:T(8,128)(2,1)S(1)}, bf16[264,640]{1,0:T(8,128)(2,1)S(1)}, u32[]{:S(2)}, u32[]{:S(2)}) collective-permute-start(bf16[264,640]{1,0:T(8,128)(2,1)S(1)} %join.2), channel_id=1, source_target_pairs={{0,6},{2,4},{4,2},{6,0},{1,7},{3,5},{5,3},{7,1},{8,14},{10,12},{12... | collective-permute-start | bytes 1013768 | tf_op jit(solution)/shard_map/ppermute | solution.py:57
  79.8 4.1 %collective-permute-done.15.left_0 = bf16[256,640]{1,0:T(8,128)(2,1)S(1)} collective-permute-done((bf16[256,640]{1,0:T(8,128)(2,1)S(1)}, bf16[256,640]{1,0:T(8,128)(2,1)S(1)}, u32[]{:S(2)}, u32[]{:S(2)}) %collective-permute-start.15) | collective-permute-done | bytes 327712 | tf_op jit(solution)/shard_map/ppermute | solution.py:57
  83.9 0.1 collective-permute-done.16.right_1
  84.0 0.8 add_near.1.own
  84.8 2.8 %collective-permute-done.20.left_1 = bf16[264,640]{1,0:T(8,128)(2,1)S(1)} collective-permute-done((bf16[264,640]{1,0:T(8,128)(2,1)S(1)}, bf16[264,640]{1,0:T(8,128)(2,1)S(1)}, u32[]{:S(2)}, u32[]{:S(2)}) %collective-permute-start.20) | collective-permute-done | bytes 337952 | tf_op jit(solution)/shard_map/ppermute | solution.py:57
  87.6 0.1 collective-permute-done.19.right_0
  87.6 1.7 %norm.1 = bf16[512,640]{1,0:T(8,128)(2,1)} custom-call(s32[3]{0:T(128)S(1)} %copy-done, f32[512,640]{1,0:T(8,128)S(1)} %add_near.1.own, f32[8,512]{1,0:T(8,128)S(1)} %get-tuple-element.110.sums, bf16[264,640]{1,0:T(8,128)(2,1)S(1)} %collective-permute-done.17.half.near, bf16[264,640]{1,0:T(8,128)(2,1)S(1)} %collective-permute-done.18.half.other, ...), custom_call_target="tpu_custom_call" | custom-call | flops 1000000 | bytes 1000000 | tf_op jit(solution)/shard_map/norm/pallas_call | solution.py:569
  (19 shorter events, 0.0 us)
Async XLA Ops:
  1.1 13.6 %collective-permute-start = (bf16[256,640]{1,0:T(8,128)(2,1)S(1)}, bf16[256,640]{1,0:T(8,128)(2,1)S(1)}, u32[]{:S(2)}, u32[]{:S(2)}) collective-permute-start(bf16[256,640]{1,0:T(8,128)(2,1)S(1)} %get-tuple-element.116), channel_id=1, source_target_pairs={{0,2},{2,0},{4,6},{6,4},{1,3},{3,1},{5,7},{7,5},{8,10},{10,8},{12,... | collective-permute-start | bytes 983048 | tf_op jit(solution)/shard_map/ppermute | solution.py:57
  2.8 14.7 %collective-permute-start.2 = (bf16[256,640]{1,0:T(8,128)(2,1)S(1)}, bf16[256,640]{1,0:T(8,128)(2,1)S(1)}, u32[]{:S(2)}, u32[]{:S(2)}) collective-permute-start(bf16[256,640]{1,0:T(8,128)(2,1)S(1)} %get-tuple-element.115), channel_id=1, source_target_pairs={{0,6},{2,4},{4,2},{6,0},{1,7},{3,5},{5,3},{7,1},{8,14},{10,12},{12... | collective-permute-start | bytes 983048 | tf_op jit(solution)/shard_map/ppermute | solution.py:57
  4.9 15.6 %collective-permute-start.4 = (bf16[256,640]{1,0:T(8,128)(2,1)S(1)}, bf16[256,640]{1,0:T(8,128)(2,1)S(1)}, u32[]{:S(2)}, u32[]{:S(2)}) collective-permute-start(bf16[256,640]{1,0:T(8,128)(2,1)S(1)} %get-tuple-element.115), channel_id=1, source_target_pairs={{0,2},{2,0},{4,6},{6,4},{1,3},{3,1},{5,7},{7,5},{8,10},{10,8},{12,... | collective-permute-start | bytes 983048 | tf_op jit(solution)/shard_map/ppermute | solution.py:57
  5.5 16.2 %collective-permute-start.5 = (bf16[256,640]{1,0:T(8,128)(2,1)S(1)}, bf16[256,640]{1,0:T(8,128)(2,1)S(1)}, u32[]{:S(2)}, u32[]{:S(2)}) collective-permute-start(bf16[256,640]{1,0:T(8,128)(2,1)S(1)} %get-tuple-element.116), channel_id=1, source_target_pairs={{0,6},{2,4},{4,2},{6,0},{1,7},{3,5},{5,3},{7,1},{8,14},{10,12},{12... | collective-permute-start | bytes 983048 | tf_op jit(solution)/shard_map/ppermute | solution.py:57
  7.5 0.9 %copy-start.1 = (bf16[2560,20]{0,1:T(8,128)(2,1)S(1)}, bf16[2560,20]{0,1:T(8,128)(2,1)}, u32[]{:S(2)}) copy-start(bf16[2560,20]{0,1:T(8,128)(2,1)} %param.16) | copy-start | bytes 307204
  8.4 6.3 %copy-start.4 = (f32[20]{0:T(128)S(1)}, f32[20]{0:T(128)}, u32[]{:S(2)}) copy-start(f32[20]{0:T(128)} %param.18) | copy-start | bytes 244
  8.4 6.3 %copy-start.5 = (f32[20]{0:T(128)S(1)}, f32[20]{0:T(128)}, u32[]{:S(2)}) copy-start(f32[20]{0:T(128)} %param.17) | copy-start | bytes 244
  8.4 9.3 %copy-start = (s32[3]{0:T(128)S(1)}, s32[3]{0:T(128)}, u32[]{:S(2)}) copy-start(s32[3]{0:T(128)} %pad_add_fusion.idx) | copy-start | bytes 40
  14.7 12.5 %collective-permute-start.1 = (bf16[256,640]{1,0:T(8,128)(2,1)S(1)}, bf16[256,640]{1,0:T(8,128)(2,1)S(1)}, u32[]{:S(2)}, u32[]{:S(2)}) collective-permute-start(bf16[256,640]{1,0:T(8,128)(2,1)S(1)} %collective-permute-done.l_0), channel_id=1, source_target_pairs={{0,6},{2,4},{4,2},{6,0},{1,7},{3,5},{5,3},{7,1},{8,14},{10,12},{12... | collective-permute-start | bytes 983048 | tf_op jit(solution)/shard_map/ppermute | solution.py:57
  17.5 9.8 %collective-permute-start.3 = (bf16[256,640]{1,0:T(8,128)(2,1)S(1)}, bf16[256,640]{1,0:T(8,128)(2,1)S(1)}, u32[]{:S(2)}, u32[]{:S(2)}) collective-permute-start(bf16[256,640]{1,0:T(8,128)(2,1)S(1)} %collective-permute-done.2.r_1), channel_id=1, source_target_pairs={{0,2},{2,0},{4,6},{6,4},{1,3},{3,1},{5,7},{7,5},{8,10},{10,8},{12,... | collective-permute-start | bytes 983048 | tf_op jit(solution)/shard_map/ppermute | solution.py:57
  23.6 3.7 %copy-start.2 = (s32[512]{0:T(512)S(1)}, s32[512]{0:T(512)}, u32[]{:S(2)}) copy-start(s32[512]{0:T(512)} %param.12) | copy-start | bytes 6148
  32.2 7.8 %collective-permute-start.6 = (bf16[32,1408]{1,0:T(8,128)(2,1)S(1)}, bf16[32,1408]{1,0:T(8,128)(2,1)S(1)}, u32[]{:S(2)}, u32[]{:S(2)}) collective-permute-start(bf16[32,1408]{1,0:T(8,128)(2,1)S(1)} %get-tuple-element.74), channel_id=1, source_target_pairs={{0,8},{8,0},{16,24},{24,16},{1,9},{9,1},{17,25},{25,17},{2,10},{10... | collective-permute-start | bytes 270344 | tf_op jit(solution)/shard_map/ppermute | solution.py:57
  34.2 7.2 %collective-permute-start.7 = (bf16[32,1408]{1,0:T(8,128)(2,1)S(1)}, bf16[32,1408]{1,0:T(8,128)(2,1)S(1)}, u32[]{:S(2)}, u32[]{:S(2)}) collective-permute-start(bf16[32,1408]{1,0:T(8,128)(2,1)S(1)} %get-tuple-element.75), channel_id=1, source_target_pairs={{0,16},{8,24},{16,0},{24,8},{1,17},{9,25},{17,1},{25,9},{2,18},{10... | collective-permute-start | bytes 270344 | tf_op jit(solution)/shard_map/ppermute | solution.py:57
  37.8 5.7 %collective-permute-start.8 = (bf16[32,1408]{1,0:T(8,128)(2,1)S(1)}, bf16[32,1408]{1,0:T(8,128)(2,1)S(1)}, u32[]{:S(2)}, u32[]{:S(2)}) collective-permute-start(bf16[32,1408]{1,0:T(8,128)(2,1)S(1)} %get-tuple-element.76), channel_id=1, source_target_pairs={{0,24},{8,16},{16,8},{24,0},{1,25},{9,17},{17,9},{25,1},{2,26},{10... | collective-permute-start | bytes 270344 | tf_op jit(solution)/shard_map/ppermute | solution.py:57
  44.3 14.7 %copy-start.3 = (f32[1280]{0:T(1024)S(1)}, f32[1280]{0:T(1024)}, u32[]{:S(2)}) copy-start(f32[1280]{0:T(1024)} %param.20) | copy-start | bytes 15364
  44.4 6.5 %collective-permute-start.10 = (bf16[32,1408]{1,0:T(8,128)(2,1)S(1)}, bf16[32,1408]{1,0:T(8,128)(2,1)S(1)}, u32[]{:S(2)}, u32[]{:S(2)}) collective-permute-start(bf16[32,1408]{1,0:T(8,128)(2,1)S(1)} %row_total.1.t0), channel_id=1, source_target_pairs={{0,64},{32,96},{64,0},{96,32},{1,65},{33,97},{65,1},{97,33},{2,66}... | collective-permute-start | bytes 270344 | tf_op jit(solution)/shard_map/ppermute | solution.py:57
  47.6 5.7 %collective-permute-start.11 = (bf16[32,1408]{1,0:T(8,128)(2,1)S(1)}, bf16[32,1408]{1,0:T(8,128)(2,1)S(1)}, u32[]{:S(2)}, u32[]{:S(2)}) collective-permute-start(bf16[32,1408]{1,0:T(8,128)(2,1)S(1)} %row_total.1.t0), channel_id=1, source_target_pairs={{0,96},{32,64},{64,32},{96,0},{1,97},{33,65},{65,33},{97,1},{2,98}... | collective-permute-start | bytes 270344 | tf_op jit(solution)/shard_map/ppermute | solution.py:57
  48.7 4.7 %collective-permute-start.9 = (bf16[32,1408]{1,0:T(8,128)(2,1)S(1)}, bf16[32,1408]{1,0:T(8,128)(2,1)S(1)}, u32[]{:S(2)}, u32[]{:S(2)}) collective-permute-start(bf16[32,1408]{1,0:T(8,128)(2,1)S(1)} %row_total.1.t0), channel_id=1, source_target_pairs={{0,32},{32,0},{64,96},{96,64},{1,33},{33,1},{65,97},{97,65},{2,34}... | collective-permute-start | bytes 270344 | tf_op jit(solution)/shard_map/ppermute | solution.py:57
  54.3 7.4 %collective-permute-start.12 = (bf16[32,1280]{1,0:T(8,128)(2,1)S(1)}, bf16[32,1280]{1,0:T(8,128)(2,1)S(1)}, u32[]{:S(2)}, u32[]{:S(2)}) collective-permute-start(bf16[32,1280]{1,0:T(8,128)(2,1)S(1)} %get-tuple-element.96), channel_id=1, source_target_pairs={{0,8},{8,0},{16,24},{24,16},{1,9},{9,1},{17,25},{25,17},{2,10},{10... | collective-permute-start | bytes 245768 | tf_op jit(solution)/shard_map/ppermute | solution.py:57
  54.4 7.4 %collective-permute-start.13 = (bf16[32,1280]{1,0:T(8,128)(2,1)S(1)}, bf16[32,1280]{1,0:T(8,128)(2,1)S(1)}, u32[]{:S(2)}, u32[]{:S(2)}) collective-permute-start(bf16[32,1280]{1,0:T(8,128)(2,1)S(1)} %get-tuple-element.97), channel_id=1, source_target_pairs={{0,16},{8,24},{16,0},{24,8},{1,17},{9,25},{17,1},{25,9},{2,18},{10... | collective-permute-start | bytes 245768 | tf_op jit(solution)/shard_map/ppermute | solution.py:57
  56.0 5.7 %collective-permute-start.14 = (bf16[32,1280]{1,0:T(8,128)(2,1)S(1)}, bf16[32,1280]{1,0:T(8,128)(2,1)S(1)}, u32[]{:S(2)}, u32[]{:S(2)}) collective-permute-start(bf16[32,1280]{1,0:T(8,128)(2,1)S(1)} %get-tuple-element.98), channel_id=1, source_target_pairs={{0,24},{8,16},{16,8},{24,0},{1,25},{9,17},{17,9},{25,1},{2,26},{10... | collective-permute-start | bytes 245768 | tf_op jit(solution)/shard_map/ppermute | solution.py:57
  59.1 2.7 %slice-start = ((s8[6553600]{0:T(1024)(128)(4,1)}), s8[4194304]{0:T(1024)(128)(4,1)S(1)}, s32[]{:S(2)}) async-start(s8[6553600]{0:T(1024)(128)(4,1)} %bitcast.9), calls=%async_computation | async-start | bytes 8388608
  59.1 2.9 %slice-start.1 = ((s8[6553600]{0:T(1024)(128)(4,1)}), s8[2359296]{0:T(1024)(128)(4,1)S(1)}, s32[]{:S(2)}) async-start(s8[6553600]{0:T(1024)(128)(4,1)} %bitcast.9), calls=%async_computation.1 | async-start | bytes 4718592
  64.9 10.7 %collective-permute-start.18 = (bf16[264,640]{1,0:T(8,128)(2,1)S(1)}, bf16[264,640]{1,0:T(8,128)(2,1)S(1)}, u32[]{:S(2)}, u32[]{:S(2)}) collective-permute-start(bf16[264,640]{1,0:T(8,128)(2,1)S(1)} %get-tuple-element.112), channel_id=1, source_target_pairs={{0,6},{2,4},{4,2},{6,0},{1,7},{3,5},{5,3},{7,1},{8,14},{10,12},{12... | collective-permute-start | bytes 1013768 | tf_op jit(solution)/shard_map/ppermute | solution.py:57
  67.1 10.9 %collective-permute-start.17 = (bf16[264,640]{1,0:T(8,128)(2,1)S(1)}, bf16[264,640]{1,0:T(8,128)(2,1)S(1)}, u32[]{:S(2)}, u32[]{:S(2)}) collective-permute-start(bf16[264,640]{1,0:T(8,128)(2,1)S(1)} %get-tuple-element.111), channel_id=1, source_target_pairs={{0,2},{2,0},{4,6},{6,4},{1,3},{3,1},{5,7},{7,5},{8,10},{10,8},{12,... | collective-permute-start | bytes 1013768 | tf_op jit(solution)/shard_map/ppermute | solution.py:57
  68.8 15.1 %collective-permute-start.15 = (bf16[256,640]{1,0:T(8,128)(2,1)S(1)}, bf16[256,640]{1,0:T(8,128)(2,1)S(1)}, u32[]{:S(2)}, u32[]{:S(2)}) collective-permute-start(bf16[256,640]{1,0:T(8,128)(2,1)S(1)} %get-tuple-element.108), channel_id=1, source_target_pairs={{0,2},{2,0},{4,6},{6,4},{1,3},{3,1},{5,7},{7,5},{8,10},{10,8},{12,... | collective-permute-start | bytes 983048 | tf_op jit(solution)/shard_map/ppermute | solution.py:57
  72.7 11.3 %collective-permute-start.16 = (bf16[256,640]{1,0:T(8,128)(2,1)S(1)}, bf16[256,640]{1,0:T(8,128)(2,1)S(1)}, u32[]{:S(2)}, u32[]{:S(2)}) collective-permute-start(bf16[256,640]{1,0:T(8,128)(2,1)S(1)} %get-tuple-element.109), channel_id=1, source_target_pairs={{0,6},{2,4},{4,2},{6,0},{1,7},{3,5},{5,3},{7,1},{8,14},{10,12},{12... | collective-permute-start | bytes 983048 | tf_op jit(solution)/shard_map/ppermute | solution.py:57
  76.2 11.3 %collective-permute-start.20 = (bf16[264,640]{1,0:T(8,128)(2,1)S(1)}, bf16[264,640]{1,0:T(8,128)(2,1)S(1)}, u32[]{:S(2)}, u32[]{:S(2)}) collective-permute-start(bf16[264,640]{1,0:T(8,128)(2,1)S(1)} %join.3), channel_id=1, source_target_pairs={{0,2},{2,0},{4,6},{6,4},{1,3},{3,1},{5,7},{7,5},{8,10},{10,8},{12,... | collective-permute-start | bytes 1013768 | tf_op jit(solution)/shard_map/ppermute | solution.py:57
  78.6 9.1 %collective-permute-start.19 = (bf16[264,640]{1,0:T(8,128)(2,1)S(1)}, bf16[264,640]{1,0:T(8,128)(2,1)S(1)}, u32[]{:S(2)}, u32[]{:S(2)}) collective-permute-start(bf16[264,640]{1,0:T(8,128)(2,1)S(1)} %join.2), channel_id=1, source_target_pairs={{0,6},{2,4},{4,2},{6,0},{1,7},{3,5},{5,3},{7,1},{8,14},{10,12},{12... | collective-permute-start | bytes 1013768 | tf_op jit(solution)/shard_map/ppermute | solution.py:57

commit v5 on v4

--- a/solution.py
+++ b/solution.py
@@ -99,8 +99,13 @@
     out_bd[:, 2 * NSTATE :] = dot_nt(tokens, w_dt[:, feats])
 
 
-def load_body(idx, w_dt, tok, w_x, w_z, w_bc, acc_x, acc_bd, v_tok, v_dt, v_x, v_z, v_bc, sems):
-    copies = [pltpu.make_async_copy(tok, v_tok, sems.at[0])]
+def load_body(
+    idx, w_dt, tok, w_x, w_z, w_bc, acc_x, acc_bd, v_tok, v_dt, v_x, v_z, v_bc, narrow, sems
+):
+    copies = [
+        pltpu.make_async_copy(w_dt, narrow, sems.at[0]),
+        pltpu.make_async_copy(tok, v_tok, sems.at[1]),
+    ]
     for bits in range(4):
         feats = block_of(idx, bits)
         for source, target in ((w_x, v_x), (w_bc, v_bc)):
@@ -110,19 +115,19 @@
     for copy in copies:
         copy.start()
     v_dt[...] = jnp.zeros_like(v_dt)
-    v_dt[: w_dt.shape[0], :] = w_dt[...]
-    for copy in copies[:3]:
+    copies[0].wait()
+    v_dt[: w_dt.shape[0], :] = narrow[...]
+    for copy in copies[1:4]:
         copy.wait()
     own_parts(idx, v_tok[...], v_x, v_bc, v_dt, acc_x, acc_bd)
-    for copy in copies[3:]:
+    for copy in copies[4:]:
         copy.wait()
 
 
 def load_weights(idx, tok, w_dt, w_x, w_z, w_bc):
-    w_dt = pltpu.with_memory_space_constraint(w_dt, pltpu.VMEM)
     return pl.pallas_call(
         load_body,
-        in_specs=[SMEM, VMEM, HBM, HBM, HBM, HBM],
+        in_specs=[SMEM, *[HBM] * 5],
         out_specs=[VMEM] * 7,
         out_shape=[
             pltpu.VMEM((ROWS, WIDTH), F32),
@@ -133,7 +138,7 @@
             pltpu.VMEM(w_z.shape, BF16),
             pltpu.VMEM(w_bc.shape, BF16),
         ],
-        scratch_shapes=[pltpu.SemaphoreType.DMA((10,))],
+        scratch_shapes=[pltpu.VMEM(w_dt.shape, BF16), pltpu.SemaphoreType.DMA((11,))],
         compiler_params=pltpu.CompilerParams(vmem_limit_bytes=36 * MIB),
         cost_estimate=cost(2 * ROWS * FEAT * (WIDTH + BD), 15e6),
         name="load_weights",
@@ -204,8 +209,8 @@
     lower = (row >= col).astype(BF16)
     keeps, throughs = [], []
     for g in range(2):
-        hi, mid, lo = three(decay[span(g, GROUP)])
-        cum = dot(lower, hi) + (dot(lower, mid) + dot(lower, lo))
+        sums = dot(lower, jnp.concatenate(three(decay[span(g, GROUP)]), 1))
+        cum = sums[:, :LANES] + (sums[:, LANES : 2 * LANES] + sums[:, 2 * LANES :])
         cum_o[span(g, GROUP), :] = cum
         last = cum[GROUP - 1 :, :]
         seg, closing = cum[:, LANES - 1 :], last[:, LANES - 1 :]
@@ -214,13 +219,14 @@
     keep = jnp.concatenate(keeps, 0)
     keep_hi = keep.astype(BF16)
     keep_lo = (keep - keep_hi.astype(F32)).astype(BF16)
+    keep = jnp.concatenate([keep_hi, keep_lo], 1)
     through = jnp.concatenate([terms(t, 8, LANES) for t in throughs], 0).astype(BF16)
     tail = terms(throughs[0] * throughs[1], QUARTER, LANES).astype(BF16)
     for j in range(STEPS):
         inner = silu(acc_x[:, span(j)] + dot(tokens, w_x[feats, span(j)])).astype(BF16)
         inner_o[:, span(j)] = inner
         heads = head_rows(j)
-        wide = dot(keep_hi, heads) + dot(keep_lo, heads)
+        wide = dot(keep, jnp.concatenate([heads, heads], 0))
         scaled = (wide * inner.astype(F32)).astype(BF16)
         state0 = dot(b_t[:, :GROUP], scaled[:GROUP])
         state1 = dot(b_t[:, GROUP:], scaled[GROUP:])
@@ -400,9 +406,13 @@
     hi = enter.astype(BF16)
     lo = (enter - hi.astype(F32)).astype(BF16)
     lane = lax.broadcasted_iota(jnp.int32, (GROUP, LANES), 1)
+    skips = []
     for j in range(STEPS):
         heads = head_rows(j)
         ent_o[:, span(j)] = dot(hi, heads) + dot(lo, heads)
+        wide = dot(terms(skip[...], 16, LANES).astype(BF16), heads)
+        wide = wide[0:1] + wide[1:2] + wide[2:3]
+        skips += [wide[:, :LANES], wide[:, LANES:]]
     for pair in range(WIDTH // LANES):
         both = inner_r[rows, span(pair, LANES)]
         ys = []
@@ -415,7 +425,7 @@
             low = (low * scores[half:, :] * step).astype(BF16)
             ys.append(jnp.concatenate([dot(top, both[:half]), dot(low, both)], 0))
         y = jnp.where(lane < HEADDIM, ys[0], ys[1])
-        out[:, span(pair, LANES)] = y + skip[:, span(pair, LANES)] * both.astype(F32)
+        out[:, span(pair, LANES)] = y + skips[pair] * both.astype(F32)
 
 
 def mix(g, idx, inner, b, c, cum, step, skip):
@@ -546,36 +556,54 @@
     )[0]
 
 
-def norm_body(idx, own, sums, near, other, right_0, left_1, out, made, sems):
-    squares = sums[0:1, :] + squares_of(right_0)
+def settle_body(idx, own, sums, near, other, left_1, out, factor, made, sem):
+    squares = sums[0:1, :] + squares_of(left_1)
     squares = squares + (squares_of(near) + squares_of(other))
     stack = terms(squares, 16, ROWS).astype(BF16)
-    factor = lax.rsqrt(dot_tn(stack, jnp.ones((16, LANES), BF16)) / DI + 1e-05)
-    copies = []
-    for g, last in enumerate((right_0, left_1)):
-        rows = span(g, GROUP)
-        for k in range(FEAT // LANES):
-            lanes = span(k, LANES)
-            value = own[rows, lanes] + last[:GROUP, lanes].astype(F32)
-            made[rows, lanes] = (value * factor[rows]).astype(BF16)
-        copies.append(pltpu.make_async_copy(made.at[rows, :], out.at[rows, :], sems.at[g]))
-        copies[-1].start()
-    for copy in copies:
-        copy.wait()
-
-
-def norm(idx, *args):
+    scale = lax.rsqrt(dot_tn(stack, jnp.ones((16, LANES), BF16)) / DI + 1e-05)
+    factor[...] = scale[:GROUP]
+    for k in range(FEAT // LANES):
+        lanes = span(k, LANES)
+        value = own[GROUP:, lanes] + left_1[:GROUP, lanes].astype(F32)
+        made[:, lanes] = (value * scale[GROUP:]).astype(BF16)
+    copy = pltpu.make_async_copy(made, out.at[GROUP:, :], sem)
+    copy.start()
+    copy.wait()
+
+
+def end_call(body, name, idx, args, outs, specs, more=()):
     args = [pltpu.with_memory_space_constraint(a, pltpu.VMEM) for a in args]
     return pl.pallas_call(
-        norm_body,
-        in_specs=[SMEM, *[VMEM] * len(args)],
-        out_specs=HBM,
-        out_shape=jax.ShapeDtypeStruct((ROWS, FEAT), BF16),
-        scratch_shapes=[pltpu.VMEM((ROWS, FEAT), BF16), pltpu.SemaphoreType.DMA((2,))],
+        body,
+        in_specs=[SMEM, *[VMEM] * len(args), *[HBM] * len(more)],
+        out_specs=specs,
+        out_shape=outs,
+        scratch_shapes=[pltpu.VMEM((GROUP, FEAT), BF16), pltpu.SemaphoreType.DMA],
+        input_output_aliases={1 + len(args): 0} if more else {},
         compiler_params=pltpu.CompilerParams(vmem_limit_bytes=8 * MIB),
         cost_estimate=cost(1e6, 1e6),
-        name="norm",
-    )(idx, *args)
+        name=name,
+    )(idx, *args, *more)
+
+
+def settle(idx, *args):
+    outs = [jax.ShapeDtypeStruct((ROWS, FEAT), BF16), pltpu.VMEM((GROUP, LANES), F32)]
+    return end_call(settle_body, "settle", idx, args, outs, [HBM, VMEM])
+
+
+def norm_body(idx, own, factor, right_0, so_far, out, made, sem):
+    for k in range(FEAT // LANES):
+        lanes = span(k, LANES)
+        value = own[:GROUP, lanes] + right_0[:GROUP, lanes].astype(F32)
+        made[:, lanes] = (value * factor[...]).astype(BF16)
+    copy = pltpu.make_async_copy(made, out.at[:GROUP, :], sem)
+    copy.start()
+    copy.wait()
+
+
+def norm(idx, own, factor, right_0, so_far):
+    outs = jax.ShapeDtypeStruct((ROWS, FEAT), BF16)
+    return end_call(norm_body, "norm", idx, (own, factor, right_0), outs, HBM, (so_far,))
 
 
 def on_device(tokens, resets, w_x, w_z, w_bc, w_dt, dt_bias, decay_rate, d_skip, norm_gain, w_out):
@@ -584,11 +612,12 @@
     heads = w_dt.shape[1]
     top, low = tokens[:GROUP], tokens[GROUP:]
     l_0, r_1 = swapped(top, "head", 1), swapped(low, "head", 3)
+    top, low, idx = lax.optimization_barrier((top, low, idx))
     l_1, r_0 = swapped(low, "head", 1), swapped(top, "head", 3)
     bias = jnp.pad(dt_bias, (0, LANES - heads)).reshape(1, LANES)
     rate = jnp.pad(decay_rate, (0, LANES - heads)).reshape(1, LANES)
     starts = resets.reshape(1, ROWS)
-    skip = jnp.repeat(d_skip, HEADDIM).reshape(1, WIDTH)
+    skip = jnp.pad(d_skip, (0, LANES - heads)).reshape(1, LANES)
     gain = norm_gain.reshape(1, WIDTH)
 
     acc_x, acc_bd, tokens, w_dt, w_x, w_z, w_bc = load_weights(
@@ -625,7 +654,8 @@
     right_0 = swapped(join(idx, part_0, top), "head", 3)
     left_1 = swapped(join(idx, part_1, low), "head", 1)
     own = add_near(idx, own, left_0, right_1)
-    return norm(idx, own, sums, top, low, right_0, left_1)
+    half, factor = settle(idx, own, sums, top, low, left_1)
+    return norm(idx, own, factor, right_0, half)
 
 
 def solution(mesh):

time: 89.7 us -> 89.3 us (level)
  Pallas kernels: 39.7 us -> 40.9 us
  local copies, waits for them, and re-layouts: 3.13 us -> 2.07 us
    pallas_call x2 -> x3, Pallas kernels: 7.99 us -> 9.3 us  [the longest x1 6.34 us: load_weights(): pl.pallas_call(load_body, in_specs=[SMEM, *[HBM] * 5], out_specs=[VMEM] *...]
    unnamed x16 -> x14, local copies, waits for them, and re-layouts: 1.19 us -> 0.28 us
  transfers between devices with their start and end apart: 21 -> 21, of which waited for: 10 -> 10; matrix products, arithmetic and copies ran while one was open for 2% -> 1% of each run, Pallas kernels for 32% -> 34%
where the time goes in v5:
time: 89.3 us; the launch traced here: 89.2 us
  Pallas kernels  40.9 us (46%)
  starting transfers between devices  29.6 us (33%)
  waiting for transfers between devices  15.5 us (17%)
  local copies, waits for them, and re-layouts  2.07 us (2%)
    pallas_call x16, Pallas kernels, call(): pl.pallas_call(body, in_specs=[SMEM, *[VMEM] * len(args)], out_specs=[VME...  31.6 us
    ppermute x21, starting transfers between devices, swapped(): return lax.ppermute(array, axis, [(i, i ^ bits) for i in range(4)])  29.6 us
    ppermute x21, waiting for transfers between devices, swapped(): return lax.ppermute(array, axis, [(i, i ^ bits) for i in range(4)])  15.5 us
    pallas_call x1, Pallas kernels, load_weights(): pl.pallas_call(load_body, in_specs=[SMEM, *[HBM] * 5], out_specs=[VMEM] *...  6.34 us
    pallas_call x2, Pallas kernels, end_call(): pl.pallas_call(body, in_specs=[SMEM, *[VMEM] * len(args), *[HBM] * len(mo...  2.96 us
  transfers between devices with their start and end apart: 21, of which 10 were waited for; matrix products, arithmetic and copies ran while one was open for 1% of the time, Pallas kernels for 34%

profile of v5, /device:TPU:0, one launch (start us, length us, event | category | flops | bytes accessed | tf_op | source)
XLA Modules:
  0.0 89.2 jit_solution(8334996584165571451)
XLA Ops:
  0.0 1.1 %fusion = (bf16[256,640]{1,0:T(8,128)(2,1)S(1)}, bf16[256,640]{1,0:T(8,128)(2,1)S(1)}) fusion(bf16[512,640]{1,0:T(8,128)(2,1)} %tok.1), kind=kLoop, calls=%fused_computation.4 | loop fusion | bytes 1310720 | tf_op jit(solution)/shard_map/slice | solution.py:613
  1.1 1.7 %collective-permute-start = (bf16[256,640]{1,0:T(8,128)(2,1)S(1)}, bf16[256,640]{1,0:T(8,128)(2,1)S(1)}, u32[]{:S(2)}, u32[]{:S(2)}) collective-permute-start(bf16[256,640]{1,0:T(8,128)(2,1)S(1)} %get-tuple-element.67), channel_id=1, source_target_pairs={{0,2},{2,0},{4,6},{6,4},{1,3},{3,1},{5,7},{7,5},{8,10},{10,8},{12,... | collective-permute-start | bytes 983048 | tf_op jit(solution)/shard_map/ppermute | solution.py:57
  2.8 2.1 %collective-permute-start.2 = (bf16[256,640]{1,0:T(8,128)(2,1)S(1)}, bf16[256,640]{1,0:T(8,128)(2,1)S(1)}, u32[]{:S(2)}, u32[]{:S(2)}) collective-permute-start(bf16[256,640]{1,0:T(8,128)(2,1)S(1)} %get-tuple-element.66), channel_id=1, source_target_pairs={{0,6},{2,4},{4,2},{6,0},{1,7},{3,5},{5,3},{7,1},{8,14},{10,12},{12... | collective-permute-start | bytes 983048 | tf_op jit(solution)/shard_map/ppermute | solution.py:57
  4.9 0.6 pad_add_fusion.idx
  5.5 0.6 collective-permute-start.4
  6.1 0.6 collective-permute-start.5
  6.7 0.7 pad_bitcast_fusion.skip
  7.4 6.3 %load_weights.1 = (f32[512,1280]{1,0:T(8,128)S(1)}, f32[512,384]{1,0:T(8,128)S(1)}, bf16[512,640]{1,0:T(8,128)(2,1)S(1)}, bf16[128,2560]{1,0:T(8,128)(2,1)S(1)},...) custom-call(s32[3]{0:T(128)} %pad_add_fusion.idx, ...), custom_call_target="tpu_custom_call" | custom-call | flops 1090519040 | bytes 15000000 | tf_op jit(solution)/shard_map/load_weights/pallas_call | solution.py:128
  13.8 0.0 collective-permute-done.l_0
  13.8 2.7 %collective-permute-start.1 = (bf16[256,640]{1,0:T(8,128)(2,1)S(1)}, bf16[256,640]{1,0:T(8,128)(2,1)S(1)}, u32[]{:S(2)}, u32[]{:S(2)}) collective-permute-start(bf16[256,640]{1,0:T(8,128)(2,1)S(1)} %collective-permute-done.l_0), channel_id=1, source_target_pairs={{0,6},{2,4},{4,2},{6,0},{1,7},{3,5},{5,3},{7,1},{8,14},{10,12},{12... | collective-permute-start | bytes 983048 | tf_op jit(solution)/shard_map/ppermute | solution.py:57
  16.5 0.0 collective-permute-done.2.r_1
  16.5 0.2 collective-permute-start.3
  16.7 2.8 %gate_first.1.acc_z = f32[512,1280]{1,0:T(8,128)S(1)} custom-call(s32[3]{0:T(128)S(1)} %copy-done, bf16[512,640]{1,0:T(8,128)(2,1)S(1)} %get-tuple-element.69.tok, bf16[256,640]{1,0:T(8,128)(2,1)S(1)} %collective-permute-done.l_0, bf16[256,640]{1,0:T(8,128)(2,1)S(1)} %collective-permute-done.2.r_1, bf16[2560,1280]{1,0:T(8,128)(2,1)S(1)} %get-tuple-element.113.w_z), custom_call_target="tpu_custom_call" | custom-call | flops 1677721600 | bytes 1000000 | tf_op jit(solution)/shard_map/gate_first/pallas_call | solution.py:72
  19.5 2.2 %collective-permute-done.5.r_0 = bf16[256,640]{1,0:T(8,128)(2,1)S(1)} collective-permute-done((bf16[256,640]{1,0:T(8,128)(2,1)S(1)}, bf16[256,640]{1,0:T(8,128)(2,1)S(1)}, u32[]{:S(2)}, u32[]{:S(2)}) %collective-permute-start.5) | collective-permute-done | bytes 327712 | tf_op jit(solution)/shard_map/ppermute | solution.py:57
  21.7 1.9 %gate_second.1.acc_z = f32[512,1280]{1,0:T(8,128)S(1)} custom-call(s32[3]{0:T(128)S(1)} %copy-done, bf16[256,640]{1,0:T(8,128)(2,1)S(1)} %collective-permute-done.4.l_1, bf16[256,640]{1,0:T(8,128)(2,1)S(1)} %collective-permute-done.5.r_0, bf16[2560,1280]{1,0:T(8,128)(2,1)S(1)} %get-tuple-element.113.w_z, ...), custom_call_target="tpu_custom_call", output_to_operand_aliasing={{}: (4, {})} | custom-call | flops 838860800 | bytes 1000000 | tf_op jit(solution)/shard_map/gate_second/pallas_call | solution.py:72
  23.6 0.0 copy-start.1
  23.6 3.3 %project.1 = (f32[512,1280]{1,0:T(8,128)S(1)}, f32[512,384]{1,0:T(8,128)S(1)}) custom-call(s32[3]{0:T(128)S(1)} %copy-done, bf16[256,640]{1,0:T(8,128)(2,1)S(1)} %collective-permute-done.l_0, bf16[256,640]{1,0:T(8,128)(2,1)S(1)} %collective-permute-done.4.l_1, ...), custom_call_target="tpu_custom_call", output_to_operand_aliasing={{0}: (8, {}), {1}: (9, {})} | custom-call | flops 2181038080 | bytes 1000000 | tf_op jit(solution)/shard_map/project/pallas_call | solution.py:72
  26.9 0.3 collective-permute-done.1.tok_0.t_0
  27.2 0.0 collective-permute-done.3.tok_1.t_1
  27.2 4.9 %device_state.1 = (bf16[512,1280]{1,0:T(8,128)(2,1)S(1)}, bf16[512,128]{1,0:T(8,128)(2,1)S(1)}, bf16[512,128]{1,0:T(8,128)(2,1)S(1)}, f32[512,128]{1,0:T(8,128)S...) custom-call(s32[3]{0:T(128)S(1)} %copy-done, ...), custom_call_target="tpu_custom_call" | custom-call | flops 1090519040 | bytes 1000000 | tf_op jit(solution)/shard_map/device_state/pallas_call | solution.py:72
  32.1 2.0 %collective-permute-start.6 = (bf16[32,1408]{1,0:T(8,128)(2,1)S(1)}, bf16[32,1408]{1,0:T(8,128)(2,1)S(1)}, u32[]{:S(2)}, u32[]{:S(2)}) collective-permute-start(bf16[32,1408]{1,0:T(8,128)(2,1)S(1)} %get-tuple-element.82), channel_id=1, source_target_pairs={{0,8},{8,0},{16,24},{24,16},{1,9},{9,1},{17,25},{25,17},{2,10},{10... | collective-permute-start | bytes 270344 | tf_op jit(solution)/shard_map/ppermute | solution.py:57
  34.1 3.6 %collective-permute-start.7 = (bf16[32,1408]{1,0:T(8,128)(2,1)S(1)}, bf16[32,1408]{1,0:T(8,128)(2,1)S(1)}, u32[]{:S(2)}, u32[]{:S(2)}) collective-permute-start(bf16[32,1408]{1,0:T(8,128)(2,1)S(1)} %get-tuple-element.83), channel_id=1, source_target_pairs={{0,16},{8,24},{16,0},{24,8},{1,17},{9,25},{17,1},{25,9},{2,18},{10... | collective-permute-start | bytes 270344 | tf_op jit(solution)/shard_map/ppermute | solution.py:57
  37.7 0.0 collective-permute-start.8
  37.7 2.2 %mix.2 = (f32[256,1280]{1,0:T(8,128)S(1)}, f32[256,1280]{1,0:T(8,128)S(1)}) custom-call(s32[3]{0:T(128)S(1)} %copy-done, bf16[512,1280]{1,0:T(8,128)(2,1)S(1)} %get-tuple-element.85.inner_r, bf16[512,128]{1,0:T(8,128)(2,1)S(1)} %get-tuple-element.86.b_r, bf16[512,128]{1,0:T(8,128)(2,1)S(1)} %get-tuple-element.87.c_r, ...), custom_call_target="tpu_custom_call" | custom-call | flops 2000000000 | bytes 1000000 | tf_op jit(solution)/shard_map/mix/pallas_call | solution.py:72
  39.9 0.0 collective-permute-done.6.m1
  39.9 1.3 %collective-permute-done.7.m2 = bf16[32,1408]{1,0:T(8,128)(2,1)S(1)} collective-permute-done((bf16[32,1408]{1,0:T(8,128)(2,1)S(1)}, bf16[32,1408]{1,0:T(8,128)(2,1)S(1)}, u32[]{:S(2)}, u32[]{:S(2)}) %collective-permute-start.7) | collective-permute-done | bytes 90144 | tf_op jit(solution)/shard_map/ppermute | solution.py:57
  41.3 2.2 %collective-permute-done.8.m3 = bf16[32,1408]{1,0:T(8,128)(2,1)S(1)} collective-permute-done((bf16[32,1408]{1,0:T(8,128)(2,1)S(1)}, bf16[32,1408]{1,0:T(8,128)(2,1)S(1)}, u32[]{:S(2)}, u32[]{:S(2)}) %collective-permute-start.8) | collective-permute-done | bytes 90144 | tf_op jit(solution)/shard_map/ppermute | solution.py:57
  43.4 0.8 row_total.1.t0
  44.2 0.0 copy-start.2
  44.2 3.3 %collective-permute-start.10 = (bf16[32,1408]{1,0:T(8,128)(2,1)S(1)}, bf16[32,1408]{1,0:T(8,128)(2,1)S(1)}, u32[]{:S(2)}, u32[]{:S(2)}) collective-permute-start(bf16[32,1408]{1,0:T(8,128)(2,1)S(1)} %row_total.1.t0), channel_id=1, source_target_pairs={{0,64},{32,96},{64,0},{96,32},{1,65},{33,97},{65,1},{97,33},{2,66}... | collective-permute-start | bytes 270344 | tf_op jit(solution)/shard_map/ppermute | solution.py:57
  47.5 1.1 %collective-permute-start.11 = (bf16[32,1408]{1,0:T(8,128)(2,1)S(1)}, bf16[32,1408]{1,0:T(8,128)(2,1)S(1)}, u32[]{:S(2)}, u32[]{:S(2)}) collective-permute-start(bf16[32,1408]{1,0:T(8,128)(2,1)S(1)} %row_total.1.t0), channel_id=1, source_target_pairs={{0,96},{32,64},{64,32},{96,0},{1,97},{33,65},{65,33},{97,1},{2,98}... | collective-permute-start | bytes 270344 | tf_op jit(solution)/shard_map/ppermute | solution.py:57
  48.6 0.0 collective-permute-start.9
  48.6 2.2 %mix.3 = (f32[256,1280]{1,0:T(8,128)S(1)}, f32[256,1280]{1,0:T(8,128)S(1)}) custom-call(s32[3]{0:T(128)S(1)} %copy-done, bf16[512,1280]{1,0:T(8,128)(2,1)S(1)} %get-tuple-element.85.inner_r, bf16[512,128]{1,0:T(8,128)(2,1)S(1)} %get-tuple-element.86.b_r, bf16[512,128]{1,0:T(8,128)(2,1)S(1)} %get-tuple-element.87.c_r, ...), custom_call_target="tpu_custom_call" | custom-call | flops 2000000000 | bytes 1000000 | tf_op jit(solution)/shard_map/mix/pallas_call | solution.py:72
  50.8 2.4 %collective-permute-done.11.t3 = bf16[32,1408]{1,0:T(8,128)(2,1)S(1)} collective-permute-done((bf16[32,1408]{1,0:T(8,128)(2,1)S(1)}, bf16[32,1408]{1,0:T(8,128)(2,1)S(1)}, u32[]{:S(2)}, u32[]{:S(2)}) %collective-permute-start.11) | collective-permute-done | bytes 90144 | tf_op jit(solution)/shard_map/ppermute | solution.py:57
  53.2 0.9 %prefixes.1 = (bf16[32,1280]{1,0:T(8,128)(2,1)S(1)}, bf16[32,1280]{1,0:T(8,128)(2,1)S(1)}, bf16[32,1280]{1,0:T(8,128)(2,1)S(1)}, bf16[32,1280]{1,0:T(8,128)(2,1)S(1)}) custom-call(s32[3]{0:T(128)S(1)} %copy-done, bf16[32,1408]{1,0:T(8,128)(2,1)S(1)} %get-tuple-element.92.m0, bf16[32,1408]{1,0:T(8,128)(2,1)S(1)} %collective-permute-done.6.m1, ...), custom_call_target="tpu_custom_call" | custom-call | flops 100000000 | bytes 1000000 | tf_op jit(solution)/shard_map/prefixes/pallas_call | solution.py:72
  54.2 0.1 collective-permute-start.12
  54.3 1.7 %collective-permute-start.13 = (bf16[32,1280]{1,0:T(8,128)(2,1)S(1)}, bf16[32,1280]{1,0:T(8,128)(2,1)S(1)}, u32[]{:S(2)}, u32[]{:S(2)}) collective-permute-start(bf16[32,1280]{1,0:T(8,128)(2,1)S(1)} %get-tuple-element.105), channel_id=1, source_target_pairs={{0,16},{8,24},{16,0},{24,8},{1,17},{9,25},{17,1},{25,9},{2,18},{10... | collective-permute-start | bytes 245768 | tf_op jit(solution)/shard_map/ppermute | solution.py:57
  55.9 3.0 %collective-permute-start.14 = (bf16[32,1280]{1,0:T(8,128)(2,1)S(1)}, bf16[32,1280]{1,0:T(8,128)(2,1)S(1)}, u32[]{:S(2)}, u32[]{:S(2)}) collective-permute-start(bf16[32,1280]{1,0:T(8,128)(2,1)S(1)} %get-tuple-element.106), channel_id=1, source_target_pairs={{0,24},{8,16},{16,8},{24,0},{1,25},{9,17},{17,9},{25,1},{2,26},{10... | collective-permute-start | bytes 245768 | tf_op jit(solution)/shard_map/ppermute | solution.py:57
  59.0 0.0 slice-start.1
  59.0 2.6 %gate.1.zs_r = f32[512,1280]{1,0:T(8,128)S(1)} custom-call(s32[3]{0:T(128)S(1)} %copy-done, bf16[256,640]{1,0:T(8,128)(2,1)S(1)} %collective-permute-done.1.tok_0.t_0, bf16[256,640]{1,0:T(8,128)(2,1)S(1)} %collective-permute-done.3.tok_1.t_1, bf16[2560,1280]{1,0:T(8,128)(2,1)S(1)} %get-tuple-element.113.w_z, ...), custom_call_target="tpu_custom_call", output_to_operand_aliasing={{}: (4, {})} | custom-call | flops 838860800 | bytes 1000000 | tf_op jit(solution)/shard_map/gate/pallas_call | solution.py:72
  61.6 0.0 collective-permute-done.12.h1
  61.6 0.0 collective-permute-done.14.h3
  61.6 0.2 slice-done.1
  61.9 2.9 %gated_rows.1 = (bf16[512,1280]{1,0:T(8,128)(2,1)S(1)}, f32[8,512]{1,0:T(8,128)S(1)}, bf16[264,640]{1,0:T(8,128)(2,1)S(1)}, bf16[264,640]{1,0:T(8,128)(2,1)S(1)}) custom-call(s32[3]{0:T(128)S(1)} %copy-done, bf16[32,1280]{1,0:T(8,128)(2,1)S(1)} %get-tuple-element.103.h0, bf16[32,1280]{1,0:T(8,128)(2,1)S(1)} %collective-permute-done.12.h1, ...), custom_call_target="tpu_custom_call" | custom-call | flops 1090519040 | bytes 1000000 | tf_op jit(solution)/shard_map/gated_rows/pallas_call | solution.py:72
  64.8 0.1 collective-permute-start.17
  64.9 2.2 %collective-permute-start.18 = (bf16[264,640]{1,0:T(8,128)(2,1)S(1)}, bf16[264,640]{1,0:T(8,128)(2,1)S(1)}, u32[]{:S(2)}, u32[]{:S(2)}) collective-permute-start(bf16[264,640]{1,0:T(8,128)(2,1)S(1)} %get-tuple-element.120), channel_id=1, source_target_pairs={{0,6},{2,4},{4,2},{6,0},{1,7},{3,5},{5,3},{7,1},{8,14},{10,12},{12... | collective-permute-start | bytes 1013768 | tf_op jit(solution)/shard_map/ppermute | solution.py:57
  67.1 1.7 %near_block.2 = (bf16[256,640]{1,0:T(8,128)(2,1)S(1)}, f32[256,640]{1,0:T(8,128)S(1)}) custom-call(s32[3]{0:T(128)S(1)} %copy-done, bf16[512,1280]{1,0:T(8,128)(2,1)S(1)} %get-tuple-element.115.rows, bf16[1280,2560]{1,0:T(8,128)(2,1)S(1)} %bitcast.12), custom_call_target="tpu_custom_call" | custom-call | flops 1000000 | bytes 1000000 | tf_op jit(solution)/shard_map/near_block/pallas_call | solution.py:72
  68.8 1.4 %collective-permute-start.15 = (bf16[256,640]{1,0:T(8,128)(2,1)S(1)}, bf16[256,640]{1,0:T(8,128)(2,1)S(1)}, u32[]{:S(2)}, u32[]{:S(2)}) collective-permute-start(bf16[256,640]{1,0:T(8,128)(2,1)S(1)} %get-tuple-element.116), channel_id=1, source_target_pairs={{0,2},{2,0},{4,6},{6,4},{1,3},{3,1},{5,7},{7,5},{8,10},{10,8},{12,... | collective-permute-start | bytes 983048 | tf_op jit(solution)/shard_map/ppermute | solution.py:57
  70.2 1.7 %near_block.3 = (bf16[256,640]{1,0:T(8,128)(2,1)S(1)}, f32[256,640]{1,0:T(8,128)S(1)}) custom-call(s32[3]{0:T(128)S(1)} %copy-done, bf16[512,1280]{1,0:T(8,128)(2,1)S(1)} %get-tuple-element.115.rows, bf16[1280,2560]{1,0:T(8,128)(2,1)S(1)} %bitcast.12), custom_call_target="tpu_custom_call" | custom-call | flops 1000000 | bytes 1000000 | tf_op jit(solution)/shard_map/near_block/pallas_call | solution.py:72
  72.0 1.2 %collective-permute-start.16 = (bf16[256,640]{1,0:T(8,128)(2,1)S(1)}, bf16[256,640]{1,0:T(8,128)(2,1)S(1)}, u32[]{:S(2)}, u32[]{:S(2)}) collective-permute-start(bf16[256,640]{1,0:T(8,128)(2,1)S(1)} %get-tuple-element.117), channel_id=1, source_target_pairs={{0,6},{2,4},{4,2},{6,0},{1,7},{3,5},{5,3},{7,1},{8,14},{10,12},{12... | collective-permute-start | bytes 983048 | tf_op jit(solution)/shard_map/ppermute | solution.py:57
  73.2 1.7 %own_block.1.own = f32[512,640]{1,0:T(8,128)S(1)} custom-call(s32[3]{0:T(128)S(1)} %copy-done, bf16[512,1280]{1,0:T(8,128)(2,1)S(1)} %get-tuple-element.115.rows, bf16[1280,2560]{1,0:T(8,128)(2,1)S(1)} %bitcast.12), custom_call_target="tpu_custom_call" | custom-call | flops 1000000 | bytes 1000000 | tf_op jit(solution)/shard_map/own_block/pallas_call | solution.py:72
  74.9 0.1 collective-permute-done.17.near.half
  75.0 0.6 join.3
  75.6 2.1 %collective-permute-start.20 = (bf16[264,640]{1,0:T(8,128)(2,1)S(1)}, bf16[264,640]{1,0:T(8,128)(2,1)S(1)}, u32[]{:S(2)}, u32[]{:S(2)}) collective-permute-start(bf16[264,640]{1,0:T(8,128)(2,1)S(1)} %join.3), channel_id=1, source_target_pairs={{0,6},{2,4},{4,2},{6,0},{1,7},{3,5},{5,3},{7,1},{8,14},{10,12},{12... | collective-permute-start | bytes 1013768 | tf_op jit(solution)/shard_map/ppermute | solution.py:57
  77.8 0.0 collective-permute-done.18.half.other
  77.8 0.6 join.2
  78.4 0.1 collective-permute-start.19
  78.5 2.2 %collective-permute-done.15.left_0 = bf16[256,640]{1,0:T(8,128)(2,1)S(1)} collective-permute-done((bf16[256,640]{1,0:T(8,128)(2,1)S(1)}, bf16[256,640]{1,0:T(8,128)(2,1)S(1)}, u32[]{:S(2)}, u32[]{:S(2)}) %collective-permute-start.15) | collective-permute-done | bytes 327712 | tf_op jit(solution)/shard_map/ppermute | solution.py:57
  80.7 3.2 %collective-permute-done.16.right_1 = bf16[256,640]{1,0:T(8,128)(2,1)S(1)} collective-permute-done((bf16[256,640]{1,0:T(8,128)(2,1)S(1)}, bf16[256,640]{1,0:T(8,128)(2,1)S(1)}, u32[]{:S(2)}, u32[]{:S(2)}) %collective-permute-start.16) | collective-permute-done | bytes 327712 | tf_op jit(solution)/shard_map/ppermute | solution.py:57
  83.9 0.8 add_near.1.own
  84.7 1.1 %collective-permute-done.19.left_1 = bf16[264,640]{1,0:T(8,128)(2,1)S(1)} collective-permute-done((bf16[264,640]{1,0:T(8,128)(2,1)S(1)}, bf16[264,640]{1,0:T(8,128)(2,1)S(1)}, u32[]{:S(2)}, u32[]{:S(2)}) %collective-permute-start.19) | collective-permute-done | bytes 337952 | tf_op jit(solution)/shard_map/ppermute | solution.py:57
  85.8 1.6 %settle.1 = (bf16[512,640]{1,0:T(8,128)(2,1)}, f32[256,128]{1,0:T(8,128)S(1)}) custom-call(s32[3]{0:T(128)S(1)} %copy-done, f32[512,640]{1,0:T(8,128)S(1)} %add_near.1.own, f32[8,512]{1,0:T(8,128)S(1)} %get-tuple-element.118.sums, bf16[264,640]{1,0:T(8,128)(2,1)S(1)} %collective-permute-done.17.near.half, ...), custom_call_target="tpu_custom_call" | custom-call | flops 1000000 | bytes 1000000 | tf_op jit(solution)/shard_map/settle/pallas_call | solution.py:576
  87.4 0.3 collective-permute-done.20.right_0
  87.6 1.4 %norm.1 = bf16[512,640]{1,0:T(8,128)(2,1)} custom-call(s32[3]{0:T(128)S(1)} %copy-done, f32[512,640]{1,0:T(8,128)S(1)} %add_near.1.own, f32[256,128]{1,0:T(8,128)S(1)} %get-tuple-element.122.factor, bf16[264,640]{1,0:T(8,128)(2,1)S(1)} %collective-permute-done.20.right_0, bf16[512,640]{1,0:T(8,128)(2,1)} %get-tuple-element.124.so_far), custom_call_target="tpu_custom_call", output_to_operand_aliasing={{}: (4, {})} | custom-call | flops 1000000 | bytes 1000000 | tf_op jit(solution)/shard_map/norm/pallas_call | solution.py:576
  (17 shorter events, 0.0 us)
Async XLA Ops:
  1.1 12.6 %collective-permute-start = (bf16[256,640]{1,0:T(8,128)(2,1)S(1)}, bf16[256,640]{1,0:T(8,128)(2,1)S(1)}, u32[]{:S(2)}, u32[]{:S(2)}) collective-permute-start(bf16[256,640]{1,0:T(8,128)(2,1)S(1)} %get-tuple-element.67), channel_id=1, source_target_pairs={{0,2},{2,0},{4,6},{6,4},{1,3},{3,1},{5,7},{7,5},{8,10},{10,8},{12,... | collective-permute-start | bytes 983048 | tf_op jit(solution)/shard_map/ppermute | solution.py:57
  2.8 13.7 %collective-permute-start.2 = (bf16[256,640]{1,0:T(8,128)(2,1)S(1)}, bf16[256,640]{1,0:T(8,128)(2,1)S(1)}, u32[]{:S(2)}, u32[]{:S(2)}) collective-permute-start(bf16[256,640]{1,0:T(8,128)(2,1)S(1)} %get-tuple-element.66), channel_id=1, source_target_pairs={{0,6},{2,4},{4,2},{6,0},{1,7},{3,5},{5,3},{7,1},{8,14},{10,12},{12... | collective-permute-start | bytes 983048 | tf_op jit(solution)/shard_map/ppermute | solution.py:57
  5.5 14.0 %collective-permute-start.4 = (bf16[256,640]{1,0:T(8,128)(2,1)S(1)}, bf16[256,640]{1,0:T(8,128)(2,1)S(1)}, u32[]{:S(2)}, u32[]{:S(2)}) collective-permute-start(bf16[256,640]{1,0:T(8,128)(2,1)S(1)} %get-tuple-element.66), channel_id=1, source_target_pairs={{0,2},{2,0},{4,6},{6,4},{1,3},{3,1},{5,7},{7,5},{8,10},{10,8},{12,... | collective-permute-start | bytes 983048 | tf_op jit(solution)/shard_map/ppermute | solution.py:57
  6.1 15.6 %collective-permute-start.5 = (bf16[256,640]{1,0:T(8,128)(2,1)S(1)}, bf16[256,640]{1,0:T(8,128)(2,1)S(1)}, u32[]{:S(2)}, u32[]{:S(2)}) collective-permute-start(bf16[256,640]{1,0:T(8,128)(2,1)S(1)} %get-tuple-element.67), channel_id=1, source_target_pairs={{0,6},{2,4},{4,2},{6,0},{1,7},{3,5},{5,3},{7,1},{8,14},{10,12},{12... | collective-permute-start | bytes 983048 | tf_op jit(solution)/shard_map/ppermute | solution.py:57
  7.4 6.4 %copy-start.3 = (f32[20]{0:T(128)S(1)}, f32[20]{0:T(128)}, u32[]{:S(2)}) copy-start(f32[20]{0:T(128)} %param.18) | copy-start | bytes 244
  7.4 6.4 %copy-start.4 = (f32[20]{0:T(128)S(1)}, f32[20]{0:T(128)}, u32[]{:S(2)}) copy-start(f32[20]{0:T(128)} %param.17) | copy-start | bytes 244
  7.4 9.3 %copy-start = (s32[3]{0:T(128)S(1)}, s32[3]{0:T(128)}, u32[]{:S(2)}) copy-start(s32[3]{0:T(128)} %pad_add_fusion.idx) | copy-start | bytes 40
  13.8 13.4 %collective-permute-start.1 = (bf16[256,640]{1,0:T(8,128)(2,1)S(1)}, bf16[256,640]{1,0:T(8,128)(2,1)S(1)}, u32[]{:S(2)}, u32[]{:S(2)}) collective-permute-start(bf16[256,640]{1,0:T(8,128)(2,1)S(1)} %collective-permute-done.l_0), channel_id=1, source_target_pairs={{0,6},{2,4},{4,2},{6,0},{1,7},{3,5},{5,3},{7,1},{8,14},{10,12},{12... | collective-permute-start | bytes 983048 | tf_op jit(solution)/shard_map/ppermute | solution.py:57
  16.5 10.7 %collective-permute-start.3 = (bf16[256,640]{1,0:T(8,128)(2,1)S(1)}, bf16[256,640]{1,0:T(8,128)(2,1)S(1)}, u32[]{:S(2)}, u32[]{:S(2)}) collective-permute-start(bf16[256,640]{1,0:T(8,128)(2,1)S(1)} %collective-permute-done.2.r_1), channel_id=1, source_target_pairs={{0,2},{2,0},{4,6},{6,4},{1,3},{3,1},{5,7},{7,5},{8,10},{10,8},{12,... | collective-permute-start | bytes 983048 | tf_op jit(solution)/shard_map/ppermute | solution.py:57
  23.6 3.6 %copy-start.1 = (s32[512]{0:T(512)S(1)}, s32[512]{0:T(512)}, u32[]{:S(2)}) copy-start(s32[512]{0:T(512)} %param.12) | copy-start | bytes 6148
  32.1 7.8 %collective-permute-start.6 = (bf16[32,1408]{1,0:T(8,128)(2,1)S(1)}, bf16[32,1408]{1,0:T(8,128)(2,1)S(1)}, u32[]{:S(2)}, u32[]{:S(2)}) collective-permute-start(bf16[32,1408]{1,0:T(8,128)(2,1)S(1)} %get-tuple-element.82), channel_id=1, source_target_pairs={{0,8},{8,0},{16,24},{24,16},{1,9},{9,1},{17,25},{25,17},{2,10},{10... | collective-permute-start | bytes 270344 | tf_op jit(solution)/shard_map/ppermute | solution.py:57
  34.1 7.2 %collective-permute-start.7 = (bf16[32,1408]{1,0:T(8,128)(2,1)S(1)}, bf16[32,1408]{1,0:T(8,128)(2,1)S(1)}, u32[]{:S(2)}, u32[]{:S(2)}) collective-permute-start(bf16[32,1408]{1,0:T(8,128)(2,1)S(1)} %get-tuple-element.83), channel_id=1, source_target_pairs={{0,16},{8,24},{16,0},{24,8},{1,17},{9,25},{17,1},{25,9},{2,18},{10... | collective-permute-start | bytes 270344 | tf_op jit(solution)/shard_map/ppermute | solution.py:57
  37.7 5.7 %collective-permute-start.8 = (bf16[32,1408]{1,0:T(8,128)(2,1)S(1)}, bf16[32,1408]{1,0:T(8,128)(2,1)S(1)}, u32[]{:S(2)}, u32[]{:S(2)}) collective-permute-start(bf16[32,1408]{1,0:T(8,128)(2,1)S(1)} %get-tuple-element.84), channel_id=1, source_target_pairs={{0,24},{8,16},{16,8},{24,0},{1,25},{9,17},{17,9},{25,1},{2,26},{10... | collective-permute-start | bytes 270344 | tf_op jit(solution)/shard_map/ppermute | solution.py:57
  44.2 14.7 %copy-start.2 = (f32[1280]{0:T(1024)S(1)}, f32[1280]{0:T(1024)}, u32[]{:S(2)}) copy-start(f32[1280]{0:T(1024)} %param.20) | copy-start | bytes 15364
  44.2 6.6 %collective-permute-start.10 = (bf16[32,1408]{1,0:T(8,128)(2,1)S(1)}, bf16[32,1408]{1,0:T(8,128)(2,1)S(1)}, u32[]{:S(2)}, u32[]{:S(2)}) collective-permute-start(bf16[32,1408]{1,0:T(8,128)(2,1)S(1)} %row_total.1.t0), channel_id=1, source_target_pairs={{0,64},{32,96},{64,0},{96,32},{1,65},{33,97},{65,1},{97,33},{2,66}... | collective-permute-start | bytes 270344 | tf_op jit(solution)/shard_map/ppermute | solution.py:57
  47.5 5.7 %collective-permute-start.11 = (bf16[32,1408]{1,0:T(8,128)(2,1)S(1)}, bf16[32,1408]{1,0:T(8,128)(2,1)S(1)}, u32[]{:S(2)}, u32[]{:S(2)}) collective-permute-start(bf16[32,1408]{1,0:T(8,128)(2,1)S(1)} %row_total.1.t0), channel_id=1, source_target_pairs={{0,96},{32,64},{64,32},{96,0},{1,97},{33,65},{65,33},{97,1},{2,98}... | collective-permute-start | bytes 270344 | tf_op jit(solution)/shard_map/ppermute | solution.py:57
  48.6 4.7 %collective-permute-start.9 = (bf16[32,1408]{1,0:T(8,128)(2,1)S(1)}, bf16[32,1408]{1,0:T(8,128)(2,1)S(1)}, u32[]{:S(2)}, u32[]{:S(2)}) collective-permute-start(bf16[32,1408]{1,0:T(8,128)(2,1)S(1)} %row_total.1.t0), channel_id=1, source_target_pairs={{0,32},{32,0},{64,96},{96,64},{1,33},{33,1},{65,97},{97,65},{2,34}... | collective-permute-start | bytes 270344 | tf_op jit(solution)/shard_map/ppermute | solution.py:57
  54.2 7.4 %collective-permute-start.12 = (bf16[32,1280]{1,0:T(8,128)(2,1)S(1)}, bf16[32,1280]{1,0:T(8,128)(2,1)S(1)}, u32[]{:S(2)}, u32[]{:S(2)}) collective-permute-start(bf16[32,1280]{1,0:T(8,128)(2,1)S(1)} %get-tuple-element.104), channel_id=1, source_target_pairs={{0,8},{8,0},{16,24},{24,16},{1,9},{9,1},{17,25},{25,17},{2,10},{10... | collective-permute-start | bytes 245768 | tf_op jit(solution)/shard_map/ppermute | solution.py:57
  54.3 7.4 %collective-permute-start.13 = (bf16[32,1280]{1,0:T(8,128)(2,1)S(1)}, bf16[32,1280]{1,0:T(8,128)(2,1)S(1)}, u32[]{:S(2)}, u32[]{:S(2)}) collective-permute-start(bf16[32,1280]{1,0:T(8,128)(2,1)S(1)} %get-tuple-element.105), channel_id=1, source_target_pairs={{0,16},{8,24},{16,0},{24,8},{1,17},{9,25},{17,1},{25,9},{2,18},{10... | collective-permute-start | bytes 245768 | tf_op jit(solution)/shard_map/ppermute | solution.py:57
  55.9 5.7 %collective-permute-start.14 = (bf16[32,1280]{1,0:T(8,128)(2,1)S(1)}, bf16[32,1280]{1,0:T(8,128)(2,1)S(1)}, u32[]{:S(2)}, u32[]{:S(2)}) collective-permute-start(bf16[32,1280]{1,0:T(8,128)(2,1)S(1)} %get-tuple-element.106), channel_id=1, source_target_pairs={{0,24},{8,16},{16,8},{24,0},{1,25},{9,17},{17,9},{25,1},{2,26},{10... | collective-permute-start | bytes 245768 | tf_op jit(solution)/shard_map/ppermute | solution.py:57
  58.9 2.7 %slice-start = ((s8[6553600]{0:T(1024)(128)(4,1)}), s8[4194304]{0:T(1024)(128)(4,1)S(1)}, s32[]{:S(2)}) async-start(s8[6553600]{0:T(1024)(128)(4,1)} %bitcast.11), calls=%async_computation | async-start | bytes 8388608
  59.0 2.9 %slice-start.1 = ((s8[6553600]{0:T(1024)(128)(4,1)}), s8[2359296]{0:T(1024)(128)(4,1)S(1)}, s32[]{:S(2)}) async-start(s8[6553600]{0:T(1024)(128)(4,1)} %bitcast.11), calls=%async_computation.1 | async-start | bytes 4718592
  64.8 10.2 %collective-permute-start.17 = (bf16[264,640]{1,0:T(8,128)(2,1)S(1)}, bf16[264,640]{1,0:T(8,128)(2,1)S(1)}, u32[]{:S(2)}, u32[]{:S(2)}) collective-permute-start(bf16[264,640]{1,0:T(8,128)(2,1)S(1)} %get-tuple-element.119), channel_id=1, source_target_pairs={{0,2},{2,0},{4,6},{6,4},{1,3},{3,1},{5,7},{7,5},{8,10},{10,8},{12,... | collective-permute-start | bytes 1013768 | tf_op jit(solution)/shard_map/ppermute | solution.py:57
  64.9 12.9 %collective-permute-start.18 = (bf16[264,640]{1,0:T(8,128)(2,1)S(1)}, bf16[264,640]{1,0:T(8,128)(2,1)S(1)}, u32[]{:S(2)}, u32[]{:S(2)}) collective-permute-start(bf16[264,640]{1,0:T(8,128)(2,1)S(1)} %get-tuple-element.120), channel_id=1, source_target_pairs={{0,6},{2,4},{4,2},{6,0},{1,7},{3,5},{5,3},{7,1},{8,14},{10,12},{12... | collective-permute-start | bytes 1013768 | tf_op jit(solution)/shard_map/ppermute | solution.py:57
  68.8 11.9 %collective-permute-start.15 = (bf16[256,640]{1,0:T(8,128)(2,1)S(1)}, bf16[256,640]{1,0:T(8,128)(2,1)S(1)}, u32[]{:S(2)}, u32[]{:S(2)}) collective-permute-start(bf16[256,640]{1,0:T(8,128)(2,1)S(1)} %get-tuple-element.116), channel_id=1, source_target_pairs={{0,2},{2,0},{4,6},{6,4},{1,3},{3,1},{5,7},{7,5},{8,10},{10,8},{12,... | collective-permute-start | bytes 983048 | tf_op jit(solution)/shard_map/ppermute | solution.py:57
  72.0 11.9 %collective-permute-start.16 = (bf16[256,640]{1,0:T(8,128)(2,1)S(1)}, bf16[256,640]{1,0:T(8,128)(2,1)S(1)}, u32[]{:S(2)}, u32[]{:S(2)}) collective-permute-start(bf16[256,640]{1,0:T(8,128)(2,1)S(1)} %get-tuple-element.117), channel_id=1, source_target_pairs={{0,6},{2,4},{4,2},{6,0},{1,7},{3,5},{5,3},{7,1},{8,14},{10,12},{12... | collective-permute-start | bytes 983048 | tf_op jit(solution)/shard_map/ppermute | solution.py:57
  75.6 12.0 %collective-permute-start.20 = (bf16[264,640]{1,0:T(8,128)(2,1)S(1)}, bf16[264,640]{1,0:T(8,128)(2,1)S(1)}, u32[]{:S(2)}, u32[]{:S(2)}) collective-permute-start(bf16[264,640]{1,0:T(8,128)(2,1)S(1)} %join.3), channel_id=1, source_target_pairs={{0,6},{2,4},{4,2},{6,0},{1,7},{3,5},{5,3},{7,1},{8,14},{10,12},{12... | collective-permute-start | bytes 1013768 | tf_op jit(solution)/shard_map/ppermute | solution.py:57
  78.4 7.4 %collective-permute-start.19 = (bf16[264,640]{1,0:T(8,128)(2,1)S(1)}, bf16[264,640]{1,0:T(8,128)(2,1)S(1)}, u32[]{:S(2)}, u32[]{:S(2)}) collective-permute-start(bf16[264,640]{1,0:T(8,128)(2,1)S(1)} %join.2), channel_id=1, source_target_pairs={{0,2},{2,0},{4,6},{6,4},{1,3},{3,1},{5,7},{7,5},{8,10},{10,8},{12,... | collective-permute-start | bytes 1013768 | tf_op jit(solution)/shard_map/ppermute | solution.py:57

commit v6 on v5

--- a/solution.py
+++ b/solution.py
@@ -192,11 +192,13 @@
 ):
     tokens = jnp.concatenate([tok_0[...], tok_1[...]], 0)
     feats = block_of(idx, 2)
+    logits_part = dot_nt(tokens, w_dt[:, feats])
     mapped = silu(acc_bd[:, : 2 * NSTATE] + dot(tokens, w_bc[feats, :]))
+    ahead = dot(tokens, w_x[feats, span(0)])
     b_t = mapped[:, :NSTATE].T.astype(BF16)
     b_o[...] = mapped[:, :NSTATE].astype(BF16)
     c_o[...] = mapped[:, NSTATE:].astype(BF16)
-    logits = acc_bd[:, 2 * NSTATE :] + dot_nt(tokens, w_dt[:, feats]) + bias[...]
+    logits = acc_bd[:, 2 * NSTATE :] + logits_part + bias[...]
     step = jnp.maximum(logits, 0.0) + jnp.log1p(jnp.exp(-jnp.abs(logits)))
     step_o[...] = step
     lane = lax.broadcasted_iota(jnp.int32, (ROWS, LANES), 1)
@@ -223,7 +225,10 @@
     through = jnp.concatenate([terms(t, 8, LANES) for t in throughs], 0).astype(BF16)
     tail = terms(throughs[0] * throughs[1], QUARTER, LANES).astype(BF16)
     for j in range(STEPS):
-        inner = silu(acc_x[:, span(j)] + dot(tokens, w_x[feats, span(j)])).astype(BF16)
+        part = ahead
+        if j + 1 < STEPS:
+            ahead = dot(tokens, w_x[feats, span(j + 1)])
+        inner = silu(acc_x[:, span(j)] + part).astype(BF16)
         inner_o[:, span(j)] = inner
         heads = head_rows(j)
         wide = dot(keep, jnp.concatenate([heads, heads], 0))
@@ -462,23 +467,31 @@
     for d, part in enumerate((h0, h1, h2, h3)):
         start = pl.multiple_of((idx[2] ^ d) * QUARTER, QUARTER)
         state[pl.ds(start, QUARTER), :] = part[...]
+    def carried(g, j):
+        enter = state[:, span(j)]
+        if g:
+            enter = first[:, span(j)] + thr[0:1, span(j)] * enter.astype(F32)
+            enter = enter.astype(BF16)
+        return dot(c_r[span(g, GROUP), :], enter)
+
     ones = jnp.ones((8, LANES), BF16)
-    for g, (u, ent) in enumerate(((u0, e0), (u1, e1))):
-        rows = span(g, GROUP)
-        squares = jnp.zeros((GROUP, LANES), F32)
-        for j in range(STEPS):
-            enter = state[:, span(j)]
-            if g:
-                enter = first[:, span(j)] + thr[0:1, span(j)] * enter.astype(F32)
-                enter = enter.astype(BF16)
-            carried = dot(c_r[rows, :], enter)
-            gated = (u[:, span(j)] + ent[:, span(j)] * carried) * zs_r[rows, span(j)]
-            rows_o[rows, span(j)] = (gated * gain[:, span(j)]).astype(BF16)
-            square = gated * gated
-            squares = squares + (square[:, :LANES] + square[:, LANES:])
-        hi, mid, lo = three(squares)
-        sums_o[:, rows] = dot_nt(ones, hi) + (dot_nt(ones, mid) + dot_nt(ones, lo))
-    part = dot(rows_o[...], w_out[:, block_cols(idx, 2)]).astype(BF16)
+    steps = [(g, j) for g in range(2) for j in range(STEPS)]
+    squares = [jnp.zeros((GROUP, LANES), F32), jnp.zeros((GROUP, LANES), F32)]
+    ahead = carried(0, 0)
+    for n, (g, j) in enumerate(steps):
+        now = ahead
+        if n + 1 < len(steps):
+            ahead = carried(*steps[n + 1])
+        rows, u, ent = span(g, GROUP), (u0, u1)[g], (e0, e1)[g]
+        gated = (u[:, span(j)] + ent[:, span(j)] * now) * zs_r[rows, span(j)]
+        rows_o[rows, span(j)] = (gated * gain[:, span(j)]).astype(BF16)
+        square = gated * gated
+        squares[g] = squares[g] + (square[:, :LANES] + square[:, LANES:])
+    part = dot(rows_o[...], w_out[:, block_cols(idx, 2)])
+    for g in range(2):
+        hi, mid, lo = three(squares[g])
+        sums_o[:, span(g, GROUP)] = dot_nt(ones, hi) + (dot_nt(ones, mid) + dot_nt(ones, lo))
+    part = part.astype(BF16)
     tail = tail_rows(sums_o[0:1, :])
     for g, out in enumerate((top, low)):
         out[:GROUP, :] = part[span(g, GROUP)]

time: 89.3 us -> 88 us (0.985)
  Pallas kernels: 40.9 us -> 39.6 us
    pallas_call x16, Pallas kernels: 31.6 us -> 30.3 us  [call(): pl.pallas_call(body, in_specs=[SMEM, *[VMEM] * len(args)], out_specs=[VME...]
where the time goes in v6:
time: 88 us; the launch traced here: 87.8 us
  Pallas kernels  39.6 us (45%)
  starting transfers between devices  29.6 us (34%)
  waiting for transfers between devices  15.4 us (18%)
  local copies, waits for them, and re-layouts  2.07 us (2%)
    pallas_call x16, Pallas kernels, call(): pl.pallas_call(body, in_specs=[SMEM, *[VMEM] * len(args)], out_specs=[VME...  30.3 us
    ppermute x21, starting transfers between devices, swapped(): return lax.ppermute(array, axis, [(i, i ^ bits) for i in range(4)])  29.6 us
    ppermute x21, waiting for transfers between devices, swapped(): return lax.ppermute(array, axis, [(i, i ^ bits) for i in range(4)])  15.4 us
    pallas_call x1, Pallas kernels, load_weights(): pl.pallas_call(load_body, in_specs=[SMEM, *[HBM] * 5], out_specs=[VMEM] *...  6.34 us
    pallas_call x2, Pallas kernels, end_call(): pl.pallas_call(body, in_specs=[SMEM, *[VMEM] * len(args), *[HBM] * len(mo...  2.96 us
  transfers between devices with their start and end apart: 21, of which 10 were waited for; matrix products, arithmetic and copies ran while one was open for 1% of the time, Pallas kernels for 34%

profile of v6, /device:TPU:0, one launch (start us, length us, event | category | flops | bytes accessed | tf_op | source)
XLA Modules:
  0.0 87.8 jit_solution(1379130370206996593)
XLA Ops:
  0.0 1.1 %fusion = (bf16[256,640]{1,0:T(8,128)(2,1)S(1)}, bf16[256,640]{1,0:T(8,128)(2,1)S(1)}) fusion(bf16[512,640]{1,0:T(8,128)(2,1)} %tok.1), kind=kLoop, calls=%fused_computation.4 | loop fusion | bytes 1310720 | tf_op jit(solution)/shard_map/slice | solution.py:626
  1.1 1.7 %collective-permute-start = (bf16[256,640]{1,0:T(8,128)(2,1)S(1)}, bf16[256,640]{1,0:T(8,128)(2,1)S(1)}, u32[]{:S(2)}, u32[]{:S(2)}) collective-permute-start(bf16[256,640]{1,0:T(8,128)(2,1)S(1)} %get-tuple-element.67), channel_id=1, source_target_pairs={{0,2},{2,0},{4,6},{6,4},{1,3},{3,1},{5,7},{7,5},{8,10},{10,8},{12,... | collective-permute-start | bytes 983048 | tf_op jit(solution)/shard_map/ppermute | solution.py:57
  2.8 2.1 %collective-permute-start.2 = (bf16[256,640]{1,0:T(8,128)(2,1)S(1)}, bf16[256,640]{1,0:T(8,128)(2,1)S(1)}, u32[]{:S(2)}, u32[]{:S(2)}) collective-permute-start(bf16[256,640]{1,0:T(8,128)(2,1)S(1)} %get-tuple-element.66), channel_id=1, source_target_pairs={{0,6},{2,4},{4,2},{6,0},{1,7},{3,5},{5,3},{7,1},{8,14},{10,12},{12... | collective-permute-start | bytes 983048 | tf_op jit(solution)/shard_map/ppermute | solution.py:57
  4.9 0.6 pad_add_fusion.idx
  5.5 0.6 collective-permute-start.4
  6.1 0.6 collective-permute-start.5
  6.7 0.7 pad_bitcast_fusion.skip
  7.4 6.3 %load_weights.1 = (f32[512,1280]{1,0:T(8,128)S(1)}, f32[512,384]{1,0:T(8,128)S(1)}, bf16[512,640]{1,0:T(8,128)(2,1)S(1)}, bf16[128,2560]{1,0:T(8,128)(2,1)S(1)},...) custom-call(s32[3]{0:T(128)} %pad_add_fusion.idx, ...), custom_call_target="tpu_custom_call" | custom-call | flops 1090519040 | bytes 15000000 | tf_op jit(solution)/shard_map/load_weights/pallas_call | solution.py:128
  13.8 0.0 collective-permute-done.l_0
  13.8 2.7 %collective-permute-start.1 = (bf16[256,640]{1,0:T(8,128)(2,1)S(1)}, bf16[256,640]{1,0:T(8,128)(2,1)S(1)}, u32[]{:S(2)}, u32[]{:S(2)}) collective-permute-start(bf16[256,640]{1,0:T(8,128)(2,1)S(1)} %collective-permute-done.l_0), channel_id=1, source_target_pairs={{0,6},{2,4},{4,2},{6,0},{1,7},{3,5},{5,3},{7,1},{8,14},{10,12},{12... | collective-permute-start | bytes 983048 | tf_op jit(solution)/shard_map/ppermute | solution.py:57
  16.5 0.0 collective-permute-done.2.r_1
  16.5 0.2 collective-permute-start.3
  16.7 2.8 %gate_first.1.acc_z = f32[512,1280]{1,0:T(8,128)S(1)} custom-call(s32[3]{0:T(128)S(1)} %copy-done, bf16[512,640]{1,0:T(8,128)(2,1)S(1)} %get-tuple-element.69.tok, bf16[256,640]{1,0:T(8,128)(2,1)S(1)} %collective-permute-done.l_0, bf16[256,640]{1,0:T(8,128)(2,1)S(1)} %collective-permute-done.2.r_1, bf16[2560,1280]{1,0:T(8,128)(2,1)S(1)} %get-tuple-element.113.w_z), custom_call_target="tpu_custom_call" | custom-call | flops 1677721600 | bytes 1000000 | tf_op jit(solution)/shard_map/gate_first/pallas_call | solution.py:72
  19.5 0.0 collective-permute-done.4.l_1
  19.5 2.2 %collective-permute-done.5.r_0 = bf16[256,640]{1,0:T(8,128)(2,1)S(1)} collective-permute-done((bf16[256,640]{1,0:T(8,128)(2,1)S(1)}, bf16[256,640]{1,0:T(8,128)(2,1)S(1)}, u32[]{:S(2)}, u32[]{:S(2)}) %collective-permute-start.5) | collective-permute-done | bytes 327712 | tf_op jit(solution)/shard_map/ppermute | solution.py:57
  21.7 1.9 %gate_second.1.acc_z = f32[512,1280]{1,0:T(8,128)S(1)} custom-call(s32[3]{0:T(128)S(1)} %copy-done, bf16[256,640]{1,0:T(8,128)(2,1)S(1)} %collective-permute-done.4.l_1, bf16[256,640]{1,0:T(8,128)(2,1)S(1)} %collective-permute-done.5.r_0, bf16[2560,1280]{1,0:T(8,128)(2,1)S(1)} %get-tuple-element.113.w_z, ...), custom_call_target="tpu_custom_call", output_to_operand_aliasing={{}: (4, {})} | custom-call | flops 838860800 | bytes 1000000 | tf_op jit(solution)/shard_map/gate_second/pallas_call | solution.py:72
  23.6 0.0 copy-start.1
  23.6 3.3 %project.1 = (f32[512,1280]{1,0:T(8,128)S(1)}, f32[512,384]{1,0:T(8,128)S(1)}) custom-call(s32[3]{0:T(128)S(1)} %copy-done, bf16[256,640]{1,0:T(8,128)(2,1)S(1)} %collective-permute-done.l_0, bf16[256,640]{1,0:T(8,128)(2,1)S(1)} %collective-permute-done.4.l_1, ...), custom_call_target="tpu_custom_call", output_to_operand_aliasing={{0}: (8, {}), {1}: (9, {})} | custom-call | flops 2181038080 | bytes 1000000 | tf_op jit(solution)/shard_map/project/pallas_call | solution.py:72
  26.9 0.3 collective-permute-done.1.tok_0.t_0
  27.2 0.0 collective-permute-done.3.tok_1.t_1
  27.2 3.6 %device_state.1 = (bf16[512,1280]{1,0:T(8,128)(2,1)S(1)}, bf16[512,128]{1,0:T(8,128)(2,1)S(1)}, bf16[512,128]{1,0:T(8,128)(2,1)S(1)}, f32[512,128]{1,0:T(8,128)S...) custom-call(s32[3]{0:T(128)S(1)} %copy-done, ...), custom_call_target="tpu_custom_call" | custom-call | flops 1090519040 | bytes 1000000 | tf_op jit(solution)/shard_map/device_state/pallas_call | solution.py:72
  30.9 2.0 %collective-permute-start.6 = (bf16[32,1408]{1,0:T(8,128)(2,1)S(1)}, bf16[32,1408]{1,0:T(8,128)(2,1)S(1)}, u32[]{:S(2)}, u32[]{:S(2)}) collective-permute-start(bf16[32,1408]{1,0:T(8,128)(2,1)S(1)} %get-tuple-element.82), channel_id=1, source_target_pairs={{0,8},{8,0},{16,24},{24,16},{1,9},{9,1},{17,25},{25,17},{2,10},{10... | collective-permute-start | bytes 270344 | tf_op jit(solution)/shard_map/ppermute | solution.py:57
  32.9 3.6 %collective-permute-start.7 = (bf16[32,1408]{1,0:T(8,128)(2,1)S(1)}, bf16[32,1408]{1,0:T(8,128)(2,1)S(1)}, u32[]{:S(2)}, u32[]{:S(2)}) collective-permute-start(bf16[32,1408]{1,0:T(8,128)(2,1)S(1)} %get-tuple-element.83), channel_id=1, source_target_pairs={{0,16},{8,24},{16,0},{24,8},{1,17},{9,25},{17,1},{25,9},{2,18},{10... | collective-permute-start | bytes 270344 | tf_op jit(solution)/shard_map/ppermute | solution.py:57
  36.5 0.0 collective-permute-start.8
  36.5 2.2 %mix.2 = (f32[256,1280]{1,0:T(8,128)S(1)}, f32[256,1280]{1,0:T(8,128)S(1)}) custom-call(s32[3]{0:T(128)S(1)} %copy-done, bf16[512,1280]{1,0:T(8,128)(2,1)S(1)} %get-tuple-element.85.inner_r, bf16[512,128]{1,0:T(8,128)(2,1)S(1)} %get-tuple-element.86.b_r, bf16[512,128]{1,0:T(8,128)(2,1)S(1)} %get-tuple-element.87.c_r, ...), custom_call_target="tpu_custom_call" | custom-call | flops 2000000000 | bytes 1000000 | tf_op jit(solution)/shard_map/mix/pallas_call | solution.py:72
  38.7 1.3 %collective-permute-done.7.m2 = bf16[32,1408]{1,0:T(8,128)(2,1)S(1)} collective-permute-done((bf16[32,1408]{1,0:T(8,128)(2,1)S(1)}, bf16[32,1408]{1,0:T(8,128)(2,1)S(1)}, u32[]{:S(2)}, u32[]{:S(2)}) %collective-permute-start.7) | collective-permute-done | bytes 90144 | tf_op jit(solution)/shard_map/ppermute | solution.py:57
  40.0 2.2 %collective-permute-done.8.m3 = bf16[32,1408]{1,0:T(8,128)(2,1)S(1)} collective-permute-done((bf16[32,1408]{1,0:T(8,128)(2,1)S(1)}, bf16[32,1408]{1,0:T(8,128)(2,1)S(1)}, u32[]{:S(2)}, u32[]{:S(2)}) %collective-permute-start.8) | collective-permute-done | bytes 90144 | tf_op jit(solution)/shard_map/ppermute | solution.py:57
  42.2 0.8 row_total.1.t0
  43.0 0.0 copy-start.2
  43.0 3.3 %collective-permute-start.10 = (bf16[32,1408]{1,0:T(8,128)(2,1)S(1)}, bf16[32,1408]{1,0:T(8,128)(2,1)S(1)}, u32[]{:S(2)}, u32[]{:S(2)}) collective-permute-start(bf16[32,1408]{1,0:T(8,128)(2,1)S(1)} %row_total.1.t0), channel_id=1, source_target_pairs={{0,64},{32,96},{64,0},{96,32},{1,65},{33,97},{65,1},{97,33},{2,66}... | collective-permute-start | bytes 270344 | tf_op jit(solution)/shard_map/ppermute | solution.py:57
  46.3 1.1 %collective-permute-start.11 = (bf16[32,1408]{1,0:T(8,128)(2,1)S(1)}, bf16[32,1408]{1,0:T(8,128)(2,1)S(1)}, u32[]{:S(2)}, u32[]{:S(2)}) collective-permute-start(bf16[32,1408]{1,0:T(8,128)(2,1)S(1)} %row_total.1.t0), channel_id=1, source_target_pairs={{0,96},{32,64},{64,32},{96,0},{1,97},{33,65},{65,33},{97,1},{2,98}... | collective-permute-start | bytes 270344 | tf_op jit(solution)/shard_map/ppermute | solution.py:57
  47.3 2.2 %mix.3 = (f32[256,1280]{1,0:T(8,128)S(1)}, f32[256,1280]{1,0:T(8,128)S(1)}) custom-call(s32[3]{0:T(128)S(1)} %copy-done, bf16[512,1280]{1,0:T(8,128)(2,1)S(1)} %get-tuple-element.85.inner_r, bf16[512,128]{1,0:T(8,128)(2,1)S(1)} %get-tuple-element.86.b_r, bf16[512,128]{1,0:T(8,128)(2,1)S(1)} %get-tuple-element.87.c_r, ...), custom_call_target="tpu_custom_call" | custom-call | flops 2000000000 | bytes 1000000 | tf_op jit(solution)/shard_map/mix/pallas_call | solution.py:72
  49.5 0.0 collective-permute-done.10.t2
  49.6 2.5 %collective-permute-done.11.t3 = bf16[32,1408]{1,0:T(8,128)(2,1)S(1)} collective-permute-done((bf16[32,1408]{1,0:T(8,128)(2,1)S(1)}, bf16[32,1408]{1,0:T(8,128)(2,1)S(1)}, u32[]{:S(2)}, u32[]{:S(2)}) %collective-permute-start.11) | collective-permute-done | bytes 90144 | tf_op jit(solution)/shard_map/ppermute | solution.py:57
  52.0 0.0 collective-permute-done.9.t1
  52.0 0.9 %prefixes.1 = (bf16[32,1280]{1,0:T(8,128)(2,1)S(1)}, bf16[32,1280]{1,0:T(8,128)(2,1)S(1)}, bf16[32,1280]{1,0:T(8,128)(2,1)S(1)}, bf16[32,1280]{1,0:T(8,128)(2,1)S(1)}) custom-call(s32[3]{0:T(128)S(1)} %copy-done, bf16[32,1408]{1,0:T(8,128)(2,1)S(1)} %get-tuple-element.92.m0, bf16[32,1408]{1,0:T(8,128)(2,1)S(1)} %collective-permute-done.6.m1, ...), custom_call_target="tpu_custom_call" | custom-call | flops 100000000 | bytes 1000000 | tf_op jit(solution)/shard_map/prefixes/pallas_call | solution.py:72
  52.9 0.1 collective-permute-start.12
  53.0 1.6 %collective-permute-start.13 = (bf16[32,1280]{1,0:T(8,128)(2,1)S(1)}, bf16[32,1280]{1,0:T(8,128)(2,1)S(1)}, u32[]{:S(2)}, u32[]{:S(2)}) collective-permute-start(bf16[32,1280]{1,0:T(8,128)(2,1)S(1)} %get-tuple-element.105), channel_id=1, source_target_pairs={{0,16},{8,24},{16,0},{24,8},{1,17},{9,25},{17,1},{25,9},{2,18},{10... | collective-permute-start | bytes 245768 | tf_op jit(solution)/shard_map/ppermute | solution.py:57
  54.7 3.0 %collective-permute-start.14 = (bf16[32,1280]{1,0:T(8,128)(2,1)S(1)}, bf16[32,1280]{1,0:T(8,128)(2,1)S(1)}, u32[]{:S(2)}, u32[]{:S(2)}) collective-permute-start(bf16[32,1280]{1,0:T(8,128)(2,1)S(1)} %get-tuple-element.106), channel_id=1, source_target_pairs={{0,24},{8,16},{16,8},{24,0},{1,25},{9,17},{17,9},{25,1},{2,26},{10... | collective-permute-start | bytes 245768 | tf_op jit(solution)/shard_map/ppermute | solution.py:57
  57.7 0.0 slice-start.1
  57.7 2.6 %gate.1.zs_r = f32[512,1280]{1,0:T(8,128)S(1)} custom-call(s32[3]{0:T(128)S(1)} %copy-done, bf16[256,640]{1,0:T(8,128)(2,1)S(1)} %collective-permute-done.1.tok_0.t_0, bf16[256,640]{1,0:T(8,128)(2,1)S(1)} %collective-permute-done.3.tok_1.t_1, bf16[2560,1280]{1,0:T(8,128)(2,1)S(1)} %get-tuple-element.113.w_z, ...), custom_call_target="tpu_custom_call", output_to_operand_aliasing={{}: (4, {})} | custom-call | flops 838860800 | bytes 1000000 | tf_op jit(solution)/shard_map/gate/pallas_call | solution.py:72
  60.4 0.0 collective-permute-done.12.h1
  60.4 0.0 collective-permute-done.14.h3
  60.4 0.2 slice-done.1
  60.7 2.8 %gated_rows.1 = (bf16[512,1280]{1,0:T(8,128)(2,1)S(1)}, f32[8,512]{1,0:T(8,128)S(1)}, bf16[264,640]{1,0:T(8,128)(2,1)S(1)}, bf16[264,640]{1,0:T(8,128)(2,1)S(1)}) custom-call(s32[3]{0:T(128)S(1)} %copy-done, bf16[32,1280]{1,0:T(8,128)(2,1)S(1)} %get-tuple-element.103.h0, bf16[32,1280]{1,0:T(8,128)(2,1)S(1)} %collective-permute-done.12.h1, ...), custom_call_target="tpu_custom_call" | custom-call | flops 1090519040 | bytes 1000000 | tf_op jit(solution)/shard_map/gated_rows/pallas_call | solution.py:72
  63.4 0.1 collective-permute-start.17
  63.5 2.2 %collective-permute-start.18 = (bf16[264,640]{1,0:T(8,128)(2,1)S(1)}, bf16[264,640]{1,0:T(8,128)(2,1)S(1)}, u32[]{:S(2)}, u32[]{:S(2)}) collective-permute-start(bf16[264,640]{1,0:T(8,128)(2,1)S(1)} %get-tuple-element.120), channel_id=1, source_target_pairs={{0,6},{2,4},{4,2},{6,0},{1,7},{3,5},{5,3},{7,1},{8,14},{10,12},{12... | collective-permute-start | bytes 1013768 | tf_op jit(solution)/shard_map/ppermute | solution.py:57
  65.8 1.7 %near_block.2 = (bf16[256,640]{1,0:T(8,128)(2,1)S(1)}, f32[256,640]{1,0:T(8,128)S(1)}) custom-call(s32[3]{0:T(128)S(1)} %copy-done, bf16[512,1280]{1,0:T(8,128)(2,1)S(1)} %get-tuple-element.115.rows, bf16[1280,2560]{1,0:T(8,128)(2,1)S(1)} %bitcast.12), custom_call_target="tpu_custom_call" | custom-call | flops 1000000 | bytes 1000000 | tf_op jit(solution)/shard_map/near_block/pallas_call | solution.py:72
  67.5 1.4 %collective-permute-start.15 = (bf16[256,640]{1,0:T(8,128)(2,1)S(1)}, bf16[256,640]{1,0:T(8,128)(2,1)S(1)}, u32[]{:S(2)}, u32[]{:S(2)}) collective-permute-start(bf16[256,640]{1,0:T(8,128)(2,1)S(1)} %get-tuple-element.116), channel_id=1, source_target_pairs={{0,2},{2,0},{4,6},{6,4},{1,3},{3,1},{5,7},{7,5},{8,10},{10,8},{12,... | collective-permute-start | bytes 983048 | tf_op jit(solution)/shard_map/ppermute | solution.py:57
  68.9 1.7 %near_block.3 = (bf16[256,640]{1,0:T(8,128)(2,1)S(1)}, f32[256,640]{1,0:T(8,128)S(1)}) custom-call(s32[3]{0:T(128)S(1)} %copy-done, bf16[512,1280]{1,0:T(8,128)(2,1)S(1)} %get-tuple-element.115.rows, bf16[1280,2560]{1,0:T(8,128)(2,1)S(1)} %bitcast.12), custom_call_target="tpu_custom_call" | custom-call | flops 1000000 | bytes 1000000 | tf_op jit(solution)/shard_map/near_block/pallas_call | solution.py:72
  70.7 1.2 %collective-permute-start.16 = (bf16[256,640]{1,0:T(8,128)(2,1)S(1)}, bf16[256,640]{1,0:T(8,128)(2,1)S(1)}, u32[]{:S(2)}, u32[]{:S(2)}) collective-permute-start(bf16[256,640]{1,0:T(8,128)(2,1)S(1)} %get-tuple-element.117), channel_id=1, source_target_pairs={{0,6},{2,4},{4,2},{6,0},{1,7},{3,5},{5,3},{7,1},{8,14},{10,12},{12... | collective-permute-start | bytes 983048 | tf_op jit(solution)/shard_map/ppermute | solution.py:57
  71.8 1.7 %own_block.1.own = f32[512,640]{1,0:T(8,128)S(1)} custom-call(s32[3]{0:T(128)S(1)} %copy-done, bf16[512,1280]{1,0:T(8,128)(2,1)S(1)} %get-tuple-element.115.rows, bf16[1280,2560]{1,0:T(8,128)(2,1)S(1)} %bitcast.12), custom_call_target="tpu_custom_call" | custom-call | flops 1000000 | bytes 1000000 | tf_op jit(solution)/shard_map/own_block/pallas_call | solution.py:72
  73.5 0.2 collective-permute-done.17.near.half
  73.7 0.6 join.3
  74.3 2.1 %collective-permute-start.20 = (bf16[264,640]{1,0:T(8,128)(2,1)S(1)}, bf16[264,640]{1,0:T(8,128)(2,1)S(1)}, u32[]{:S(2)}, u32[]{:S(2)}) collective-permute-start(bf16[264,640]{1,0:T(8,128)(2,1)S(1)} %join.3), channel_id=1, source_target_pairs={{0,6},{2,4},{4,2},{6,0},{1,7},{3,5},{5,3},{7,1},{8,14},{10,12},{12... | collective-permute-start | bytes 1013768 | tf_op jit(solution)/shard_map/ppermute | solution.py:57
  76.4 0.6 join.2
  77.1 0.1 collective-permute-start.19
  77.1 2.2 %collective-permute-done.15.left_0 = bf16[256,640]{1,0:T(8,128)(2,1)S(1)} collective-permute-done((bf16[256,640]{1,0:T(8,128)(2,1)S(1)}, bf16[256,640]{1,0:T(8,128)(2,1)S(1)}, u32[]{:S(2)}, u32[]{:S(2)}) %collective-permute-start.15) | collective-permute-done | bytes 327712 | tf_op jit(solution)/shard_map/ppermute | solution.py:57
  79.4 3.2 %collective-permute-done.16.right_1 = bf16[256,640]{1,0:T(8,128)(2,1)S(1)} collective-permute-done((bf16[256,640]{1,0:T(8,128)(2,1)S(1)}, bf16[256,640]{1,0:T(8,128)(2,1)S(1)}, u32[]{:S(2)}, u32[]{:S(2)}) %collective-permute-start.16) | collective-permute-done | bytes 327712 | tf_op jit(solution)/shard_map/ppermute | solution.py:57
  82.6 0.8 add_near.1.own
  83.4 1.1 %collective-permute-done.19.left_1 = bf16[264,640]{1,0:T(8,128)(2,1)S(1)} collective-permute-done((bf16[264,640]{1,0:T(8,128)(2,1)S(1)}, bf16[264,640]{1,0:T(8,128)(2,1)S(1)}, u32[]{:S(2)}, u32[]{:S(2)}) %collective-permute-start.19) | collective-permute-done | bytes 337952 | tf_op jit(solution)/shard_map/ppermute | solution.py:57
  84.4 1.6 %settle.1 = (bf16[512,640]{1,0:T(8,128)(2,1)}, f32[256,128]{1,0:T(8,128)S(1)}) custom-call(s32[3]{0:T(128)S(1)} %copy-done, f32[512,640]{1,0:T(8,128)S(1)} %add_near.1.own, f32[8,512]{1,0:T(8,128)S(1)} %get-tuple-element.118.sums, bf16[264,640]{1,0:T(8,128)(2,1)S(1)} %collective-permute-done.17.near.half, ...), custom_call_target="tpu_custom_call" | custom-call | flops 1000000 | bytes 1000000 | tf_op jit(solution)/shard_map/settle/pallas_call | solution.py:589
  86.0 0.2 collective-permute-done.20.right_0
  86.3 1.4 %norm.1 = bf16[512,640]{1,0:T(8,128)(2,1)} custom-call(s32[3]{0:T(128)S(1)} %copy-done, f32[512,640]{1,0:T(8,128)S(1)} %add_near.1.own, f32[256,128]{1,0:T(8,128)S(1)} %get-tuple-element.122.factor, bf16[264,640]{1,0:T(8,128)(2,1)S(1)} %collective-permute-done.20.right_0, bf16[512,640]{1,0:T(8,128)(2,1)} %get-tuple-element.124.so_far), custom_call_target="tpu_custom_call", output_to_operand_aliasing={{}: (4, {})} | custom-call | flops 1000000 | bytes 1000000 | tf_op jit(solution)/shard_map/norm/pallas_call | solution.py:589
  (17 shorter events, 0.0 us)
Async XLA Ops:
  1.1 12.6 %collective-permute-start = (bf16[256,640]{1,0:T(8,128)(2,1)S(1)}, bf16[256,640]{1,0:T(8,128)(2,1)S(1)}, u32[]{:S(2)}, u32[]{:S(2)}) collective-permute-start(bf16[256,640]{1,0:T(8,128)(2,1)S(1)} %get-tuple-element.67), channel_id=1, source_target_pairs={{0,2},{2,0},{4,6},{6,4},{1,3},{3,1},{5,7},{7,5},{8,10},{10,8},{12,... | collective-permute-start | bytes 983048 | tf_op jit(solution)/shard_map/ppermute | solution.py:57
  2.8 13.7 %collective-permute-start.2 = (bf16[256,640]{1,0:T(8,128)(2,1)S(1)}, bf16[256,640]{1,0:T(8,128)(2,1)S(1)}, u32[]{:S(2)}, u32[]{:S(2)}) collective-permute-start(bf16[256,640]{1,0:T(8,128)(2,1)S(1)} %get-tuple-element.66), channel_id=1, source_target_pairs={{0,6},{2,4},{4,2},{6,0},{1,7},{3,5},{5,3},{7,1},{8,14},{10,12},{12... | collective-permute-start | bytes 983048 | tf_op jit(solution)/shard_map/ppermute | solution.py:57
  5.5 14.0 %collective-permute-start.4 = (bf16[256,640]{1,0:T(8,128)(2,1)S(1)}, bf16[256,640]{1,0:T(8,128)(2,1)S(1)}, u32[]{:S(2)}, u32[]{:S(2)}) collective-permute-start(bf16[256,640]{1,0:T(8,128)(2,1)S(1)} %get-tuple-element.66), channel_id=1, source_target_pairs={{0,2},{2,0},{4,6},{6,4},{1,3},{3,1},{5,7},{7,5},{8,10},{10,8},{12,... | collective-permute-start | bytes 983048 | tf_op jit(solution)/shard_map/ppermute | solution.py:57
  6.1 15.6 %collective-permute-start.5 = (bf16[256,640]{1,0:T(8,128)(2,1)S(1)}, bf16[256,640]{1,0:T(8,128)(2,1)S(1)}, u32[]{:S(2)}, u32[]{:S(2)}) collective-permute-start(bf16[256,640]{1,0:T(8,128)(2,1)S(1)} %get-tuple-element.67), channel_id=1, source_target_pairs={{0,6},{2,4},{4,2},{6,0},{1,7},{3,5},{5,3},{7,1},{8,14},{10,12},{12... | collective-permute-start | bytes 983048 | tf_op jit(solution)/shard_map/ppermute | solution.py:57
  7.4 6.4 %copy-start.3 = (f32[20]{0:T(128)S(1)}, f32[20]{0:T(128)}, u32[]{:S(2)}) copy-start(f32[20]{0:T(128)} %param.18) | copy-start | bytes 244
  7.4 6.4 %copy-start.4 = (f32[20]{0:T(128)S(1)}, f32[20]{0:T(128)}, u32[]{:S(2)}) copy-start(f32[20]{0:T(128)} %param.17) | copy-start | bytes 244
  7.4 9.3 %copy-start = (s32[3]{0:T(128)S(1)}, s32[3]{0:T(128)}, u32[]{:S(2)}) copy-start(s32[3]{0:T(128)} %pad_add_fusion.idx) | copy-start | bytes 40
  13.8 13.4 %collective-permute-start.1 = (bf16[256,640]{1,0:T(8,128)(2,1)S(1)}, bf16[256,640]{1,0:T(8,128)(2,1)S(1)}, u32[]{:S(2)}, u32[]{:S(2)}) collective-permute-start(bf16[256,640]{1,0:T(8,128)(2,1)S(1)} %collective-permute-done.l_0), channel_id=1, source_target_pairs={{0,6},{2,4},{4,2},{6,0},{1,7},{3,5},{5,3},{7,1},{8,14},{10,12},{12... | collective-permute-start | bytes 983048 | tf_op jit(solution)/shard_map/ppermute | solution.py:57
  16.5 10.7 %collective-permute-start.3 = (bf16[256,640]{1,0:T(8,128)(2,1)S(1)}, bf16[256,640]{1,0:T(8,128)(2,1)S(1)}, u32[]{:S(2)}, u32[]{:S(2)}) collective-permute-start(bf16[256,640]{1,0:T(8,128)(2,1)S(1)} %collective-permute-done.2.r_1), channel_id=1, source_target_pairs={{0,2},{2,0},{4,6},{6,4},{1,3},{3,1},{5,7},{7,5},{8,10},{10,8},{12,... | collective-permute-start | bytes 983048 | tf_op jit(solution)/shard_map/ppermute | solution.py:57
  23.6 3.6 %copy-start.1 = (s32[512]{0:T(512)S(1)}, s32[512]{0:T(512)}, u32[]{:S(2)}) copy-start(s32[512]{0:T(512)} %param.12) | copy-start | bytes 6148
  30.9 7.8 %collective-permute-start.6 = (bf16[32,1408]{1,0:T(8,128)(2,1)S(1)}, bf16[32,1408]{1,0:T(8,128)(2,1)S(1)}, u32[]{:S(2)}, u32[]{:S(2)}) collective-permute-start(bf16[32,1408]{1,0:T(8,128)(2,1)S(1)} %get-tuple-element.82), channel_id=1, source_target_pairs={{0,8},{8,0},{16,24},{24,16},{1,9},{9,1},{17,25},{25,17},{2,10},{10... | collective-permute-start | bytes 270344 | tf_op jit(solution)/shard_map/ppermute | solution.py:57
  32.9 7.2 %collective-permute-start.7 = (bf16[32,1408]{1,0:T(8,128)(2,1)S(1)}, bf16[32,1408]{1,0:T(8,128)(2,1)S(1)}, u32[]{:S(2)}, u32[]{:S(2)}) collective-permute-start(bf16[32,1408]{1,0:T(8,128)(2,1)S(1)} %get-tuple-element.83), channel_id=1, source_target_pairs={{0,16},{8,24},{16,0},{24,8},{1,17},{9,25},{17,1},{25,9},{2,18},{10... | collective-permute-start | bytes 270344 | tf_op jit(solution)/shard_map/ppermute | solution.py:57
  36.5 5.7 %collective-permute-start.8 = (bf16[32,1408]{1,0:T(8,128)(2,1)S(1)}, bf16[32,1408]{1,0:T(8,128)(2,1)S(1)}, u32[]{:S(2)}, u32[]{:S(2)}) collective-permute-start(bf16[32,1408]{1,0:T(8,128)(2,1)S(1)} %get-tuple-element.84), channel_id=1, source_target_pairs={{0,24},{8,16},{16,8},{24,0},{1,25},{9,17},{17,9},{25,1},{2,26},{10... | collective-permute-start | bytes 270344 | tf_op jit(solution)/shard_map/ppermute | solution.py:57
  43.0 14.7 %copy-start.2 = (f32[1280]{0:T(1024)S(1)}, f32[1280]{0:T(1024)}, u32[]{:S(2)}) copy-start(f32[1280]{0:T(1024)} %param.20) | copy-start | bytes 15364
  43.0 6.6 %collective-permute-start.10 = (bf16[32,1408]{1,0:T(8,128)(2,1)S(1)}, bf16[32,1408]{1,0:T(8,128)(2,1)S(1)}, u32[]{:S(2)}, u32[]{:S(2)}) collective-permute-start(bf16[32,1408]{1,0:T(8,128)(2,1)S(1)} %row_total.1.t0), channel_id=1, source_target_pairs={{0,64},{32,96},{64,0},{96,32},{1,65},{33,97},{65,1},{97,33},{2,66}... | collective-permute-start | bytes 270344 | tf_op jit(solution)/shard_map/ppermute | solution.py:57
  46.3 5.7 %collective-permute-start.11 = (bf16[32,1408]{1,0:T(8,128)(2,1)S(1)}, bf16[32,1408]{1,0:T(8,128)(2,1)S(1)}, u32[]{:S(2)}, u32[]{:S(2)}) collective-permute-start(bf16[32,1408]{1,0:T(8,128)(2,1)S(1)} %row_total.1.t0), channel_id=1, source_target_pairs={{0,96},{32,64},{64,32},{96,0},{1,97},{33,65},{65,33},{97,1},{2,98}... | collective-permute-start | bytes 270344 | tf_op jit(solution)/shard_map/ppermute | solution.py:57
  47.3 4.7 %collective-permute-start.9 = (bf16[32,1408]{1,0:T(8,128)(2,1)S(1)}, bf16[32,1408]{1,0:T(8,128)(2,1)S(1)}, u32[]{:S(2)}, u32[]{:S(2)}) collective-permute-start(bf16[32,1408]{1,0:T(8,128)(2,1)S(1)} %row_total.1.t0), channel_id=1, source_target_pairs={{0,32},{32,0},{64,96},{96,64},{1,33},{33,1},{65,97},{97,65},{2,34}... | collective-permute-start | bytes 270344 | tf_op jit(solution)/shard_map/ppermute | solution.py:57
  52.9 7.4 %collective-permute-start.12 = (bf16[32,1280]{1,0:T(8,128)(2,1)S(1)}, bf16[32,1280]{1,0:T(8,128)(2,1)S(1)}, u32[]{:S(2)}, u32[]{:S(2)}) collective-permute-start(bf16[32,1280]{1,0:T(8,128)(2,1)S(1)} %get-tuple-element.104), channel_id=1, source_target_pairs={{0,8},{8,0},{16,24},{24,16},{1,9},{9,1},{17,25},{25,17},{2,10},{10... | collective-permute-start | bytes 245768 | tf_op jit(solution)/shard_map/ppermute | solution.py:57
  53.0 7.4 %collective-permute-start.13 = (bf16[32,1280]{1,0:T(8,128)(2,1)S(1)}, bf16[32,1280]{1,0:T(8,128)(2,1)S(1)}, u32[]{:S(2)}, u32[]{:S(2)}) collective-permute-start(bf16[32,1280]{1,0:T(8,128)(2,1)S(1)} %get-tuple-element.105), channel_id=1, source_target_pairs={{0,16},{8,24},{16,0},{24,8},{1,17},{9,25},{17,1},{25,9},{2,18},{10... | collective-permute-start | bytes 245768 | tf_op jit(solution)/shard_map/ppermute | solution.py:57
  54.7 5.7 %collective-permute-start.14 = (bf16[32,1280]{1,0:T(8,128)(2,1)S(1)}, bf16[32,1280]{1,0:T(8,128)(2,1)S(1)}, u32[]{:S(2)}, u32[]{:S(2)}) collective-permute-start(bf16[32,1280]{1,0:T(8,128)(2,1)S(1)} %get-tuple-element.106), channel_id=1, source_target_pairs={{0,24},{8,16},{16,8},{24,0},{1,25},{9,17},{17,9},{25,1},{2,26},{10... | collective-permute-start | bytes 245768 | tf_op jit(solution)/shard_map/ppermute | solution.py:57
  57.7 2.7 %slice-start = ((s8[6553600]{0:T(1024)(128)(4,1)}), s8[4194304]{0:T(1024)(128)(4,1)S(1)}, s32[]{:S(2)}) async-start(s8[6553600]{0:T(1024)(128)(4,1)} %bitcast.11), calls=%async_computation | async-start | bytes 8388608
  57.7 2.9 %slice-start.1 = ((s8[6553600]{0:T(1024)(128)(4,1)}), s8[2359296]{0:T(1024)(128)(4,1)S(1)}, s32[]{:S(2)}) async-start(s8[6553600]{0:T(1024)(128)(4,1)} %bitcast.11), calls=%async_computation.1 | async-start | bytes 4718592
  63.4 10.2 %collective-permute-start.17 = (bf16[264,640]{1,0:T(8,128)(2,1)S(1)}, bf16[264,640]{1,0:T(8,128)(2,1)S(1)}, u32[]{:S(2)}, u32[]{:S(2)}) collective-permute-start(bf16[264,640]{1,0:T(8,128)(2,1)S(1)} %get-tuple-element.119), channel_id=1, source_target_pairs={{0,2},{2,0},{4,6},{6,4},{1,3},{3,1},{5,7},{7,5},{8,10},{10,8},{12,... | collective-permute-start | bytes 1013768 | tf_op jit(solution)/shard_map/ppermute | solution.py:57
  63.5 12.9 %collective-permute-start.18 = (bf16[264,640]{1,0:T(8,128)(2,1)S(1)}, bf16[264,640]{1,0:T(8,128)(2,1)S(1)}, u32[]{:S(2)}, u32[]{:S(2)}) collective-permute-start(bf16[264,640]{1,0:T(8,128)(2,1)S(1)} %get-tuple-element.120), channel_id=1, source_target_pairs={{0,6},{2,4},{4,2},{6,0},{1,7},{3,5},{5,3},{7,1},{8,14},{10,12},{12... | collective-permute-start | bytes 1013768 | tf_op jit(solution)/shard_map/ppermute | solution.py:57
  67.5 11.9 %collective-permute-start.15 = (bf16[256,640]{1,0:T(8,128)(2,1)S(1)}, bf16[256,640]{1,0:T(8,128)(2,1)S(1)}, u32[]{:S(2)}, u32[]{:S(2)}) collective-permute-start(bf16[256,640]{1,0:T(8,128)(2,1)S(1)} %get-tuple-element.116), channel_id=1, source_target_pairs={{0,2},{2,0},{4,6},{6,4},{1,3},{3,1},{5,7},{7,5},{8,10},{10,8},{12,... | collective-permute-start | bytes 983048 | tf_op jit(solution)/shard_map/ppermute | solution.py:57
  70.7 11.9 %collective-permute-start.16 = (bf16[256,640]{1,0:T(8,128)(2,1)S(1)}, bf16[256,640]{1,0:T(8,128)(2,1)S(1)}, u32[]{:S(2)}, u32[]{:S(2)}) collective-permute-start(bf16[256,640]{1,0:T(8,128)(2,1)S(1)} %get-tuple-element.117), channel_id=1, source_target_pairs={{0,6},{2,4},{4,2},{6,0},{1,7},{3,5},{5,3},{7,1},{8,14},{10,12},{12... | collective-permute-start | bytes 983048 | tf_op jit(solution)/shard_map/ppermute | solution.py:57
  74.3 12.0 %collective-permute-start.20 = (bf16[264,640]{1,0:T(8,128)(2,1)S(1)}, bf16[264,640]{1,0:T(8,128)(2,1)S(1)}, u32[]{:S(2)}, u32[]{:S(2)}) collective-permute-start(bf16[264,640]{1,0:T(8,128)(2,1)S(1)} %join.3), channel_id=1, source_target_pairs={{0,6},{2,4},{4,2},{6,0},{1,7},{3,5},{5,3},{7,1},{8,14},{10,12},{12... | collective-permute-start | bytes 1013768 | tf_op jit(solution)/shard_map/ppermute | solution.py:57
  77.1 7.4 %collective-permute-start.19 = (bf16[264,640]{1,0:T(8,128)(2,1)S(1)}, bf16[264,640]{1,0:T(8,128)(2,1)S(1)}, u32[]{:S(2)}, u32[]{:S(2)}) collective-permute-start(bf16[264,640]{1,0:T(8,128)(2,1)S(1)} %join.2), channel_id=1, source_target_pairs={{0,2},{2,0},{4,6},{6,4},{1,3},{3,1},{5,7},{7,5},{8,10},{10,8},{12,... | collective-permute-start | bytes 1013768 | tf_op jit(solution)/shard_map/ppermute | solution.py:57

commit v7 on v6

--- a/solution.py
+++ b/solution.py
@@ -569,7 +569,7 @@
     )[0]
 
 
-def settle_body(idx, own, sums, near, other, left_1, out, factor, made, sem):
+def settle_body(idx, own, sums, near, other, left_1, out, factor, made, sems):
     squares = sums[0:1, :] + squares_of(left_1)
     squares = squares + (squares_of(near) + squares_of(other))
     stack = terms(squares, 16, ROWS).astype(BF16)
@@ -579,7 +579,7 @@
         lanes = span(k, LANES)
         value = own[GROUP:, lanes] + left_1[:GROUP, lanes].astype(F32)
         made[:, lanes] = (value * scale[GROUP:]).astype(BF16)
-    copy = pltpu.make_async_copy(made, out.at[GROUP:, :], sem)
+    copy = pltpu.make_async_copy(made, out.at[GROUP:, :], sems.at[0])
     copy.start()
     copy.wait()
 
@@ -591,7 +591,7 @@
         in_specs=[SMEM, *[VMEM] * len(args), *[HBM] * len(more)],
         out_specs=specs,
         out_shape=outs,
-        scratch_shapes=[pltpu.VMEM((GROUP, FEAT), BF16), pltpu.SemaphoreType.DMA],
+        scratch_shapes=[pltpu.VMEM((GROUP, FEAT), BF16), pltpu.SemaphoreType.DMA((2,))],
         input_output_aliases={1 + len(args): 0} if more else {},
         compiler_params=pltpu.CompilerParams(vmem_limit_bytes=8 * MIB),
         cost_estimate=cost(1e6, 1e6),
@@ -604,14 +604,18 @@
     return end_call(settle_body, "settle", idx, args, outs, [HBM, VMEM])
 
 
-def norm_body(idx, own, factor, right_0, so_far, out, made, sem):
-    for k in range(FEAT // LANES):
-        lanes = span(k, LANES)
-        value = own[:GROUP, lanes] + right_0[:GROUP, lanes].astype(F32)
-        made[:, lanes] = (value * factor[...]).astype(BF16)
-    copy = pltpu.make_async_copy(made, out.at[:GROUP, :], sem)
-    copy.start()
-    copy.wait()
+def norm_body(idx, own, factor, right_0, so_far, out, made, sems):
+    copies = []
+    for part in range(2):
+        rows = span(part, GROUP // 2)
+        for k in range(FEAT // LANES):
+            lanes = span(k, LANES)
+            value = own[rows, lanes] + right_0[rows, lanes].astype(F32)
+            made[rows, lanes] = (value * factor[rows, :]).astype(BF16)
+        copies.append(pltpu.make_async_copy(made.at[rows, :], out.at[rows, :], sems.at[part]))
+        copies[-1].start()
+    for copy in copies:
+        copy.wait()
 
 
 def norm(idx, own, factor, right_0, so_far):

time: 88 us -> 87.9 us (level)
  no operation moved by 1% of the time
where the time goes in v7:
time: 87.9 us; the launch traced here: 87.8 us
  Pallas kernels  39.6 us (45%)
  starting transfers between devices  29.6 us (34%)
  waiting for transfers between devices  15.4 us (18%)
  local copies, waits for them, and re-layouts  2.07 us (2%)
    pallas_call x16, Pallas kernels, call(): pl.pallas_call(body, in_specs=[SMEM, *[VMEM] * len(args)], out_specs=[VME...  30.3 us
    ppermute x21, starting transfers between devices, swapped(): return lax.ppermute(array, axis, [(i, i ^ bits) for i in range(4)])  29.6 us
    ppermute x21, waiting for transfers between devices, swapped(): return lax.ppermute(array, axis, [(i, i ^ bits) for i in range(4)])  15.4 us
    pallas_call x1, Pallas kernels, load_weights(): pl.pallas_call(load_body, in_specs=[SMEM, *[HBM] * 5], out_specs=[VMEM] *...  6.34 us
    pallas_call x2, Pallas kernels, end_call(): pl.pallas_call(body, in_specs=[SMEM, *[VMEM] * len(args), *[HBM] * len(mo...  2.92 us
  transfers between devices with their start and end apart: 21, of which 10 were waited for; matrix products, arithmetic and copies ran while one was open for 1% of the time, Pallas kernels for 34%

profile of v7, /device:TPU:0, one launch (start us, length us, event | category | flops | bytes accessed | tf_op | source)
XLA Modules:
  0.0 87.8 jit_solution(14506053626611823570)
XLA Ops:
  0.0 1.1 %fusion = (bf16[256,640]{1,0:T(8,128)(2,1)S(1)}, bf16[256,640]{1,0:T(8,128)(2,1)S(1)}) fusion(bf16[512,640]{1,0:T(8,128)(2,1)} %tok.1), kind=kLoop, calls=%fused_computation.4 | loop fusion | bytes 1310720 | tf_op jit(solution)/shard_map/slice | solution.py:630
  1.1 1.7 %collective-permute-start = (bf16[256,640]{1,0:T(8,128)(2,1)S(1)}, bf16[256,640]{1,0:T(8,128)(2,1)S(1)}, u32[]{:S(2)}, u32[]{:S(2)}) collective-permute-start(bf16[256,640]{1,0:T(8,128)(2,1)S(1)} %get-tuple-element.67), channel_id=1, source_target_pairs={{0,2},{2,0},{4,6},{6,4},{1,3},{3,1},{5,7},{7,5},{8,10},{10,8},{12,... | collective-permute-start | bytes 983048 | tf_op jit(solution)/shard_map/ppermute | solution.py:57
  2.8 2.1 %collective-permute-start.2 = (bf16[256,640]{1,0:T(8,128)(2,1)S(1)}, bf16[256,640]{1,0:T(8,128)(2,1)S(1)}, u32[]{:S(2)}, u32[]{:S(2)}) collective-permute-start(bf16[256,640]{1,0:T(8,128)(2,1)S(1)} %get-tuple-element.66), channel_id=1, source_target_pairs={{0,6},{2,4},{4,2},{6,0},{1,7},{3,5},{5,3},{7,1},{8,14},{10,12},{12... | collective-permute-start | bytes 983048 | tf_op jit(solution)/shard_map/ppermute | solution.py:57
  4.9 0.6 pad_add_fusion.idx
  5.5 0.6 collective-permute-start.4
  6.1 0.6 collective-permute-start.5
  6.7 0.7 pad_bitcast_fusion.skip
  7.4 6.3 %load_weights.1 = (f32[512,1280]{1,0:T(8,128)S(1)}, f32[512,384]{1,0:T(8,128)S(1)}, bf16[512,640]{1,0:T(8,128)(2,1)S(1)}, bf16[128,2560]{1,0:T(8,128)(2,1)S(1)},...) custom-call(s32[3]{0:T(128)} %pad_add_fusion.idx, ...), custom_call_target="tpu_custom_call" | custom-call | flops 1090519040 | bytes 15000000 | tf_op jit(solution)/shard_map/load_weights/pallas_call | solution.py:128
  13.8 0.0 collective-permute-done.l_0
  13.8 2.7 %collective-permute-start.1 = (bf16[256,640]{1,0:T(8,128)(2,1)S(1)}, bf16[256,640]{1,0:T(8,128)(2,1)S(1)}, u32[]{:S(2)}, u32[]{:S(2)}) collective-permute-start(bf16[256,640]{1,0:T(8,128)(2,1)S(1)} %collective-permute-done.l_0), channel_id=1, source_target_pairs={{0,6},{2,4},{4,2},{6,0},{1,7},{3,5},{5,3},{7,1},{8,14},{10,12},{12... | collective-permute-start | bytes 983048 | tf_op jit(solution)/shard_map/ppermute | solution.py:57
  16.5 0.0 collective-permute-done.2.r_1
  16.5 0.2 collective-permute-start.3
  16.7 2.8 %gate_first.1.acc_z = f32[512,1280]{1,0:T(8,128)S(1)} custom-call(s32[3]{0:T(128)S(1)} %copy-done, bf16[512,640]{1,0:T(8,128)(2,1)S(1)} %get-tuple-element.69.tok, bf16[256,640]{1,0:T(8,128)(2,1)S(1)} %collective-permute-done.l_0, bf16[256,640]{1,0:T(8,128)(2,1)S(1)} %collective-permute-done.2.r_1, bf16[2560,1280]{1,0:T(8,128)(2,1)S(1)} %get-tuple-element.113.w_z), custom_call_target="tpu_custom_call" | custom-call | flops 1677721600 | bytes 1000000 | tf_op jit(solution)/shard_map/gate_first/pallas_call | solution.py:72
  19.5 0.0 collective-permute-done.4.l_1
  19.5 2.2 %collective-permute-done.5.r_0 = bf16[256,640]{1,0:T(8,128)(2,1)S(1)} collective-permute-done((bf16[256,640]{1,0:T(8,128)(2,1)S(1)}, bf16[256,640]{1,0:T(8,128)(2,1)S(1)}, u32[]{:S(2)}, u32[]{:S(2)}) %collective-permute-start.5) | collective-permute-done | bytes 327712 | tf_op jit(solution)/shard_map/ppermute | solution.py:57
  21.7 1.9 %gate_second.1.acc_z = f32[512,1280]{1,0:T(8,128)S(1)} custom-call(s32[3]{0:T(128)S(1)} %copy-done, bf16[256,640]{1,0:T(8,128)(2,1)S(1)} %collective-permute-done.4.l_1, bf16[256,640]{1,0:T(8,128)(2,1)S(1)} %collective-permute-done.5.r_0, bf16[2560,1280]{1,0:T(8,128)(2,1)S(1)} %get-tuple-element.113.w_z, ...), custom_call_target="tpu_custom_call", output_to_operand_aliasing={{}: (4, {})} | custom-call | flops 838860800 | bytes 1000000 | tf_op jit(solution)/shard_map/gate_second/pallas_call | solution.py:72
  23.6 0.0 copy-start.1
  23.6 3.3 %project.1 = (f32[512,1280]{1,0:T(8,128)S(1)}, f32[512,384]{1,0:T(8,128)S(1)}) custom-call(s32[3]{0:T(128)S(1)} %copy-done, bf16[256,640]{1,0:T(8,128)(2,1)S(1)} %collective-permute-done.l_0, bf16[256,640]{1,0:T(8,128)(2,1)S(1)} %collective-permute-done.4.l_1, ...), custom_call_target="tpu_custom_call", output_to_operand_aliasing={{0}: (8, {}), {1}: (9, {})} | custom-call | flops 2181038080 | bytes 1000000 | tf_op jit(solution)/shard_map/project/pallas_call | solution.py:72
  26.9 0.3 collective-permute-done.1.tok_0.t_0
  27.2 0.0 collective-permute-done.3.tok_1.t_1
  27.2 3.6 %device_state.1 = (bf16[512,1280]{1,0:T(8,128)(2,1)S(1)}, bf16[512,128]{1,0:T(8,128)(2,1)S(1)}, bf16[512,128]{1,0:T(8,128)(2,1)S(1)}, f32[512,128]{1,0:T(8,128)S...) custom-call(s32[3]{0:T(128)S(1)} %copy-done, ...), custom_call_target="tpu_custom_call" | custom-call | flops 1090519040 | bytes 1000000 | tf_op jit(solution)/shard_map/device_state/pallas_call | solution.py:72
  30.9 2.0 %collective-permute-start.6 = (bf16[32,1408]{1,0:T(8,128)(2,1)S(1)}, bf16[32,1408]{1,0:T(8,128)(2,1)S(1)}, u32[]{:S(2)}, u32[]{:S(2)}) collective-permute-start(bf16[32,1408]{1,0:T(8,128)(2,1)S(1)} %get-tuple-element.82), channel_id=1, source_target_pairs={{0,8},{8,0},{16,24},{24,16},{1,9},{9,1},{17,25},{25,17},{2,10},{10... | collective-permute-start | bytes 270344 | tf_op jit(solution)/shard_map/ppermute | solution.py:57
  32.9 3.6 %collective-permute-start.7 = (bf16[32,1408]{1,0:T(8,128)(2,1)S(1)}, bf16[32,1408]{1,0:T(8,128)(2,1)S(1)}, u32[]{:S(2)}, u32[]{:S(2)}) collective-permute-start(bf16[32,1408]{1,0:T(8,128)(2,1)S(1)} %get-tuple-element.83), channel_id=1, source_target_pairs={{0,16},{8,24},{16,0},{24,8},{1,17},{9,25},{17,1},{25,9},{2,18},{10... | collective-permute-start | bytes 270344 | tf_op jit(solution)/shard_map/ppermute | solution.py:57
  36.5 0.0 collective-permute-start.8
  36.5 2.2 %mix.2 = (f32[256,1280]{1,0:T(8,128)S(1)}, f32[256,1280]{1,0:T(8,128)S(1)}) custom-call(s32[3]{0:T(128)S(1)} %copy-done, bf16[512,1280]{1,0:T(8,128)(2,1)S(1)} %get-tuple-element.85.inner_r, bf16[512,128]{1,0:T(8,128)(2,1)S(1)} %get-tuple-element.86.b_r, bf16[512,128]{1,0:T(8,128)(2,1)S(1)} %get-tuple-element.87.c_r, ...), custom_call_target="tpu_custom_call" | custom-call | flops 2000000000 | bytes 1000000 | tf_op jit(solution)/shard_map/mix/pallas_call | solution.py:72
  38.7 1.3 %collective-permute-done.7.m2 = bf16[32,1408]{1,0:T(8,128)(2,1)S(1)} collective-permute-done((bf16[32,1408]{1,0:T(8,128)(2,1)S(1)}, bf16[32,1408]{1,0:T(8,128)(2,1)S(1)}, u32[]{:S(2)}, u32[]{:S(2)}) %collective-permute-start.7) | collective-permute-done | bytes 90144 | tf_op jit(solution)/shard_map/ppermute | solution.py:57
  40.0 2.2 %collective-permute-done.8.m3 = bf16[32,1408]{1,0:T(8,128)(2,1)S(1)} collective-permute-done((bf16[32,1408]{1,0:T(8,128)(2,1)S(1)}, bf16[32,1408]{1,0:T(8,128)(2,1)S(1)}, u32[]{:S(2)}, u32[]{:S(2)}) %collective-permute-start.8) | collective-permute-done | bytes 90144 | tf_op jit(solution)/shard_map/ppermute | solution.py:57
  42.2 0.8 row_total.1.t0
  43.0 0.0 copy-start.2
  43.0 3.3 %collective-permute-start.10 = (bf16[32,1408]{1,0:T(8,128)(2,1)S(1)}, bf16[32,1408]{1,0:T(8,128)(2,1)S(1)}, u32[]{:S(2)}, u32[]{:S(2)}) collective-permute-start(bf16[32,1408]{1,0:T(8,128)(2,1)S(1)} %row_total.1.t0), channel_id=1, source_target_pairs={{0,64},{32,96},{64,0},{96,32},{1,65},{33,97},{65,1},{97,33},{2,66}... | collective-permute-start | bytes 270344 | tf_op jit(solution)/shard_map/ppermute | solution.py:57
  46.3 1.1 %collective-permute-start.11 = (bf16[32,1408]{1,0:T(8,128)(2,1)S(1)}, bf16[32,1408]{1,0:T(8,128)(2,1)S(1)}, u32[]{:S(2)}, u32[]{:S(2)}) collective-permute-start(bf16[32,1408]{1,0:T(8,128)(2,1)S(1)} %row_total.1.t0), channel_id=1, source_target_pairs={{0,96},{32,64},{64,32},{96,0},{1,97},{33,65},{65,33},{97,1},{2,98}... | collective-permute-start | bytes 270344 | tf_op jit(solution)/shard_map/ppermute | solution.py:57
  47.3 2.2 %mix.3 = (f32[256,1280]{1,0:T(8,128)S(1)}, f32[256,1280]{1,0:T(8,128)S(1)}) custom-call(s32[3]{0:T(128)S(1)} %copy-done, bf16[512,1280]{1,0:T(8,128)(2,1)S(1)} %get-tuple-element.85.inner_r, bf16[512,128]{1,0:T(8,128)(2,1)S(1)} %get-tuple-element.86.b_r, bf16[512,128]{1,0:T(8,128)(2,1)S(1)} %get-tuple-element.87.c_r, ...), custom_call_target="tpu_custom_call" | custom-call | flops 2000000000 | bytes 1000000 | tf_op jit(solution)/shard_map/mix/pallas_call | solution.py:72
  49.5 0.0 collective-permute-done.10.t2
  49.6 2.5 %collective-permute-done.11.t3 = bf16[32,1408]{1,0:T(8,128)(2,1)S(1)} collective-permute-done((bf16[32,1408]{1,0:T(8,128)(2,1)S(1)}, bf16[32,1408]{1,0:T(8,128)(2,1)S(1)}, u32[]{:S(2)}, u32[]{:S(2)}) %collective-permute-start.11) | collective-permute-done | bytes 90144 | tf_op jit(solution)/shard_map/ppermute | solution.py:57
  52.0 0.0 collective-permute-done.9.t1
  52.0 0.9 %prefixes.1 = (bf16[32,1280]{1,0:T(8,128)(2,1)S(1)}, bf16[32,1280]{1,0:T(8,128)(2,1)S(1)}, bf16[32,1280]{1,0:T(8,128)(2,1)S(1)}, bf16[32,1280]{1,0:T(8,128)(2,1)S(1)}) custom-call(s32[3]{0:T(128)S(1)} %copy-done, bf16[32,1408]{1,0:T(8,128)(2,1)S(1)} %get-tuple-element.92.m0, bf16[32,1408]{1,0:T(8,128)(2,1)S(1)} %collective-permute-done.6.m1, ...), custom_call_target="tpu_custom_call" | custom-call | flops 100000000 | bytes 1000000 | tf_op jit(solution)/shard_map/prefixes/pallas_call | solution.py:72
  52.9 0.1 collective-permute-start.12
  53.0 1.6 %collective-permute-start.13 = (bf16[32,1280]{1,0:T(8,128)(2,1)S(1)}, bf16[32,1280]{1,0:T(8,128)(2,1)S(1)}, u32[]{:S(2)}, u32[]{:S(2)}) collective-permute-start(bf16[32,1280]{1,0:T(8,128)(2,1)S(1)} %get-tuple-element.105), channel_id=1, source_target_pairs={{0,16},{8,24},{16,0},{24,8},{1,17},{9,25},{17,1},{25,9},{2,18},{10... | collective-permute-start | bytes 245768 | tf_op jit(solution)/shard_map/ppermute | solution.py:57
  54.7 3.0 %collective-permute-start.14 = (bf16[32,1280]{1,0:T(8,128)(2,1)S(1)}, bf16[32,1280]{1,0:T(8,128)(2,1)S(1)}, u32[]{:S(2)}, u32[]{:S(2)}) collective-permute-start(bf16[32,1280]{1,0:T(8,128)(2,1)S(1)} %get-tuple-element.106), channel_id=1, source_target_pairs={{0,24},{8,16},{16,8},{24,0},{1,25},{9,17},{17,9},{25,1},{2,26},{10... | collective-permute-start | bytes 245768 | tf_op jit(solution)/shard_map/ppermute | solution.py:57
  57.7 0.0 slice-start.1
  57.7 2.6 %gate.1.zs_r = f32[512,1280]{1,0:T(8,128)S(1)} custom-call(s32[3]{0:T(128)S(1)} %copy-done, bf16[256,640]{1,0:T(8,128)(2,1)S(1)} %collective-permute-done.1.tok_0.t_0, bf16[256,640]{1,0:T(8,128)(2,1)S(1)} %collective-permute-done.3.tok_1.t_1, bf16[2560,1280]{1,0:T(8,128)(2,1)S(1)} %get-tuple-element.113.w_z, ...), custom_call_target="tpu_custom_call", output_to_operand_aliasing={{}: (4, {})} | custom-call | flops 838860800 | bytes 1000000 | tf_op jit(solution)/shard_map/gate/pallas_call | solution.py:72
  60.4 0.0 collective-permute-done.12.h1
  60.4 0.0 collective-permute-done.14.h3
  60.4 0.2 slice-done.1
  60.7 2.8 %gated_rows.1 = (bf16[512,1280]{1,0:T(8,128)(2,1)S(1)}, f32[8,512]{1,0:T(8,128)S(1)}, bf16[264,640]{1,0:T(8,128)(2,1)S(1)}, bf16[264,640]{1,0:T(8,128)(2,1)S(1)}) custom-call(s32[3]{0:T(128)S(1)} %copy-done, bf16[32,1280]{1,0:T(8,128)(2,1)S(1)} %get-tuple-element.103.h0, bf16[32,1280]{1,0:T(8,128)(2,1)S(1)} %collective-permute-done.12.h1, ...), custom_call_target="tpu_custom_call" | custom-call | flops 1090519040 | bytes 1000000 | tf_op jit(solution)/shard_map/gated_rows/pallas_call | solution.py:72
  63.4 0.1 collective-permute-start.17
  63.5 2.2 %collective-permute-start.18 = (bf16[264,640]{1,0:T(8,128)(2,1)S(1)}, bf16[264,640]{1,0:T(8,128)(2,1)S(1)}, u32[]{:S(2)}, u32[]{:S(2)}) collective-permute-start(bf16[264,640]{1,0:T(8,128)(2,1)S(1)} %get-tuple-element.120), channel_id=1, source_target_pairs={{0,6},{2,4},{4,2},{6,0},{1,7},{3,5},{5,3},{7,1},{8,14},{10,12},{12... | collective-permute-start | bytes 1013768 | tf_op jit(solution)/shard_map/ppermute | solution.py:57
  65.8 1.7 %near_block.2 = (bf16[256,640]{1,0:T(8,128)(2,1)S(1)}, f32[256,640]{1,0:T(8,128)S(1)}) custom-call(s32[3]{0:T(128)S(1)} %copy-done, bf16[512,1280]{1,0:T(8,128)(2,1)S(1)} %get-tuple-element.115.rows, bf16[1280,2560]{1,0:T(8,128)(2,1)S(1)} %bitcast.12), custom_call_target="tpu_custom_call" | custom-call | flops 1000000 | bytes 1000000 | tf_op jit(solution)/shard_map/near_block/pallas_call | solution.py:72
  67.5 1.4 %collective-permute-start.15 = (bf16[256,640]{1,0:T(8,128)(2,1)S(1)}, bf16[256,640]{1,0:T(8,128)(2,1)S(1)}, u32[]{:S(2)}, u32[]{:S(2)}) collective-permute-start(bf16[256,640]{1,0:T(8,128)(2,1)S(1)} %get-tuple-element.116), channel_id=1, source_target_pairs={{0,2},{2,0},{4,6},{6,4},{1,3},{3,1},{5,7},{7,5},{8,10},{10,8},{12,... | collective-permute-start | bytes 983048 | tf_op jit(solution)/shard_map/ppermute | solution.py:57
  68.9 1.7 %near_block.3 = (bf16[256,640]{1,0:T(8,128)(2,1)S(1)}, f32[256,640]{1,0:T(8,128)S(1)}) custom-call(s32[3]{0:T(128)S(1)} %copy-done, bf16[512,1280]{1,0:T(8,128)(2,1)S(1)} %get-tuple-element.115.rows, bf16[1280,2560]{1,0:T(8,128)(2,1)S(1)} %bitcast.12), custom_call_target="tpu_custom_call" | custom-call | flops 1000000 | bytes 1000000 | tf_op jit(solution)/shard_map/near_block/pallas_call | solution.py:72
  70.7 1.2 %collective-permute-start.16 = (bf16[256,640]{1,0:T(8,128)(2,1)S(1)}, bf16[256,640]{1,0:T(8,128)(2,1)S(1)}, u32[]{:S(2)}, u32[]{:S(2)}) collective-permute-start(bf16[256,640]{1,0:T(8,128)(2,1)S(1)} %get-tuple-element.117), channel_id=1, source_target_pairs={{0,6},{2,4},{4,2},{6,0},{1,7},{3,5},{5,3},{7,1},{8,14},{10,12},{12... | collective-permute-start | bytes 983048 | tf_op jit(solution)/shard_map/ppermute | solution.py:57
  71.8 1.7 %own_block.1.own = f32[512,640]{1,0:T(8,128)S(1)} custom-call(s32[3]{0:T(128)S(1)} %copy-done, bf16[512,1280]{1,0:T(8,128)(2,1)S(1)} %get-tuple-element.115.rows, bf16[1280,2560]{1,0:T(8,128)(2,1)S(1)} %bitcast.12), custom_call_target="tpu_custom_call" | custom-call | flops 1000000 | bytes 1000000 | tf_op jit(solution)/shard_map/own_block/pallas_call | solution.py:72
  73.5 0.2 collective-permute-done.17.near.half
  73.7 0.6 join.3
  74.3 2.1 %collective-permute-start.20 = (bf16[264,640]{1,0:T(8,128)(2,1)S(1)}, bf16[264,640]{1,0:T(8,128)(2,1)S(1)}, u32[]{:S(2)}, u32[]{:S(2)}) collective-permute-start(bf16[264,640]{1,0:T(8,128)(2,1)S(1)} %join.3), channel_id=1, source_target_pairs={{0,6},{2,4},{4,2},{6,0},{1,7},{3,5},{5,3},{7,1},{8,14},{10,12},{12... | collective-permute-start | bytes 1013768 | tf_op jit(solution)/shard_map/ppermute | solution.py:57
  76.4 0.6 join.2
  77.1 0.1 collective-permute-start.19
  77.1 2.2 %collective-permute-done.15.left_0 = bf16[256,640]{1,0:T(8,128)(2,1)S(1)} collective-permute-done((bf16[256,640]{1,0:T(8,128)(2,1)S(1)}, bf16[256,640]{1,0:T(8,128)(2,1)S(1)}, u32[]{:S(2)}, u32[]{:S(2)}) %collective-permute-start.15) | collective-permute-done | bytes 327712 | tf_op jit(solution)/shard_map/ppermute | solution.py:57
  79.4 3.2 %collective-permute-done.16.right_1 = bf16[256,640]{1,0:T(8,128)(2,1)S(1)} collective-permute-done((bf16[256,640]{1,0:T(8,128)(2,1)S(1)}, bf16[256,640]{1,0:T(8,128)(2,1)S(1)}, u32[]{:S(2)}, u32[]{:S(2)}) %collective-permute-start.16) | collective-permute-done | bytes 327712 | tf_op jit(solution)/shard_map/ppermute | solution.py:57
  82.6 0.8 add_near.1.own
  83.4 1.1 %collective-permute-done.19.left_1 = bf16[264,640]{1,0:T(8,128)(2,1)S(1)} collective-permute-done((bf16[264,640]{1,0:T(8,128)(2,1)S(1)}, bf16[264,640]{1,0:T(8,128)(2,1)S(1)}, u32[]{:S(2)}, u32[]{:S(2)}) %collective-permute-start.19) | collective-permute-done | bytes 337952 | tf_op jit(solution)/shard_map/ppermute | solution.py:57
  84.4 1.6 %settle.1 = (bf16[512,640]{1,0:T(8,128)(2,1)}, f32[256,128]{1,0:T(8,128)S(1)}) custom-call(s32[3]{0:T(128)S(1)} %copy-done, f32[512,640]{1,0:T(8,128)S(1)} %add_near.1.own, f32[8,512]{1,0:T(8,128)S(1)} %get-tuple-element.118.sums, bf16[264,640]{1,0:T(8,128)(2,1)S(1)} %collective-permute-done.17.near.half, ...), custom_call_target="tpu_custom_call" | custom-call | flops 1000000 | bytes 1000000 | tf_op jit(solution)/shard_map/settle/pallas_call | solution.py:589
  86.0 0.2 collective-permute-done.20.right_0
  86.3 1.3 %norm.1 = bf16[512,640]{1,0:T(8,128)(2,1)} custom-call(s32[3]{0:T(128)S(1)} %copy-done, f32[512,640]{1,0:T(8,128)S(1)} %add_near.1.own, f32[256,128]{1,0:T(8,128)S(1)} %get-tuple-element.122.factor, bf16[264,640]{1,0:T(8,128)(2,1)S(1)} %collective-permute-done.20.right_0, bf16[512,640]{1,0:T(8,128)(2,1)} %get-tuple-element.124.so_far), custom_call_target="tpu_custom_call", output_to_operand_aliasing={{}: (4, {})} | custom-call | flops 1000000 | bytes 1000000 | tf_op jit(solution)/shard_map/norm/pallas_call | solution.py:589
  (17 shorter events, 0.0 us)
Async XLA Ops:
  1.1 12.6 %collective-permute-start = (bf16[256,640]{1,0:T(8,128)(2,1)S(1)}, bf16[256,640]{1,0:T(8,128)(2,1)S(1)}, u32[]{:S(2)}, u32[]{:S(2)}) collective-permute-start(bf16[256,640]{1,0:T(8,128)(2,1)S(1)} %get-tuple-element.67), channel_id=1, source_target_pairs={{0,2},{2,0},{4,6},{6,4},{1,3},{3,1},{5,7},{7,5},{8,10},{10,8},{12,... | collective-permute-start | bytes 983048 | tf_op jit(solution)/shard_map/ppermute | solution.py:57
  2.8 13.7 %collective-permute-start.2 = (bf16[256,640]{1,0:T(8,128)(2,1)S(1)}, bf16[256,640]{1,0:T(8,128)(2,1)S(1)}, u32[]{:S(2)}, u32[]{:S(2)}) collective-permute-start(bf16[256,640]{1,0:T(8,128)(2,1)S(1)} %get-tuple-element.66), channel_id=1, source_target_pairs={{0,6},{2,4},{4,2},{6,0},{1,7},{3,5},{5,3},{7,1},{8,14},{10,12},{12... | collective-permute-start | bytes 983048 | tf_op jit(solution)/shard_map/ppermute | solution.py:57
  5.5 14.0 %collective-permute-start.4 = (bf16[256,640]{1,0:T(8,128)(2,1)S(1)}, bf16[256,640]{1,0:T(8,128)(2,1)S(1)}, u32[]{:S(2)}, u32[]{:S(2)}) collective-permute-start(bf16[256,640]{1,0:T(8,128)(2,1)S(1)} %get-tuple-element.66), channel_id=1, source_target_pairs={{0,2},{2,0},{4,6},{6,4},{1,3},{3,1},{5,7},{7,5},{8,10},{10,8},{12,... | collective-permute-start | bytes 983048 | tf_op jit(solution)/shard_map/ppermute | solution.py:57
  6.1 15.6 %collective-permute-start.5 = (bf16[256,640]{1,0:T(8,128)(2,1)S(1)}, bf16[256,640]{1,0:T(8,128)(2,1)S(1)}, u32[]{:S(2)}, u32[]{:S(2)}) collective-permute-start(bf16[256,640]{1,0:T(8,128)(2,1)S(1)} %get-tuple-element.67), channel_id=1, source_target_pairs={{0,6},{2,4},{4,2},{6,0},{1,7},{3,5},{5,3},{7,1},{8,14},{10,12},{12... | collective-permute-start | bytes 983048 | tf_op jit(solution)/shard_map/ppermute | solution.py:57
  7.4 6.4 %copy-start.3 = (f32[20]{0:T(128)S(1)}, f32[20]{0:T(128)}, u32[]{:S(2)}) copy-start(f32[20]{0:T(128)} %param.18) | copy-start | bytes 244
  7.4 6.4 %copy-start.4 = (f32[20]{0:T(128)S(1)}, f32[20]{0:T(128)}, u32[]{:S(2)}) copy-start(f32[20]{0:T(128)} %param.17) | copy-start | bytes 244
  7.4 9.3 %copy-start = (s32[3]{0:T(128)S(1)}, s32[3]{0:T(128)}, u32[]{:S(2)}) copy-start(s32[3]{0:T(128)} %pad_add_fusion.idx) | copy-start | bytes 40
  13.8 13.4 %collective-permute-start.1 = (bf16[256,640]{1,0:T(8,128)(2,1)S(1)}, bf16[256,640]{1,0:T(8,128)(2,1)S(1)}, u32[]{:S(2)}, u32[]{:S(2)}) collective-permute-start(bf16[256,640]{1,0:T(8,128)(2,1)S(1)} %collective-permute-done.l_0), channel_id=1, source_target_pairs={{0,6},{2,4},{4,2},{6,0},{1,7},{3,5},{5,3},{7,1},{8,14},{10,12},{12... | collective-permute-start | bytes 983048 | tf_op jit(solution)/shard_map/ppermute | solution.py:57
  16.5 10.7 %collective-permute-start.3 = (bf16[256,640]{1,0:T(8,128)(2,1)S(1)}, bf16[256,640]{1,0:T(8,128)(2,1)S(1)}, u32[]{:S(2)}, u32[]{:S(2)}) collective-permute-start(bf16[256,640]{1,0:T(8,128)(2,1)S(1)} %collective-permute-done.2.r_1), channel_id=1, source_target_pairs={{0,2},{2,0},{4,6},{6,4},{1,3},{3,1},{5,7},{7,5},{8,10},{10,8},{12,... | collective-permute-start | bytes 983048 | tf_op jit(solution)/shard_map/ppermute | solution.py:57
  23.6 3.6 %copy-start.1 = (s32[512]{0:T(512)S(1)}, s32[512]{0:T(512)}, u32[]{:S(2)}) copy-start(s32[512]{0:T(512)} %param.12) | copy-start | bytes 6148
  30.9 7.8 %collective-permute-start.6 = (bf16[32,1408]{1,0:T(8,128)(2,1)S(1)}, bf16[32,1408]{1,0:T(8,128)(2,1)S(1)}, u32[]{:S(2)}, u32[]{:S(2)}) collective-permute-start(bf16[32,1408]{1,0:T(8,128)(2,1)S(1)} %get-tuple-element.82), channel_id=1, source_target_pairs={{0,8},{8,0},{16,24},{24,16},{1,9},{9,1},{17,25},{25,17},{2,10},{10... | collective-permute-start | bytes 270344 | tf_op jit(solution)/shard_map/ppermute | solution.py:57
  32.9 7.2 %collective-permute-start.7 = (bf16[32,1408]{1,0:T(8,128)(2,1)S(1)}, bf16[32,1408]{1,0:T(8,128)(2,1)S(1)}, u32[]{:S(2)}, u32[]{:S(2)}) collective-permute-start(bf16[32,1408]{1,0:T(8,128)(2,1)S(1)} %get-tuple-element.83), channel_id=1, source_target_pairs={{0,16},{8,24},{16,0},{24,8},{1,17},{9,25},{17,1},{25,9},{2,18},{10... | collective-permute-start | bytes 270344 | tf_op jit(solution)/shard_map/ppermute | solution.py:57
  36.5 5.7 %collective-permute-start.8 = (bf16[32,1408]{1,0:T(8,128)(2,1)S(1)}, bf16[32,1408]{1,0:T(8,128)(2,1)S(1)}, u32[]{:S(2)}, u32[]{:S(2)}) collective-permute-start(bf16[32,1408]{1,0:T(8,128)(2,1)S(1)} %get-tuple-element.84), channel_id=1, source_target_pairs={{0,24},{8,16},{16,8},{24,0},{1,25},{9,17},{17,9},{25,1},{2,26},{10... | collective-permute-start | bytes 270344 | tf_op jit(solution)/shard_map/ppermute | solution.py:57
  43.0 14.7 %copy-start.2 = (f32[1280]{0:T(1024)S(1)}, f32[1280]{0:T(1024)}, u32[]{:S(2)}) copy-start(f32[1280]{0:T(1024)} %param.20) | copy-start | bytes 15364
  43.0 6.6 %collective-permute-start.10 = (bf16[32,1408]{1,0:T(8,128)(2,1)S(1)}, bf16[32,1408]{1,0:T(8,128)(2,1)S(1)}, u32[]{:S(2)}, u32[]{:S(2)}) collective-permute-start(bf16[32,1408]{1,0:T(8,128)(2,1)S(1)} %row_total.1.t0), channel_id=1, source_target_pairs={{0,64},{32,96},{64,0},{96,32},{1,65},{33,97},{65,1},{97,33},{2,66}... | collective-permute-start | bytes 270344 | tf_op jit(solution)/shard_map/ppermute | solution.py:57
  46.3 5.7 %collective-permute-start.11 = (bf16[32,1408]{1,0:T(8,128)(2,1)S(1)}, bf16[32,1408]{1,0:T(8,128)(2,1)S(1)}, u32[]{:S(2)}, u32[]{:S(2)}) collective-permute-start(bf16[32,1408]{1,0:T(8,128)(2,1)S(1)} %row_total.1.t0), channel_id=1, source_target_pairs={{0,96},{32,64},{64,32},{96,0},{1,97},{33,65},{65,33},{97,1},{2,98}... | collective-permute-start | bytes 270344 | tf_op jit(solution)/shard_map/ppermute | solution.py:57
  47.3 4.7 %collective-permute-start.9 = (bf16[32,1408]{1,0:T(8,128)(2,1)S(1)}, bf16[32,1408]{1,0:T(8,128)(2,1)S(1)}, u32[]{:S(2)}, u32[]{:S(2)}) collective-permute-start(bf16[32,1408]{1,0:T(8,128)(2,1)S(1)} %row_total.1.t0), channel_id=1, source_target_pairs={{0,32},{32,0},{64,96},{96,64},{1,33},{33,1},{65,97},{97,65},{2,34}... | collective-permute-start | bytes 270344 | tf_op jit(solution)/shard_map/ppermute | solution.py:57
  52.9 7.4 %collective-permute-start.12 = (bf16[32,1280]{1,0:T(8,128)(2,1)S(1)}, bf16[32,1280]{1,0:T(8,128)(2,1)S(1)}, u32[]{:S(2)}, u32[]{:S(2)}) collective-permute-start(bf16[32,1280]{1,0:T(8,128)(2,1)S(1)} %get-tuple-element.104), channel_id=1, source_target_pairs={{0,8},{8,0},{16,24},{24,16},{1,9},{9,1},{17,25},{25,17},{2,10},{10... | collective-permute-start | bytes 245768 | tf_op jit(solution)/shard_map/ppermute | solution.py:57
  53.0 7.4 %collective-permute-start.13 = (bf16[32,1280]{1,0:T(8,128)(2,1)S(1)}, bf16[32,1280]{1,0:T(8,128)(2,1)S(1)}, u32[]{:S(2)}, u32[]{:S(2)}) collective-permute-start(bf16[32,1280]{1,0:T(8,128)(2,1)S(1)} %get-tuple-element.105), channel_id=1, source_target_pairs={{0,16},{8,24},{16,0},{24,8},{1,17},{9,25},{17,1},{25,9},{2,18},{10... | collective-permute-start | bytes 245768 | tf_op jit(solution)/shard_map/ppermute | solution.py:57
  54.7 5.7 %collective-permute-start.14 = (bf16[32,1280]{1,0:T(8,128)(2,1)S(1)}, bf16[32,1280]{1,0:T(8,128)(2,1)S(1)}, u32[]{:S(2)}, u32[]{:S(2)}) collective-permute-start(bf16[32,1280]{1,0:T(8,128)(2,1)S(1)} %get-tuple-element.106), channel_id=1, source_target_pairs={{0,24},{8,16},{16,8},{24,0},{1,25},{9,17},{17,9},{25,1},{2,26},{10... | collective-permute-start | bytes 245768 | tf_op jit(solution)/shard_map/ppermute | solution.py:57
  57.7 2.7 %slice-start = ((s8[6553600]{0:T(1024)(128)(4,1)}), s8[4194304]{0:T(1024)(128)(4,1)S(1)}, s32[]{:S(2)}) async-start(s8[6553600]{0:T(1024)(128)(4,1)} %bitcast.11), calls=%async_computation | async-start | bytes 8388608
  57.7 2.9 %slice-start.1 = ((s8[6553600]{0:T(1024)(128)(4,1)}), s8[2359296]{0:T(1024)(128)(4,1)S(1)}, s32[]{:S(2)}) async-start(s8[6553600]{0:T(1024)(128)(4,1)} %bitcast.11), calls=%async_computation.1 | async-start | bytes 4718592
  63.4 10.2 %collective-permute-start.17 = (bf16[264,640]{1,0:T(8,128)(2,1)S(1)}, bf16[264,640]{1,0:T(8,128)(2,1)S(1)}, u32[]{:S(2)}, u32[]{:S(2)}) collective-permute-start(bf16[264,640]{1,0:T(8,128)(2,1)S(1)} %get-tuple-element.119), channel_id=1, source_target_pairs={{0,2},{2,0},{4,6},{6,4},{1,3},{3,1},{5,7},{7,5},{8,10},{10,8},{12,... | collective-permute-start | bytes 1013768 | tf_op jit(solution)/shard_map/ppermute | solution.py:57
  63.5 12.9 %collective-permute-start.18 = (bf16[264,640]{1,0:T(8,128)(2,1)S(1)}, bf16[264,640]{1,0:T(8,128)(2,1)S(1)}, u32[]{:S(2)}, u32[]{:S(2)}) collective-permute-start(bf16[264,640]{1,0:T(8,128)(2,1)S(1)} %get-tuple-element.120), channel_id=1, source_target_pairs={{0,6},{2,4},{4,2},{6,0},{1,7},{3,5},{5,3},{7,1},{8,14},{10,12},{12... | collective-permute-start | bytes 1013768 | tf_op jit(solution)/shard_map/ppermute | solution.py:57
  67.5 11.9 %collective-permute-start.15 = (bf16[256,640]{1,0:T(8,128)(2,1)S(1)}, bf16[256,640]{1,0:T(8,128)(2,1)S(1)}, u32[]{:S(2)}, u32[]{:S(2)}) collective-permute-start(bf16[256,640]{1,0:T(8,128)(2,1)S(1)} %get-tuple-element.116), channel_id=1, source_target_pairs={{0,2},{2,0},{4,6},{6,4},{1,3},{3,1},{5,7},{7,5},{8,10},{10,8},{12,... | collective-permute-start | bytes 983048 | tf_op jit(solution)/shard_map/ppermute | solution.py:57
  70.7 11.9 %collective-permute-start.16 = (bf16[256,640]{1,0:T(8,128)(2,1)S(1)}, bf16[256,640]{1,0:T(8,128)(2,1)S(1)}, u32[]{:S(2)}, u32[]{:S(2)}) collective-permute-start(bf16[256,640]{1,0:T(8,128)(2,1)S(1)} %get-tuple-element.117), channel_id=1, source_target_pairs={{0,6},{2,4},{4,2},{6,0},{1,7},{3,5},{5,3},{7,1},{8,14},{10,12},{12... | collective-permute-start | bytes 983048 | tf_op jit(solution)/shard_map/ppermute | solution.py:57
  74.3 12.0 %collective-permute-start.20 = (bf16[264,640]{1,0:T(8,128)(2,1)S(1)}, bf16[264,640]{1,0:T(8,128)(2,1)S(1)}, u32[]{:S(2)}, u32[]{:S(2)}) collective-permute-start(bf16[264,640]{1,0:T(8,128)(2,1)S(1)} %join.3), channel_id=1, source_target_pairs={{0,6},{2,4},{4,2},{6,0},{1,7},{3,5},{5,3},{7,1},{8,14},{10,12},{12... | collective-permute-start | bytes 1013768 | tf_op jit(solution)/shard_map/ppermute | solution.py:57
  77.1 7.4 %collective-permute-start.19 = (bf16[264,640]{1,0:T(8,128)(2,1)S(1)}, bf16[264,640]{1,0:T(8,128)(2,1)S(1)}, u32[]{:S(2)}, u32[]{:S(2)}) collective-permute-start(bf16[264,640]{1,0:T(8,128)(2,1)S(1)} %join.2), channel_id=1, source_target_pairs={{0,2},{2,0},{4,6},{6,4},{1,3},{3,1},{5,7},{7,5},{8,10},{10,8},{12,... | collective-permute-start | bytes 1013768 | tf_op jit(solution)/shard_map/ppermute | solution.py:57

commit v8 on v6

--- a/solution.py
+++ b/solution.py
@@ -663,9 +663,10 @@
     left_0 = swapped(left_0, "head", 1)
     right_1, part_0 = near_block(3, 0, idx, rows, w_out)
     right_1 = swapped(right_1, "head", 3)
+    right_0, left_1 = join(idx, part_0, top), join(idx, part_1, low)
+    right_0, left_1, rows = lax.optimization_barrier((right_0, left_1, rows))
     own = own_block(idx, rows, w_out)
-    right_0 = swapped(join(idx, part_0, top), "head", 3)
-    left_1 = swapped(join(idx, part_1, low), "head", 1)
+    right_0, left_1 = swapped(right_0, "head", 3), swapped(left_1, "head", 1)
     own = add_near(idx, own, left_0, right_1)
     half, factor = settle(idx, own, sums, top, low, left_1)
     return norm(idx, own, factor, right_0, half)

time: 88 us -> 89.4 us (1.016)
  waiting for transfers between devices: 15.4 us -> 17.2 us
    ppermute x21, waiting for transfers between devices: 15.4 us -> 17.2 us  [swapped(): return lax.ppermute(array, axis, [(i, i ^ bits) for i in range(4)])]
  transfers between devices with their start and end apart: 21 -> 21, of which waited for: 10 -> 9; matrix products, arithmetic and copies ran while one was open for 1% -> 1% of each run, Pallas kernels for 34% -> 34%
where the time goes in v8:
time: 89.4 us; the launch traced here: 89.3 us
  Pallas kernels  39.6 us (44%)
  starting transfers between devices  29.3 us (33%)
  waiting for transfers between devices  17.2 us (19%)
  local copies, waits for them, and re-layouts  2.07 us (2%)
    pallas_call x16, Pallas kernels, call(): pl.pallas_call(body, in_specs=[SMEM, *[VMEM] * len(args)], out_specs=[VME...  30.3 us
    ppermute x21, starting transfers between devices, swapped(): return lax.ppermute(array, axis, [(i, i ^ bits) for i in range(4)])  29.3 us
    ppermute x21, waiting for transfers between devices, swapped(): return lax.ppermute(array, axis, [(i, i ^ bits) for i in range(4)])  17.2 us
    pallas_call x1, Pallas kernels, load_weights(): pl.pallas_call(load_body, in_specs=[SMEM, *[HBM] * 5], out_specs=[VMEM] *...  6.34 us
    pallas_call x2, Pallas kernels, end_call(): pl.pallas_call(body, in_specs=[SMEM, *[VMEM] * len(args), *[HBM] * len(mo...  2.95 us
  transfers between devices with their start and end apart: 21, of which 9 were waited for; matrix products, arithmetic and copies ran while one was open for 1% of the time, Pallas kernels for 34%

profile of v8, /device:TPU:0, one launch (start us, length us, event | category | flops | bytes accessed | tf_op | source)
XLA Modules:
  0.0 89.3 jit_solution(7299297883152259703)
XLA Ops:
  0.0 1.1 %fusion = (bf16[256,640]{1,0:T(8,128)(2,1)S(1)}, bf16[256,640]{1,0:T(8,128)(2,1)S(1)}) fusion(bf16[512,640]{1,0:T(8,128)(2,1)} %tok.1), kind=kLoop, calls=%fused_computation.4 | loop fusion | bytes 1310720 | tf_op jit(solution)/shard_map/slice | solution.py:626
  1.1 1.7 %collective-permute-start = (bf16[256,640]{1,0:T(8,128)(2,1)S(1)}, bf16[256,640]{1,0:T(8,128)(2,1)S(1)}, u32[]{:S(2)}, u32[]{:S(2)}) collective-permute-start(bf16[256,640]{1,0:T(8,128)(2,1)S(1)} %get-tuple-element.70), channel_id=1, source_target_pairs={{0,2},{2,0},{4,6},{6,4},{1,3},{3,1},{5,7},{7,5},{8,10},{10,8},{12,... | collective-permute-start | bytes 983048 | tf_op jit(solution)/shard_map/ppermute | solution.py:57
  2.8 2.1 %collective-permute-start.2 = (bf16[256,640]{1,0:T(8,128)(2,1)S(1)}, bf16[256,640]{1,0:T(8,128)(2,1)S(1)}, u32[]{:S(2)}, u32[]{:S(2)}) collective-permute-start(bf16[256,640]{1,0:T(8,128)(2,1)S(1)} %get-tuple-element.69), channel_id=1, source_target_pairs={{0,6},{2,4},{4,2},{6,0},{1,7},{3,5},{5,3},{7,1},{8,14},{10,12},{12... | collective-permute-start | bytes 983048 | tf_op jit(solution)/shard_map/ppermute | solution.py:57
  4.9 0.6 pad_add_fusion.idx
  5.5 0.6 collective-permute-start.4
  6.1 0.6 collective-permute-start.5
  6.7 0.7 pad_bitcast_fusion.skip
  7.4 6.3 %load_weights.1 = (f32[512,1280]{1,0:T(8,128)S(1)}, f32[512,384]{1,0:T(8,128)S(1)}, bf16[512,640]{1,0:T(8,128)(2,1)S(1)}, bf16[128,2560]{1,0:T(8,128)(2,1)S(1)},...) custom-call(s32[3]{0:T(128)} %pad_add_fusion.idx, ...), custom_call_target="tpu_custom_call" | custom-call | flops 1090519040 | bytes 15000000 | tf_op jit(solution)/shard_map/load_weights/pallas_call | solution.py:128
  13.8 0.0 collective-permute-done.l_0
  13.8 2.7 %collective-permute-start.1 = (bf16[256,640]{1,0:T(8,128)(2,1)S(1)}, bf16[256,640]{1,0:T(8,128)(2,1)S(1)}, u32[]{:S(2)}, u32[]{:S(2)}) collective-permute-start(bf16[256,640]{1,0:T(8,128)(2,1)S(1)} %collective-permute-done.l_0), channel_id=1, source_target_pairs={{0,6},{2,4},{4,2},{6,0},{1,7},{3,5},{5,3},{7,1},{8,14},{10,12},{12... | collective-permute-start | bytes 983048 | tf_op jit(solution)/shard_map/ppermute | solution.py:57
  16.5 0.2 collective-permute-start.3
  16.7 2.8 %gate_first.1.acc_z = f32[512,1280]{1,0:T(8,128)S(1)} custom-call(s32[3]{0:T(128)S(1)} %copy-done, bf16[512,640]{1,0:T(8,128)(2,1)S(1)} %get-tuple-element.72.tok, bf16[256,640]{1,0:T(8,128)(2,1)S(1)} %collective-permute-done.l_0, bf16[256,640]{1,0:T(8,128)(2,1)S(1)} %collective-permute-done.2.r_1, bf16[2560,1280]{1,0:T(8,128)(2,1)S(1)} %get-tuple-element.116.w_z), custom_call_target="tpu_custom_call" | custom-call | flops 1677721600 | bytes 1000000 | tf_op jit(solution)/shard_map/gate_first/pallas_call | solution.py:72
  19.5 0.0 collective-permute-done.4.l_1
  19.5 2.2 %collective-permute-done.5.r_0 = bf16[256,640]{1,0:T(8,128)(2,1)S(1)} collective-permute-done((bf16[256,640]{1,0:T(8,128)(2,1)S(1)}, bf16[256,640]{1,0:T(8,128)(2,1)S(1)}, u32[]{:S(2)}, u32[]{:S(2)}) %collective-permute-start.5) | collective-permute-done | bytes 327712 | tf_op jit(solution)/shard_map/ppermute | solution.py:57
  21.7 1.9 %gate_second.1.acc_z = f32[512,1280]{1,0:T(8,128)S(1)} custom-call(s32[3]{0:T(128)S(1)} %copy-done, bf16[256,640]{1,0:T(8,128)(2,1)S(1)} %collective-permute-done.4.l_1, bf16[256,640]{1,0:T(8,128)(2,1)S(1)} %collective-permute-done.5.r_0, bf16[2560,1280]{1,0:T(8,128)(2,1)S(1)} %get-tuple-element.116.w_z, ...), custom_call_target="tpu_custom_call", output_to_operand_aliasing={{}: (4, {})} | custom-call | flops 838860800 | bytes 1000000 | tf_op jit(solution)/shard_map/gate_second/pallas_call | solution.py:72
  23.6 0.0 copy-start.1
  23.6 3.3 %project.1 = (f32[512,1280]{1,0:T(8,128)S(1)}, f32[512,384]{1,0:T(8,128)S(1)}) custom-call(s32[3]{0:T(128)S(1)} %copy-done, bf16[256,640]{1,0:T(8,128)(2,1)S(1)} %collective-permute-done.l_0, bf16[256,640]{1,0:T(8,128)(2,1)S(1)} %collective-permute-done.4.l_1, ...), custom_call_target="tpu_custom_call", output_to_operand_aliasing={{0}: (8, {}), {1}: (9, {})} | custom-call | flops 2181038080 | bytes 1000000 | tf_op jit(solution)/shard_map/project/pallas_call | solution.py:72
  26.9 0.3 collective-permute-done.1.tok_0.t_0
  27.2 0.0 collective-permute-done.3.tok_1.t_1
  27.2 3.6 %device_state.1 = (bf16[512,1280]{1,0:T(8,128)(2,1)S(1)}, bf16[512,128]{1,0:T(8,128)(2,1)S(1)}, bf16[512,128]{1,0:T(8,128)(2,1)S(1)}, f32[512,128]{1,0:T(8,128)S...) custom-call(s32[3]{0:T(128)S(1)} %copy-done, ...), custom_call_target="tpu_custom_call" | custom-call | flops 1090519040 | bytes 1000000 | tf_op jit(solution)/shard_map/device_state/pallas_call | solution.py:72
  30.9 2.0 %collective-permute-start.6 = (bf16[32,1408]{1,0:T(8,128)(2,1)S(1)}, bf16[32,1408]{1,0:T(8,128)(2,1)S(1)}, u32[]{:S(2)}, u32[]{:S(2)}) collective-permute-start(bf16[32,1408]{1,0:T(8,128)(2,1)S(1)} %get-tuple-element.85), channel_id=1, source_target_pairs={{0,8},{8,0},{16,24},{24,16},{1,9},{9,1},{17,25},{25,17},{2,10},{10... | collective-permute-start | bytes 270344 | tf_op jit(solution)/shard_map/ppermute | solution.py:57
  32.9 3.6 %collective-permute-start.7 = (bf16[32,1408]{1,0:T(8,128)(2,1)S(1)}, bf16[32,1408]{1,0:T(8,128)(2,1)S(1)}, u32[]{:S(2)}, u32[]{:S(2)}) collective-permute-start(bf16[32,1408]{1,0:T(8,128)(2,1)S(1)} %get-tuple-element.86), channel_id=1, source_target_pairs={{0,16},{8,24},{16,0},{24,8},{1,17},{9,25},{17,1},{25,9},{2,18},{10... | collective-permute-start | bytes 270344 | tf_op jit(solution)/shard_map/ppermute | solution.py:57
  36.5 0.0 collective-permute-start.8
  36.5 2.2 %mix.2 = (f32[256,1280]{1,0:T(8,128)S(1)}, f32[256,1280]{1,0:T(8,128)S(1)}) custom-call(s32[3]{0:T(128)S(1)} %copy-done, bf16[512,1280]{1,0:T(8,128)(2,1)S(1)} %get-tuple-element.88.inner_r, bf16[512,128]{1,0:T(8,128)(2,1)S(1)} %get-tuple-element.89.b_r, bf16[512,128]{1,0:T(8,128)(2,1)S(1)} %get-tuple-element.90.c_r, ...), custom_call_target="tpu_custom_call" | custom-call | flops 2000000000 | bytes 1000000 | tf_op jit(solution)/shard_map/mix/pallas_call | solution.py:72
  38.7 0.0 collective-permute-done.6.m1
  38.7 1.3 %collective-permute-done.7.m2 = bf16[32,1408]{1,0:T(8,128)(2,1)S(1)} collective-permute-done((bf16[32,1408]{1,0:T(8,128)(2,1)S(1)}, bf16[32,1408]{1,0:T(8,128)(2,1)S(1)}, u32[]{:S(2)}, u32[]{:S(2)}) %collective-permute-start.7) | collective-permute-done | bytes 90144 | tf_op jit(solution)/shard_map/ppermute | solution.py:57
  40.0 2.2 %collective-permute-done.8.m3 = bf16[32,1408]{1,0:T(8,128)(2,1)S(1)} collective-permute-done((bf16[32,1408]{1,0:T(8,128)(2,1)S(1)}, bf16[32,1408]{1,0:T(8,128)(2,1)S(1)}, u32[]{:S(2)}, u32[]{:S(2)}) %collective-permute-start.8) | collective-permute-done | bytes 90144 | tf_op jit(solution)/shard_map/ppermute | solution.py:57
  42.2 0.8 row_total.1.t0
  43.0 0.0 copy-start.2
  43.0 3.3 %collective-permute-start.10 = (bf16[32,1408]{1,0:T(8,128)(2,1)S(1)}, bf16[32,1408]{1,0:T(8,128)(2,1)S(1)}, u32[]{:S(2)}, u32[]{:S(2)}) collective-permute-start(bf16[32,1408]{1,0:T(8,128)(2,1)S(1)} %row_total.1.t0), channel_id=1, source_target_pairs={{0,64},{32,96},{64,0},{96,32},{1,65},{33,97},{65,1},{97,33},{2,66}... | collective-permute-start | bytes 270344 | tf_op jit(solution)/shard_map/ppermute | solution.py:57
  46.3 1.1 %collective-permute-start.11 = (bf16[32,1408]{1,0:T(8,128)(2,1)S(1)}, bf16[32,1408]{1,0:T(8,128)(2,1)S(1)}, u32[]{:S(2)}, u32[]{:S(2)}) collective-permute-start(bf16[32,1408]{1,0:T(8,128)(2,1)S(1)} %row_total.1.t0), channel_id=1, source_target_pairs={{0,96},{32,64},{64,32},{96,0},{1,97},{33,65},{65,33},{97,1},{2,98}... | collective-permute-start | bytes 270344 | tf_op jit(solution)/shard_map/ppermute | solution.py:57
  47.3 2.2 %mix.3 = (f32[256,1280]{1,0:T(8,128)S(1)}, f32[256,1280]{1,0:T(8,128)S(1)}) custom-call(s32[3]{0:T(128)S(1)} %copy-done, bf16[512,1280]{1,0:T(8,128)(2,1)S(1)} %get-tuple-element.88.inner_r, bf16[512,128]{1,0:T(8,128)(2,1)S(1)} %get-tuple-element.89.b_r, bf16[512,128]{1,0:T(8,128)(2,1)S(1)} %get-tuple-element.90.c_r, ...), custom_call_target="tpu_custom_call" | custom-call | flops 2000000000 | bytes 1000000 | tf_op jit(solution)/shard_map/mix/pallas_call | solution.py:72
  49.5 0.0 collective-permute-done.10.t2
  49.6 2.5 %collective-permute-done.11.t3 = bf16[32,1408]{1,0:T(8,128)(2,1)S(1)} collective-permute-done((bf16[32,1408]{1,0:T(8,128)(2,1)S(1)}, bf16[32,1408]{1,0:T(8,128)(2,1)S(1)}, u32[]{:S(2)}, u32[]{:S(2)}) %collective-permute-start.11) | collective-permute-done | bytes 90144 | tf_op jit(solution)/shard_map/ppermute | solution.py:57
  52.0 0.0 collective-permute-done.9.t1
  52.0 0.9 %prefixes.1 = (bf16[32,1280]{1,0:T(8,128)(2,1)S(1)}, bf16[32,1280]{1,0:T(8,128)(2,1)S(1)}, bf16[32,1280]{1,0:T(8,128)(2,1)S(1)}, bf16[32,1280]{1,0:T(8,128)(2,1)S(1)}) custom-call(s32[3]{0:T(128)S(1)} %copy-done, bf16[32,1408]{1,0:T(8,128)(2,1)S(1)} %get-tuple-element.95.m0, bf16[32,1408]{1,0:T(8,128)(2,1)S(1)} %collective-permute-done.6.m1, ...), custom_call_target="tpu_custom_call" | custom-call | flops 100000000 | bytes 1000000 | tf_op jit(solution)/shard_map/prefixes/pallas_call | solution.py:72
  52.9 0.1 collective-permute-start.12
  53.0 1.6 %collective-permute-start.13 = (bf16[32,1280]{1,0:T(8,128)(2,1)S(1)}, bf16[32,1280]{1,0:T(8,128)(2,1)S(1)}, u32[]{:S(2)}, u32[]{:S(2)}) collective-permute-start(bf16[32,1280]{1,0:T(8,128)(2,1)S(1)} %get-tuple-element.108), channel_id=1, source_target_pairs={{0,16},{8,24},{16,0},{24,8},{1,17},{9,25},{17,1},{25,9},{2,18},{10... | collective-permute-start | bytes 245768 | tf_op jit(solution)/shard_map/ppermute | solution.py:57
  54.7 3.0 %collective-permute-start.14 = (bf16[32,1280]{1,0:T(8,128)(2,1)S(1)}, bf16[32,1280]{1,0:T(8,128)(2,1)S(1)}, u32[]{:S(2)}, u32[]{:S(2)}) collective-permute-start(bf16[32,1280]{1,0:T(8,128)(2,1)S(1)} %get-tuple-element.109), channel_id=1, source_target_pairs={{0,24},{8,16},{16,8},{24,0},{1,25},{9,17},{17,9},{25,1},{2,26},{10... | collective-permute-start | bytes 245768 | tf_op jit(solution)/shard_map/ppermute | solution.py:57
  57.7 0.0 slice-start.1
  57.7 2.6 %gate.1.zs_r = f32[512,1280]{1,0:T(8,128)S(1)} custom-call(s32[3]{0:T(128)S(1)} %copy-done, bf16[256,640]{1,0:T(8,128)(2,1)S(1)} %collective-permute-done.1.tok_0.t_0, bf16[256,640]{1,0:T(8,128)(2,1)S(1)} %collective-permute-done.3.tok_1.t_1, bf16[2560,1280]{1,0:T(8,128)(2,1)S(1)} %get-tuple-element.116.w_z, ...), custom_call_target="tpu_custom_call", output_to_operand_aliasing={{}: (4, {})} | custom-call | flops 838860800 | bytes 1000000 | tf_op jit(solution)/shard_map/gate/pallas_call | solution.py:72
  60.4 0.0 collective-permute-done.13.h2
  60.4 0.0 collective-permute-done.14.h3
  60.4 0.2 slice-done.1
  60.7 2.8 %gated_rows.1 = (bf16[512,1280]{1,0:T(8,128)(2,1)S(1)}, f32[8,512]{1,0:T(8,128)S(1)}, bf16[264,640]{1,0:T(8,128)(2,1)S(1)}, bf16[264,640]{1,0:T(8,128)(2,1)S(1)}) custom-call(s32[3]{0:T(128)S(1)} %copy-done, bf16[32,1280]{1,0:T(8,128)(2,1)S(1)} %get-tuple-element.106.h0, bf16[32,1280]{1,0:T(8,128)(2,1)S(1)} %collective-permute-done.12.h1, ...), custom_call_target="tpu_custom_call" | custom-call | flops 1090519040 | bytes 1000000 | tf_op jit(solution)/shard_map/gated_rows/pallas_call | solution.py:72
  63.4 2.2 %collective-permute-start.16 = (bf16[264,640]{1,0:T(8,128)(2,1)S(1)}, bf16[264,640]{1,0:T(8,128)(2,1)S(1)}, u32[]{:S(2)}, u32[]{:S(2)}) collective-permute-start(bf16[264,640]{1,0:T(8,128)(2,1)S(1)} %get-tuple-element.122), channel_id=1, source_target_pairs={{0,6},{2,4},{4,2},{6,0},{1,7},{3,5},{5,3},{7,1},{8,14},{10,12},{12... | collective-permute-start | bytes 1013768 | tf_op jit(solution)/shard_map/ppermute | solution.py:57
  65.7 0.0 collective-permute-start.15
  65.7 1.7 %near_block.3 = (bf16[256,640]{1,0:T(8,128)(2,1)S(1)}, f32[256,640]{1,0:T(8,128)S(1)}) custom-call(s32[3]{0:T(128)S(1)} %copy-done, bf16[512,1280]{1,0:T(8,128)(2,1)S(1)} %get-tuple-element.123.rows, bf16[1280,2560]{1,0:T(8,128)(2,1)S(1)} %bitcast.12), custom_call_target="tpu_custom_call" | custom-call | flops 1000000 | bytes 1000000 | tf_op jit(solution)/shard_map/near_block/pallas_call | solution.py:72
  67.4 2.1 %collective-permute-start.17 = (bf16[256,640]{1,0:T(8,128)(2,1)S(1)}, bf16[256,640]{1,0:T(8,128)(2,1)S(1)}, u32[]{:S(2)}, u32[]{:S(2)}) collective-permute-start(bf16[256,640]{1,0:T(8,128)(2,1)S(1)} %get-tuple-element.124), channel_id=1, source_target_pairs={{0,2},{2,0},{4,6},{6,4},{1,3},{3,1},{5,7},{7,5},{8,10},{10,8},{12,... | collective-permute-start | bytes 983048 | tf_op jit(solution)/shard_map/ppermute | solution.py:57
  69.5 1.7 %near_block.2 = (bf16[256,640]{1,0:T(8,128)(2,1)S(1)}, f32[256,640]{1,0:T(8,128)S(1)}) custom-call(s32[3]{0:T(128)S(1)} %copy-done, bf16[512,1280]{1,0:T(8,128)(2,1)S(1)} %get-tuple-element.123.rows, bf16[1280,2560]{1,0:T(8,128)(2,1)S(1)} %bitcast.12), custom_call_target="tpu_custom_call" | custom-call | flops 1000000 | bytes 1000000 | tf_op jit(solution)/shard_map/near_block/pallas_call | solution.py:72
  71.3 1.2 %collective-permute-start.18 = (bf16[256,640]{1,0:T(8,128)(2,1)S(1)}, bf16[256,640]{1,0:T(8,128)(2,1)S(1)}, u32[]{:S(2)}, u32[]{:S(2)}) collective-permute-start(bf16[256,640]{1,0:T(8,128)(2,1)S(1)} %get-tuple-element.125), channel_id=1, source_target_pairs={{0,6},{2,4},{4,2},{6,0},{1,7},{3,5},{5,3},{7,1},{8,14},{10,12},{12... | collective-permute-start | bytes 983048 | tf_op jit(solution)/shard_map/ppermute | solution.py:57
  72.4 0.4 collective-permute-done.16.half.other
  72.8 0.6 join.3
  73.4 3.1 %collective-permute-done.15.half.near = bf16[264,640]{1,0:T(8,128)(2,1)S(1)} collective-permute-done((bf16[264,640]{1,0:T(8,128)(2,1)S(1)}, bf16[264,640]{1,0:T(8,128)(2,1)S(1)}, u32[]{:S(2)}, u32[]{:S(2)}) %collective-permute-start.15) | collective-permute-done | bytes 337952 | tf_op jit(solution)/shard_map/ppermute | solution.py:57
  76.5 0.6 join.2
  77.2 0.1 collective-permute-start.19
  77.3 1.2 %collective-permute-start.20 = (bf16[264,640]{1,0:T(8,128)(2,1)S(1)}, bf16[264,640]{1,0:T(8,128)(2,1)S(1)}, u32[]{:S(2)}, u32[]{:S(2)}) collective-permute-start(bf16[264,640]{1,0:T(8,128)(2,1)S(1)} %join.2), channel_id=1, source_target_pairs={{0,6},{2,4},{4,2},{6,0},{1,7},{3,5},{5,3},{7,1},{8,14},{10,12},{12... | collective-permute-start | bytes 1013768 | tf_op jit(solution)/shard_map/ppermute | solution.py:57
  78.4 1.7 %own_block.1.own = f32[512,640]{1,0:T(8,128)S(1)} custom-call(s32[3]{0:T(128)S(1)} %copy-done, bf16[512,1280]{1,0:T(8,128)(2,1)S(1)} %get-tuple-element.123.rows, bf16[1280,2560]{1,0:T(8,128)(2,1)S(1)} %bitcast.12), custom_call_target="tpu_custom_call" | custom-call | flops 1000000 | bytes 1000000 | tf_op jit(solution)/shard_map/own_block/pallas_call | solution.py:72
  80.1 2.4 %collective-permute-done.17.left_0 = bf16[256,640]{1,0:T(8,128)(2,1)S(1)} collective-permute-done((bf16[256,640]{1,0:T(8,128)(2,1)S(1)}, bf16[256,640]{1,0:T(8,128)(2,1)S(1)}, u32[]{:S(2)}, u32[]{:S(2)}) %collective-permute-start.17) | collective-permute-done | bytes 327712 | tf_op jit(solution)/shard_map/ppermute | solution.py:57
  82.5 0.0 collective-permute-done.18.right_1
  82.6 0.8 add_near.1.own
  83.3 2.8 %collective-permute-done.19.left_1 = bf16[264,640]{1,0:T(8,128)(2,1)S(1)} collective-permute-done((bf16[264,640]{1,0:T(8,128)(2,1)S(1)}, bf16[264,640]{1,0:T(8,128)(2,1)S(1)}, u32[]{:S(2)}, u32[]{:S(2)}) %collective-permute-start.19) | collective-permute-done | bytes 337952 | tf_op jit(solution)/shard_map/ppermute | solution.py:57
  86.1 1.6 %settle.1 = (bf16[512,640]{1,0:T(8,128)(2,1)}, f32[256,128]{1,0:T(8,128)S(1)}) custom-call(s32[3]{0:T(128)S(1)} %copy-done, f32[512,640]{1,0:T(8,128)S(1)} %add_near.1.own, f32[8,512]{1,0:T(8,128)S(1)} %get-tuple-element.126.sums, bf16[264,640]{1,0:T(8,128)(2,1)S(1)} %collective-permute-done.15.half.near, ...), custom_call_target="tpu_custom_call" | custom-call | flops 1000000 | bytes 1000000 | tf_op jit(solution)/shard_map/settle/pallas_call | solution.py:589
  87.7 1.4 %norm.1 = bf16[512,640]{1,0:T(8,128)(2,1)} custom-call(s32[3]{0:T(128)S(1)} %copy-done, f32[512,640]{1,0:T(8,128)S(1)} %add_near.1.own, f32[256,128]{1,0:T(8,128)S(1)} %get-tuple-element.128.factor, bf16[264,640]{1,0:T(8,128)(2,1)S(1)} %collective-permute-done.20.right_0, bf16[512,640]{1,0:T(8,128)(2,1)} %get-tuple-element.130.so_far), custom_call_target="tpu_custom_call", output_to_operand_aliasing={{}: (4, {})} | custom-call | flops 1000000 | bytes 1000000 | tf_op jit(solution)/shard_map/norm/pallas_call | solution.py:589
  (17 shorter events, 0.0 us)
Async XLA Ops:
  1.1 12.6 %collective-permute-start = (bf16[256,640]{1,0:T(8,128)(2,1)S(1)}, bf16[256,640]{1,0:T(8,128)(2,1)S(1)}, u32[]{:S(2)}, u32[]{:S(2)}) collective-permute-start(bf16[256,640]{1,0:T(8,128)(2,1)S(1)} %get-tuple-element.70), channel_id=1, source_target_pairs={{0,2},{2,0},{4,6},{6,4},{1,3},{3,1},{5,7},{7,5},{8,10},{10,8},{12,... | collective-permute-start | bytes 983048 | tf_op jit(solution)/shard_map/ppermute | solution.py:57
  2.8 13.7 %collective-permute-start.2 = (bf16[256,640]{1,0:T(8,128)(2,1)S(1)}, bf16[256,640]{1,0:T(8,128)(2,1)S(1)}, u32[]{:S(2)}, u32[]{:S(2)}) collective-permute-start(bf16[256,640]{1,0:T(8,128)(2,1)S(1)} %get-tuple-element.69), channel_id=1, source_target_pairs={{0,6},{2,4},{4,2},{6,0},{1,7},{3,5},{5,3},{7,1},{8,14},{10,12},{12... | collective-permute-start | bytes 983048 | tf_op jit(solution)/shard_map/ppermute | solution.py:57
  5.5 14.0 %collective-permute-start.4 = (bf16[256,640]{1,0:T(8,128)(2,1)S(1)}, bf16[256,640]{1,0:T(8,128)(2,1)S(1)}, u32[]{:S(2)}, u32[]{:S(2)}) collective-permute-start(bf16[256,640]{1,0:T(8,128)(2,1)S(1)} %get-tuple-element.69), channel_id=1, source_target_pairs={{0,2},{2,0},{4,6},{6,4},{1,3},{3,1},{5,7},{7,5},{8,10},{10,8},{12,... | collective-permute-start | bytes 983048 | tf_op jit(solution)/shard_map/ppermute | solution.py:57
  6.1 15.6 %collective-permute-start.5 = (bf16[256,640]{1,0:T(8,128)(2,1)S(1)}, bf16[256,640]{1,0:T(8,128)(2,1)S(1)}, u32[]{:S(2)}, u32[]{:S(2)}) collective-permute-start(bf16[256,640]{1,0:T(8,128)(2,1)S(1)} %get-tuple-element.70), channel_id=1, source_target_pairs={{0,6},{2,4},{4,2},{6,0},{1,7},{3,5},{5,3},{7,1},{8,14},{10,12},{12... | collective-permute-start | bytes 983048 | tf_op jit(solution)/shard_map/ppermute | solution.py:57
  7.4 6.4 %copy-start.3 = (f32[20]{0:T(128)S(1)}, f32[20]{0:T(128)}, u32[]{:S(2)}) copy-start(f32[20]{0:T(128)} %param.18) | copy-start | bytes 244
  7.4 6.4 %copy-start.4 = (f32[20]{0:T(128)S(1)}, f32[20]{0:T(128)}, u32[]{:S(2)}) copy-start(f32[20]{0:T(128)} %param.17) | copy-start | bytes 244
  7.4 9.3 %copy-start = (s32[3]{0:T(128)S(1)}, s32[3]{0:T(128)}, u32[]{:S(2)}) copy-start(s32[3]{0:T(128)} %pad_add_fusion.idx) | copy-start | bytes 40
  13.8 13.4 %collective-permute-start.1 = (bf16[256,640]{1,0:T(8,128)(2,1)S(1)}, bf16[256,640]{1,0:T(8,128)(2,1)S(1)}, u32[]{:S(2)}, u32[]{:S(2)}) collective-permute-start(bf16[256,640]{1,0:T(8,128)(2,1)S(1)} %collective-permute-done.l_0), channel_id=1, source_target_pairs={{0,6},{2,4},{4,2},{6,0},{1,7},{3,5},{5,3},{7,1},{8,14},{10,12},{12... | collective-permute-start | bytes 983048 | tf_op jit(solution)/shard_map/ppermute | solution.py:57
  16.5 10.7 %collective-permute-start.3 = (bf16[256,640]{1,0:T(8,128)(2,1)S(1)}, bf16[256,640]{1,0:T(8,128)(2,1)S(1)}, u32[]{:S(2)}, u32[]{:S(2)}) collective-permute-start(bf16[256,640]{1,0:T(8,128)(2,1)S(1)} %collective-permute-done.2.r_1), channel_id=1, source_target_pairs={{0,2},{2,0},{4,6},{6,4},{1,3},{3,1},{5,7},{7,5},{8,10},{10,8},{12,... | collective-permute-start | bytes 983048 | tf_op jit(solution)/shard_map/ppermute | solution.py:57
  23.6 3.6 %copy-start.1 = (s32[512]{0:T(512)S(1)}, s32[512]{0:T(512)}, u32[]{:S(2)}) copy-start(s32[512]{0:T(512)} %param.12) | copy-start | bytes 6148
  30.9 7.8 %collective-permute-start.6 = (bf16[32,1408]{1,0:T(8,128)(2,1)S(1)}, bf16[32,1408]{1,0:T(8,128)(2,1)S(1)}, u32[]{:S(2)}, u32[]{:S(2)}) collective-permute-start(bf16[32,1408]{1,0:T(8,128)(2,1)S(1)} %get-tuple-element.85), channel_id=1, source_target_pairs={{0,8},{8,0},{16,24},{24,16},{1,9},{9,1},{17,25},{25,17},{2,10},{10... | collective-permute-start | bytes 270344 | tf_op jit(solution)/shard_map/ppermute | solution.py:57
  32.9 7.2 %collective-permute-start.7 = (bf16[32,1408]{1,0:T(8,128)(2,1)S(1)}, bf16[32,1408]{1,0:T(8,128)(2,1)S(1)}, u32[]{:S(2)}, u32[]{:S(2)}) collective-permute-start(bf16[32,1408]{1,0:T(8,128)(2,1)S(1)} %get-tuple-element.86), channel_id=1, source_target_pairs={{0,16},{8,24},{16,0},{24,8},{1,17},{9,25},{17,1},{25,9},{2,18},{10... | collective-permute-start | bytes 270344 | tf_op jit(solution)/shard_map/ppermute | solution.py:57
  36.5 5.7 %collective-permute-start.8 = (bf16[32,1408]{1,0:T(8,128)(2,1)S(1)}, bf16[32,1408]{1,0:T(8,128)(2,1)S(1)}, u32[]{:S(2)}, u32[]{:S(2)}) collective-permute-start(bf16[32,1408]{1,0:T(8,128)(2,1)S(1)} %get-tuple-element.87), channel_id=1, source_target_pairs={{0,24},{8,16},{16,8},{24,0},{1,25},{9,17},{17,9},{25,1},{2,26},{10... | collective-permute-start | bytes 270344 | tf_op jit(solution)/shard_map/ppermute | solution.py:57
  43.0 14.7 %copy-start.2 = (f32[1280]{0:T(1024)S(1)}, f32[1280]{0:T(1024)}, u32[]{:S(2)}) copy-start(f32[1280]{0:T(1024)} %param.20) | copy-start | bytes 15364
  43.0 6.6 %collective-permute-start.10 = (bf16[32,1408]{1,0:T(8,128)(2,1)S(1)}, bf16[32,1408]{1,0:T(8,128)(2,1)S(1)}, u32[]{:S(2)}, u32[]{:S(2)}) collective-permute-start(bf16[32,1408]{1,0:T(8,128)(2,1)S(1)} %row_total.1.t0), channel_id=1, source_target_pairs={{0,64},{32,96},{64,0},{96,32},{1,65},{33,97},{65,1},{97,33},{2,66}... | collective-permute-start | bytes 270344 | tf_op jit(solution)/shard_map/ppermute | solution.py:57
  46.3 5.7 %collective-permute-start.11 = (bf16[32,1408]{1,0:T(8,128)(2,1)S(1)}, bf16[32,1408]{1,0:T(8,128)(2,1)S(1)}, u32[]{:S(2)}, u32[]{:S(2)}) collective-permute-start(bf16[32,1408]{1,0:T(8,128)(2,1)S(1)} %row_total.1.t0), channel_id=1, source_target_pairs={{0,96},{32,64},{64,32},{96,0},{1,97},{33,65},{65,33},{97,1},{2,98}... | collective-permute-start | bytes 270344 | tf_op jit(solution)/shard_map/ppermute | solution.py:57
  47.3 4.7 %collective-permute-start.9 = (bf16[32,1408]{1,0:T(8,128)(2,1)S(1)}, bf16[32,1408]{1,0:T(8,128)(2,1)S(1)}, u32[]{:S(2)}, u32[]{:S(2)}) collective-permute-start(bf16[32,1408]{1,0:T(8,128)(2,1)S(1)} %row_total.1.t0), channel_id=1, source_target_pairs={{0,32},{32,0},{64,96},{96,64},{1,33},{33,1},{65,97},{97,65},{2,34}... | collective-permute-start | bytes 270344 | tf_op jit(solution)/shard_map/ppermute | solution.py:57
  52.9 7.4 %collective-permute-start.12 = (bf16[32,1280]{1,0:T(8,128)(2,1)S(1)}, bf16[32,1280]{1,0:T(8,128)(2,1)S(1)}, u32[]{:S(2)}, u32[]{:S(2)}) collective-permute-start(bf16[32,1280]{1,0:T(8,128)(2,1)S(1)} %get-tuple-element.107), channel_id=1, source_target_pairs={{0,8},{8,0},{16,24},{24,16},{1,9},{9,1},{17,25},{25,17},{2,10},{10... | collective-permute-start | bytes 245768 | tf_op jit(solution)/shard_map/ppermute | solution.py:57
  53.0 7.4 %collective-permute-start.13 = (bf16[32,1280]{1,0:T(8,128)(2,1)S(1)}, bf16[32,1280]{1,0:T(8,128)(2,1)S(1)}, u32[]{:S(2)}, u32[]{:S(2)}) collective-permute-start(bf16[32,1280]{1,0:T(8,128)(2,1)S(1)} %get-tuple-element.108), channel_id=1, source_target_pairs={{0,16},{8,24},{16,0},{24,8},{1,17},{9,25},{17,1},{25,9},{2,18},{10... | collective-permute-start | bytes 245768 | tf_op jit(solution)/shard_map/ppermute | solution.py:57
  54.7 5.7 %collective-permute-start.14 = (bf16[32,1280]{1,0:T(8,128)(2,1)S(1)}, bf16[32,1280]{1,0:T(8,128)(2,1)S(1)}, u32[]{:S(2)}, u32[]{:S(2)}) collective-permute-start(bf16[32,1280]{1,0:T(8,128)(2,1)S(1)} %get-tuple-element.109), channel_id=1, source_target_pairs={{0,24},{8,16},{16,8},{24,0},{1,25},{9,17},{17,9},{25,1},{2,26},{10... | collective-permute-start | bytes 245768 | tf_op jit(solution)/shard_map/ppermute | solution.py:57
  57.7 2.7 %slice-start = ((s8[6553600]{0:T(1024)(128)(4,1)}), s8[4194304]{0:T(1024)(128)(4,1)S(1)}, s32[]{:S(2)}) async-start(s8[6553600]{0:T(1024)(128)(4,1)} %bitcast.11), calls=%async_computation | async-start | bytes 8388608
  57.7 2.9 %slice-start.1 = ((s8[6553600]{0:T(1024)(128)(4,1)}), s8[2359296]{0:T(1024)(128)(4,1)S(1)}, s32[]{:S(2)}) async-start(s8[6553600]{0:T(1024)(128)(4,1)} %bitcast.11), calls=%async_computation.1 | async-start | bytes 4718592
  63.4 9.4 %collective-permute-start.16 = (bf16[264,640]{1,0:T(8,128)(2,1)S(1)}, bf16[264,640]{1,0:T(8,128)(2,1)S(1)}, u32[]{:S(2)}, u32[]{:S(2)}) collective-permute-start(bf16[264,640]{1,0:T(8,128)(2,1)S(1)} %get-tuple-element.122), channel_id=1, source_target_pairs={{0,6},{2,4},{4,2},{6,0},{1,7},{3,5},{5,3},{7,1},{8,14},{10,12},{12... | collective-permute-start | bytes 1013768 | tf_op jit(solution)/shard_map/ppermute | solution.py:57
  65.7 10.9 %collective-permute-start.15 = (bf16[264,640]{1,0:T(8,128)(2,1)S(1)}, bf16[264,640]{1,0:T(8,128)(2,1)S(1)}, u32[]{:S(2)}, u32[]{:S(2)}) collective-permute-start(bf16[264,640]{1,0:T(8,128)(2,1)S(1)} %get-tuple-element.120), channel_id=1, source_target_pairs={{0,2},{2,0},{4,6},{6,4},{1,3},{3,1},{5,7},{7,5},{8,10},{10,8},{12,... | collective-permute-start | bytes 1013768 | tf_op jit(solution)/shard_map/ppermute | solution.py:57
  67.4 15.1 %collective-permute-start.17 = (bf16[256,640]{1,0:T(8,128)(2,1)S(1)}, bf16[256,640]{1,0:T(8,128)(2,1)S(1)}, u32[]{:S(2)}, u32[]{:S(2)}) collective-permute-start(bf16[256,640]{1,0:T(8,128)(2,1)S(1)} %get-tuple-element.124), channel_id=1, source_target_pairs={{0,2},{2,0},{4,6},{6,4},{1,3},{3,1},{5,7},{7,5},{8,10},{10,8},{12,... | collective-permute-start | bytes 983048 | tf_op jit(solution)/shard_map/ppermute | solution.py:57
  71.3 11.3 %collective-permute-start.18 = (bf16[256,640]{1,0:T(8,128)(2,1)S(1)}, bf16[256,640]{1,0:T(8,128)(2,1)S(1)}, u32[]{:S(2)}, u32[]{:S(2)}) collective-permute-start(bf16[256,640]{1,0:T(8,128)(2,1)S(1)} %get-tuple-element.125), channel_id=1, source_target_pairs={{0,6},{2,4},{4,2},{6,0},{1,7},{3,5},{5,3},{7,1},{8,14},{10,12},{12... | collective-permute-start | bytes 983048 | tf_op jit(solution)/shard_map/ppermute | solution.py:57
  77.2 9.0 %collective-permute-start.19 = (bf16[264,640]{1,0:T(8,128)(2,1)S(1)}, bf16[264,640]{1,0:T(8,128)(2,1)S(1)}, u32[]{:S(2)}, u32[]{:S(2)}) collective-permute-start(bf16[264,640]{1,0:T(8,128)(2,1)S(1)} %join.3), channel_id=1, source_target_pairs={{0,2},{2,0},{4,6},{6,4},{1,3},{3,1},{5,7},{7,5},{8,10},{10,8},{12,... | collective-permute-start | bytes 1013768 | tf_op jit(solution)/shard_map/ppermute | solution.py:57
  77.3 10.5 %collective-permute-start.20 = (bf16[264,640]{1,0:T(8,128)(2,1)S(1)}, bf16[264,640]{1,0:T(8,128)(2,1)S(1)}, u32[]{:S(2)}, u32[]{:S(2)}) collective-permute-start(bf16[264,640]{1,0:T(8,128)(2,1)S(1)} %join.2), channel_id=1, source_target_pairs={{0,6},{2,4},{4,2},{6,0},{1,7},{3,5},{5,3},{7,1},{8,14},{10,12},{12... | collective-permute-start | bytes 1013768 | tf_op jit(solution)/shard_map/ppermute | solution.py:57
